TPU v7x, 32 devices: a whole 2x2x4 slice. The times are simulated.
32 devices in a mesh: seq: 4 (over y, x), user: 8 (over z, core).
Axes of the slice: x: 2, y: 2, z: 4, core: 2. Of those that a mesh axis runs over, the one named last changes fastest.
Arguments:
- events: bfloat16 [8, 512, 1536], P('user', 'seq'), may hold values from -6 to 6
- scenario: int32 [8, 512], P('user', 'seq'), may hold values from 0 to 7, as said below
- lengths: int32 [8, 4], P('user'), may hold values from 1 to 256, 512 in all within a row
- offsets: int32 [8, 4], P('user'), may hold values from 0 to 4, as said below
- gain: float32 [1536], replicated, may hold values from 0.1 to 1.9
- w_proj: bfloat16 [8, 1536, 3072], P('user'), may hold values from -0.15625 to 0.15625
- cotangent: bfloat16 [8, 512, 768], P('user', 'seq'), may hold values from -6 to 6
Outputs:
- output: bfloat16 [8, 512, 768], P('user', 'seq')
- grad_events: bfloat16 [8, 512, 1536], P('user', 'seq')
Inputs may be any that keep to these rules, and one draw needn't show every extreme that they name: Among the 128 positions of one device (aligned blocks along a pack), no scenario is named more than 20 times; on every device one scenario is named exactly 20 times, the same one on all devices of one index of seq; the others share the remaining positions as evenly as possible. `offsets`: every pack has a history with 4.
All inputs are finite; a program needn't handle non-finite values.
Results may differ from a plain program's by a relative error of at most 0.009.
Values may be sent and summed in bfloat16 or wider, within the bound.
No kernel may reach another device: no remote copies, remote signals or barrier semaphores. Data moves between devices by JAX's collectives and lax.ppermute only.
A program may use at most 64 MiB of HBM per device.

v0:
```python
import jax
import jax.numpy as jnp
from jax import lax
from jax.sharding import PartitionSpec as P

HEADS = 6
HD = 128
SCEN = 8
MB = 128
CAP = 20
REACH = 4


eps = 1e-05


def passed_along(block, axis, distance):
    devices = range(lax.axis_size(axis))
    route = [(i - distance, i) for i in devices if i - distance in devices]
    return lax.ppermute(block, axis, route)


def silu_slope(pre_value):
    sig_value = jax.nn.sigmoid(pre_value)
    return sig_value * (1.0 + pre_value * (1.0 - sig_value))


def visible_mask(query_pos, key_pos, hist_ends, hist_reach):
    query_hist = jnp.sum((query_pos[:, None] >= hist_ends[None, :]).astype(jnp.int32), axis=1)
    key_hist = jnp.sum((key_pos[:, None] >= hist_ends[None, :]).astype(jnp.int32), axis=1)
    hist_hot = query_hist[:, None] == jnp.arange(hist_ends.shape[0], dtype=jnp.int32)[None, :]
    reach_limit = jnp.sum(jnp.where(hist_hot, hist_reach[None, :], 0), axis=1)
    same_hist = query_hist[:, None] == key_hist[None, :]
    causal = (key_pos[None, :] <= query_pos[:, None]) & (key_pos[None, :] >= 0)
    near_block = query_pos[:, None] // MB - key_pos[None, :] // MB <= reach_limit[:, None]
    return same_hist & causal & near_block


def split_heads(matrix):
    return matrix.reshape(matrix.shape[0], HEADS, HD)


def neighbour(stacked, distance):
    return passed_along(stacked, "seq", distance)


def shards(events, scenario, lengths, offsets, gain, w_proj, cotangent):
    n_seq = lax.axis_size("seq")
    n_user = lax.axis_size("user")
    slice_count = n_user // SCEN
    row_count = events.shape[1]
    feat_count = events.shape[2]
    head_width = HEADS * HD
    seq_index = lax.axis_index("seq")
    score_scale = HD ** (-0.5)
    events_f = events[0].astype(jnp.float32)
    row_inv = lax.rsqrt(jnp.mean(events_f * events_f, axis=1, keepdims=True) + eps)
    normed = (events_f * row_inv * gain[None, :]).astype(jnp.bfloat16)
    scen_ids = scenario[0]
    scen_hot = (scen_ids[:, None] == jnp.arange(SCEN, dtype=jnp.int32)[None, :]).astype(jnp.int32)
    slot_rank = jnp.sum((jnp.cumsum(scen_hot, axis=0) - 1) * scen_hot, axis=1)
    outbox = jnp.zeros((SCEN, CAP, feat_count), jnp.bfloat16).at[scen_ids, slot_rank].set(normed)
    w_local = w_proj[0]
    sendbox = jnp.broadcast_to(outbox[:, None], (SCEN, slice_count, CAP, feat_count)).reshape(
        n_user, CAP, feat_count
    )
    inbound = lax.all_to_all(sendbox, "user", split_axis=0, concat_axis=0, tiled=True)
    pre_slots = jnp.einsum("scd,dp->scp", inbound, w_local, preferred_element_type=jnp.float32)
    proj_slots = jax.nn.silu(pre_slots).astype(jnp.bfloat16)
    returned = lax.all_to_all(proj_slots, "user", split_axis=0, concat_axis=0, tiled=True)
    slice_width = returned.shape[2]
    returned = returned.reshape(SCEN, slice_count, CAP, slice_width)
    projected = returned[scen_ids, :, slot_rank, :].reshape(row_count, slice_count * slice_width)
    gate_u = projected[:, :head_width]
    values = projected[:, head_width : 2 * head_width]
    queries = projected[:, 2 * head_width : 3 * head_width]
    keys_own = projected[:, 3 * head_width :]
    hist_ends = jnp.cumsum(lengths[0])
    hist_reach = offsets[0]
    first_pos = seq_index * row_count
    reach_dev = min(REACH, n_seq - 1)
    local_pos = first_pos + jnp.arange(row_count, dtype=jnp.int32)
    pair_own = jnp.stack([keys_own, values])
    earlier_list = [neighbour(pair_own, distance) for distance in range(reach_dev, 0, -1)]
    window = jnp.concatenate(earlier_list + [pair_own], axis=1)
    key_pos = (
        first_pos - reach_dev * row_count + jnp.arange((reach_dev + 1) * row_count, dtype=jnp.int32)
    )
    mask_tile = visible_mask(local_pos, key_pos, hist_ends, hist_reach)
    window_keys = split_heads(window[0])
    window_values = split_heads(window[1])
    query_heads = split_heads(queries)
    scores = (
        jnp.einsum("qhd,khd->hqk", query_heads, window_keys, preferred_element_type=jnp.float32)
        * score_scale
    )
    weight = jnp.where(mask_tile[None], jax.nn.silu(scores), 0.0).astype(jnp.bfloat16)
    mixed = jnp.einsum(
        "hqk,khd->qhd", weight, window_values, preferred_element_type=jnp.float32
    ).reshape(row_count, head_width)
    row_scale = lax.rsqrt(jnp.mean(mixed * mixed, axis=1, keepdims=True) + eps)
    normed_mix = mixed * row_scale
    gate_f = gate_u.astype(jnp.float32)
    output = (gate_f * normed_mix).astype(jnp.bfloat16)
    cotan_f = cotangent[0].astype(jnp.float32)
    grad_gate = cotan_f * normed_mix
    grad_norm = cotan_f * gate_f
    grad_mixed = (
        row_scale
        * (grad_norm - normed_mix * jnp.mean(grad_norm * normed_mix, axis=1, keepdims=True))
    ).astype(jnp.bfloat16)
    grad_heads = split_heads(grad_mixed)
    grad_att = jnp.einsum(
        "qhd,khd->hqk", grad_heads, window_values, preferred_element_type=jnp.float32
    )
    grad_score = jnp.where(mask_tile[None], grad_att * silu_slope(scores), 0.0).astype(jnp.bfloat16)
    grad_queries = (
        jnp.einsum(
            "hqk,khd->qhd", grad_score, window_keys, preferred_element_type=jnp.float32
        ).reshape(row_count, head_width)
        * score_scale
    )
    own_score = grad_score[:, :, -row_count:]
    own_weight = weight[:, :, -row_count:]
    grad_keys = (
        jnp.einsum("hqk,qhd->khd", own_score, query_heads, preferred_element_type=jnp.float32)
        * score_scale
    )
    grad_values = jnp.einsum(
        "hqk,qhd->khd", own_weight, grad_heads, preferred_element_type=jnp.float32
    )
    pair_query = jnp.stack([queries, grad_mixed])
    later_list = [neighbour(pair_query, -distance) for distance in range(1, reach_dev + 1)]
    later = jnp.concatenate(later_list, axis=1)
    later_pos = first_pos + row_count + jnp.arange(reach_dev * row_count, dtype=jnp.int32)
    later_mask = visible_mask(later_pos, local_pos, hist_ends, hist_reach)
    later_queries = split_heads(later[0])
    later_grads = split_heads(later[1])
    later_scores = (
        jnp.einsum(
            "qhd,khd->hqk", later_queries, split_heads(keys_own), preferred_element_type=jnp.float32
        )
        * score_scale
    )
    later_weight = jnp.where(later_mask[None], jax.nn.silu(later_scores), 0.0).astype(jnp.bfloat16)
    later_att = jnp.einsum(
        "qhd,khd->hqk", later_grads, split_heads(values), preferred_element_type=jnp.float32
    )
    later_score = jnp.where(later_mask[None], later_att * silu_slope(later_scores), 0.0).astype(
        jnp.bfloat16
    )
    grad_keys = (
        grad_keys
        + jnp.einsum("hqk,qhd->khd", later_score, later_queries, preferred_element_type=jnp.float32)
        * score_scale
    )
    grad_values = grad_values + jnp.einsum(
        "hqk,qhd->khd", later_weight, later_grads, preferred_element_type=jnp.float32
    )
    grad_proj = jnp.concatenate(
        [
            grad_gate,
            grad_values.reshape(row_count, head_width),
            grad_queries,
            grad_keys.reshape(row_count, head_width),
        ],
        axis=1,
    ).astype(jnp.bfloat16)
    grad_box = (
        jnp.zeros((SCEN, slice_count, CAP, slice_width), jnp.bfloat16)
        .at[scen_ids, :, slot_rank, :]
        .set(grad_proj.reshape(row_count, slice_count, slice_width))
    )
    grad_inbound = lax.all_to_all(
        grad_box.reshape(n_user, CAP, slice_width), "user", split_axis=0, concat_axis=0, tiled=True
    )
    grad_pre = (grad_inbound.astype(jnp.float32) * silu_slope(pre_slots)).astype(jnp.bfloat16)
    term_slots = jnp.einsum("scp,dp->scd", grad_pre, w_local, preferred_element_type=jnp.float32)
    gathered = lax.all_to_all(
        term_slots.astype(jnp.bfloat16), "user", split_axis=0, concat_axis=0, tiled=True
    ).astype(term_slots.dtype)
    summed = jnp.sum(gathered.reshape(SCEN, slice_count, CAP, feat_count), axis=1)
    grad_normed = summed[scen_ids, slot_rank]
    scaled = grad_normed * gain[None, :]
    normed_f = events_f * row_inv
    grad_events = row_inv * (scaled - normed_f * jnp.mean(scaled * normed_f, axis=1, keepdims=True))
    return (output[None], grad_events.astype(jnp.bfloat16)[None])


def solution(mesh):
    placed = (
        P("user", "seq", None),
        P("user", "seq"),
        P("user", None),
        P("user", None),
        P(),
        P("user", None, None),
        P("user", "seq", None),
    )
    return jax.shard_map(
        shards,
        mesh=mesh,
        in_specs=placed,
        out_specs=(P("user", "seq", None), P("user", "seq", None)),
        check_vma=False,
    )
```

profile of v0, /device:TPU:2, one launch (start us, length us, event | category | flops | bytes accessed | tf_op | source)
XLA Modules:
  0.0 219.4 jit_solution(17313438782347871899)
XLA Ops:
  0.6 1.2 fusion.26
  1.8 0.7 fusion.48
  2.7 0.8 select_reduce_fusion
  3.5 0.7 fusion.57
  4.2 1.2 fusion.24
  5.4 10.1 %scatter_fusion = bf16[8,20,1536]{2,0,1:T(8,128)(2,1)S(1)} fusion(bf16[8,20,1536]{2,0,1:T(8,128)(2,1)S(1)} %broadcast_in_dim.60, s32[128]{0:T(128)S(1)} %get-tuple-element.2, bf16[128,1536]{1,0:T(8,128)(2,1)S(1)} %fusion.24), kind=kCustom, calls=%fused_computation.2 | custom fusion | bytes 1180672 | tf_op jit(solution)/shard_map/scatter | solution.py:62
  15.7 21.4 %all_to_all.20 = bf16[8,20,1536]{2,1,0:T(8,128)(2,1)S(1)} all-to-all(bf16[8,20,1536]{2,1,0:T(8,128)(2,1)S(1)} %copy.95), channel_id=1, replica_groups=mesh['seq'=4,'user'=8] {'user'}, dimensions={0} | all-to-all | bytes 983040 | tf_op jit(solution)/shard_map/all_to_all | solution.py:67
  37.1 7.5 %multiply_convert_fusion.1 = (bf16[8,20,3072]{2,1,0:T(8,128)(2,1)}, f32[8,20,3072]{2,1,0:T(8,128)}) fusion(bf16[8,20,1536]{2,1,0:T(8,128)(2,1)S(1)} %all_to_all.20, bf16[1,1536,3072]{2,1,0:T(8,128)(2,1)} %param.12), kind=kOutput, calls=%fused_computation.10 | convolution fusion | flops 1512407040 | bytes 12877824 | tf_op jit(solution)/shard_map/scd,dp->scp/dot_general | solution.py:68
  44.6 3.7 %all-to-all-start.1 = ((bf16[8,20,3072]{2,1,0:T(8,128)(2,1)}), bf16[8,20,3072]{2,1,0:T(8,128)(2,1)S(1)}, u32[]{:S(2)}, u32[]{:S(2)}) async-start(bf16[8,20,3072]{2,1,0:T(8,128)(2,1)} %get-tuple-element.18), calls=%async_computation.1 | async-start | bytes 2359296 | tf_op jit(solution)/shard_map/all_to_all | solution.py:70
  48.9 0.9 fusion.47
  49.8 27.8 %all-to-all-done.1 = bf16[8,20,3072]{2,1,0:T(8,128)(2,1)S(1)} async-done(((bf16[8,20,3072]{2,1,0:T(8,128)(2,1)}), bf16[8,20,3072]{2,1,0:T(8,128)(2,1)S(1)}, u32[]{:S(2)}, u32[]{:S(2)}) %all-to-all-start.1) | async-done | bytes 983072 | tf_op jit(solution)/shard_map/all_to_all | solution.py:70
  77.6 0.5 copy.96
  78.2 3.1 %gather_fusion = bf16[128,3072]{1,0:T(8,128)(2,1)S(1)} fusion(bf16[8,20,3072]{2,0,1:T(8,128)(2,1)S(1)} %copy.96, s32[128]{0:T(128)S(1)} %bitcast.111), kind=kCustom, calls=%fused_computation | custom fusion | bytes 1573888 | tf_op jit(solution)/shard_map/gather | solution.py:73
  81.4 0.8 pad_maximum_fusion
  82.2 3.4 %collective-permute-start.2 = (bf16[2,128,768]{2,1,0:T(8,128)(2,1)}, bf16[2,128,768]{2,1,0:T(8,128)(2,1)S(1)}, u32[]{:S(2)}, u32[]{:S(2)}) collective-permute-start(bf16[2,128,768]{2,1,0:T(8,128)(2,1)} %pad_maximum_fusion), channel_id=1, source_target_pairs={{0,8},{8,16},{16,24},{1,9},{9,17},{17,25},{2,10},{10,18},{18,26},{... | collective-permute-start | bytes 1179656 | tf_op jit(solution)/shard_map/ppermute | solution.py:20
  85.5 1.3 collective-permute-start.1
  86.9 0.7 collective-permute-start
  87.7 0.8 fusion.40
  88.5 0.8 copy.106
  89.3 0.8 copy.111
  90.3 6.0 %collective-permute-done.2 = bf16[2,128,768]{2,1,0:T(8,128)(2,1)S(1)} collective-permute-done((bf16[2,128,768]{2,1,0:T(8,128)(2,1)}, bf16[2,128,768]{2,1,0:T(8,128)(2,1)S(1)}, u32[]{:S(2)}, u32[]{:S(2)}) %collective-permute-start.2) | collective-permute-done | bytes 393248 | tf_op jit(solution)/shard_map/ppermute | solution.py:20
  96.2 7.5 %collective-permute-done.1 = bf16[2,128,768]{2,1,0:T(8,128)(2,1)S(1)} collective-permute-done((bf16[2,128,768]{2,1,0:T(8,128)(2,1)}, bf16[2,128,768]{2,1,0:T(8,128)(2,1)S(1)}, u32[]{:S(2)}, u32[]{:S(2)}) %collective-permute-start.1) | collective-permute-done | bytes 393248 | tf_op jit(solution)/shard_map/ppermute | solution.py:20
  104.5 2.8 %select_convert_fusion.1 = (bf16[6,128,512]{2,1,0:T(8,128)(2,1)S(1)}, f32[6,128,512]{2,1,0:T(8,128)}) fusion(pred[128,512]{1,0:T(8,128)(4,1)} %fusion.40, bf16[128,6,128]{0,2,1:T(8,128)(2,1)S(1)} %bitcast.122, bf16[512,6,128]{0,2,1:T(8,128)(2,1)S(1)} %bitcast.113), kind=kOutput, calls=%fused_computation.14 | convolution fusion | flops 103415808 | bytes 3407872 | tf_op jit(solution)/shard_map/qhd,khd->hqk/dot_general | solution.py:94
  107.3 0.4 fusion.39
  107.7 0.5 copy-done.1
  108.3 1.2 fusion.41
  109.5 1.8 multiply_convert_fusion.3
  111.4 0.8 pad_maximum_fusion.1
  112.2 0.7 collective-permute-start.5
  112.9 1.3 collective-permute-start.4
  114.2 2.8 %collective-permute-start.3 = (bf16[2,128,768]{2,1,0:T(8,128)(2,1)}, bf16[2,128,768]{2,1,0:T(8,128)(2,1)}, u32[]{:S(2)}, u32[]{:S(2)}) collective-permute-start(bf16[2,128,768]{2,1,0:T(8,128)(2,1)} %pad_maximum_fusion.1), channel_id=1, source_target_pairs={{8,0},{16,8},{24,16},{9,1},{17,9},{25,17},{10,2},{18,10},{26,18},{... | collective-permute-start | bytes 1179656 | tf_op jit(solution)/shard_map/ppermute | solution.py:20
  117.1 1.9 fusion.45
  118.9 1.7 select_convert_fusion
  121.1 0.9 fusion.43
  122.1 7.0 %collective-permute-done.3 = bf16[2,128,768]{2,1,0:T(8,128)(2,1)} collective-permute-done((bf16[2,128,768]{2,1,0:T(8,128)(2,1)}, bf16[2,128,768]{2,1,0:T(8,128)(2,1)}, u32[]{:S(2)}, u32[]{:S(2)}) %collective-permute-start.3) | collective-permute-done | bytes 393248 | tf_op jit(solution)/shard_map/ppermute | solution.py:20
  129.1 1.0 constant_dynamic-update-slice_fusion.2
  130.2 4.6 %collective-permute-done.4 = bf16[2,128,768]{2,1,0:T(8,128)(2,1)} collective-permute-done((bf16[2,128,768]{2,1,0:T(8,128)(2,1)}, bf16[2,128,768]{2,1,0:T(8,128)(2,1)}, u32[]{:S(2)}, u32[]{:S(2)}) %collective-permute-start.4) | collective-permute-done | bytes 393248 | tf_op jit(solution)/shard_map/ppermute | solution.py:20
  134.8 1.0 constant_dynamic-update-slice_fusion.1
  137.4 1.2 fusion.19
  138.6 1.1 copy.114
  139.7 1.9 fusion.18
  141.9 15.4 %scatter_fusion.1 = bf16[8,20,3072]{2,0,1:T(8,128)(2,1)S(1)} fusion(bf16[8,20,3072]{2,0,1:T(8,128)(2,1)S(1)} %broadcast.574, s32[128]{0:T(128)S(1)} %get-tuple-element.2, bf16[128,3072]{1,0:T(8,128)(2,1)S(1)} %maximum_bitcast_fusion), kind=kCustom, calls=%fused_computation.3 | custom fusion | bytes 2360320 | tf_op jit(solution)/shard_map/scatter | solution.py:172
  157.3 0.6 copy.117
  157.8 32.4 %all_to_all.21 = bf16[8,20,3072]{2,1,0:T(8,128)(2,1)S(1)} all-to-all(bf16[8,20,3072]{2,1,0:T(8,128)(2,1)S(1)} %copy.117), channel_id=1, replica_groups=mesh['seq'=4,'user'=8] {'user'}, dimensions={0} | all-to-all | bytes 1966080 | tf_op jit(solution)/shard_map/all_to_all | solution.py:174
  190.2 7.1 %fusion.4 = bf16[8,20,1536]{2,1,0:T(8,128)(2,1)S(1)} fusion(bf16[1,1536,3072]{2,1,0:T(8,128)(2,1)} %param.12, f32[8,20,3072]{2,1,0:T(8,128)S(1)} %copy-done.10, bf16[8,20,3072]{2,1,0:T(8,128)(2,1)S(1)} %all_to_all.21), kind=kOutput, calls=%fused_computation.8 | convolution fusion | flops 1515110400 | bytes 12877824 | tf_op jit(solution)/shard_map/scp,dp->scd/dot_general | solution.py:178
  197.3 19.1 %all_to_all.22 = bf16[8,20,1536]{2,1,0:T(8,128)(2,1)S(1)} all-to-all(bf16[8,20,1536]{2,1,0:T(8,128)(2,1)S(1)} %fusion.4), channel_id=1, replica_groups=mesh['seq'=4,'user'=8] {'user'}, dimensions={0} | all-to-all | bytes 983040 | tf_op jit(solution)/shard_map/all_to_all | solution.py:179
  216.6 1.4 gather_fusion.1
  218.3 1.0 fusion.30
  (61 shorter events, 5.2 us)
Async XLA Ops:
  44.6 3.7 %copy-start.8 = (s32[1,4]{1,0:T(1,128)S(1)}, s32[1,4]{1,0:T(1,128)}, u32[]{:S(2)}) copy-start(s32[1,4]{1,0:T(1,128)} %param.9) | copy-start | bytes 52
  44.6 4.0 %copy-start.7 = (s32[1,4]{1,0:T(1,128)S(1)}, s32[1,4]{1,0:T(1,128)}, u32[]{:S(2)}) copy-start(s32[1,4]{1,0:T(1,128)} %param.10) | copy-start | bytes 52
  44.6 33.0 %all-to-all-start.1 = ((bf16[8,20,3072]{2,1,0:T(8,128)(2,1)}), bf16[8,20,3072]{2,1,0:T(8,128)(2,1)S(1)}, u32[]{:S(2)}, u32[]{:S(2)}) async-start(bf16[8,20,3072]{2,1,0:T(8,128)(2,1)} %get-tuple-element.18), calls=%async_computation.1 | async-start | bytes 2359296 | tf_op jit(solution)/shard_map/all_to_all | solution.py:70
  82.2 14.1 %collective-permute-start.2 = (bf16[2,128,768]{2,1,0:T(8,128)(2,1)}, bf16[2,128,768]{2,1,0:T(8,128)(2,1)S(1)}, u32[]{:S(2)}, u32[]{:S(2)}) collective-permute-start(bf16[2,128,768]{2,1,0:T(8,128)(2,1)} %pad_maximum_fusion), channel_id=1, source_target_pairs={{0,8},{8,16},{16,24},{1,9},{9,17},{17,25},{2,10},{10,18},{18,26},{... | collective-permute-start | bytes 1179656 | tf_op jit(solution)/shard_map/ppermute | solution.py:20
  85.5 18.1 %collective-permute-start.1 = (bf16[2,128,768]{2,1,0:T(8,128)(2,1)}, bf16[2,128,768]{2,1,0:T(8,128)(2,1)S(1)}, u32[]{:S(2)}, u32[]{:S(2)}) collective-permute-start(bf16[2,128,768]{2,1,0:T(8,128)(2,1)} %pad_maximum_fusion), channel_id=1, source_target_pairs={{0,16},{8,24},{1,17},{9,25},{2,18},{10,26},{3,19},{11,27},{4,20},{... | collective-permute-start | bytes 1179656 | tf_op jit(solution)/shard_map/ppermute | solution.py:20
  86.9 16.8 %collective-permute-start = (bf16[2,128,768]{2,1,0:T(8,128)(2,1)}, bf16[2,128,768]{2,1,0:T(8,128)(2,1)S(1)}, u32[]{:S(2)}, u32[]{:S(2)}) collective-permute-start(bf16[2,128,768]{2,1,0:T(8,128)(2,1)} %pad_maximum_fusion), channel_id=1, source_target_pairs={{0,24},{1,25},{2,26},{3,27},{4,28},{5,29},{6,30},{7,31}} | collective-permute-start | bytes 1179656 | tf_op jit(solution)/shard_map/ppermute | solution.py:20
  107.3 0.9 copy-start.1
  111.4 7.5 %copy-start.9 = (f32[6,128,512]{2,1,0:T(8,128)S(1)}, f32[6,128,512]{2,1,0:T(8,128)}, u32[]{:S(2)}) copy-start(f32[6,128,512]{2,1,0:T(8,128)} %get-tuple-element.21) | copy-start | bytes 4718596
  112.2 23.6 %collective-permute-start.5 = (bf16[2,128,768]{2,1,0:T(8,128)(2,1)}, bf16[2,128,768]{2,1,0:T(8,128)(2,1)S(1)}, u32[]{:S(2)}, u32[]{:S(2)}) collective-permute-start(bf16[2,128,768]{2,1,0:T(8,128)(2,1)} %pad_maximum_fusion.1), channel_id=1, source_target_pairs={{24,0},{25,1},{26,2},{27,3},{28,4},{29,5},{30,6},{31,7}} | collective-permute-start | bytes 1179656 | tf_op jit(solution)/shard_map/ppermute | solution.py:20
  112.9 21.9 %collective-permute-start.4 = (bf16[2,128,768]{2,1,0:T(8,128)(2,1)}, bf16[2,128,768]{2,1,0:T(8,128)(2,1)}, u32[]{:S(2)}, u32[]{:S(2)}) collective-permute-start(bf16[2,128,768]{2,1,0:T(8,128)(2,1)} %pad_maximum_fusion.1), channel_id=1, source_target_pairs={{16,0},{24,8},{17,1},{25,9},{18,2},{26,10},{19,3},{27,11},{20,4},{... | collective-permute-start | bytes 1179656 | tf_op jit(solution)/shard_map/ppermute | solution.py:20
  114.2 14.9 %collective-permute-start.3 = (bf16[2,128,768]{2,1,0:T(8,128)(2,1)}, bf16[2,128,768]{2,1,0:T(8,128)(2,1)}, u32[]{:S(2)}, u32[]{:S(2)}) collective-permute-start(bf16[2,128,768]{2,1,0:T(8,128)(2,1)} %pad_maximum_fusion.1), channel_id=1, source_target_pairs={{8,0},{16,8},{24,16},{9,1},{17,9},{25,17},{10,2},{18,10},{26,18},{... | collective-permute-start | bytes 1179656 | tf_op jit(solution)/shard_map/ppermute | solution.py:20
  135.9 0.9 copy-start.2
  136.3 1.0 copy-start.3
  136.6 0.9 copy-start.6
  137.4 2.3 %copy-start.4 = (bf16[128,768]{0,1:T(8,128)(2,1)S(1)}, bf16[128,768]{0,1:T(8,128)(2,1)}, u32[]{:S(2)}) copy-start(bf16[128,768]{0,1:T(8,128)(2,1)} %copy.111) | copy-start | bytes 589828
  157.8 32.4 %copy-start.10 = (f32[8,20,3072]{2,1,0:T(8,128)S(1)}, f32[8,20,3072]{2,1,0:T(8,128)}, u32[]{:S(2)}) copy-start(f32[8,20,3072]{2,1,0:T(8,128)} %get-tuple-element.19) | copy-start | bytes 5898244
  216.6 1.4 copy-start
  216.6 1.4 copy-start.5
where the time goes:
time: 221 us; the launch traced here: 219 us
  blocking collectives  72.9 us (33%)
  waiting for transfers between devices  52.9 us (24%)
  local copies, waits for them, and re-layouts  39.3 us (18%)
  matrix products  26.1 us (12%)
  starting transfers between devices  13.9 us (6%)
  other arithmetic  13.3 us (6%)
    all_to_all x1, blocking collectives, shards(): lax.all_to_all(grad_box.reshape(n_user, CAP, slice_width), 'user', split_...  32.4 us
    all_to_all x1, waiting for transfers between devices, shards(): lax.all_to_all(proj_slots, 'user', split_axis=0, concat_axis=0, tiled=True)  27.8 us
    ppermute x6, waiting for transfers between devices, passed_along(): return lax.ppermute(block, axis, route)  25.1 us
    all_to_all x1, blocking collectives, shards(): lax.all_to_all(sendbox, 'user', split_axis=0, concat_axis=0, tiled=True)  21.4 us
    all_to_all x1, blocking collectives, shards(): lax.all_to_all(term_slots.astype(jnp.bfloat16), 'user', split_axis=0, con...  19.1 us
    scatter x2, local copies, waits for them, and re-layouts, shards(): grad_box = jnp.zeros((SCEN, slice_count, CAP, slice_width), jnp.bfloat16)...  15.9 us
    scatter x2, local copies, waits for them, and re-layouts, shards(): jnp.zeros((SCEN, CAP, feat_count), jnp.bfloat16).at[scen_ids, slot_rank]  10.3 us
    ppermute x6, starting transfers between devices, passed_along(): return lax.ppermute(block, axis, route)  10.2 us
  transfers between devices with their start and end apart: 7, of which 5 were waited for; matrix products, arithmetic and copies ran while one was open for 5% of the time, Pallas kernels for 0%

commit v1 on v0

v1 whole, which is shorter than its diff:
```python
import functools

import jax
import jax.numpy as jnp
from jax import lax
from jax.experimental import pallas as pl
from jax.experimental.pallas import tpu as pltpu
from jax.sharding import PartitionSpec as P

HEADS = 6
HD = 128
SCEN = 8
MB = 128
CAP = 20
REACH = 4

MAIN = 16
EXTRA = CAP - MAIN
FOLD = MAIN // EXTRA

eps = 1e-05
f32 = jnp.float32
bf16 = jnp.bfloat16
NT = (((1,), (1,)), ((), ()))


def whole(count):
    return [pl.BlockSpec(memory_space=pltpu.VMEM) for _ in range(count)]


def call(kernel, outs, operands, name, flops=1 << 24, smem=0, limit=None):
    specs = whole(len(operands) - smem) + [
        pl.BlockSpec(memory_space=pltpu.SMEM) for _ in range(smem)
    ]
    moved = sum(o.size * o.dtype.itemsize for o in list(outs) + list(operands))
    return pl.pallas_call(
        kernel,
        out_shape=tuple(outs),
        in_specs=specs,
        out_specs=tuple(whole(len(outs))),
        name=name,
        cost_estimate=pl.CostEstimate(flops=flops, bytes_accessed=moved, transcendentals=0),
        compiler_params=pltpu.CompilerParams(vmem_limit_bytes=limit or (24 << 20)),
    )(*operands)


def shape(dims, dtype):
    return jax.ShapeDtypeStruct(dims, dtype)


def dot(a, b):
    return jnp.dot(a, b, preferred_element_type=f32)


def dot_nt(a, b):
    return lax.dot_general(a, b, NT, preferred_element_type=f32)


def sigmoid(v):
    return 0.5 * jnp.tanh(0.5 * v) + 0.5


def iotas(rows, cols):
    return (
        lax.broadcasted_iota(jnp.int32, (rows, cols), 0),
        lax.broadcasted_iota(jnp.int32, (rows, cols), 1),
    )


def hot(condition):
    return jnp.where(condition, 1.0, 0.0).astype(bf16)


def slot_matrices(scen_row, by_slot):
    rows = scen_row.shape[1]
    down, along = iotas(rows, rows)
    scen_b = jnp.broadcast_to(scen_row.astype(f32), (rows, rows))
    scen_col = jnp.sum(jnp.where(down == along, scen_b, 0.0), axis=1, keepdims=True)
    same = scen_b == scen_col
    if by_slot:
        scen = scen_row.astype(f32)
        rank = jnp.sum(jnp.where(same & (down < along), 1.0, 0.0), axis=0, keepdims=True)
        down, along = iotas(SCEN * MAIN, rows)
        slot = down.astype(f32)
    else:
        scen = scen_col
        rank = jnp.sum(jnp.where(same & (along < down), 1.0, 0.0), axis=1, keepdims=True)
        down, along = iotas(rows, SCEN * MAIN)
        slot = along.astype(f32)
    main = jnp.where(rank < MAIN, scen * MAIN + rank, -1.0)
    out = [hot(slot == main)]
    for piece in range(FOLD):
        extra = jnp.where(rank >= MAIN, scen * MAIN + EXTRA * piece + (rank - MAIN), -1.0)
        out.append(hot(slot == extra))
    return out


def to_slots(matrices, value, wire_ref):
    cols = value.shape[1]
    piece = cols // FOLD
    wire_ref[:, :cols] = dot(matrices[0], value).astype(bf16)
    extra = dot(matrices[1], value[:, :piece])
    for part in range(1, FOLD):
        extra = extra + dot(matrices[1 + part], value[:, part * piece : (part + 1) * piece])
    wire_ref[:, cols:] = extra.astype(bf16)


def from_slots(matrices, wire_ref):
    cols = wire_ref.shape[1] * FOLD // (FOLD + 1)
    piece = cols // FOLD
    extra = wire_ref[:, cols:]
    out = []
    for part in range(FOLD):
        left = jnp.concatenate([matrices[0], matrices[1 + part]], axis=1)
        right = jnp.concatenate([wire_ref[:, part * piece : (part + 1) * piece], extra], axis=0)
        out.append(dot(left, right))
    return jnp.concatenate(out, axis=1)


def parts_to_slots(slots_ref, parts, wires):
    matrices = [slots_ref[i] for i in range(1 + FOLD)]
    if len(wires) == 1:
        parts = [jnp.concatenate(parts, axis=1)]
    for part, wire_ref in zip(parts, wires):
        to_slots(matrices, part, wire_ref)


def extra_matrix(count, part, by_row):
    if by_row:
        down, along = iotas(count * EXTRA, count * MAIN)
    else:
        along, down = iotas(count * MAIN, count * EXTRA)
    group = sum((down >= EXTRA * i).astype(jnp.int32) for i in range(1, count))
    return hot(along == down + group * (MAIN - EXTRA) + EXTRA * part)


def unfold(wire_ref):
    count = wire_ref.shape[0] // MAIN
    cols = wire_ref.shape[1] * FOLD // (FOLD + 1)
    extra = wire_ref[:, cols:]
    pieces = [dot(extra_matrix(count, part, True), extra) for part in range(FOLD)]
    return jnp.concatenate([wire_ref[:, :cols], jnp.concatenate(pieces, axis=1).astype(bf16)], axis=0)


def fold(value, wire_ref):
    rows, cols = wire_ref.shape[0], value.shape[1]
    count = rows // MAIN
    piece = cols // FOLD
    wire_ref[:, :cols] = value[:rows]
    extra = sum(
        dot(extra_matrix(count, part, False), value[rows:, part * piece : (part + 1) * piece])
        for part in range(FOLD)
    )
    wire_ref[:, cols:] = extra.astype(bf16)


def enter_kernel(events_ref, gain_ref, scen_ref, wire_ref, slots_ref):
    events = events_ref[...].astype(f32)
    row_inv = lax.rsqrt(jnp.mean(events * events, axis=1, keepdims=True) + eps)
    normed = (events * row_inv * gain_ref[...]).astype(bf16)
    matrices = slot_matrices(scen_ref[...], True)
    for i, matrix in enumerate(matrices):
        slots_ref[i] = matrix
    to_slots(matrices, normed, wire_ref)


def history_of(pos, ends):
    return sum((pos >= end).astype(jnp.int32) for end in ends)


def limit_of(history, limits):
    return sum(jnp.where(history == i, limit, 0) for i, limit in enumerate(limits))


def mask_kernel(blocks, scen_ref, lengths_ref, offsets_ref, first_ref, rows_ref, see_ref, seen_ref):
    for i, matrix in enumerate(slot_matrices(scen_ref[...], False)):
        rows_ref[i] = matrix
    rows = see_ref.shape[0]
    ends, total = [], 0
    for i in range(lengths_ref.shape[1]):
        total = total + lengths_ref[0, i]
        ends.append(total)
    limits = [offsets_ref[0, i] for i in range(offsets_ref.shape[1])]
    first = first_ref[0]
    shift = MB.bit_length() - 1

    def visible(query, key):
        query_hist, key_hist = history_of(query, ends), history_of(key, ends)
        near = (query >> shift) - (key >> shift) <= limit_of(query_hist, limits)
        return jnp.where((query_hist == key_hist) & (key <= query) & (key >= 0) & near, 1.0, 0.0)

    down = lax.broadcasted_iota(jnp.int32, (rows, rows), 0)
    along = lax.broadcasted_iota(jnp.int32, (rows, rows), 1)
    for block in range(blocks):
        span = slice(block * rows, (block + 1) * rows)
        see_ref[:, span] = visible(first + down, first - block * rows + along)
        seen_ref[:, span] = visible(first + block * rows + along, first + down)


def project_kernel(parts, wire_ref, w_ref, out_ref, slope_ref):
    rows = unfold(wire_ref)
    width = HEADS * HD
    done = []
    for i, part in enumerate(parts):
        pre = dot(rows, w_ref[:, part * width : (part + 1) * width])
        sig = sigmoid(pre)
        slope_ref[:, i * width : (i + 1) * width] = sig * (1.0 + pre * (1.0 - sig))
        done.append((pre * sig).astype(bf16))
    fold(jnp.concatenate(done, axis=1), out_ref)


def rows_kernel(wire_ref, rows_ref, out_ref):
    matrices = [rows_ref[i] for i in range(1 + FOLD)]
    out_ref[...] = from_slots(matrices, wire_ref).astype(bf16)


def head_cols(head, part=0):
    start = (part * HEADS + head) * HD
    return slice(start, start + HD)


def forward_kernel(blocks, see_ref, gq_ref, cotan_ref, *refs):
    pairs, (out_ref, grad_ref, gate_ref, mixed_ref) = refs[:blocks], refs[blocks:]
    rows = gq_ref.shape[0]
    scale = HD ** (-0.5)
    total = jnp.zeros((rows, 1), f32)
    for head in range(HEADS):
        query = gq_ref[:, head_cols(head, 1)]
        mixed = jnp.zeros((rows, HD), f32)
        for block in range(blocks):
            score = dot_nt(query, pairs[block][:, head_cols(head, 1)]) * scale
            weight = score * sigmoid(score) * see_ref[:, block * rows : (block + 1) * rows]
            mixed = mixed + dot(weight.astype(bf16), pairs[block][:, head_cols(head)])
        mixed_ref[:, head_cols(head)] = mixed
        total = total + jnp.sum(mixed * mixed, axis=1, keepdims=True)
    width = HEADS * HD
    row_scale = lax.rsqrt(total / width + eps)
    normed = mixed_ref[...] * row_scale
    gate = gq_ref[:, :width].astype(f32)
    cotan = cotan_ref[...].astype(f32)
    grad_norm = cotan * gate
    mean = jnp.mean(grad_norm * normed, axis=1, keepdims=True)
    grad_ref[...] = (row_scale * (grad_norm - normed * mean)).astype(bf16)
    out_ref[...] = (gate * normed).astype(bf16)
    gate_ref[...] = (cotan * normed).astype(bf16)


def slope_of(score):
    sig = sigmoid(score)
    return sig, sig * (1.0 + score * (1.0 - sig))


def query_kernel(blocks, see_ref, gq_ref, grad_ref, gate_ref, slots_ref, *refs):
    pairs, wires = refs[:blocks], refs[blocks:]
    rows = gq_ref.shape[0]
    scale = HD ** (-0.5)
    done = []
    for head in range(HEADS):
        query = gq_ref[:, head_cols(head, 1)]
        grad = grad_ref[:, head_cols(head)]
        grad_query = jnp.zeros((rows, HD), f32)
        for block in range(blocks):
            key = pairs[block][:, head_cols(head, 1)]
            score = dot_nt(query, key) * scale
            _, slope = slope_of(score)
            att = dot_nt(grad, pairs[block][:, head_cols(head)])
            grad_score = att * slope * see_ref[:, block * rows : (block + 1) * rows]
            grad_query = grad_query + dot(grad_score.astype(bf16), key)
        done.append((grad_query * scale).astype(bf16))
    parts_to_slots(slots_ref, [gate_ref[...], jnp.concatenate(done, axis=1)], wires)


def key_kernel(blocks, seen_ref, pair_ref, slots_ref, *refs):
    queries, grads, wires = refs[:blocks], refs[blocks : 2 * blocks], refs[2 * blocks :]
    rows = pair_ref.shape[0]
    scale = HD ** (-0.5)
    grad_keys, grad_values = [], []
    for head in range(HEADS):
        key = pair_ref[:, head_cols(head, 1)]
        value = pair_ref[:, head_cols(head)]
        grad_key = jnp.zeros((rows, HD), f32)
        grad_value = jnp.zeros((rows, HD), f32)
        for block in range(blocks):
            mask = seen_ref[:, block * rows : (block + 1) * rows]
            query = queries[block][:, head_cols(head, 1 if block == 0 else 0)]
            grad = grads[block][:, head_cols(head)]
            score = dot_nt(key, query) * scale
            sig, slope = slope_of(score)
            weight = score * sig * mask
            grad_score = dot_nt(value, grad) * slope * mask
            grad_key = grad_key + dot(grad_score.astype(bf16), query)
            grad_value = grad_value + dot(weight.astype(bf16), grad)
        grad_keys.append((grad_key * scale).astype(bf16))
        grad_values.append(grad_value.astype(bf16))
    parts = [jnp.concatenate(one, axis=1) for one in (grad_values, grad_keys)]
    parts_to_slots(slots_ref, parts, wires)


def owner_term(parts, wire_ref, slope_ref, w_ref):
    width = HEADS * HD
    grad_pre = (unfold(wire_ref).astype(f32) * slope_ref[...]).astype(bf16)
    term = None
    for i, part in enumerate(parts):
        one = dot_nt(
            grad_pre[:, i * width : (i + 1) * width], w_ref[:, part * width : (part + 1) * width]
        )
        term = one if term is None else term + one
    return term


def term_kernel(parts, wire_ref, slope_ref, w_ref, out_ref):
    out_ref[...] = owner_term(parts, wire_ref, slope_ref, w_ref)


def last_term_kernel(parts, wire_ref, slope_ref, w_ref, *refs):
    term = owner_term(parts, wire_ref, slope_ref, w_ref)
    for other_ref in refs[:-1]:
        term = term + other_ref[...]
    fold(term.astype(bf16), refs[-1])


def leave_kernel(rows_ref, events_ref, gain_ref, *refs):
    wires, out_ref = refs[:-1], refs[-1]
    matrices = [rows_ref[i] for i in range(1 + FOLD)]
    scaled = sum(from_slots(matrices, wire_ref) for wire_ref in wires) * gain_ref[...]
    events = events_ref[...].astype(f32)
    row_inv = lax.rsqrt(jnp.mean(events * events, axis=1, keepdims=True) + eps)
    normed = events * row_inv
    mean = jnp.mean(scaled * normed, axis=1, keepdims=True)
    out_ref[...] = (row_inv * (scaled - normed * mean)).astype(bf16)


def exchange(wire):
    blocks = wire.reshape(-1, MAIN, wire.shape[1])
    done = lax.all_to_all(blocks, "user", split_axis=0, concat_axis=0, tiled=True)
    return done.reshape(wire.shape)


def shifted(block, distance):
    devices = range(lax.axis_size("seq"))
    route = [(i - distance, i) for i in devices if i - distance in devices]
    return lax.ppermute(block, "seq", route)


def wires_of(split, boxes):
    if split == 1:
        return boxes[0]
    cols = boxes[0].shape[1]
    return jnp.stack([box.reshape(SCEN, MAIN, cols) for box in boxes], axis=1).reshape(-1, cols)


def slices_of(split, box):
    if split == 1:
        return [box]
    cols = box.shape[1]
    blocks = box.reshape(SCEN, split, MAIN, cols)
    return [blocks[:, i].reshape(-1, cols) for i in range(split)]


def shards(events, scenario, lengths, offsets, gain, w_proj, cotangent):
    n_seq = lax.axis_size("seq")
    n_user = lax.axis_size("user")
    split = n_user // SCEN
    rows, feats = events.shape[1:]
    width = HEADS * HD
    longest = n_seq * rows // 2
    reach = min(REACH, n_seq - 1, (longest - 2) // rows + 1)
    blocks = reach + 1
    slots = SCEN * MAIN

    def wire(senders, cols):
        return shape((senders * MAIN, cols * (FOLD + 1) // FOLD), bf16)

    matrices = shape((1 + FOLD, rows, slots), bf16)
    events, w_local, cotan = events[0], w_proj[0], cotangent[0]
    gain = gain[None]
    first = (lax.axis_index("seq") * rows).astype(jnp.int32)[None]

    outbox, to_slot = call(
        enter_kernel, [wire(SCEN, feats), matrices], [events, gain, scenario], "enter"
    )
    inbound = exchange(wires_of(split, [outbox] * split))
    to_row, see, seen = call(
        functools.partial(mask_kernel, blocks),
        [matrices] + [shape((rows, blocks * rows), f32)] * 2,
        [scenario, lengths, offsets, first],
        "masks",
        smem=3,
    )

    def project(parts, name):
        cols = len(parts) * width
        return call(
            functools.partial(project_kernel, parts),
            [wire(n_user, cols), shape((n_user * CAP, cols), f32)],
            [inbound, w_local],
            name,
        )

    def rows_of(box, name):
        cols = box.shape[1] * FOLD // (FOLD + 1)
        return call(rows_kernel, [shape((rows, cols), bf16)], [box, to_row], name)[0]

    together = split == 1
    if together:
        pair_parts, query_parts = (1, 3), (0, 2)
        pair_box, pair_slope = project(pair_parts, "pair")
        pair_back = exchange(pair_box)
        query_box, query_slope = project(query_parts, "query")
        pair_own = rows_of(pair_back, "pairs")
        pairs = [pair_own] + [shifted(pair_own, d) for d in range(1, blocks)]
        gq = rows_of(exchange(query_box), "queries")
    else:
        box, slope = project((0,), "all")
        gate, value, query, key = [
            rows_of(part, "part") for part in slices_of(split, exchange(box))
        ]
        pair_own = jnp.concatenate([value, key], axis=1)
        gq = jnp.concatenate([gate, query], axis=1)
        pairs = [pair_own] + [shifted(pair_own, d) for d in range(1, blocks)]
    query_own = gq[:, width:]
    queries = [gq] + [shifted(query_own, -d) for d in range(1, blocks)]
    half = shape((rows, width), bf16)
    output, grad_own, grad_gate, _ = call(
        functools.partial(forward_kernel, blocks),
        [half, half, half, shape((rows, width), f32)],
        [see, gq, cotan] + pairs,
        "forward",
    )
    grads = [grad_own] + [shifted(grad_own, -d) for d in range(1, blocks)]
    boxes = [wire(SCEN, 2 * width)] if together else [wire(SCEN, width)] * 2
    query_grad = call(
        functools.partial(query_kernel, blocks),
        boxes,
        [see, gq, grad_own, grad_gate, to_slot] + pairs,
        "query_grad",
    )
    if together:
        query_grad = exchange(query_grad[0])
    pair_grad = call(
        functools.partial(key_kernel, blocks),
        boxes,
        [seen, pair_own, to_slot] + queries + grads,
        "pair_grad",
    )
    term = shape((n_user * CAP, feats), f32)
    if together:
        pair_grad = exchange(pair_grad[0])
        (query_term,) = call(
            functools.partial(term_kernel, query_parts),
            [term],
            [query_grad, query_slope, w_local],
            "term",
        )
        last_parts, last = pair_parts, [pair_grad, pair_slope, w_local, query_term]
    else:
        order = [query_grad[0], pair_grad[0], query_grad[1], pair_grad[1]]
        last_parts, last = (0,), [exchange(wires_of(split, order)), slope, w_local]
    (term_box,) = call(
        functools.partial(last_term_kernel, last_parts), [wire(n_user, feats)], last, "last_term"
    )
    (grad_events,) = call(
        leave_kernel,
        [shape((rows, feats), bf16)],
        [to_row, events, gain] + slices_of(split, exchange(term_box)),
        "leave",
    )
    return output[None], grad_events[None]


def solution(mesh):
    placed = (
        P("user", "seq", None),
        P("user", "seq"),
        P("user", None),
        P("user", None),
        P(),
        P("user", None, None),
        P("user", "seq", None),
    )
    return jax.shard_map(
        shards,
        mesh=mesh,
        in_specs=placed,
        out_specs=(P("user", "seq", None), P("user", "seq", None)),
        check_vma=False,
    )
```

time: 221 us -> 158 us (0.71)
  blocking collectives: 72.9 us -> 36.3 us
  matrix products: 26.1 us -> 0 us
  starting transfers between devices: 13.9 us -> 36.1 us
  Pallas kernels: 0 us -> 21 us
  local copies, waits for them, and re-layouts: 39.3 us -> 23.3 us
  other arithmetic: 13.3 us -> 0 us
  waiting for transfers between devices: 52.9 us -> 39.9 us
    all_to_all x3 -> x2, blocking collectives: 72.9 us -> 36.3 us  [exchange(): lax.all_to_all(blocks, 'user', split_axis=0, concat_axis=0, tiled=True)]
    scatter x4 -> x0, local copies, waits for them, and re-layouts: 26.2 us -> none  [the longest x2 15.9 us: shards(): grad_box = jnp.zeros((SCEN, slice_count, CAP, slice_width), jnp.bfloat16)...]
    dot_general x11 -> x0, matrix products: 26.1 us -> none  [the longest x1 7.51 us: shards(): jnp.einsum('scd,dp->scp', inbound, w_local, preferred_element_type=jnp.fl...]
    pallas_call x0 -> x12, Pallas kernels: none -> 21 us  [call(): pl.pallas_call(kernel, out_shape=tuple(outs), in_specs=specs, out_specs=t...]
    unnamed x24 -> x36, local copies, waits for them, and re-layouts: 3.04 us -> 22.6 us
    all_to_all x1 -> x4, starting transfers between devices: 3.69 us -> 16.4 us  [exchange(): lax.all_to_all(blocks, 'user', split_axis=0, concat_axis=0, tiled=True)]
    ppermute x6, starting transfers between devices: 10.2 us -> 19.7 us  [shifted(): return lax.ppermute(block, 'seq', route)]
    ppermute x6, waiting for transfers between devices: 25.1 us -> 16 us  [shifted(): return lax.ppermute(block, 'seq', route)]
  transfers between devices with their start and end apart: 7 -> 10, of which waited for: 5 -> 7; matrix products, arithmetic and copies ran while one was open for 5% -> 0% of each run, Pallas kernels for 0% -> 6%
where the time goes in v1:
time: 158 us; the launch traced here: 157 us
  waiting for transfers between devices  39.9 us (25%)
  blocking collectives  36.3 us (23%)
  starting transfers between devices  36.1 us (23%)
  local copies, waits for them, and re-layouts  23.3 us (15%)
  Pallas kernels  21 us (13%)
    all_to_all x2, blocking collectives, exchange(): lax.all_to_all(blocks, 'user', split_axis=0, concat_axis=0, tiled=True)  36.3 us
    all_to_all x4, waiting for transfers between devices, exchange(): lax.all_to_all(blocks, 'user', split_axis=0, concat_axis=0, tiled=True)  23.9 us
    unnamed x36, local copies, waits for them, and re-layouts  22.6 us
    pallas_call x12, Pallas kernels, call(): pl.pallas_call(kernel, out_shape=tuple(outs), in_specs=specs, out_specs=t...  21 us
    ppermute x6, starting transfers between devices, shifted(): return lax.ppermute(block, 'seq', route)  19.7 us
    all_to_all x4, starting transfers between devices, exchange(): lax.all_to_all(blocks, 'user', split_axis=0, concat_axis=0, tiled=True)  16.4 us
    ppermute x6, waiting for transfers between devices, shifted(): return lax.ppermute(block, 'seq', route)  16 us
  transfers between devices with their start and end apart: 10, of which 7 were waited for; matrix products, arithmetic and copies ran while one was open for 0% of the time, Pallas kernels for 6%

profile of v1, /device:TPU:2, one launch (start us, length us, event | category | flops | bytes accessed | tf_op | source)
XLA Modules:
  0.0 157.5 jit_solution(5665344498678966559)
XLA Ops:
  0.6 0.7 broadcast_in_dim.13.gain_ref
  1.3 1.0 copy-done.4
  2.3 0.7 copy-done.14
  3.0 0.5 enter.1
  3.5 19.3 %all_to_all.30 = bf16[8,16,1920]{2,1,0:T(8,128)(2,1)S(1)} all-to-all(bf16[8,16,1920]{2,1,0:T(8,128)(2,1)S(1)} %bitcast.32), channel_id=1, replica_groups=mesh['seq'=4,'user'=8] {'user'}, dimensions={0} | all-to-all | bytes 983040 | tf_op jit(solution)/shard_map/all_to_all | solution.py:335
  22.8 3.7 %copy-done = bf16[1,1536,3072]{2,1,0:T(8,128)(2,1)S(1)} copy-done((bf16[1,1536,3072]{2,1,0:T(8,128)(2,1)S(1)}, bf16[1,1536,3072]{2,1,0:T(8,128)(2,1)}, u32[]{:S(2)}) %copy-start) | copy-done | bytes 9437208
  26.5 2.2 %pair.1 = (bf16[128,1920]{1,0:T(8,128)(2,1)}, f32[160,1536]{1,0:T(8,128)S(1)}) custom-call(bf16[128,1920]{1,0:T(8,128)(2,1)S(1)} %bitcast.22, bf16[1536,3072]{1,0:T(8,128)(2,1)S(1)} %bitcast.18), custom_call_target="tpu_custom_call" | custom-call | flops 16777216 | bytes 11403264 | tf_op jit(solution)/shard_map/pair/pallas_call | solution.py:36
  28.7 3.5 %all-to-all-start.2 = ((bf16[8,16,1920]{2,1,0:T(8,128)(2,1)}), bf16[8,16,1920]{2,1,0:T(8,128)(2,1)S(1)}, u32[]{:S(2)}, u32[]{:S(2)}) async-start(bf16[8,16,1920]{2,1,0:T(8,128)(2,1)} %bitcast.8), calls=%async_computation.2 | async-start | bytes 983040 | tf_op jit(solution)/shard_map/all_to_all | solution.py:335
  32.2 0.0 copy-start.1
  32.2 3.7 %copy-done.1 = bf16[1,1536,3072]{2,1,0:T(8,128)(2,1)S(1)} copy-done((bf16[1,1536,3072]{2,1,0:T(8,128)(2,1)S(1)}, bf16[1,1536,3072]{2,1,0:T(8,128)(2,1)}, u32[]{:S(2)}) %copy-start.1) | copy-done | bytes 9437208
  35.9 2.2 %query.1 = (bf16[128,1920]{1,0:T(8,128)(2,1)}, f32[160,1536]{1,0:T(8,128)S(1)}) custom-call(bf16[128,1920]{1,0:T(8,128)(2,1)S(1)} %bitcast.23, bf16[1536,3072]{1,0:T(8,128)(2,1)S(1)} %bitcast.19), custom_call_target="tpu_custom_call" | custom-call | flops 16777216 | bytes 11403264 | tf_op jit(solution)/shard_map/query/pallas_call | solution.py:36
  38.1 1.0 copy-done.6
  39.1 7.7 %all-to-all-done.2 = bf16[8,16,1920]{2,1,0:T(8,128)(2,1)S(1)} async-done(((bf16[8,16,1920]{2,1,0:T(8,128)(2,1)}), bf16[8,16,1920]{2,1,0:T(8,128)(2,1)S(1)}, u32[]{:S(2)}, u32[]{:S(2)}) %all-to-all-start.2) | async-done | bytes 491552 | tf_op jit(solution)/shard_map/all_to_all | solution.py:335
  46.8 3.5 %all-to-all-start.1 = ((bf16[8,16,1920]{2,1,0:T(8,128)(2,1)}), bf16[8,16,1920]{2,1,0:T(8,128)(2,1)S(1)}, u32[]{:S(2)}, u32[]{:S(2)}) async-start(bf16[8,16,1920]{2,1,0:T(8,128)(2,1)} %bitcast.5), calls=%async_computation.1 | async-start | bytes 983040 | tf_op jit(solution)/shard_map/all_to_all | solution.py:335
  50.3 0.9 masks.1
  51.2 0.3 pairs.1.refs_0_.pair_ref
  51.5 0.4 copy-done.11
  51.9 3.4 %collective-permute-start = (bf16[128,1536]{1,0:T(8,128)(2,1)S(1)}, bf16[128,1536]{1,0:T(8,128)(2,1)S(1)}, u32[]{:S(2)}, u32[]{:S(2)}) collective-permute-start(bf16[128,1536]{1,0:T(8,128)(2,1)S(1)} %pairs.1.refs_0_.pair_ref), channel_id=1, source_target_pairs={{0,8},{8,16},{16,24},{1,9},{9,17},{17,25},{2,10},{10,18},{18,26},{... | collective-permute-start | bytes 1179656 | tf_op jit(solution)/shard_map/ppermute | solution.py:342
  55.3 1.3 collective-permute-start.1
  56.6 8.2 %all-to-all-done.1 = bf16[8,16,1920]{2,1,0:T(8,128)(2,1)S(1)} async-done(((bf16[8,16,1920]{2,1,0:T(8,128)(2,1)}), bf16[8,16,1920]{2,1,0:T(8,128)(2,1)S(1)}, u32[]{:S(2)}, u32[]{:S(2)}) %all-to-all-start.1) | async-done | bytes 491552 | tf_op jit(solution)/shard_map/all_to_all | solution.py:335
  64.8 0.3 queries.1.gq_ref.refs_0_
  65.1 0.0 collective-permute-done.refs_1_
  65.2 0.3 collective-permute-done.1.refs_2_
  65.5 0.9 copy-done.13
  66.4 2.4 %forward.1 = (bf16[128,768]{1,0:T(8,128)(2,1)}, bf16[128,768]{1,0:T(8,128)(2,1)S(1)}, bf16[128,768]{1,0:T(8,128)(2,1)S(1)}, f32[128,768]{1,0:T(8,128)}) custom-call(f32[128,384]{1,0:T(8,128)S(1)} %get-tuple-element.14.see_ref, bf16[128,1536]{1,0:T(8,128)(2,1)S(1)} %queries.1.gq_ref.refs_0_, bf16[128,768]{1,0:T(8,128)(2,1)S(1)} %bitcast.33, ...), custom_call_target="tpu_custom_call" | custom-call | flops 16777216 | bytes 2949120 | tf_op jit(solution)/shard_map/forward/pallas_call | solution.py:36
  68.8 0.9 copy-done.9
  69.7 3.4 %query_grad.1 = bf16[128,1920]{1,0:T(8,128)(2,1)} custom-call(f32[128,384]{1,0:T(8,128)S(1)} %get-tuple-element.14.see_ref, bf16[128,1536]{1,0:T(8,128)(2,1)S(1)} %queries.1.gq_ref.refs_0_, bf16[128,768]{1,0:T(8,128)(2,1)S(1)} %get-tuple-element.22.refs_3_.grad_ref, bf16[128,768]{1,0:T(8,128)(2,1)S(1)} %get-tuple-element.24.gate_ref, ...), custom_call_target="tpu_custom_call" | custom-call | flops 16777216 | bytes 2818048 | tf_op jit(solution)/shard_map/query_grad/pallas_call | solution.py:36
  73.1 4.7 %all-to-all-start.4 = ((bf16[8,16,1920]{2,1,0:T(8,128)(2,1)}), bf16[8,16,1920]{2,1,0:T(8,128)(2,1)S(1)}, u32[]{:S(2)}, u32[]{:S(2)}) async-start(bf16[8,16,1920]{2,1,0:T(8,128)(2,1)} %bitcast.13), calls=%async_computation.4 | async-start | bytes 983040 | tf_op jit(solution)/shard_map/all_to_all | solution.py:335
  77.9 10.5 %collective-permute-start.2 = (bf16[128,768]{1,0:T(8,128)(2,1)S(1)}, bf16[128,768]{1,0:T(8,128)(2,1)S(1)}, u32[]{:S(2)}, u32[]{:S(2)}) collective-permute-start(bf16[128,768]{1,0:T(8,128)(2,1)S(1)} %slice.4), channel_id=1, source_target_pairs={{8,0},{16,8},{24,16},{9,1},{17,9},{25,17},{10,2},{18,10},{26,18},{... | collective-permute-start | bytes 589832 | tf_op jit(solution)/shard_map/ppermute | solution.py:342
  88.4 1.3 collective-permute-start.3
  89.7 1.9 %collective-permute-start.4 = (bf16[128,768]{1,0:T(8,128)(2,1)S(1)}, bf16[128,768]{1,0:T(8,128)(2,1)S(1)}, u32[]{:S(2)}, u32[]{:S(2)}) collective-permute-start(bf16[128,768]{1,0:T(8,128)(2,1)S(1)} %get-tuple-element.22.refs_3_.grad_ref), channel_id=1, source_target_pairs={{8,0},{16,8},{24,16},{9,1},{17,9},{25,17},{10,2},{18,10},{26,18},{... | collective-permute-start | bytes 589832 | tf_op jit(solution)/shard_map/ppermute | solution.py:342
  91.6 1.3 collective-permute-start.5
  92.9 3.2 %collective-permute-done.2.refs_1_ = bf16[128,768]{1,0:T(8,128)(2,1)S(1)} collective-permute-done((bf16[128,768]{1,0:T(8,128)(2,1)S(1)}, bf16[128,768]{1,0:T(8,128)(2,1)S(1)}, u32[]{:S(2)}, u32[]{:S(2)}) %collective-permute-start.2) | collective-permute-done | bytes 196640 | tf_op jit(solution)/shard_map/ppermute | solution.py:342
  96.1 8.2 %collective-permute-done.3.refs_2_ = bf16[128,768]{1,0:T(8,128)(2,1)S(1)} collective-permute-done((bf16[128,768]{1,0:T(8,128)(2,1)S(1)}, bf16[128,768]{1,0:T(8,128)(2,1)S(1)}, u32[]{:S(2)}, u32[]{:S(2)}) %collective-permute-start.3) | collective-permute-done | bytes 196640 | tf_op jit(solution)/shard_map/ppermute | solution.py:342
  104.3 4.2 %collective-permute-done.5.refs_5_ = bf16[128,768]{1,0:T(8,128)(2,1)S(1)} collective-permute-done((bf16[128,768]{1,0:T(8,128)(2,1)S(1)}, bf16[128,768]{1,0:T(8,128)(2,1)S(1)}, u32[]{:S(2)}, u32[]{:S(2)}) %collective-permute-start.5) | collective-permute-done | bytes 196640 | tf_op jit(solution)/shard_map/ppermute | solution.py:342
  108.5 0.9 copy-done.10
  109.4 0.9 copy-done.12
  110.3 3.9 %pair_grad.1 = bf16[128,1920]{1,0:T(8,128)(2,1)} custom-call(f32[128,384]{1,0:T(8,128)S(1)} %copy-done.12, bf16[128,1536]{1,0:T(8,128)(2,1)S(1)} %pairs.1.refs_0_.pair_ref, bf16[5,128,128]{2,1,0:T(8,128)(2,1)S(1)} %copy-done.10, bf16[128,1536]{1,0:T(8,128)(2,1)S(1)} %queries.1.gq_ref.refs_0_, bf16[128,768]{1,0:T(8,128)(2,1)S(1)} %collective-permute-done.2.refs_1_, ...), custom_call_target="tpu_custom_call" | custom-call | flops 16777216 | bytes 2621440 | tf_op jit(solution)/shard_map/pair_grad/pallas_call | solution.py:36
  114.2 0.0 all-to-all-done.4
  114.2 4.7 %all-to-all-start.3 = ((bf16[8,16,1920]{2,1,0:T(8,128)(2,1)}), bf16[8,16,1920]{2,1,0:T(8,128)(2,1)S(1)}, u32[]{:S(2)}, u32[]{:S(2)}) async-start(bf16[8,16,1920]{2,1,0:T(8,128)(2,1)} %bitcast.11), calls=%async_computation.3 | async-start | bytes 983040 | tf_op jit(solution)/shard_map/all_to_all | solution.py:335
  118.9 3.7 %copy-done.2 = bf16[1,1536,3072]{2,1,0:T(8,128)(2,1)S(1)} copy-done((bf16[1,1536,3072]{2,1,0:T(8,128)(2,1)S(1)}, bf16[1,1536,3072]{2,1,0:T(8,128)(2,1)}, u32[]{:S(2)}) %copy-start.2) | copy-done | bytes 9437208
  122.6 1.2 copy-done.7
  123.8 1.8 %term.1.refs_0_ = f32[160,1536]{1,0:T(8,128)S(1)} custom-call(bf16[128,1920]{1,0:T(8,128)(2,1)S(1)} %bitcast.24, f32[160,1536]{1,0:T(8,128)S(1)} %copy-done.7, bf16[1536,3072]{1,0:T(8,128)(2,1)S(1)} %bitcast.20), custom_call_target="tpu_custom_call" | custom-call | flops 16777216 | bytes 11894784 | tf_op jit(solution)/shard_map/term/pallas_call | solution.py:36
  125.6 8.0 %all-to-all-done.3 = bf16[8,16,1920]{2,1,0:T(8,128)(2,1)S(1)} async-done(((bf16[8,16,1920]{2,1,0:T(8,128)(2,1)}), bf16[8,16,1920]{2,1,0:T(8,128)(2,1)S(1)}, u32[]{:S(2)}, u32[]{:S(2)}) %all-to-all-start.3) | async-done | bytes 491552 | tf_op jit(solution)/shard_map/all_to_all | solution.py:335
  133.6 3.7 %copy-done.3 = bf16[1,1536,3072]{2,1,0:T(8,128)(2,1)S(1)} copy-done((bf16[1,1536,3072]{2,1,0:T(8,128)(2,1)S(1)}, bf16[1,1536,3072]{2,1,0:T(8,128)(2,1)}, u32[]{:S(2)}) %copy-start.3) | copy-done | bytes 9437208
  137.3 1.9 %last_term.1 = bf16[128,1920]{1,0:T(8,128)(2,1)S(1)} custom-call(bf16[128,1920]{1,0:T(8,128)(2,1)S(1)} %bitcast.27, f32[160,1536]{1,0:T(8,128)S(1)} %get-tuple-element.23.slope_ref, bf16[1536,3072]{1,0:T(8,128)(2,1)S(1)} %bitcast.21, f32[160,1536]{1,0:T(8,128)S(1)} %term.1.refs_0_), custom_call_target="tpu_custom_call" | custom-call | flops 16777216 | bytes 12386304 | tf_op jit(solution)/shard_map/last_term/pallas_call | solution.py:36
  139.2 17.0 %all_to_all.31 = bf16[8,16,1920]{2,1,0:T(8,128)(2,1)S(1)} all-to-all(bf16[8,16,1920]{2,1,0:T(8,128)(2,1)S(1)} %bitcast.28), channel_id=1, replica_groups=mesh['seq'=4,'user'=8] {'user'}, dimensions={0} | all-to-all | bytes 983040 | tf_op jit(solution)/shard_map/all_to_all | solution.py:335
  156.2 1.2 leave.1
  (24 shorter events, 0.1 us)
Async XLA Ops:
  1.3 1.0 copy-start.4
  2.3 0.7 copy-start.14
  3.5 19.3 %copy-start.8 = (bf16[5,128,128]{2,1,0:T(8,128)(2,1)}, bf16[5,128,128]{2,1,0:T(8,128)(2,1)S(1)}, u32[]{:S(2)}) copy-start(bf16[5,128,128]{2,1,0:T(8,128)(2,1)S(1)} %get-tuple-element.21.slots_ref) | copy-start | bytes 491524
  22.8 3.7 %copy-start = (bf16[1,1536,3072]{2,1,0:T(8,128)(2,1)S(1)}, bf16[1,1536,3072]{2,1,0:T(8,128)(2,1)}, u32[]{:S(2)}) copy-start(bf16[1,1536,3072]{2,1,0:T(8,128)(2,1)} %param.12) | copy-start | bytes 28311556
  26.5 23.7 %copy-start.15 = (s32[1,128]{1,0:T(1,128)S(1)}, s32[1,128]{1,0:T(1,128)}, u32[]{:S(2)}) copy-start(s32[1,128]{1,0:T(1,128)} %scen_ref.3) | copy-start | bytes 1540
  26.5 23.7 %copy-start.16 = (s32[1,4]{1,0:T(1,128)S(1)}, s32[1,4]{1,0:T(1,128)}, u32[]{:S(2)}) copy-start(s32[1,4]{1,0:T(1,128)} %lengths_ref.1) | copy-start | bytes 52
  26.5 23.8 %copy-start.17 = (s32[1,4]{1,0:T(1,128)S(1)}, s32[1,4]{1,0:T(1,128)}, u32[]{:S(2)}) copy-start(s32[1,4]{1,0:T(1,128)} %offsets_ref.1) | copy-start | bytes 52
  28.7 18.0 %all-to-all-start.2 = ((bf16[8,16,1920]{2,1,0:T(8,128)(2,1)}), bf16[8,16,1920]{2,1,0:T(8,128)(2,1)S(1)}, u32[]{:S(2)}, u32[]{:S(2)}) async-start(bf16[8,16,1920]{2,1,0:T(8,128)(2,1)} %bitcast.8), calls=%async_computation.2 | async-start | bytes 983040 | tf_op jit(solution)/shard_map/all_to_all | solution.py:335
  32.2 3.7 %copy-start.1 = (bf16[1,1536,3072]{2,1,0:T(8,128)(2,1)S(1)}, bf16[1,1536,3072]{2,1,0:T(8,128)(2,1)}, u32[]{:S(2)}) copy-start(bf16[1,1536,3072]{2,1,0:T(8,128)(2,1)} %param.12) | copy-start | bytes 28311556
  38.1 1.0 copy-start.6
  46.8 18.0 %all-to-all-start.1 = ((bf16[8,16,1920]{2,1,0:T(8,128)(2,1)}), bf16[8,16,1920]{2,1,0:T(8,128)(2,1)S(1)}, u32[]{:S(2)}, u32[]{:S(2)}) async-start(bf16[8,16,1920]{2,1,0:T(8,128)(2,1)} %bitcast.5), calls=%async_computation.1 | async-start | bytes 983040 | tf_op jit(solution)/shard_map/all_to_all | solution.py:335
  51.2 0.7 copy-start.11
  51.9 13.3 %collective-permute-start = (bf16[128,1536]{1,0:T(8,128)(2,1)S(1)}, bf16[128,1536]{1,0:T(8,128)(2,1)S(1)}, u32[]{:S(2)}, u32[]{:S(2)}) collective-permute-start(bf16[128,1536]{1,0:T(8,128)(2,1)S(1)} %pairs.1.refs_0_.pair_ref), channel_id=1, source_target_pairs={{0,8},{8,16},{16,24},{1,9},{9,17},{17,25},{2,10},{10,18},{18,26},{... | collective-permute-start | bytes 1179656 | tf_op jit(solution)/shard_map/ppermute | solution.py:342
  55.3 10.2 %collective-permute-start.1 = (bf16[128,1536]{1,0:T(8,128)(2,1)S(1)}, bf16[128,1536]{1,0:T(8,128)(2,1)S(1)}, u32[]{:S(2)}, u32[]{:S(2)}) collective-permute-start(bf16[128,1536]{1,0:T(8,128)(2,1)S(1)} %pairs.1.refs_0_.pair_ref), channel_id=1, source_target_pairs={{0,16},{8,24},{1,17},{9,25},{2,18},{10,26},{3,19},{11,27},{4,20},{... | collective-permute-start | bytes 1179656 | tf_op jit(solution)/shard_map/ppermute | solution.py:342
  65.5 0.9 copy-start.13
  68.8 0.9 copy-start.9
  73.1 41.1 %all-to-all-start.4 = ((bf16[8,16,1920]{2,1,0:T(8,128)(2,1)}), bf16[8,16,1920]{2,1,0:T(8,128)(2,1)S(1)}, u32[]{:S(2)}, u32[]{:S(2)}) async-start(bf16[8,16,1920]{2,1,0:T(8,128)(2,1)} %bitcast.13), calls=%async_computation.4 | async-start | bytes 983040 | tf_op jit(solution)/shard_map/all_to_all | solution.py:335
  77.9 18.3 %collective-permute-start.2 = (bf16[128,768]{1,0:T(8,128)(2,1)S(1)}, bf16[128,768]{1,0:T(8,128)(2,1)S(1)}, u32[]{:S(2)}, u32[]{:S(2)}) collective-permute-start(bf16[128,768]{1,0:T(8,128)(2,1)S(1)} %slice.4), channel_id=1, source_target_pairs={{8,0},{16,8},{24,16},{9,1},{17,9},{25,17},{10,2},{18,10},{26,18},{... | collective-permute-start | bytes 589832 | tf_op jit(solution)/shard_map/ppermute | solution.py:342
  88.4 16.0 %collective-permute-start.3 = (bf16[128,768]{1,0:T(8,128)(2,1)S(1)}, bf16[128,768]{1,0:T(8,128)(2,1)S(1)}, u32[]{:S(2)}, u32[]{:S(2)}) collective-permute-start(bf16[128,768]{1,0:T(8,128)(2,1)S(1)} %slice.4), channel_id=1, source_target_pairs={{16,0},{24,8},{17,1},{25,9},{18,2},{26,10},{19,3},{27,11},{20,4},{... | collective-permute-start | bytes 589832 | tf_op jit(solution)/shard_map/ppermute | solution.py:342
  89.7 14.7 %collective-permute-start.4 = (bf16[128,768]{1,0:T(8,128)(2,1)S(1)}, bf16[128,768]{1,0:T(8,128)(2,1)S(1)}, u32[]{:S(2)}, u32[]{:S(2)}) collective-permute-start(bf16[128,768]{1,0:T(8,128)(2,1)S(1)} %get-tuple-element.22.refs_3_.grad_ref), channel_id=1, source_target_pairs={{8,0},{16,8},{24,16},{9,1},{17,9},{25,17},{10,2},{18,10},{26,18},{... | collective-permute-start | bytes 589832 | tf_op jit(solution)/shard_map/ppermute | solution.py:342
  91.6 16.9 %collective-permute-start.5 = (bf16[128,768]{1,0:T(8,128)(2,1)S(1)}, bf16[128,768]{1,0:T(8,128)(2,1)S(1)}, u32[]{:S(2)}, u32[]{:S(2)}) collective-permute-start(bf16[128,768]{1,0:T(8,128)(2,1)S(1)} %get-tuple-element.22.refs_3_.grad_ref), channel_id=1, source_target_pairs={{16,0},{24,8},{17,1},{25,9},{18,2},{26,10},{19,3},{27,11},{20,4},{... | collective-permute-start | bytes 589832 | tf_op jit(solution)/shard_map/ppermute | solution.py:342
  108.5 0.9 copy-start.10
  109.4 0.9 copy-start.12
  114.2 19.3 %all-to-all-start.3 = ((bf16[8,16,1920]{2,1,0:T(8,128)(2,1)}), bf16[8,16,1920]{2,1,0:T(8,128)(2,1)S(1)}, u32[]{:S(2)}, u32[]{:S(2)}) async-start(bf16[8,16,1920]{2,1,0:T(8,128)(2,1)} %bitcast.11), calls=%async_computation.3 | async-start | bytes 983040 | tf_op jit(solution)/shard_map/all_to_all | solution.py:335
  118.9 3.7 %copy-start.2 = (bf16[1,1536,3072]{2,1,0:T(8,128)(2,1)S(1)}, bf16[1,1536,3072]{2,1,0:T(8,128)(2,1)}, u32[]{:S(2)}) copy-start(bf16[1,1536,3072]{2,1,0:T(8,128)(2,1)} %param.12) | copy-start | bytes 28311556
  122.6 1.2 copy-start.7
  123.8 32.4 %copy-start.5 = (bf16[1,128,1536]{2,1,0:T(8,128)(2,1)S(1)}, bf16[1,128,1536]{2,1,0:T(8,128)(2,1)}, u32[]{:S(2)}) copy-start(bf16[1,128,1536]{2,1,0:T(8,128)(2,1)} %param.7) | copy-start | bytes 1179652
  133.6 3.7 %copy-start.3 = (bf16[1,1536,3072]{2,1,0:T(8,128)(2,1)S(1)}, bf16[1,1536,3072]{2,1,0:T(8,128)(2,1)}, u32[]{:S(2)}) copy-start(bf16[1,1536,3072]{2,1,0:T(8,128)(2,1)} %param.12) | copy-start | bytes 28311556

commit v2 on v1

--- a/solution.py
+++ b/solution.py
@@ -69,6 +69,21 @@
 
 def hot(condition):
     return jnp.where(condition, 1.0, 0.0).astype(bf16)
+
+
+def load(refs, cols):
+    parts = [ref[:, cols] for ref in refs]
+    return parts[0] if len(parts) == 1 else jnp.concatenate(parts, axis=0)
+
+
+def store(refs, cols, value):
+    rows = refs[0].shape[0]
+    for i, ref in enumerate(refs):
+        ref[:, cols] = value[i * rows : (i + 1) * rows]
+
+
+def main_cols(refs):
+    return refs[0].shape[1] * FOLD // (FOLD + 1)
 
 
 def slot_matrices(scen_row, by_slot):
@@ -95,24 +110,24 @@
     return out
 
 
-def to_slots(matrices, value, wire_ref):
+def to_slots(matrices, value, refs):
     cols = value.shape[1]
     piece = cols // FOLD
-    wire_ref[:, :cols] = dot(matrices[0], value).astype(bf16)
+    store(refs, slice(0, cols), dot(matrices[0], value).astype(bf16))
     extra = dot(matrices[1], value[:, :piece])
     for part in range(1, FOLD):
         extra = extra + dot(matrices[1 + part], value[:, part * piece : (part + 1) * piece])
-    wire_ref[:, cols:] = extra.astype(bf16)
-
-
-def from_slots(matrices, wire_ref):
-    cols = wire_ref.shape[1] * FOLD // (FOLD + 1)
+    store(refs, slice(cols, cols + piece), extra.astype(bf16))
+
+
+def from_slots(matrices, refs):
+    cols = main_cols(refs)
     piece = cols // FOLD
-    extra = wire_ref[:, cols:]
+    extra = load(refs, slice(cols, cols + piece))
     out = []
     for part in range(FOLD):
         left = jnp.concatenate([matrices[0], matrices[1 + part]], axis=1)
-        right = jnp.concatenate([wire_ref[:, part * piece : (part + 1) * piece], extra], axis=0)
+        right = jnp.concatenate([load(refs, slice(part * piece, (part + 1) * piece)), extra], axis=0)
         out.append(dot(left, right))
     return jnp.concatenate(out, axis=1)
 
@@ -121,8 +136,8 @@
     matrices = [slots_ref[i] for i in range(1 + FOLD)]
     if len(wires) == 1:
         parts = [jnp.concatenate(parts, axis=1)]
-    for part, wire_ref in zip(parts, wires):
-        to_slots(matrices, part, wire_ref)
+    for part, refs in zip(parts, wires):
+        to_slots(matrices, part, refs)
 
 
 def extra_matrix(count, part, by_row):
@@ -134,34 +149,39 @@
     return hot(along == down + group * (MAIN - EXTRA) + EXTRA * part)
 
 
-def unfold(wire_ref):
-    count = wire_ref.shape[0] // MAIN
-    cols = wire_ref.shape[1] * FOLD // (FOLD + 1)
-    extra = wire_ref[:, cols:]
+def unfold(refs):
+    count = sum(ref.shape[0] for ref in refs) // MAIN
+    cols = main_cols(refs)
+    extra = load(refs, slice(cols, cols + cols // FOLD))
     pieces = [dot(extra_matrix(count, part, True), extra) for part in range(FOLD)]
-    return jnp.concatenate([wire_ref[:, :cols], jnp.concatenate(pieces, axis=1).astype(bf16)], axis=0)
-
-
-def fold(value, wire_ref):
-    rows, cols = wire_ref.shape[0], value.shape[1]
+    extra = jnp.concatenate(pieces, axis=1).astype(bf16)
+    return jnp.concatenate([load(refs, slice(0, cols)), extra], axis=0)
+
+
+def fold(value, refs):
+    rows, cols = sum(ref.shape[0] for ref in refs), value.shape[1]
     count = rows // MAIN
     piece = cols // FOLD
-    wire_ref[:, :cols] = value[:rows]
+    store(refs, slice(0, cols), value[:rows])
     extra = sum(
         dot(extra_matrix(count, part, False), value[rows:, part * piece : (part + 1) * piece])
         for part in range(FOLD)
     )
-    wire_ref[:, cols:] = extra.astype(bf16)
-
-
-def enter_kernel(events_ref, gain_ref, scen_ref, wire_ref, slots_ref):
+    store(refs, slice(cols, cols + piece), extra.astype(bf16))
+
+
+def own_scenarios(scen_ref, direct):
+    return scen_ref[...] ^ lax.axis_index("user") if direct else scen_ref[...]
+
+
+def enter_kernel(direct, events_ref, gain_ref, scen_ref, slots_ref, *refs):
     events = events_ref[...].astype(f32)
     row_inv = lax.rsqrt(jnp.mean(events * events, axis=1, keepdims=True) + eps)
     normed = (events * row_inv * gain_ref[...]).astype(bf16)
-    matrices = slot_matrices(scen_ref[...], True)
+    matrices = slot_matrices(own_scenarios(scen_ref, direct), True)
     for i, matrix in enumerate(matrices):
         slots_ref[i] = matrix
-    to_slots(matrices, normed, wire_ref)
+    to_slots(matrices, normed, refs)
 
 
 def history_of(pos, ends):
@@ -172,8 +192,8 @@
     return sum(jnp.where(history == i, limit, 0) for i, limit in enumerate(limits))
 
 
-def mask_kernel(blocks, scen_ref, lengths_ref, offsets_ref, first_ref, rows_ref, see_ref, seen_ref):
-    for i, matrix in enumerate(slot_matrices(scen_ref[...], False)):
+def mask_kernel(direct, blocks, scen_ref, lengths_ref, offsets_ref, rows_ref, see_ref, seen_ref):
+    for i, matrix in enumerate(slot_matrices(own_scenarios(scen_ref, direct), False)):
         rows_ref[i] = matrix
     rows = see_ref.shape[0]
     ends, total = [], 0
@@ -181,7 +201,7 @@
         total = total + lengths_ref[0, i]
         ends.append(total)
     limits = [offsets_ref[0, i] for i in range(offsets_ref.shape[1])]
-    first = first_ref[0]
+    first = lax.axis_index("seq") * rows
     shift = MB.bit_length() - 1
 
     def visible(query, key):
@@ -197,8 +217,9 @@
         seen_ref[:, span] = visible(first + block * rows + along, first + down)
 
 
-def project_kernel(parts, wire_ref, w_ref, out_ref, slope_ref):
-    rows = unfold(wire_ref)
+def project_kernel(count, parts, w_ref, *refs):
+    ins, outs, slope_ref = refs[:count], refs[count : 2 * count], refs[2 * count]
+    rows = unfold(ins)
     width = HEADS * HD
     done = []
     for i, part in enumerate(parts):
@@ -206,12 +227,12 @@
         sig = sigmoid(pre)
         slope_ref[:, i * width : (i + 1) * width] = sig * (1.0 + pre * (1.0 - sig))
         done.append((pre * sig).astype(bf16))
-    fold(jnp.concatenate(done, axis=1), out_ref)
-
-
-def rows_kernel(wire_ref, rows_ref, out_ref):
+    fold(jnp.concatenate(done, axis=1), outs)
+
+
+def rows_kernel(rows_ref, *refs):
     matrices = [rows_ref[i] for i in range(1 + FOLD)]
-    out_ref[...] = from_slots(matrices, wire_ref).astype(bf16)
+    refs[-1][...] = from_slots(matrices, refs[:-1]).astype(bf16)
 
 
 def head_cols(head, part=0):
@@ -250,8 +271,12 @@
     return sig, sig * (1.0 + score * (1.0 - sig))
 
 
-def query_kernel(blocks, see_ref, gq_ref, grad_ref, gate_ref, slots_ref, *refs):
-    pairs, wires = refs[:blocks], refs[blocks:]
+def wires_out(count, refs):
+    return [refs[i : i + count] for i in range(0, len(refs), count)]
+
+
+def query_kernel(count, blocks, see_ref, gq_ref, grad_ref, gate_ref, slots_ref, *refs):
+    pairs, wires = refs[:blocks], wires_out(count, refs[blocks:])
     rows = gq_ref.shape[0]
     scale = HD ** (-0.5)
     done = []
@@ -270,8 +295,9 @@
     parts_to_slots(slots_ref, [gate_ref[...], jnp.concatenate(done, axis=1)], wires)
 
 
-def key_kernel(blocks, seen_ref, pair_ref, slots_ref, *refs):
-    queries, grads, wires = refs[:blocks], refs[blocks : 2 * blocks], refs[2 * blocks :]
+def key_kernel(count, blocks, seen_ref, pair_ref, slots_ref, *refs):
+    queries, grads = refs[:blocks], refs[blocks : 2 * blocks]
+    wires = wires_out(count, refs[2 * blocks :])
     rows = pair_ref.shape[0]
     scale = HD ** (-0.5)
     grad_keys, grad_values = [], []
@@ -296,9 +322,9 @@
     parts_to_slots(slots_ref, parts, wires)
 
 
-def owner_term(parts, wire_ref, slope_ref, w_ref):
+def owner_term(parts, refs, slope_ref, w_ref):
     width = HEADS * HD
-    grad_pre = (unfold(wire_ref).astype(f32) * slope_ref[...]).astype(bf16)
+    grad_pre = (unfold(refs).astype(f32) * slope_ref[...]).astype(bf16)
     term = None
     for i, part in enumerate(parts):
         one = dot_nt(
@@ -308,32 +334,39 @@
     return term
 
 
-def term_kernel(parts, wire_ref, slope_ref, w_ref, out_ref):
-    out_ref[...] = owner_term(parts, wire_ref, slope_ref, w_ref)
-
-
-def last_term_kernel(parts, wire_ref, slope_ref, w_ref, *refs):
-    term = owner_term(parts, wire_ref, slope_ref, w_ref)
-    for other_ref in refs[:-1]:
+def term_kernel(parts, slope_ref, w_ref, *refs):
+    refs[-1][...] = owner_term(parts, refs[:-1], slope_ref, w_ref)
+
+
+def last_term_kernel(count, parts, slope_ref, w_ref, *refs):
+    ins, others, outs = refs[:count], refs[count:-count], refs[-count:]
+    term = owner_term(parts, ins, slope_ref, w_ref)
+    for other_ref in others:
         term = term + other_ref[...]
-    fold(term.astype(bf16), refs[-1])
-
-
-def leave_kernel(rows_ref, events_ref, gain_ref, *refs):
-    wires, out_ref = refs[:-1], refs[-1]
+    fold(term.astype(bf16), outs)
+
+
+def leave_kernel(count, rows_ref, events_ref, gain_ref, *refs):
     matrices = [rows_ref[i] for i in range(1 + FOLD)]
-    scaled = sum(from_slots(matrices, wire_ref) for wire_ref in wires) * gain_ref[...]
+    wires = wires_out(count, refs[:-1])
+    scaled = sum(from_slots(matrices, wire) for wire in wires) * gain_ref[...]
     events = events_ref[...].astype(f32)
     row_inv = lax.rsqrt(jnp.mean(events * events, axis=1, keepdims=True) + eps)
     normed = events * row_inv
     mean = jnp.mean(scaled * normed, axis=1, keepdims=True)
-    out_ref[...] = (row_inv * (scaled - normed * mean)).astype(bf16)
-
-
-def exchange(wire):
-    blocks = wire.reshape(-1, MAIN, wire.shape[1])
-    done = lax.all_to_all(blocks, "user", split_axis=0, concat_axis=0, tiled=True)
-    return done.reshape(wire.shape)
+    refs[-1][...] = (row_inv * (scaled - normed * mean)).astype(bf16)
+
+
+def exchange(blocks):
+    if len(blocks) == 1:
+        wire = blocks[0].reshape(-1, MAIN, blocks[0].shape[1])
+        done = lax.all_to_all(wire, "user", split_axis=0, concat_axis=0, tiled=True)
+        return [done.reshape(blocks[0].shape)]
+    count = lax.axis_size("user")
+    done = list(blocks)
+    for k in range(count - 1, 0, -1):
+        done[k] = lax.ppermute(blocks[k], "user", [(i, i ^ k) for i in range(count)])
+    return done
 
 
 def shifted(block, distance):
@@ -343,15 +376,11 @@
 
 
 def wires_of(split, boxes):
-    if split == 1:
-        return boxes[0]
     cols = boxes[0].shape[1]
-    return jnp.stack([box.reshape(SCEN, MAIN, cols) for box in boxes], axis=1).reshape(-1, cols)
+    return [jnp.stack([box.reshape(SCEN, MAIN, cols) for box in boxes], axis=1).reshape(-1, cols)]
 
 
 def slices_of(split, box):
-    if split == 1:
-        return [box]
     cols = box.shape[1]
     blocks = box.reshape(SCEN, split, MAIN, cols)
     return [blocks[:, i].reshape(-1, cols) for i in range(split)]
@@ -366,58 +395,59 @@
     longest = n_seq * rows // 2
     reach = min(REACH, n_seq - 1, (longest - 2) // rows + 1)
     blocks = reach + 1
-    slots = SCEN * MAIN
-
-    def wire(senders, cols):
-        return shape((senders * MAIN, cols * (FOLD + 1) // FOLD), bf16)
-
-    matrices = shape((1 + FOLD, rows, slots), bf16)
+    direct = split == 1
+    senders = SCEN if direct else 1
+
+    def wire(rows, cols):
+        count = rows // MAIN if direct else 1
+        return [shape((rows // count, cols * (FOLD + 1) // FOLD), bf16)] * count
+
+    slots = wire(SCEN * MAIN, feats)
+    matrices = shape((1 + FOLD, rows, SCEN * MAIN), bf16)
     events, w_local, cotan = events[0], w_proj[0], cotangent[0]
     gain = gain[None]
-    first = (lax.axis_index("seq") * rows).astype(jnp.int32)[None]
-
-    outbox, to_slot = call(
-        enter_kernel, [wire(SCEN, feats), matrices], [events, gain, scenario], "enter"
-    )
-    inbound = exchange(wires_of(split, [outbox] * split))
+
+    to_slot, *outbox = call(
+        functools.partial(enter_kernel, direct),
+        [matrices] + slots,
+        [events, gain, scenario],
+        "enter",
+    )
+    inbound = exchange(outbox if direct else wires_of(split, outbox * split))
     to_row, see, seen = call(
-        functools.partial(mask_kernel, blocks),
+        functools.partial(mask_kernel, direct, blocks),
         [matrices] + [shape((rows, blocks * rows), f32)] * 2,
-        [scenario, lengths, offsets, first],
+        [scenario, lengths, offsets],
         "masks",
-        smem=3,
+        smem=2,
     )
 
     def project(parts, name):
         cols = len(parts) * width
-        return call(
-            functools.partial(project_kernel, parts),
-            [wire(n_user, cols), shape((n_user * CAP, cols), f32)],
-            [inbound, w_local],
+        *box, slope = call(
+            functools.partial(project_kernel, senders, parts),
+            wire(n_user * MAIN, cols) + [shape((n_user * CAP, cols), f32)],
+            [w_local] + inbound,
             name,
         )
+        return exchange(box), slope
 
     def rows_of(box, name):
-        cols = box.shape[1] * FOLD // (FOLD + 1)
-        return call(rows_kernel, [shape((rows, cols), bf16)], [box, to_row], name)[0]
-
-    together = split == 1
-    if together:
+        cols = box[0].shape[1] * FOLD // (FOLD + 1)
+        return call(rows_kernel, [shape((rows, cols), bf16)], [to_row] + box, name)[0]
+
+    if direct:
         pair_parts, query_parts = (1, 3), (0, 2)
-        pair_box, pair_slope = project(pair_parts, "pair")
-        pair_back = exchange(pair_box)
-        query_box, query_slope = project(query_parts, "query")
+        pair_back, pair_slope = project(pair_parts, "pair")
+        query_back, query_slope = project(query_parts, "query")
         pair_own = rows_of(pair_back, "pairs")
-        pairs = [pair_own] + [shifted(pair_own, d) for d in range(1, blocks)]
-        gq = rows_of(exchange(query_box), "queries")
+        gq = rows_of(query_back, "queries")
     else:
-        box, slope = project((0,), "all")
-        gate, value, query, key = [
-            rows_of(part, "part") for part in slices_of(split, exchange(box))
-        ]
+        (box,), slope = project((0,), "all")
+        gate, value, query, key = [rows_of([part], "part") for part in slices_of(split, box)]
         pair_own = jnp.concatenate([value, key], axis=1)
         gq = jnp.concatenate([gate, query], axis=1)
-        pairs = [pair_own] + [shifted(pair_own, d) for d in range(1, blocks)]
+    pairs = [pair_own] + [shifted(pair_own, d) for d in range(1, blocks)]
     query_own = gq[:, width:]
     queries = [gq] + [shifted(query_own, -d) for d in range(1, blocks)]
     half = shape((rows, width), bf16)
@@ -428,41 +458,42 @@
         "forward",
     )
     grads = [grad_own] + [shifted(grad_own, -d) for d in range(1, blocks)]
-    boxes = [wire(SCEN, 2 * width)] if together else [wire(SCEN, width)] * 2
+    boxes = wire(SCEN * MAIN, 2 * width) if direct else wire(SCEN * MAIN, width) * 2
     query_grad = call(
-        functools.partial(query_kernel, blocks),
+        functools.partial(query_kernel, senders, blocks),
         boxes,
         [see, gq, grad_own, grad_gate, to_slot] + pairs,
         "query_grad",
     )
-    if together:
-        query_grad = exchange(query_grad[0])
     pair_grad = call(
-        functools.partial(key_kernel, blocks),
+        functools.partial(key_kernel, senders, blocks),
         boxes,
         [seen, pair_own, to_slot] + queries + grads,
         "pair_grad",
     )
     term = shape((n_user * CAP, feats), f32)
-    if together:
-        pair_grad = exchange(pair_grad[0])
+    if direct:
         (query_term,) = call(
             functools.partial(term_kernel, query_parts),
             [term],
-            [query_grad, query_slope, w_local],
+            [query_slope, w_local] + exchange(query_grad),
             "term",
         )
-        last_parts, last = pair_parts, [pair_grad, pair_slope, w_local, query_term]
+        last_parts, last = pair_parts, [pair_slope, w_local] + exchange(pair_grad) + [query_term]
     else:
         order = [query_grad[0], pair_grad[0], query_grad[1], pair_grad[1]]
-        last_parts, last = (0,), [exchange(wires_of(split, order)), slope, w_local]
-    (term_box,) = call(
-        functools.partial(last_term_kernel, last_parts), [wire(n_user, feats)], last, "last_term"
-    )
+        last_parts, last = (0,), [slope, w_local] + exchange(wires_of(split, order))
+    term_box = call(
+        functools.partial(last_term_kernel, senders, last_parts),
+        wire(n_user * MAIN, feats),
+        last,
+        "last_term",
+    )
+    term_back = exchange(term_box)
     (grad_events,) = call(
-        leave_kernel,
+        functools.partial(leave_kernel, senders),
         [shape((rows, feats), bf16)],
-        [to_row, events, gain] + slices_of(split, exchange(term_box)),
+        [to_row, events, gain] + (term_back if direct else slices_of(split, term_back[0])),
         "leave",
     )
     return output[None], grad_events[None]

time: 158 us -> 130 us (0.82); the launches traced: 157 us -> 127 us
  blocking collectives: 36.3 us -> 0 us
  starting transfers between devices: 36.1 us -> 68.4 us
  local copies, waits for them, and re-layouts: 23.3 us -> 6.08 us
  waiting for transfers between devices: 39.9 us -> 34.2 us
  Pallas kernels: 21 us -> 17.9 us
    ppermute x0 -> x42, starting transfers between devices: none -> 54.3 us  [exchange(): lax.ppermute(blocks[k], 'user', [(i, i ^ k) for i in range(count)])]
    all_to_all x2 -> x0, blocking collectives: 36.3 us -> none  [exchange(): lax.all_to_all(blocks, 'user', split_axis=0, concat_axis=0, tiled=True)]
    ppermute x0 -> x42, waiting for transfers between devices: none -> 30.1 us  [exchange(): lax.ppermute(blocks[k], 'user', [(i, i ^ k) for i in range(count)])]
    all_to_all x4 -> x0, waiting for transfers between devices: 23.9 us -> none  [exchange(): lax.all_to_all(blocks, 'user', split_axis=0, concat_axis=0, tiled=True)]
    unnamed x36 -> x16, local copies, waits for them, and re-layouts: 22.6 us -> 5.35 us
    all_to_all x4 -> x0, starting transfers between devices: 16.4 us -> none  [exchange(): lax.all_to_all(blocks, 'user', split_axis=0, concat_axis=0, tiled=True)]
    ppermute x6, waiting for transfers between devices: 16 us -> 4.1 us  [shifted(): return lax.ppermute(block, 'seq', route)]
    ppermute x6, starting transfers between devices: 19.7 us -> 14 us  [shifted(): return lax.ppermute(block, 'seq', route)]
  transfers between devices with their start and end apart: 10 -> 48, of which waited for: 7 -> 12; matrix products, arithmetic and copies ran while one was open for 0% -> 0% of each run, Pallas kernels for 6% -> 10%
where the time goes in v2:
time: 130 us; the launch traced here: 127 us
  starting transfers between devices  68.4 us (53%)
  waiting for transfers between devices  34.2 us (26%)
  Pallas kernels  17.9 us (14%)
  local copies, waits for them, and re-layouts  6.08 us (5%)
    ppermute x42, starting transfers between devices, exchange(): lax.ppermute(blocks[k], 'user', [(i, i ^ k) for i in range(count)])  54.3 us
    ppermute x42, waiting for transfers between devices, exchange(): lax.ppermute(blocks[k], 'user', [(i, i ^ k) for i in range(count)])  30.1 us
    pallas_call x12, Pallas kernels, call(): pl.pallas_call(kernel, out_shape=tuple(outs), in_specs=specs, out_specs=t...  17.9 us
    ppermute x6, starting transfers between devices, shifted(): return lax.ppermute(block, 'seq', route)  14 us
    unnamed x16, local copies, waits for them, and re-layouts  5.35 us
    ppermute x6, waiting for transfers between devices, shifted(): return lax.ppermute(block, 'seq', route)  4.1 us
  transfers between devices with their start and end apart: 48, of which 12 were waited for; matrix products, arithmetic and copies ran while one was open for 0% of the time, Pallas kernels for 10%

profile of v2, /device:TPU:2, one launch (start us, length us, event | category | flops | bytes accessed | tf_op | source)
XLA Modules:
  0.0 127.4 jit_solution(321710591413408007)
XLA Ops:
  3.6 1.6 %collective-permute-start.1 = (bf16[16,1920]{1,0:T(8,128)(2,1)S(1)}, bf16[16,1920]{1,0:T(8,128)(2,1)S(1)}, u32[]{:S(2)}, u32[]{:S(2)}) collective-permute-start(bf16[16,1920]{1,0:T(8,128)(2,1)S(1)} %get-tuple-element.63), channel_id=1, source_target_pairs={{0,2},{1,3},{2,0},{3,1},{4,6},{5,7},{6,4},{7,5},{8,10},{9,11},{10,... | collective-permute-start | bytes 184328 | tf_op jit(solution)/shard_map/ppermute | solution.py:368
  5.5 2.6 %collective-permute-start.3 = (bf16[16,1920]{1,0:T(8,128)(2,1)S(1)}, bf16[16,1920]{1,0:T(8,128)(2,1)S(1)}, u32[]{:S(2)}, u32[]{:S(2)}) collective-permute-start(bf16[16,1920]{1,0:T(8,128)(2,1)S(1)} %get-tuple-element.65), channel_id=1, source_target_pairs={{0,4},{1,5},{2,6},{3,7},{4,0},{5,1},{6,2},{7,3},{8,12},{9,13},{10,... | collective-permute-start | bytes 184328 | tf_op jit(solution)/shard_map/ppermute | solution.py:368
  8.1 3.6 %collective-permute-start.5 = (bf16[16,1920]{1,0:T(8,128)(2,1)S(1)}, bf16[16,1920]{1,0:T(8,128)(2,1)S(1)}, u32[]{:S(2)}, u32[]{:S(2)}) collective-permute-start(bf16[16,1920]{1,0:T(8,128)(2,1)S(1)} %get-tuple-element.67), channel_id=1, source_target_pairs={{0,6},{1,7},{2,4},{3,5},{4,2},{5,3},{6,0},{7,1},{8,14},{9,15},{10,... | collective-permute-start | bytes 184328 | tf_op jit(solution)/shard_map/ppermute | solution.py:368
  11.8 6.4 %collective-permute-done.4.refs_5_ = bf16[16,1920]{1,0:T(8,128)(2,1)S(1)} collective-permute-done((bf16[16,1920]{1,0:T(8,128)(2,1)S(1)}, bf16[16,1920]{1,0:T(8,128)(2,1)S(1)}, u32[]{:S(2)}, u32[]{:S(2)}) %collective-permute-start.4) | collective-permute-done | bytes 61472 | tf_op jit(solution)/shard_map/ppermute | solution.py:368
  18.2 3.7 %copy-done = bf16[1,1536,3072]{2,1,0:T(8,128)(2,1)S(1)} copy-done((bf16[1,1536,3072]{2,1,0:T(8,128)(2,1)S(1)}, bf16[1,1536,3072]{2,1,0:T(8,128)(2,1)}, u32[]{:S(2)}) %copy-start) | copy-done | bytes 9437208
  21.9 1.4 %pair.1 = (bf16[16,1920]{1,0:T(8,128)(2,1)S(1)}, bf16[16,1920]{1,0:T(8,128)(2,1)S(1)}, bf16[16,1920]{1,0:T(8,128)(2,1)S(1)}, bf16[16,1920]{1,0:T(8,128)(2,1)S(1)...) custom-call(bf16[1536,3072]{1,0:T(8,128)(2,1)S(1)} %bitcast.5, ...), custom_call_target="tpu_custom_call" | custom-call | flops 16777216 | bytes 11403264 | tf_op jit(solution)/shard_map/pair/pallas_call | solution.py:36
  23.5 3.2 %collective-permute-start.15 = (bf16[16,1920]{1,0:T(8,128)(2,1)S(1)}, bf16[16,1920]{1,0:T(8,128)(2,1)S(1)}, u32[]{:S(2)}, u32[]{:S(2)}) collective-permute-start(bf16[16,1920]{1,0:T(8,128)(2,1)S(1)} %get-tuple-element.79), channel_id=1, source_target_pairs={{0,2},{1,3},{2,0},{3,1},{4,6},{5,7},{6,4},{7,5},{8,10},{9,11},{10,... | collective-permute-start | bytes 184328 | tf_op jit(solution)/shard_map/ppermute | solution.py:368
  26.7 2.8 %collective-permute-start.17 = (bf16[16,1920]{1,0:T(8,128)(2,1)S(1)}, bf16[16,1920]{1,0:T(8,128)(2,1)S(1)}, u32[]{:S(2)}, u32[]{:S(2)}) collective-permute-start(bf16[16,1920]{1,0:T(8,128)(2,1)S(1)} %get-tuple-element.81), channel_id=1, source_target_pairs={{0,4},{1,5},{2,6},{3,7},{4,0},{5,1},{6,2},{7,3},{8,12},{9,13},{10,... | collective-permute-start | bytes 184328 | tf_op jit(solution)/shard_map/ppermute | solution.py:368
  29.5 2.1 %collective-permute-start.19 = (bf16[16,1920]{1,0:T(8,128)(2,1)S(1)}, bf16[16,1920]{1,0:T(8,128)(2,1)S(1)}, u32[]{:S(2)}, u32[]{:S(2)}) collective-permute-start(bf16[16,1920]{1,0:T(8,128)(2,1)S(1)} %get-tuple-element.83), channel_id=1, source_target_pairs={{0,6},{1,7},{2,4},{3,5},{4,2},{5,3},{6,0},{7,1},{8,14},{9,15},{10,... | collective-permute-start | bytes 184328 | tf_op jit(solution)/shard_map/ppermute | solution.py:368
  31.6 1.3 %collective-permute-start.20 = (bf16[16,1920]{1,0:T(8,128)(2,1)S(1)}, bf16[16,1920]{1,0:T(8,128)(2,1)S(1)}, u32[]{:S(2)}, u32[]{:S(2)}) collective-permute-start(bf16[16,1920]{1,0:T(8,128)(2,1)S(1)} %get-tuple-element.84), channel_id=1, source_target_pairs={{0,7},{1,6},{2,5},{3,4},{4,3},{5,2},{6,1},{7,0},{8,15},{9,14},{10,... | collective-permute-start | bytes 184328 | tf_op jit(solution)/shard_map/ppermute | solution.py:368
  33.8 5.5 %collective-permute-done.18.refs_5_ = bf16[16,1920]{1,0:T(8,128)(2,1)S(1)} collective-permute-done((bf16[16,1920]{1,0:T(8,128)(2,1)S(1)}, bf16[16,1920]{1,0:T(8,128)(2,1)S(1)}, u32[]{:S(2)}, u32[]{:S(2)}) %collective-permute-start.18) | collective-permute-done | bytes 61472 | tf_op jit(solution)/shard_map/ppermute | solution.py:368
  39.6 3.4 %collective-permute-start.21 = (bf16[128,1536]{1,0:T(8,128)(2,1)S(1)}, bf16[128,1536]{1,0:T(8,128)(2,1)S(1)}, u32[]{:S(2)}, u32[]{:S(2)}) collective-permute-start(bf16[128,1536]{1,0:T(8,128)(2,1)S(1)} %pairs.1.refs_0_.pair_ref), channel_id=1, source_target_pairs={{0,8},{8,16},{16,24},{1,9},{9,17},{17,25},{2,10},{10,18},{18,26},{... | collective-permute-start | bytes 1179656 | tf_op jit(solution)/shard_map/ppermute | solution.py:375
  43.0 1.3 %collective-permute-start.22 = (bf16[128,1536]{1,0:T(8,128)(2,1)S(1)}, bf16[128,1536]{1,0:T(8,128)(2,1)S(1)}, u32[]{:S(2)}, u32[]{:S(2)}) collective-permute-start(bf16[128,1536]{1,0:T(8,128)(2,1)S(1)} %pairs.1.refs_0_.pair_ref), channel_id=1, source_target_pairs={{0,16},{8,24},{1,17},{9,25},{2,18},{10,26},{3,19},{11,27},{4,20},{... | collective-permute-start | bytes 1179656 | tf_op jit(solution)/shard_map/ppermute | solution.py:375
  44.4 1.5 %query.1 = (bf16[16,1920]{1,0:T(8,128)(2,1)S(1)}, bf16[16,1920]{1,0:T(8,128)(2,1)S(1)}, bf16[16,1920]{1,0:T(8,128)(2,1)S(1)}, bf16[16,1920]{1,0:T(8,128)(2,1)S(1...) custom-call(bf16[1536,3072]{1,0:T(8,128)(2,1)S(1)} %bitcast.6, ...), custom_call_target="tpu_custom_call" | custom-call | flops 16777216 | bytes 11403264 | tf_op jit(solution)/shard_map/query/pallas_call | solution.py:36
  45.9 3.3 %collective-permute-start.10 = (bf16[16,1920]{1,0:T(8,128)(2,1)S(1)}, bf16[16,1920]{1,0:T(8,128)(2,1)S(1)}, u32[]{:S(2)}, u32[]{:S(2)}) collective-permute-start(bf16[16,1920]{1,0:T(8,128)(2,1)S(1)} %get-tuple-element.73), channel_id=1, source_target_pairs={{0,4},{1,5},{2,6},{3,7},{4,0},{5,1},{6,2},{7,3},{8,12},{9,13},{10,... | collective-permute-start | bytes 184328 | tf_op jit(solution)/shard_map/ppermute | solution.py:368
  49.2 2.3 %collective-permute-start.12 = (bf16[16,1920]{1,0:T(8,128)(2,1)S(1)}, bf16[16,1920]{1,0:T(8,128)(2,1)S(1)}, u32[]{:S(2)}, u32[]{:S(2)}) collective-permute-start(bf16[16,1920]{1,0:T(8,128)(2,1)S(1)} %get-tuple-element.75), channel_id=1, source_target_pairs={{0,6},{1,7},{2,4},{3,5},{4,2},{5,3},{6,0},{7,1},{8,14},{9,15},{10,... | collective-permute-start | bytes 184328 | tf_op jit(solution)/shard_map/ppermute | solution.py:368
  51.5 1.1 collective-permute-start.13
  52.5 5.3 %collective-permute-done.11.refs_5_ = bf16[16,1920]{1,0:T(8,128)(2,1)S(1)} collective-permute-done((bf16[16,1920]{1,0:T(8,128)(2,1)S(1)}, bf16[16,1920]{1,0:T(8,128)(2,1)S(1)}, u32[]{:S(2)}, u32[]{:S(2)}) %collective-permute-start.11) | collective-permute-done | bytes 61472 | tf_op jit(solution)/shard_map/ppermute | solution.py:368
  57.9 1.8 %collective-permute-start.8 = (bf16[16,1920]{1,0:T(8,128)(2,1)S(1)}, bf16[16,1920]{1,0:T(8,128)(2,1)S(1)}, u32[]{:S(2)}, u32[]{:S(2)}) collective-permute-start(bf16[16,1920]{1,0:T(8,128)(2,1)S(1)} %get-tuple-element.71), channel_id=1, source_target_pairs={{0,2},{1,3},{2,0},{3,1},{4,6},{5,7},{6,4},{7,5},{8,10},{9,11},{10,... | collective-permute-start | bytes 184328 | tf_op jit(solution)/shard_map/ppermute | solution.py:368
  59.7 1.7 %collective-permute-start.9 = (bf16[16,1920]{1,0:T(8,128)(2,1)S(1)}, bf16[16,1920]{1,0:T(8,128)(2,1)S(1)}, u32[]{:S(2)}, u32[]{:S(2)}) collective-permute-start(bf16[16,1920]{1,0:T(8,128)(2,1)S(1)} %get-tuple-element.72), channel_id=1, source_target_pairs={{0,3},{1,2},{2,1},{3,0},{4,7},{5,6},{6,5},{7,4},{8,11},{9,10},{10,... | collective-permute-start | bytes 184328 | tf_op jit(solution)/shard_map/ppermute | solution.py:368
  62.2 1.2 collective-permute-done.9.refs_3_
  63.8 4.6 %collective-permute-start.23 = (bf16[128,768]{1,0:T(8,128)(2,1)S(1)}, bf16[128,768]{1,0:T(8,128)(2,1)S(1)}, u32[]{:S(2)}, u32[]{:S(2)}) collective-permute-start(bf16[128,768]{1,0:T(8,128)(2,1)S(1)} %slice.4), channel_id=1, source_target_pairs={{8,0},{16,8},{24,16},{9,1},{17,9},{25,17},{10,2},{18,10},{26,18},{... | collective-permute-start | bytes 589832 | tf_op jit(solution)/shard_map/ppermute | solution.py:375
  68.4 1.3 %collective-permute-start.24 = (bf16[128,768]{1,0:T(8,128)(2,1)S(1)}, bf16[128,768]{1,0:T(8,128)(2,1)S(1)}, u32[]{:S(2)}, u32[]{:S(2)}) collective-permute-start(bf16[128,768]{1,0:T(8,128)(2,1)S(1)} %slice.4), channel_id=1, source_target_pairs={{16,0},{24,8},{17,1},{25,9},{18,2},{26,10},{19,3},{27,11},{20,4},{... | collective-permute-start | bytes 589832 | tf_op jit(solution)/shard_map/ppermute | solution.py:375
  69.8 2.4 %forward.1 = (bf16[128,768]{1,0:T(8,128)(2,1)}, bf16[128,768]{1,0:T(8,128)(2,1)S(1)}, bf16[128,768]{1,0:T(8,128)(2,1)S(1)}, f32[128,768]{1,0:T(8,128)}) custom-call(f32[128,384]{1,0:T(8,128)S(1)} %get-tuple-element.59.see_ref, bf16[128,1536]{1,0:T(8,128)(2,1)S(1)} %queries.1.gq_ref.refs_0_, bf16[128,768]{1,0:T(8,128)(2,1)S(1)} %bitcast.11, ...), custom_call_target="tpu_custom_call" | custom-call | flops 16777216 | bytes 2949120 | tf_op jit(solution)/shard_map/forward/pallas_call | solution.py:36
  72.2 1.9 %collective-permute-start.25 = (bf16[128,768]{1,0:T(8,128)(2,1)S(1)}, bf16[128,768]{1,0:T(8,128)(2,1)S(1)}, u32[]{:S(2)}, u32[]{:S(2)}) collective-permute-start(bf16[128,768]{1,0:T(8,128)(2,1)S(1)} %get-tuple-element.89.refs_3_.grad_ref), channel_id=1, source_target_pairs={{8,0},{16,8},{24,16},{9,1},{17,9},{25,17},{10,2},{18,10},{26,18},{... | collective-permute-start | bytes 589832 | tf_op jit(solution)/shard_map/ppermute | solution.py:375
  74.1 1.5 %collective-permute-start.26 = (bf16[128,768]{1,0:T(8,128)(2,1)S(1)}, bf16[128,768]{1,0:T(8,128)(2,1)S(1)}, u32[]{:S(2)}, u32[]{:S(2)}) collective-permute-start(bf16[128,768]{1,0:T(8,128)(2,1)S(1)} %get-tuple-element.89.refs_3_.grad_ref), channel_id=1, source_target_pairs={{16,0},{24,8},{17,1},{25,9},{18,2},{26,10},{19,3},{27,11},{20,4},{... | collective-permute-start | bytes 589832 | tf_op jit(solution)/shard_map/ppermute | solution.py:375
  75.6 2.6 %query_grad.1 = (bf16[16,1920]{1,0:T(8,128)(2,1)S(1)}, bf16[16,1920]{1,0:T(8,128)(2,1)S(1)}, bf16[16,1920]{1,0:T(8,128)(2,1)S(1)}, bf16[16,1920]{1,0:T(8,128)(2,...) custom-call(f32[128,384]{1,0:T(8,128)S(1)} %get-tuple-element.59.see, ...), custom_call_target="tpu_custom_call" | custom-call | flops 16777216 | bytes 2818048 | tf_op jit(solution)/shard_map/query_grad/pallas_call | solution.py:36
  78.7 1.7 %collective-permute-start.35 = (bf16[16,1920]{1,0:T(8,128)(2,1)S(1)}, bf16[16,1920]{1,0:T(8,128)(2,1)S(1)}, u32[]{:S(2)}, u32[]{:S(2)}) collective-permute-start(bf16[16,1920]{1,0:T(8,128)(2,1)S(1)} %get-tuple-element.102), channel_id=1, source_target_pairs={{0,2},{1,3},{2,0},{3,1},{4,6},{5,7},{6,4},{7,5},{8,10},{9,11},{10,... | collective-permute-start | bytes 184328 | tf_op jit(solution)/shard_map/ppermute | solution.py:368
  80.6 1.8 %collective-permute-done.25.refs_4_ = bf16[128,768]{1,0:T(8,128)(2,1)S(1)} collective-permute-done((bf16[128,768]{1,0:T(8,128)(2,1)S(1)}, bf16[128,768]{1,0:T(8,128)(2,1)S(1)}, u32[]{:S(2)}, u32[]{:S(2)}) %collective-permute-start.25) | collective-permute-done | bytes 196640 | tf_op jit(solution)/shard_map/ppermute | solution.py:375
  82.4 1.8 %collective-permute-start.37 = (bf16[16,1920]{1,0:T(8,128)(2,1)S(1)}, bf16[16,1920]{1,0:T(8,128)(2,1)S(1)}, u32[]{:S(2)}, u32[]{:S(2)}) collective-permute-start(bf16[16,1920]{1,0:T(8,128)(2,1)S(1)} %get-tuple-element.104), channel_id=1, source_target_pairs={{0,4},{1,5},{2,6},{3,7},{4,0},{5,1},{6,2},{7,3},{8,12},{9,13},{10,... | collective-permute-start | bytes 184328 | tf_op jit(solution)/shard_map/ppermute | solution.py:368
  84.2 2.3 %collective-permute-done.26.refs_5_ = bf16[128,768]{1,0:T(8,128)(2,1)S(1)} collective-permute-done((bf16[128,768]{1,0:T(8,128)(2,1)S(1)}, bf16[128,768]{1,0:T(8,128)(2,1)S(1)}, u32[]{:S(2)}, u32[]{:S(2)}) %collective-permute-start.26) | collective-permute-done | bytes 196640 | tf_op jit(solution)/shard_map/ppermute | solution.py:375
  86.5 1.8 %collective-permute-start.38 = (bf16[16,1920]{1,0:T(8,128)(2,1)S(1)}, bf16[16,1920]{1,0:T(8,128)(2,1)S(1)}, u32[]{:S(2)}, u32[]{:S(2)}) collective-permute-start(bf16[16,1920]{1,0:T(8,128)(2,1)S(1)} %get-tuple-element.105), channel_id=1, source_target_pairs={{0,5},{1,4},{2,7},{3,6},{4,1},{5,0},{6,3},{7,2},{8,13},{9,12},{10,... | collective-permute-start | bytes 184328 | tf_op jit(solution)/shard_map/ppermute | solution.py:368
  88.3 3.1 %pair_grad.1 = (bf16[16,1920]{1,0:T(8,128)(2,1)S(1)}, bf16[16,1920]{1,0:T(8,128)(2,1)S(1)}, bf16[16,1920]{1,0:T(8,128)(2,1)S(1)}, bf16[16,1920]{1,0:T(8,128)(2,1...) custom-call(f32[128,384]{1,0:T(8,128)S(1)} %get-tuple-element.87.see, ...), custom_call_target="tpu_custom_call" | custom-call | flops 16777216 | bytes 2621440 | tf_op jit(solution)/shard_map/pair_grad/pallas_call | solution.py:36
  91.4 1.9 %collective-permute-start.39 = (bf16[16,1920]{1,0:T(8,128)(2,1)S(1)}, bf16[16,1920]{1,0:T(8,128)(2,1)S(1)}, u32[]{:S(2)}, u32[]{:S(2)}) collective-permute-start(bf16[16,1920]{1,0:T(8,128)(2,1)S(1)} %get-tuple-element.106), channel_id=1, source_target_pairs={{0,6},{1,7},{2,4},{3,5},{4,2},{5,3},{6,0},{7,1},{8,14},{9,15},{10,... | collective-permute-start | bytes 184328 | tf_op jit(solution)/shard_map/ppermute | solution.py:368
  93.3 1.7 %collective-permute-start.40 = (bf16[16,1920]{1,0:T(8,128)(2,1)S(1)}, bf16[16,1920]{1,0:T(8,128)(2,1)S(1)}, u32[]{:S(2)}, u32[]{:S(2)}) collective-permute-start(bf16[16,1920]{1,0:T(8,128)(2,1)S(1)} %get-tuple-element.107), channel_id=1, source_target_pairs={{0,7},{1,6},{2,5},{3,4},{4,3},{5,2},{6,1},{7,0},{8,15},{9,14},{10,... | collective-permute-start | bytes 184328 | tf_op jit(solution)/shard_map/ppermute | solution.py:368
  95.4 1.5 %collective-permute-start.29 = (bf16[16,1920]{1,0:T(8,128)(2,1)S(1)}, bf16[16,1920]{1,0:T(8,128)(2,1)S(1)}, u32[]{:S(2)}, u32[]{:S(2)}) collective-permute-start(bf16[16,1920]{1,0:T(8,128)(2,1)S(1)} %get-tuple-element.93), channel_id=1, source_target_pairs={{0,3},{1,2},{2,1},{3,0},{4,7},{5,6},{6,5},{7,4},{8,11},{9,10},{10,... | collective-permute-start | bytes 184328 | tf_op jit(solution)/shard_map/ppermute | solution.py:368
  99.8 2.4 %collective-permute-start.32 = (bf16[16,1920]{1,0:T(8,128)(2,1)S(1)}, bf16[16,1920]{1,0:T(8,128)(2,1)S(1)}, u32[]{:S(2)}, u32[]{:S(2)}) collective-permute-start(bf16[16,1920]{1,0:T(8,128)(2,1)S(1)} %get-tuple-element.96), channel_id=1, source_target_pairs={{0,6},{1,7},{2,4},{3,5},{4,2},{5,3},{6,0},{7,1},{8,14},{9,15},{10,... | collective-permute-start | bytes 184328 | tf_op jit(solution)/shard_map/ppermute | solution.py:368
  102.2 1.7 %collective-permute-start.33 = (bf16[16,1920]{1,0:T(8,128)(2,1)S(1)}, bf16[16,1920]{1,0:T(8,128)(2,1)S(1)}, u32[]{:S(2)}, u32[]{:S(2)}) collective-permute-start(bf16[16,1920]{1,0:T(8,128)(2,1)S(1)} %get-tuple-element.97), channel_id=1, source_target_pairs={{0,7},{1,6},{2,5},{3,4},{4,3},{5,2},{6,1},{7,0},{8,15},{9,14},{10,... | collective-permute-start | bytes 184328 | tf_op jit(solution)/shard_map/ppermute | solution.py:368
  103.9 1.8 %term.1.refs_8_ = f32[160,1536]{1,0:T(8,128)S(1)} custom-call(f32[160,1536]{1,0:T(8,128)S(1)} %get-tuple-element.98.slope_ref, bf16[1536,3072]{1,0:T(8,128)(2,1)S(1)} %bitcast.7, bf16[16,1920]{1,0:T(8,128)(2,1)S(1)} %get-tuple-element.100.refs_0_, bf16[16,1920]{1,0:T(8,128)(2,1)S(1)} %collective-permute-done.34.refs_1_, ...), custom_call_target="tpu_custom_call" | custom-call | flops 16777216 | bytes 11894784 | tf_op jit(solution)/shard_map/term/pallas_call | solution.py:36
  105.7 1.2 collective-permute-done.30.refs_4_
  106.8 1.9 %collective-permute-done.31.refs_5_ = bf16[16,1920]{1,0:T(8,128)(2,1)S(1)} collective-permute-done((bf16[16,1920]{1,0:T(8,128)(2,1)S(1)}, bf16[16,1920]{1,0:T(8,128)(2,1)S(1)}, u32[]{:S(2)}, u32[]{:S(2)}) %collective-permute-start.31) | collective-permute-done | bytes 61472 | tf_op jit(solution)/shard_map/ppermute | solution.py:368
  108.8 1.9 %last_term.1 = (bf16[16,1920]{1,0:T(8,128)(2,1)S(1)}, bf16[16,1920]{1,0:T(8,128)(2,1)S(1)}, bf16[16,1920]{1,0:T(8,128)(2,1)S(1)}, bf16[16,1920]{1,0:T(8,128)(2,1...) custom-call(f32[160,1536]{1,0:T(8,128)S(1)} %get-tuple-element.86.sl, ...), custom_call_target="tpu_custom_call" | custom-call | flops 16777216 | bytes 12386304 | tf_op jit(solution)/shard_map/last_term/pallas_call | solution.py:36
  111.3 2.8 %collective-permute-start.42 = (bf16[16,1920]{1,0:T(8,128)(2,1)S(1)}, bf16[16,1920]{1,0:T(8,128)(2,1)S(1)}, u32[]{:S(2)}, u32[]{:S(2)}) collective-permute-start(bf16[16,1920]{1,0:T(8,128)(2,1)S(1)} %get-tuple-element.110), channel_id=1, source_target_pairs={{0,2},{1,3},{2,0},{3,1},{4,6},{5,7},{6,4},{7,5},{8,10},{9,11},{10,... | collective-permute-start | bytes 184328 | tf_op jit(solution)/shard_map/ppermute | solution.py:368
  114.1 2.2 %collective-permute-start.44 = (bf16[16,1920]{1,0:T(8,128)(2,1)S(1)}, bf16[16,1920]{1,0:T(8,128)(2,1)S(1)}, u32[]{:S(2)}, u32[]{:S(2)}) collective-permute-start(bf16[16,1920]{1,0:T(8,128)(2,1)S(1)} %get-tuple-element.112), channel_id=1, source_target_pairs={{0,4},{1,5},{2,6},{3,7},{4,0},{5,1},{6,2},{7,3},{8,12},{9,13},{10,... | collective-permute-start | bytes 184328 | tf_op jit(solution)/shard_map/ppermute | solution.py:368
  116.6 2.1 %collective-permute-start.46 = (bf16[16,1920]{1,0:T(8,128)(2,1)S(1)}, bf16[16,1920]{1,0:T(8,128)(2,1)S(1)}, u32[]{:S(2)}, u32[]{:S(2)}) collective-permute-start(bf16[16,1920]{1,0:T(8,128)(2,1)S(1)} %get-tuple-element.114), channel_id=1, source_target_pairs={{0,6},{1,7},{2,4},{3,5},{4,2},{5,3},{6,0},{7,1},{8,14},{9,15},{10,... | collective-permute-start | bytes 184328 | tf_op jit(solution)/shard_map/ppermute | solution.py:368
  118.7 1.7 %collective-permute-start.47 = (bf16[16,1920]{1,0:T(8,128)(2,1)S(1)}, bf16[16,1920]{1,0:T(8,128)(2,1)S(1)}, u32[]{:S(2)}, u32[]{:S(2)}) collective-permute-start(bf16[16,1920]{1,0:T(8,128)(2,1)S(1)} %get-tuple-element.115), channel_id=1, source_target_pairs={{0,7},{1,6},{2,5},{3,4},{4,3},{5,2},{6,1},{7,0},{8,15},{9,14},{10,... | collective-permute-start | bytes 184328 | tf_op jit(solution)/shard_map/ppermute | solution.py:368
  120.3 5.8 %collective-permute-done.45.refs_5_ = bf16[16,1920]{1,0:T(8,128)(2,1)S(1)} collective-permute-done((bf16[16,1920]{1,0:T(8,128)(2,1)S(1)}, bf16[16,1920]{1,0:T(8,128)(2,1)S(1)}, u32[]{:S(2)}, u32[]{:S(2)}) %collective-permute-start.45) | collective-permute-done | bytes 61472 | tf_op jit(solution)/shard_map/ppermute | solution.py:368
  126.2 1.2 leave.1
  (78 shorter events, 10.9 us)
Async XLA Ops:
  3.6 4.5 %collective-permute-start = (bf16[16,1920]{1,0:T(8,128)(2,1)S(1)}, bf16[16,1920]{1,0:T(8,128)(2,1)S(1)}, u32[]{:S(2)}, u32[]{:S(2)}) collective-permute-start(bf16[16,1920]{1,0:T(8,128)(2,1)S(1)} %get-tuple-element.62), channel_id=1, source_target_pairs={{0,1},{1,0},{2,3},{3,2},{4,5},{5,4},{6,7},{7,6},{8,9},{9,8},{10,11... | collective-permute-start | bytes 184328 | tf_op jit(solution)/shard_map/ppermute | solution.py:368
  3.6 8.1 %collective-permute-start.1 = (bf16[16,1920]{1,0:T(8,128)(2,1)S(1)}, bf16[16,1920]{1,0:T(8,128)(2,1)S(1)}, u32[]{:S(2)}, u32[]{:S(2)}) collective-permute-start(bf16[16,1920]{1,0:T(8,128)(2,1)S(1)} %get-tuple-element.63), channel_id=1, source_target_pairs={{0,2},{1,3},{2,0},{3,1},{4,6},{5,7},{6,4},{7,5},{8,10},{9,11},{10,... | collective-permute-start | bytes 184328 | tf_op jit(solution)/shard_map/ppermute | solution.py:368
  5.3 6.5 %collective-permute-start.2 = (bf16[16,1920]{1,0:T(8,128)(2,1)S(1)}, bf16[16,1920]{1,0:T(8,128)(2,1)S(1)}, u32[]{:S(2)}, u32[]{:S(2)}) collective-permute-start(bf16[16,1920]{1,0:T(8,128)(2,1)S(1)} %get-tuple-element.64), channel_id=1, source_target_pairs={{0,3},{1,2},{2,1},{3,0},{4,7},{5,6},{6,5},{7,4},{8,11},{9,10},{10,... | collective-permute-start | bytes 184328 | tf_op jit(solution)/shard_map/ppermute | solution.py:368
  5.5 6.3 %collective-permute-start.3 = (bf16[16,1920]{1,0:T(8,128)(2,1)S(1)}, bf16[16,1920]{1,0:T(8,128)(2,1)S(1)}, u32[]{:S(2)}, u32[]{:S(2)}) collective-permute-start(bf16[16,1920]{1,0:T(8,128)(2,1)S(1)} %get-tuple-element.65), channel_id=1, source_target_pairs={{0,4},{1,5},{2,6},{3,7},{4,0},{5,1},{6,2},{7,3},{8,12},{9,13},{10,... | collective-permute-start | bytes 184328 | tf_op jit(solution)/shard_map/ppermute | solution.py:368
  8.1 10.1 %collective-permute-start.4 = (bf16[16,1920]{1,0:T(8,128)(2,1)S(1)}, bf16[16,1920]{1,0:T(8,128)(2,1)S(1)}, u32[]{:S(2)}, u32[]{:S(2)}) collective-permute-start(bf16[16,1920]{1,0:T(8,128)(2,1)S(1)} %get-tuple-element.66), channel_id=1, source_target_pairs={{0,5},{1,4},{2,7},{3,6},{4,1},{5,0},{6,3},{7,2},{8,13},{9,12},{10,... | collective-permute-start | bytes 184328 | tf_op jit(solution)/shard_map/ppermute | solution.py:368
  8.1 10.1 %collective-permute-start.5 = (bf16[16,1920]{1,0:T(8,128)(2,1)S(1)}, bf16[16,1920]{1,0:T(8,128)(2,1)S(1)}, u32[]{:S(2)}, u32[]{:S(2)}) collective-permute-start(bf16[16,1920]{1,0:T(8,128)(2,1)S(1)} %get-tuple-element.67), channel_id=1, source_target_pairs={{0,6},{1,7},{2,4},{3,5},{4,2},{5,3},{6,0},{7,1},{8,14},{9,15},{10,... | collective-permute-start | bytes 184328 | tf_op jit(solution)/shard_map/ppermute | solution.py:368
  11.7 6.5 %collective-permute-start.6 = (bf16[16,1920]{1,0:T(8,128)(2,1)S(1)}, bf16[16,1920]{1,0:T(8,128)(2,1)S(1)}, u32[]{:S(2)}, u32[]{:S(2)}) collective-permute-start(bf16[16,1920]{1,0:T(8,128)(2,1)S(1)} %get-tuple-element.68), channel_id=1, source_target_pairs={{0,7},{1,6},{2,5},{3,4},{4,3},{5,2},{6,1},{7,0},{8,15},{9,14},{10,... | collective-permute-start | bytes 184328 | tf_op jit(solution)/shard_map/ppermute | solution.py:368
  23.3 6.1 %collective-permute-start.14 = (bf16[16,1920]{1,0:T(8,128)(2,1)S(1)}, bf16[16,1920]{1,0:T(8,128)(2,1)S(1)}, u32[]{:S(2)}, u32[]{:S(2)}) collective-permute-start(bf16[16,1920]{1,0:T(8,128)(2,1)S(1)} %get-tuple-element.78), channel_id=1, source_target_pairs={{0,1},{1,0},{2,3},{3,2},{4,5},{5,4},{6,7},{7,6},{8,9},{9,8},{10,11... | collective-permute-start | bytes 184328 | tf_op jit(solution)/shard_map/ppermute | solution.py:368
  23.5 8.1 %collective-permute-start.15 = (bf16[16,1920]{1,0:T(8,128)(2,1)S(1)}, bf16[16,1920]{1,0:T(8,128)(2,1)S(1)}, u32[]{:S(2)}, u32[]{:S(2)}) collective-permute-start(bf16[16,1920]{1,0:T(8,128)(2,1)S(1)} %get-tuple-element.79), channel_id=1, source_target_pairs={{0,2},{1,3},{2,0},{3,1},{4,6},{5,7},{6,4},{7,5},{8,10},{9,11},{10,... | collective-permute-start | bytes 184328 | tf_op jit(solution)/shard_map/ppermute | solution.py:368
  26.7 7.1 %collective-permute-start.16 = (bf16[16,1920]{1,0:T(8,128)(2,1)S(1)}, bf16[16,1920]{1,0:T(8,128)(2,1)S(1)}, u32[]{:S(2)}, u32[]{:S(2)}) collective-permute-start(bf16[16,1920]{1,0:T(8,128)(2,1)S(1)} %get-tuple-element.80), channel_id=1, source_target_pairs={{0,3},{1,2},{2,1},{3,0},{4,7},{5,6},{6,5},{7,4},{8,11},{9,10},{10,... | collective-permute-start | bytes 184328 | tf_op jit(solution)/shard_map/ppermute | solution.py:368
  26.7 7.1 %collective-permute-start.17 = (bf16[16,1920]{1,0:T(8,128)(2,1)S(1)}, bf16[16,1920]{1,0:T(8,128)(2,1)S(1)}, u32[]{:S(2)}, u32[]{:S(2)}) collective-permute-start(bf16[16,1920]{1,0:T(8,128)(2,1)S(1)} %get-tuple-element.81), channel_id=1, source_target_pairs={{0,4},{1,5},{2,6},{3,7},{4,0},{5,1},{6,2},{7,3},{8,12},{9,13},{10,... | collective-permute-start | bytes 184328 | tf_op jit(solution)/shard_map/ppermute | solution.py:368
  29.5 9.9 %collective-permute-start.18 = (bf16[16,1920]{1,0:T(8,128)(2,1)S(1)}, bf16[16,1920]{1,0:T(8,128)(2,1)S(1)}, u32[]{:S(2)}, u32[]{:S(2)}) collective-permute-start(bf16[16,1920]{1,0:T(8,128)(2,1)S(1)} %get-tuple-element.82), channel_id=1, source_target_pairs={{0,5},{1,4},{2,7},{3,6},{4,1},{5,0},{6,3},{7,2},{8,13},{9,12},{10,... | collective-permute-start | bytes 184328 | tf_op jit(solution)/shard_map/ppermute | solution.py:368
  29.5 9.9 %collective-permute-start.19 = (bf16[16,1920]{1,0:T(8,128)(2,1)S(1)}, bf16[16,1920]{1,0:T(8,128)(2,1)S(1)}, u32[]{:S(2)}, u32[]{:S(2)}) collective-permute-start(bf16[16,1920]{1,0:T(8,128)(2,1)S(1)} %get-tuple-element.83), channel_id=1, source_target_pairs={{0,6},{1,7},{2,4},{3,5},{4,2},{5,3},{6,0},{7,1},{8,14},{9,15},{10,... | collective-permute-start | bytes 184328 | tf_op jit(solution)/shard_map/ppermute | solution.py:368
  31.6 7.7 %collective-permute-start.20 = (bf16[16,1920]{1,0:T(8,128)(2,1)S(1)}, bf16[16,1920]{1,0:T(8,128)(2,1)S(1)}, u32[]{:S(2)}, u32[]{:S(2)}) collective-permute-start(bf16[16,1920]{1,0:T(8,128)(2,1)S(1)} %get-tuple-element.84), channel_id=1, source_target_pairs={{0,7},{1,6},{2,5},{3,4},{4,3},{5,2},{6,1},{7,0},{8,15},{9,14},{10,... | collective-permute-start | bytes 184328 | tf_op jit(solution)/shard_map/ppermute | solution.py:368
  39.6 30.1 %collective-permute-start.21 = (bf16[128,1536]{1,0:T(8,128)(2,1)S(1)}, bf16[128,1536]{1,0:T(8,128)(2,1)S(1)}, u32[]{:S(2)}, u32[]{:S(2)}) collective-permute-start(bf16[128,1536]{1,0:T(8,128)(2,1)S(1)} %pairs.1.refs_0_.pair_ref), channel_id=1, source_target_pairs={{0,8},{8,16},{16,24},{1,9},{9,17},{17,25},{2,10},{10,18},{18,26},{... | collective-permute-start | bytes 1179656 | tf_op jit(solution)/shard_map/ppermute | solution.py:375
  43.0 26.7 %collective-permute-start.22 = (bf16[128,1536]{1,0:T(8,128)(2,1)S(1)}, bf16[128,1536]{1,0:T(8,128)(2,1)S(1)}, u32[]{:S(2)}, u32[]{:S(2)}) collective-permute-start(bf16[128,1536]{1,0:T(8,128)(2,1)S(1)} %pairs.1.refs_0_.pair_ref), channel_id=1, source_target_pairs={{0,16},{8,24},{1,17},{9,25},{2,18},{10,26},{3,19},{11,27},{4,20},{... | collective-permute-start | bytes 1179656 | tf_op jit(solution)/shard_map/ppermute | solution.py:375
  45.9 5.6 %collective-permute-start.10 = (bf16[16,1920]{1,0:T(8,128)(2,1)S(1)}, bf16[16,1920]{1,0:T(8,128)(2,1)S(1)}, u32[]{:S(2)}, u32[]{:S(2)}) collective-permute-start(bf16[16,1920]{1,0:T(8,128)(2,1)S(1)} %get-tuple-element.73), channel_id=1, source_target_pairs={{0,4},{1,5},{2,6},{3,7},{4,0},{5,1},{6,2},{7,3},{8,12},{9,13},{10,... | collective-permute-start | bytes 184328 | tf_op jit(solution)/shard_map/ppermute | solution.py:368
  49.2 8.6 %collective-permute-start.11 = (bf16[16,1920]{1,0:T(8,128)(2,1)S(1)}, bf16[16,1920]{1,0:T(8,128)(2,1)S(1)}, u32[]{:S(2)}, u32[]{:S(2)}) collective-permute-start(bf16[16,1920]{1,0:T(8,128)(2,1)S(1)} %get-tuple-element.74), channel_id=1, source_target_pairs={{0,5},{1,4},{2,7},{3,6},{4,1},{5,0},{6,3},{7,2},{8,13},{9,12},{10,... | collective-permute-start | bytes 184328 | tf_op jit(solution)/shard_map/ppermute | solution.py:368
  49.2 8.7 %collective-permute-start.12 = (bf16[16,1920]{1,0:T(8,128)(2,1)S(1)}, bf16[16,1920]{1,0:T(8,128)(2,1)S(1)}, u32[]{:S(2)}, u32[]{:S(2)}) collective-permute-start(bf16[16,1920]{1,0:T(8,128)(2,1)S(1)} %get-tuple-element.75), channel_id=1, source_target_pairs={{0,6},{1,7},{2,4},{3,5},{4,2},{5,3},{6,0},{7,1},{8,14},{9,15},{10,... | collective-permute-start | bytes 184328 | tf_op jit(solution)/shard_map/ppermute | solution.py:368
  51.5 8.2 %collective-permute-start.13 = (bf16[16,1920]{1,0:T(8,128)(2,1)S(1)}, bf16[16,1920]{1,0:T(8,128)(2,1)S(1)}, u32[]{:S(2)}, u32[]{:S(2)}) collective-permute-start(bf16[16,1920]{1,0:T(8,128)(2,1)S(1)} %get-tuple-element.76), channel_id=1, source_target_pairs={{0,7},{1,6},{2,5},{3,4},{4,3},{5,2},{6,1},{7,0},{8,15},{9,14},{10,... | collective-permute-start | bytes 184328 | tf_op jit(solution)/shard_map/ppermute | solution.py:368
  57.8 3.5 %collective-permute-start.7 = (bf16[16,1920]{1,0:T(8,128)(2,1)S(1)}, bf16[16,1920]{1,0:T(8,128)(2,1)S(1)}, u32[]{:S(2)}, u32[]{:S(2)}) collective-permute-start(bf16[16,1920]{1,0:T(8,128)(2,1)S(1)} %get-tuple-element.70), channel_id=1, source_target_pairs={{0,1},{1,0},{2,3},{3,2},{4,5},{5,4},{6,7},{7,6},{8,9},{9,8},{10,11... | collective-permute-start | bytes 184328 | tf_op jit(solution)/shard_map/ppermute | solution.py:368
  57.9 4.3 %collective-permute-start.8 = (bf16[16,1920]{1,0:T(8,128)(2,1)S(1)}, bf16[16,1920]{1,0:T(8,128)(2,1)S(1)}, u32[]{:S(2)}, u32[]{:S(2)}) collective-permute-start(bf16[16,1920]{1,0:T(8,128)(2,1)S(1)} %get-tuple-element.71), channel_id=1, source_target_pairs={{0,2},{1,3},{2,0},{3,1},{4,6},{5,7},{6,4},{7,5},{8,10},{9,11},{10,... | collective-permute-start | bytes 184328 | tf_op jit(solution)/shard_map/ppermute | solution.py:368
  59.7 3.8 %collective-permute-start.9 = (bf16[16,1920]{1,0:T(8,128)(2,1)S(1)}, bf16[16,1920]{1,0:T(8,128)(2,1)S(1)}, u32[]{:S(2)}, u32[]{:S(2)}) collective-permute-start(bf16[16,1920]{1,0:T(8,128)(2,1)S(1)} %get-tuple-element.72), channel_id=1, source_target_pairs={{0,3},{1,2},{2,1},{3,0},{4,7},{5,6},{6,5},{7,4},{8,11},{9,10},{10,... | collective-permute-start | bytes 184328 | tf_op jit(solution)/shard_map/ppermute | solution.py:368
  63.8 14.9 %collective-permute-start.23 = (bf16[128,768]{1,0:T(8,128)(2,1)S(1)}, bf16[128,768]{1,0:T(8,128)(2,1)S(1)}, u32[]{:S(2)}, u32[]{:S(2)}) collective-permute-start(bf16[128,768]{1,0:T(8,128)(2,1)S(1)} %slice.4), channel_id=1, source_target_pairs={{8,0},{16,8},{24,16},{9,1},{17,9},{25,17},{10,2},{18,10},{26,18},{... | collective-permute-start | bytes 589832 | tf_op jit(solution)/shard_map/ppermute | solution.py:375
  68.4 12.0 %collective-permute-start.24 = (bf16[128,768]{1,0:T(8,128)(2,1)S(1)}, bf16[128,768]{1,0:T(8,128)(2,1)S(1)}, u32[]{:S(2)}, u32[]{:S(2)}) collective-permute-start(bf16[128,768]{1,0:T(8,128)(2,1)S(1)} %slice.4), channel_id=1, source_target_pairs={{16,0},{24,8},{17,1},{25,9},{18,2},{26,10},{19,3},{27,11},{20,4},{... | collective-permute-start | bytes 589832 | tf_op jit(solution)/shard_map/ppermute | solution.py:375
  72.2 10.2 %collective-permute-start.25 = (bf16[128,768]{1,0:T(8,128)(2,1)S(1)}, bf16[128,768]{1,0:T(8,128)(2,1)S(1)}, u32[]{:S(2)}, u32[]{:S(2)}) collective-permute-start(bf16[128,768]{1,0:T(8,128)(2,1)S(1)} %get-tuple-element.89.refs_3_.grad_ref), channel_id=1, source_target_pairs={{8,0},{16,8},{24,16},{9,1},{17,9},{25,17},{10,2},{18,10},{26,18},{... | collective-permute-start | bytes 589832 | tf_op jit(solution)/shard_map/ppermute | solution.py:375
  74.1 12.4 %collective-permute-start.26 = (bf16[128,768]{1,0:T(8,128)(2,1)S(1)}, bf16[128,768]{1,0:T(8,128)(2,1)S(1)}, u32[]{:S(2)}, u32[]{:S(2)}) collective-permute-start(bf16[128,768]{1,0:T(8,128)(2,1)S(1)} %get-tuple-element.89.refs_3_.grad_ref), channel_id=1, source_target_pairs={{16,0},{24,8},{17,1},{25,9},{18,2},{26,10},{19,3},{27,11},{20,4},{... | collective-permute-start | bytes 589832 | tf_op jit(solution)/shard_map/ppermute | solution.py:375
  78.2 13.2 %collective-permute-start.34 = (bf16[16,1920]{1,0:T(8,128)(2,1)S(1)}, bf16[16,1920]{1,0:T(8,128)(2,1)S(1)}, u32[]{:S(2)}, u32[]{:S(2)}) collective-permute-start(bf16[16,1920]{1,0:T(8,128)(2,1)S(1)} %get-tuple-element.101), channel_id=1, source_target_pairs={{0,1},{1,0},{2,3},{3,2},{4,5},{5,4},{6,7},{7,6},{8,9},{9,8},{10,11... | collective-permute-start | bytes 184328 | tf_op jit(solution)/shard_map/ppermute | solution.py:368
  78.7 14.6 %collective-permute-start.35 = (bf16[16,1920]{1,0:T(8,128)(2,1)S(1)}, bf16[16,1920]{1,0:T(8,128)(2,1)S(1)}, u32[]{:S(2)}, u32[]{:S(2)}) collective-permute-start(bf16[16,1920]{1,0:T(8,128)(2,1)S(1)} %get-tuple-element.102), channel_id=1, source_target_pairs={{0,2},{1,3},{2,0},{3,1},{4,6},{5,7},{6,4},{7,5},{8,10},{9,11},{10,... | collective-permute-start | bytes 184328 | tf_op jit(solution)/shard_map/ppermute | solution.py:368
  80.5 14.6 %collective-permute-start.36 = (bf16[16,1920]{1,0:T(8,128)(2,1)S(1)}, bf16[16,1920]{1,0:T(8,128)(2,1)S(1)}, u32[]{:S(2)}, u32[]{:S(2)}) collective-permute-start(bf16[16,1920]{1,0:T(8,128)(2,1)S(1)} %get-tuple-element.103), channel_id=1, source_target_pairs={{0,3},{1,2},{2,1},{3,0},{4,7},{5,6},{6,5},{7,4},{8,11},{9,10},{10,... | collective-permute-start | bytes 184328 | tf_op jit(solution)/shard_map/ppermute | solution.py:368
  82.4 13.1 %collective-permute-start.37 = (bf16[16,1920]{1,0:T(8,128)(2,1)S(1)}, bf16[16,1920]{1,0:T(8,128)(2,1)S(1)}, u32[]{:S(2)}, u32[]{:S(2)}) collective-permute-start(bf16[16,1920]{1,0:T(8,128)(2,1)S(1)} %get-tuple-element.104), channel_id=1, source_target_pairs={{0,4},{1,5},{2,6},{3,7},{4,0},{5,1},{6,2},{7,3},{8,12},{9,13},{10,... | collective-permute-start | bytes 184328 | tf_op jit(solution)/shard_map/ppermute | solution.py:368
  86.5 9.0 %collective-permute-start.38 = (bf16[16,1920]{1,0:T(8,128)(2,1)S(1)}, bf16[16,1920]{1,0:T(8,128)(2,1)S(1)}, u32[]{:S(2)}, u32[]{:S(2)}) collective-permute-start(bf16[16,1920]{1,0:T(8,128)(2,1)S(1)} %get-tuple-element.105), channel_id=1, source_target_pairs={{0,5},{1,4},{2,7},{3,6},{4,1},{5,0},{6,3},{7,2},{8,13},{9,12},{10,... | collective-permute-start | bytes 184328 | tf_op jit(solution)/shard_map/ppermute | solution.py:368
  91.4 6.3 %collective-permute-start.39 = (bf16[16,1920]{1,0:T(8,128)(2,1)S(1)}, bf16[16,1920]{1,0:T(8,128)(2,1)S(1)}, u32[]{:S(2)}, u32[]{:S(2)}) collective-permute-start(bf16[16,1920]{1,0:T(8,128)(2,1)S(1)} %get-tuple-element.106), channel_id=1, source_target_pairs={{0,6},{1,7},{2,4},{3,5},{4,2},{5,3},{6,0},{7,1},{8,14},{9,15},{10,... | collective-permute-start | bytes 184328 | tf_op jit(solution)/shard_map/ppermute | solution.py:368
  93.3 5.6 %collective-permute-start.40 = (bf16[16,1920]{1,0:T(8,128)(2,1)S(1)}, bf16[16,1920]{1,0:T(8,128)(2,1)S(1)}, u32[]{:S(2)}, u32[]{:S(2)}) collective-permute-start(bf16[16,1920]{1,0:T(8,128)(2,1)S(1)} %get-tuple-element.107), channel_id=1, source_target_pairs={{0,7},{1,6},{2,5},{3,4},{4,3},{5,2},{6,1},{7,0},{8,15},{9,14},{10,... | collective-permute-start | bytes 184328 | tf_op jit(solution)/shard_map/ppermute | solution.py:368
  95.0 4.8 %collective-permute-start.27 = (bf16[16,1920]{1,0:T(8,128)(2,1)S(1)}, bf16[16,1920]{1,0:T(8,128)(2,1)S(1)}, u32[]{:S(2)}, u32[]{:S(2)}) collective-permute-start(bf16[16,1920]{1,0:T(8,128)(2,1)S(1)} %get-tuple-element.91), channel_id=1, source_target_pairs={{0,1},{1,0},{2,3},{3,2},{4,5},{5,4},{6,7},{7,6},{8,9},{9,8},{10,11... | collective-permute-start | bytes 184328 | tf_op jit(solution)/shard_map/ppermute | solution.py:368
  95.4 6.8 %collective-permute-start.28 = (bf16[16,1920]{1,0:T(8,128)(2,1)S(1)}, bf16[16,1920]{1,0:T(8,128)(2,1)S(1)}, u32[]{:S(2)}, u32[]{:S(2)}) collective-permute-start(bf16[16,1920]{1,0:T(8,128)(2,1)S(1)} %get-tuple-element.92), channel_id=1, source_target_pairs={{0,2},{1,3},{2,0},{3,1},{4,6},{5,7},{6,4},{7,5},{8,10},{9,11},{10,... | collective-permute-start | bytes 184328 | tf_op jit(solution)/shard_map/ppermute | solution.py:368
  95.4 10.2 %collective-permute-start.29 = (bf16[16,1920]{1,0:T(8,128)(2,1)S(1)}, bf16[16,1920]{1,0:T(8,128)(2,1)S(1)}, u32[]{:S(2)}, u32[]{:S(2)}) collective-permute-start(bf16[16,1920]{1,0:T(8,128)(2,1)S(1)} %get-tuple-element.93), channel_id=1, source_target_pairs={{0,3},{1,2},{2,1},{3,0},{4,7},{5,6},{6,5},{7,4},{8,11},{9,10},{10,... | collective-permute-start | bytes 184328 | tf_op jit(solution)/shard_map/ppermute | solution.py:368
  97.7 9.2 %collective-permute-start.30 = (bf16[16,1920]{1,0:T(8,128)(2,1)S(1)}, bf16[16,1920]{1,0:T(8,128)(2,1)S(1)}, u32[]{:S(2)}, u32[]{:S(2)}) collective-permute-start(bf16[16,1920]{1,0:T(8,128)(2,1)S(1)} %get-tuple-element.94), channel_id=1, source_target_pairs={{0,4},{1,5},{2,6},{3,7},{4,0},{5,1},{6,2},{7,3},{8,12},{9,13},{10,... | collective-permute-start | bytes 184328 | tf_op jit(solution)/shard_map/ppermute | solution.py:368
  98.9 9.8 %collective-permute-start.31 = (bf16[16,1920]{1,0:T(8,128)(2,1)S(1)}, bf16[16,1920]{1,0:T(8,128)(2,1)S(1)}, u32[]{:S(2)}, u32[]{:S(2)}) collective-permute-start(bf16[16,1920]{1,0:T(8,128)(2,1)S(1)} %get-tuple-element.95), channel_id=1, source_target_pairs={{0,5},{1,4},{2,7},{3,6},{4,1},{5,0},{6,3},{7,2},{8,13},{9,12},{10,... | collective-permute-start | bytes 184328 | tf_op jit(solution)/shard_map/ppermute | solution.py:368
  99.8 8.9 %collective-permute-start.32 = (bf16[16,1920]{1,0:T(8,128)(2,1)S(1)}, bf16[16,1920]{1,0:T(8,128)(2,1)S(1)}, u32[]{:S(2)}, u32[]{:S(2)}) collective-permute-start(bf16[16,1920]{1,0:T(8,128)(2,1)S(1)} %get-tuple-element.96), channel_id=1, source_target_pairs={{0,6},{1,7},{2,4},{3,5},{4,2},{5,3},{6,0},{7,1},{8,14},{9,15},{10,... | collective-permute-start | bytes 184328 | tf_op jit(solution)/shard_map/ppermute | solution.py:368
  102.2 6.6 %collective-permute-start.33 = (bf16[16,1920]{1,0:T(8,128)(2,1)S(1)}, bf16[16,1920]{1,0:T(8,128)(2,1)S(1)}, u32[]{:S(2)}, u32[]{:S(2)}) collective-permute-start(bf16[16,1920]{1,0:T(8,128)(2,1)S(1)} %get-tuple-element.97), channel_id=1, source_target_pairs={{0,7},{1,6},{2,5},{3,4},{4,3},{5,2},{6,1},{7,0},{8,15},{9,14},{10,... | collective-permute-start | bytes 184328 | tf_op jit(solution)/shard_map/ppermute | solution.py:368
  110.7 5.9 %collective-permute-start.41 = (bf16[16,1920]{1,0:T(8,128)(2,1)S(1)}, bf16[16,1920]{1,0:T(8,128)(2,1)S(1)}, u32[]{:S(2)}, u32[]{:S(2)}) collective-permute-start(bf16[16,1920]{1,0:T(8,128)(2,1)S(1)} %get-tuple-element.109), channel_id=1, source_target_pairs={{0,1},{1,0},{2,3},{3,2},{4,5},{5,4},{6,7},{7,6},{8,9},{9,8},{10,11... | collective-permute-start | bytes 184328 | tf_op jit(solution)/shard_map/ppermute | solution.py:368
  111.3 7.4 %collective-permute-start.42 = (bf16[16,1920]{1,0:T(8,128)(2,1)S(1)}, bf16[16,1920]{1,0:T(8,128)(2,1)S(1)}, u32[]{:S(2)}, u32[]{:S(2)}) collective-permute-start(bf16[16,1920]{1,0:T(8,128)(2,1)S(1)} %get-tuple-element.110), channel_id=1, source_target_pairs={{0,2},{1,3},{2,0},{3,1},{4,6},{5,7},{6,4},{7,5},{8,10},{9,11},{10,... | collective-permute-start | bytes 184328 | tf_op jit(solution)/shard_map/ppermute | solution.py:368
  114.1 6.2 %collective-permute-start.43 = (bf16[16,1920]{1,0:T(8,128)(2,1)S(1)}, bf16[16,1920]{1,0:T(8,128)(2,1)S(1)}, u32[]{:S(2)}, u32[]{:S(2)}) collective-permute-start(bf16[16,1920]{1,0:T(8,128)(2,1)S(1)} %get-tuple-element.111), channel_id=1, source_target_pairs={{0,3},{1,2},{2,1},{3,0},{4,7},{5,6},{6,5},{7,4},{8,11},{9,10},{10,... | collective-permute-start | bytes 184328 | tf_op jit(solution)/shard_map/ppermute | solution.py:368
  114.1 6.2 %collective-permute-start.44 = (bf16[16,1920]{1,0:T(8,128)(2,1)S(1)}, bf16[16,1920]{1,0:T(8,128)(2,1)S(1)}, u32[]{:S(2)}, u32[]{:S(2)}) collective-permute-start(bf16[16,1920]{1,0:T(8,128)(2,1)S(1)} %get-tuple-element.112), channel_id=1, source_target_pairs={{0,4},{1,5},{2,6},{3,7},{4,0},{5,1},{6,2},{7,3},{8,12},{9,13},{10,... | collective-permute-start | bytes 184328 | tf_op jit(solution)/shard_map/ppermute | solution.py:368
  116.3 9.8 %collective-permute-start.45 = (bf16[16,1920]{1,0:T(8,128)(2,1)S(1)}, bf16[16,1920]{1,0:T(8,128)(2,1)S(1)}, u32[]{:S(2)}, u32[]{:S(2)}) collective-permute-start(bf16[16,1920]{1,0:T(8,128)(2,1)S(1)} %get-tuple-element.113), channel_id=1, source_target_pairs={{0,5},{1,4},{2,7},{3,6},{4,1},{5,0},{6,3},{7,2},{8,13},{9,12},{10,... | collective-permute-start | bytes 184328 | tf_op jit(solution)/shard_map/ppermute | solution.py:368
  116.6 9.6 %collective-permute-start.46 = (bf16[16,1920]{1,0:T(8,128)(2,1)S(1)}, bf16[16,1920]{1,0:T(8,128)(2,1)S(1)}, u32[]{:S(2)}, u32[]{:S(2)}) collective-permute-start(bf16[16,1920]{1,0:T(8,128)(2,1)S(1)} %get-tuple-element.114), channel_id=1, source_target_pairs={{0,6},{1,7},{2,4},{3,5},{4,2},{5,3},{6,0},{7,1},{8,14},{9,15},{10,... | collective-permute-start | bytes 184328 | tf_op jit(solution)/shard_map/ppermute | solution.py:368
  118.7 7.5 %collective-permute-start.47 = (bf16[16,1920]{1,0:T(8,128)(2,1)S(1)}, bf16[16,1920]{1,0:T(8,128)(2,1)S(1)}, u32[]{:S(2)}, u32[]{:S(2)}) collective-permute-start(bf16[16,1920]{1,0:T(8,128)(2,1)S(1)} %get-tuple-element.115), channel_id=1, source_target_pairs={{0,7},{1,6},{2,5},{3,4},{4,3},{5,2},{6,1},{7,0},{8,15},{9,14},{10,... | collective-permute-start | bytes 184328 | tf_op jit(solution)/shard_map/ppermute | solution.py:368
  (8 other events, 162.6 us)

commit v3 on v2

--- a/solution.py
+++ b/solution.py
@@ -7,6 +7,7 @@
 from jax.experimental.pallas import tpu as pltpu
 from jax.sharding import PartitionSpec as P
 
+
 HEADS = 6
 HD = 128
 SCEN = 8
@@ -18,29 +19,27 @@
 EXTRA = CAP - MAIN
 FOLD = MAIN // EXTRA
 
+VMEM_LIMIT = 24 << 20
+VMEM_ALL = 67043328
+LANES = 128
+
 eps = 1e-05
 f32 = jnp.float32
 bf16 = jnp.bfloat16
 NT = (((1,), (1,)), ((), ()))
 
 
-def whole(count):
-    return [pl.BlockSpec(memory_space=pltpu.VMEM) for _ in range(count)]
-
-
-def call(kernel, outs, operands, name, flops=1 << 24, smem=0, limit=None):
-    specs = whole(len(operands) - smem) + [
-        pl.BlockSpec(memory_space=pltpu.SMEM) for _ in range(smem)
-    ]
+def call(kernel, outs, operands, spaces=(), scratch=(), flops=1 << 24, limit=VMEM_LIMIT):
+    spaces = list(spaces) + [pltpu.VMEM] * (len(operands) - len(spaces))
     moved = sum(o.size * o.dtype.itemsize for o in list(outs) + list(operands))
     return pl.pallas_call(
         kernel,
         out_shape=tuple(outs),
-        in_specs=specs,
-        out_specs=tuple(whole(len(outs))),
-        name=name,
+        in_specs=[pl.BlockSpec(memory_space=space) for space in spaces],
+        out_specs=tuple(pl.BlockSpec(memory_space=pltpu.VMEM) for _ in outs),
+        scratch_shapes=list(scratch),
         cost_estimate=pl.CostEstimate(flops=flops, bytes_accessed=moved, transcendentals=0),
-        compiler_params=pltpu.CompilerParams(vmem_limit_bytes=limit or (24 << 20)),
+        compiler_params=pltpu.CompilerParams(vmem_limit_bytes=limit),
     )(*operands)
 
 
@@ -72,8 +71,21 @@
 
 
 def load(refs, cols):
-    parts = [ref[:, cols] for ref in refs]
+    if swapped(refs):
+        parts = []
+        for i, ref in enumerate(refs[:-1]):
+            parts += [ref[:MAIN, cols], refs[-1][i * MAIN : (i + 1) * MAIN, cols]]
+    else:
+        parts = [ref[:, cols] for ref in refs]
     return parts[0] if len(parts) == 1 else jnp.concatenate(parts, axis=0)
+
+
+def swapped(refs):
+    return len(refs) > 1 and refs[0].shape[0] == 2 * MAIN
+
+
+def rows_in(refs):
+    return 2 * refs[-1].shape[0] if swapped(refs) else sum(ref.shape[0] for ref in refs)
 
 
 def store(refs, cols, value):
@@ -150,7 +162,7 @@
 
 
 def unfold(refs):
-    count = sum(ref.shape[0] for ref in refs) // MAIN
+    count = rows_in(refs) // MAIN
     cols = main_cols(refs)
     extra = load(refs, slice(cols, cols + cols // FOLD))
     pieces = [dot(extra_matrix(count, part, True), extra) for part in range(FOLD)]
@@ -174,10 +186,26 @@
     return scen_ref[...] ^ lax.axis_index("user") if direct else scen_ref[...]
 
 
-def enter_kernel(direct, events_ref, gain_ref, scen_ref, slots_ref, *refs):
+def gain_of(gain_ref):
+    return jnp.concatenate([gain_ref[i : i + 1] for i in range(gain_ref.shape[0])], axis=1)
+
+
+def enter_kernel(direct, events_hbm, gain_hbm, scen_hbm, slots_ref, *refs):
+    events_ref, gain_ref, scen_ref, sems = refs[-4:]
+    refs = refs[:-4]
+    loads = [
+        pltpu.make_async_copy(source, target, sems.at[i])
+        for i, (source, target) in enumerate(
+            [(events_hbm, events_ref), (gain_hbm, gain_ref), (scen_hbm, scen_ref)]
+        )
+    ]
+    for load_ in loads:
+        load_.start()
+    for load_ in loads:
+        load_.wait()
     events = events_ref[...].astype(f32)
     row_inv = lax.rsqrt(jnp.mean(events * events, axis=1, keepdims=True) + eps)
-    normed = (events * row_inv * gain_ref[...]).astype(bf16)
+    normed = (events * row_inv * gain_of(gain_ref)).astype(bf16)
     matrices = slot_matrices(own_scenarios(scen_ref, direct), True)
     for i, matrix in enumerate(matrices):
         slots_ref[i] = matrix
@@ -192,7 +220,25 @@
     return sum(jnp.where(history == i, limit, 0) for i, limit in enumerate(limits))
 
 
-def mask_kernel(direct, blocks, scen_ref, lengths_ref, offsets_ref, rows_ref, see_ref, seen_ref):
+def mask_kernel(direct, blocks, w_hbm, *refs):
+    small, (w_ref, rows_ref, see_ref, seen_ref), rest = refs[:3], refs[3:7], refs[7:]
+    lengths_ref, offsets_ref, scen_ref, sems = rest
+    count = sems.shape[0] - len(small)
+    depth = w_ref.shape[0] // count
+    loads = [
+        pltpu.make_async_copy(
+            w_hbm.at[pl.ds(i * depth, depth)], w_ref.at[pl.ds(i * depth, depth)], sems.at[i]
+        )
+        for i in range(count)
+    ]
+    first_loads = [
+        pltpu.make_async_copy(source, target, sems.at[count + i])
+        for i, (source, target) in enumerate(zip(small, rest))
+    ]
+    for load_ in first_loads + loads:
+        load_.start()
+    for load_ in first_loads:
+        load_.wait()
     for i, matrix in enumerate(slot_matrices(own_scenarios(scen_ref, direct), False)):
         rows_ref[i] = matrix
     rows = see_ref.shape[0]
@@ -215,10 +261,12 @@
         span = slice(block * rows, (block + 1) * rows)
         see_ref[:, span] = visible(first + down, first - block * rows + along)
         seen_ref[:, span] = visible(first + block * rows + along, first + down)
+    for load_ in loads:
+        load_.wait()
 
 
 def project_kernel(count, parts, w_ref, *refs):
-    ins, outs, slope_ref = refs[:count], refs[count : 2 * count], refs[2 * count]
+    ins, outs, slope_ref = refs[:count], refs[count:-1], refs[-1]
     rows = unfold(ins)
     width = HEADS * HD
     done = []
@@ -349,7 +397,7 @@
 def leave_kernel(count, rows_ref, events_ref, gain_ref, *refs):
     matrices = [rows_ref[i] for i in range(1 + FOLD)]
     wires = wires_out(count, refs[:-1])
-    scaled = sum(from_slots(matrices, wire) for wire in wires) * gain_ref[...]
+    scaled = sum(from_slots(matrices, wire) for wire in wires) * gain_of(gain_ref)
     events = events_ref[...].astype(f32)
     row_inv = lax.rsqrt(jnp.mean(events * events, axis=1, keepdims=True) + eps)
     normed = events * row_inv
@@ -358,14 +406,23 @@
 
 
 def exchange(blocks):
+    done = exchanged(blocks)
+    if 1 < len(blocks) < lax.axis_size("user"):
+        others = jnp.concatenate([block[MAIN:] for block in done], axis=0)
+        done += [lax.ppermute(others, "user", [(i, i ^ 1) for i in range(lax.axis_size("user"))])]
+    return done
+
+
+def exchanged(blocks):
+    count = lax.axis_size("user")
     if len(blocks) == 1:
         wire = blocks[0].reshape(-1, MAIN, blocks[0].shape[1])
         done = lax.all_to_all(wire, "user", split_axis=0, concat_axis=0, tiled=True)
         return [done.reshape(blocks[0].shape)]
-    count = lax.axis_size("user")
     done = list(blocks)
-    for k in range(count - 1, 0, -1):
-        done[k] = lax.ppermute(blocks[k], "user", [(i, i ^ k) for i in range(count)])
+    merged = count // len(blocks)
+    for k in range(len(blocks) - 1, 0, -1):
+        done[k] = lax.ppermute(blocks[k], "user", [(i, i ^ (merged * k)) for i in range(count)])
     return done
 
 
@@ -375,7 +432,7 @@
     return lax.ppermute(block, "seq", route)
 
 
-def wires_of(split, boxes):
+def wires_of(boxes):
     cols = boxes[0].shape[1]
     return [jnp.stack([box.reshape(SCEN, MAIN, cols) for box in boxes], axis=1).reshape(-1, cols)]
 
@@ -398,53 +455,64 @@
     direct = split == 1
     senders = SCEN if direct else 1
 
-    def wire(rows, cols):
-        count = rows // MAIN if direct else 1
+    def wire(rows, cols, merged=1):
+        count = rows // (MAIN * merged) if direct else 1
         return [shape((rows // count, cols * (FOLD + 1) // FOLD), bf16)] * count
 
     slots = wire(SCEN * MAIN, feats)
     matrices = shape((1 + FOLD, rows, SCEN * MAIN), bf16)
-    events, w_local, cotan = events[0], w_proj[0], cotangent[0]
-    gain = gain[None]
+    events, w_hbm, cotan = events[0], w_proj[0], cotangent[0]
+    gain = gain.reshape(-1, LANES)
 
     to_slot, *outbox = call(
         functools.partial(enter_kernel, direct),
         [matrices] + slots,
         [events, gain, scenario],
-        "enter",
-    )
-    inbound = exchange(outbox if direct else wires_of(split, outbox * split))
-    to_row, see, seen = call(
+        [pltpu.HBM] * 3,
+        [
+            pltpu.VMEM(events.shape, bf16),
+            pltpu.VMEM(gain.shape, f32),
+            pltpu.VMEM(scenario.shape, jnp.int32),
+            pltpu.SemaphoreType.DMA((3,)),
+        ],
+        limit=VMEM_ALL - (1 << 20),
+    )
+    inbound = exchange(outbox if direct else wires_of(outbox * split))
+    w_local, to_row, see, seen = call(
         functools.partial(mask_kernel, direct, blocks),
-        [matrices] + [shape((rows, blocks * rows), f32)] * 2,
-        [scenario, lengths, offsets],
-        "masks",
-        smem=2,
-    )
-
-    def project(parts, name):
+        [shape(w_hbm.shape, bf16), matrices] + [shape((rows, blocks * rows), f32)] * 2,
+        [w_hbm, lengths, offsets, scenario],
+        [pltpu.HBM] * 4,
+        [
+            pltpu.SMEM(lengths.shape, jnp.int32),
+            pltpu.SMEM(offsets.shape, jnp.int32),
+            pltpu.VMEM(scenario.shape, jnp.int32),
+            pltpu.SemaphoreType.DMA((7,)),
+        ],
+    )
+
+    def project(parts, merged=1):
         cols = len(parts) * width
         *box, slope = call(
             functools.partial(project_kernel, senders, parts),
-            wire(n_user * MAIN, cols) + [shape((n_user * CAP, cols), f32)],
+            wire(n_user * MAIN, cols, merged) + [shape((n_user * CAP, cols), f32)],
             [w_local] + inbound,
-            name,
         )
         return exchange(box), slope
 
-    def rows_of(box, name):
+    def rows_of(box):
         cols = box[0].shape[1] * FOLD // (FOLD + 1)
-        return call(rows_kernel, [shape((rows, cols), bf16)], [to_row] + box, name)[0]
+        return call(rows_kernel, [shape((rows, cols), bf16)], [to_row] + box)[0]
 
     if direct:
         pair_parts, query_parts = (1, 3), (0, 2)
-        pair_back, pair_slope = project(pair_parts, "pair")
-        query_back, query_slope = project(query_parts, "query")
-        pair_own = rows_of(pair_back, "pairs")
-        gq = rows_of(query_back, "queries")
+        pair_back, pair_slope = project(pair_parts)
+        query_back, query_slope = project(query_parts)
+        pair_own = rows_of(pair_back)
+        gq = rows_of(query_back)
     else:
-        (box,), slope = project((0,), "all")
-        gate, value, query, key = [rows_of([part], "part") for part in slices_of(split, box)]
+        (box,), slope = project((0,))
+        gate, value, query, key = [rows_of([part]) for part in slices_of(split, box)]
         pair_own = jnp.concatenate([value, key], axis=1)
         gq = jnp.concatenate([gate, query], axis=1)
     pairs = [pair_own] + [shifted(pair_own, d) for d in range(1, blocks)]
@@ -455,21 +523,22 @@
         functools.partial(forward_kernel, blocks),
         [half, half, half, shape((rows, width), f32)],
         [see, gq, cotan] + pairs,
-        "forward",
     )
     grads = [grad_own] + [shifted(grad_own, -d) for d in range(1, blocks)]
-    boxes = wire(SCEN * MAIN, 2 * width) if direct else wire(SCEN * MAIN, width) * 2
+
+    def boxes(merged=1):
+        cols = 2 * width if direct else width
+        return wire(SCEN * MAIN, cols, merged) * (1 if direct else 2)
+
     query_grad = call(
-        functools.partial(query_kernel, senders, blocks),
-        boxes,
+        functools.partial(query_kernel, len(boxes(2)) if direct else 1, blocks),
+        boxes(2),
         [see, gq, grad_own, grad_gate, to_slot] + pairs,
-        "query_grad",
     )
     pair_grad = call(
         functools.partial(key_kernel, senders, blocks),
-        boxes,
+        boxes(),
         [seen, pair_own, to_slot] + queries + grads,
-        "pair_grad",
     )
     term = shape((n_user * CAP, feats), f32)
     if direct:
@@ -477,24 +546,19 @@
             functools.partial(term_kernel, query_parts),
             [term],
             [query_slope, w_local] + exchange(query_grad),
-            "term",
         )
         last_parts, last = pair_parts, [pair_slope, w_local] + exchange(pair_grad) + [query_term]
     else:
         order = [query_grad[0], pair_grad[0], query_grad[1], pair_grad[1]]
-        last_parts, last = (0,), [slope, w_local] + exchange(wires_of(split, order))
+        last_parts, last = (0,), [slope, w_local] + exchange(wires_of(order))
     term_box = call(
-        functools.partial(last_term_kernel, senders, last_parts),
-        wire(n_user * MAIN, feats),
-        last,
-        "last_term",
+        functools.partial(last_term_kernel, senders, last_parts), wire(n_user * MAIN, feats), last
     )
     term_back = exchange(term_box)
     (grad_events,) = call(
         functools.partial(leave_kernel, senders),
         [shape((rows, feats), bf16)],
         [to_row, events, gain] + (term_back if direct else slices_of(split, term_back[0])),
-        "leave",
     )
     return output[None], grad_events[None]
 

time: 130 us -> 129 us (level)
  starting transfers between devices: 68.4 us -> 63.7 us
  waiting for transfers between devices: 34.2 us -> 36.6 us
  Pallas kernels: 17.9 us -> 19.9 us
    ppermute x6, waiting for transfers between devices: 4.1 us -> 10.4 us  [shifted(): return lax.ppermute(block, 'seq', route)]
    ppermute x42 -> x39, starting transfers between devices: 54.3 us -> 49.7 us  [the longest x38 49.6 us: exchanged(): lax.ppermute(blocks[k], 'user', [(i, i ^ merged * k) for i in range(count)])]
    ppermute x42 -> x39, waiting for transfers between devices: 30.1 us -> 26.2 us  [the longest x38 26.2 us: exchanged(): lax.ppermute(blocks[k], 'user', [(i, i ^ merged * k) for i in range(count)])]
    pallas_call x12, Pallas kernels: 17.9 us -> 19.9 us  [call(): pl.pallas_call(kernel, out_shape=tuple(outs), in_specs=[pl.BlockSpec(memo...]
    unnamed x16 -> x18, local copies, waits for them, and re-layouts: 5.35 us -> 5.67 us
  transfers between devices with their start and end apart: 48 -> 45, of which waited for: 12 -> 12; matrix products, arithmetic and copies ran while one was open for 0% -> 0% of each run, Pallas kernels for 10% -> 6%
where the time goes in v3:
time: 129 us; the launch traced here: 127 us
  starting transfers between devices  63.7 us (49%)
  waiting for transfers between devices  36.6 us (28%)
  Pallas kernels  19.9 us (15%)
  local copies, waits for them, and re-layouts  5.7 us (4%)
    ppermute x38, starting transfers between devices, exchanged(): lax.ppermute(blocks[k], 'user', [(i, i ^ merged * k) for i in range(count)])  49.6 us
    ppermute x38, waiting for transfers between devices, exchanged(): lax.ppermute(blocks[k], 'user', [(i, i ^ merged * k) for i in range(count)])  26.2 us
    pallas_call x12, Pallas kernels, call(): pl.pallas_call(kernel, out_shape=tuple(outs), in_specs=[pl.BlockSpec(memo...  19.9 us
    ppermute x6, starting transfers between devices, shifted(): return lax.ppermute(block, 'seq', route)  14 us
    ppermute x6, waiting for transfers between devices, shifted(): return lax.ppermute(block, 'seq', route)  10.4 us
    unnamed x18, local copies, waits for them, and re-layouts  5.67 us
  transfers between devices with their start and end apart: 45, of which 12 were waited for; matrix products, arithmetic and copies ran while one was open for 0% of the time, Pallas kernels for 6%

profile of v3, /device:TPU:2, one launch (start us, length us, event | category | flops | bytes accessed | tf_op | source)
XLA Modules:
  0.0 126.9 jit_solution(16117247815375343189)
XLA Ops:
  0.6 2.3 %shard_map.87 = (bf16[5,128,128]{2,1,0:T(8,128)(2,1)}, bf16[16,1920]{1,0:T(8,128)(2,1)}, bf16[16,1920]{1,0:T(8,128)(2,1)}, bf16[16,1920]{1,0:T(8,128)(2,1)}, bf1...) custom-call(bf16[128,1536]{1,0:T(8,128)(2,1)} %bitcast.7, ...), custom_call_target="tpu_custom_call" | custom-call | flops 16777216 | bytes 1055232 | tf_op jit(solution)/shard_map/pallas_call | solution.py:35
  3.0 1.6 %collective-permute-start.1 = (bf16[16,1920]{1,0:T(8,128)(2,1)}, bf16[16,1920]{1,0:T(8,128)(2,1)S(1)}, u32[]{:S(2)}, u32[]{:S(2)}) collective-permute-start(bf16[16,1920]{1,0:T(8,128)(2,1)} %get-tuple-element.61), channel_id=1, source_target_pairs={{0,2},{1,3},{2,0},{3,1},{4,6},{5,7},{6,4},{7,5},{8,10},{9,11},{10,... | collective-permute-start | bytes 184328 | tf_op jit(solution)/shard_map/ppermute | solution.py:425
  4.9 2.6 %collective-permute-start.3 = (bf16[16,1920]{1,0:T(8,128)(2,1)}, bf16[16,1920]{1,0:T(8,128)(2,1)S(1)}, u32[]{:S(2)}, u32[]{:S(2)}) collective-permute-start(bf16[16,1920]{1,0:T(8,128)(2,1)} %get-tuple-element.63), channel_id=1, source_target_pairs={{0,4},{1,5},{2,6},{3,7},{4,0},{5,1},{6,2},{7,3},{8,12},{9,13},{10,... | collective-permute-start | bytes 184328 | tf_op jit(solution)/shard_map/ppermute | solution.py:425
  7.5 3.6 %collective-permute-start.5 = (bf16[16,1920]{1,0:T(8,128)(2,1)}, bf16[16,1920]{1,0:T(8,128)(2,1)S(1)}, u32[]{:S(2)}, u32[]{:S(2)}) collective-permute-start(bf16[16,1920]{1,0:T(8,128)(2,1)} %get-tuple-element.65), channel_id=1, source_target_pairs={{0,6},{1,7},{2,4},{3,5},{4,2},{5,3},{6,0},{7,1},{8,14},{9,15},{10,... | collective-permute-start | bytes 184328 | tf_op jit(solution)/shard_map/ppermute | solution.py:425
  11.2 3.7 %copy-done = bf16[1,1536,3072]{2,1,0:T(8,128)(2,1)S(1)} copy-done((bf16[1,1536,3072]{2,1,0:T(8,128)(2,1)S(1)}, bf16[1,1536,3072]{2,1,0:T(8,128)(2,1)}, u32[]{:S(2)}) %copy-start) | copy-done | bytes 9437208
  16.9 1.0 shard_map.86
  18.0 1.4 %shard_map.90 = (bf16[16,1920]{1,0:T(8,128)(2,1)S(1)}, bf16[16,1920]{1,0:T(8,128)(2,1)S(1)}, bf16[16,1920]{1,0:T(8,128)(2,1)S(1)}, bf16[16,1920]{1,0:T(8,128)(2,...) custom-call(bf16[1536,3072]{1,0:T(8,128)(2,1)S(1)} %get-tuple-elemen, ...), custom_call_target="tpu_custom_call" | custom-call | flops 16777216 | bytes 11403264 | tf_op jit(solution)/shard_map/pallas_call | solution.py:35
  20.2 2.4 %collective-permute-start.15 = (bf16[16,1920]{1,0:T(8,128)(2,1)S(1)}, bf16[16,1920]{1,0:T(8,128)(2,1)S(1)}, u32[]{:S(2)}, u32[]{:S(2)}) collective-permute-start(bf16[16,1920]{1,0:T(8,128)(2,1)S(1)} %get-tuple-element.77), channel_id=1, source_target_pairs={{0,2},{1,3},{2,0},{3,1},{4,6},{5,7},{6,4},{7,5},{8,10},{9,11},{10,... | collective-permute-start | bytes 184328 | tf_op jit(solution)/shard_map/ppermute | solution.py:425
  22.6 2.8 %collective-permute-start.17 = (bf16[16,1920]{1,0:T(8,128)(2,1)S(1)}, bf16[16,1920]{1,0:T(8,128)(2,1)S(1)}, u32[]{:S(2)}, u32[]{:S(2)}) collective-permute-start(bf16[16,1920]{1,0:T(8,128)(2,1)S(1)} %get-tuple-element.79), channel_id=1, source_target_pairs={{0,4},{1,5},{2,6},{3,7},{4,0},{5,1},{6,2},{7,3},{8,12},{9,13},{10,... | collective-permute-start | bytes 184328 | tf_op jit(solution)/shard_map/ppermute | solution.py:425
  25.4 2.3 %collective-permute-start.19 = (bf16[16,1920]{1,0:T(8,128)(2,1)S(1)}, bf16[16,1920]{1,0:T(8,128)(2,1)S(1)}, u32[]{:S(2)}, u32[]{:S(2)}) collective-permute-start(bf16[16,1920]{1,0:T(8,128)(2,1)S(1)} %get-tuple-element.81), channel_id=1, source_target_pairs={{0,6},{1,7},{2,4},{3,5},{4,2},{5,3},{6,0},{7,1},{8,14},{9,15},{10,... | collective-permute-start | bytes 184328 | tf_op jit(solution)/shard_map/ppermute | solution.py:425
  27.7 1.1 collective-permute-start.20
  28.8 6.4 %collective-permute-done.18.refs_5_ = bf16[16,1920]{1,0:T(8,128)(2,1)S(1)} collective-permute-done((bf16[16,1920]{1,0:T(8,128)(2,1)S(1)}, bf16[16,1920]{1,0:T(8,128)(2,1)S(1)}, u32[]{:S(2)}, u32[]{:S(2)}) %collective-permute-start.18) | collective-permute-done | bytes 61472 | tf_op jit(solution)/shard_map/ppermute | solution.py:425
  35.6 3.4 %collective-permute-start.21 = (bf16[128,1536]{1,0:T(8,128)(2,1)S(1)}, bf16[128,1536]{1,0:T(8,128)(2,1)S(1)}, u32[]{:S(2)}, u32[]{:S(2)}) collective-permute-start(bf16[128,1536]{1,0:T(8,128)(2,1)S(1)} %shard_map.91.refs_0_.pair_ref), channel_id=1, source_target_pairs={{0,8},{8,16},{16,24},{1,9},{9,17},{17,25},{2,10},{10,18},{18,26},{... | collective-permute-start | bytes 1179656 | tf_op jit(solution)/shard_map/ppermute | solution.py:432
  39.0 1.3 %collective-permute-start.22 = (bf16[128,1536]{1,0:T(8,128)(2,1)S(1)}, bf16[128,1536]{1,0:T(8,128)(2,1)S(1)}, u32[]{:S(2)}, u32[]{:S(2)}) collective-permute-start(bf16[128,1536]{1,0:T(8,128)(2,1)S(1)} %shard_map.91.refs_0_.pair_ref), channel_id=1, source_target_pairs={{0,16},{8,24},{1,17},{9,25},{2,18},{10,26},{3,19},{11,27},{4,20},{... | collective-permute-start | bytes 1179656 | tf_op jit(solution)/shard_map/ppermute | solution.py:432
  40.3 1.5 %shard_map.88 = (bf16[16,1920]{1,0:T(8,128)(2,1)S(1)}, bf16[16,1920]{1,0:T(8,128)(2,1)S(1)}, bf16[16,1920]{1,0:T(8,128)(2,1)S(1)}, bf16[16,1920]{1,0:T(8,128)(2,...) custom-call(bf16[1536,3072]{1,0:T(8,128)(2,1)S(1)} %get-tuple-elemen, ...), custom_call_target="tpu_custom_call" | custom-call | flops 16777216 | bytes 11403264 | tf_op jit(solution)/shard_map/pallas_call | solution.py:35
  41.8 3.4 %collective-permute-start.10 = (bf16[16,1920]{1,0:T(8,128)(2,1)S(1)}, bf16[16,1920]{1,0:T(8,128)(2,1)S(1)}, u32[]{:S(2)}, u32[]{:S(2)}) collective-permute-start(bf16[16,1920]{1,0:T(8,128)(2,1)S(1)} %get-tuple-element.71), channel_id=1, source_target_pairs={{0,4},{1,5},{2,6},{3,7},{4,0},{5,1},{6,2},{7,3},{8,12},{9,13},{10,... | collective-permute-start | bytes 184328 | tf_op jit(solution)/shard_map/ppermute | solution.py:425
  45.2 2.2 %collective-permute-start.12 = (bf16[16,1920]{1,0:T(8,128)(2,1)S(1)}, bf16[16,1920]{1,0:T(8,128)(2,1)S(1)}, u32[]{:S(2)}, u32[]{:S(2)}) collective-permute-start(bf16[16,1920]{1,0:T(8,128)(2,1)S(1)} %get-tuple-element.73), channel_id=1, source_target_pairs={{0,6},{1,7},{2,4},{3,5},{4,2},{5,3},{6,0},{7,1},{8,14},{9,15},{10,... | collective-permute-start | bytes 184328 | tf_op jit(solution)/shard_map/ppermute | solution.py:425
  47.4 1.1 collective-permute-start.13
  48.5 5.2 %collective-permute-done.11.refs_5_ = bf16[16,1920]{1,0:T(8,128)(2,1)S(1)} collective-permute-done((bf16[16,1920]{1,0:T(8,128)(2,1)S(1)}, bf16[16,1920]{1,0:T(8,128)(2,1)S(1)}, u32[]{:S(2)}, u32[]{:S(2)}) %collective-permute-start.11) | collective-permute-done | bytes 61472 | tf_op jit(solution)/shard_map/ppermute | solution.py:425
  53.8 1.8 %collective-permute-start.8 = (bf16[16,1920]{1,0:T(8,128)(2,1)S(1)}, bf16[16,1920]{1,0:T(8,128)(2,1)S(1)}, u32[]{:S(2)}, u32[]{:S(2)}) collective-permute-start(bf16[16,1920]{1,0:T(8,128)(2,1)S(1)} %get-tuple-element.69), channel_id=1, source_target_pairs={{0,2},{1,3},{2,0},{3,1},{4,6},{5,7},{6,4},{7,5},{8,10},{9,11},{10,... | collective-permute-start | bytes 184328 | tf_op jit(solution)/shard_map/ppermute | solution.py:425
  55.6 1.7 %collective-permute-start.9 = (bf16[16,1920]{1,0:T(8,128)(2,1)S(1)}, bf16[16,1920]{1,0:T(8,128)(2,1)S(1)}, u32[]{:S(2)}, u32[]{:S(2)}) collective-permute-start(bf16[16,1920]{1,0:T(8,128)(2,1)S(1)} %get-tuple-element.70), channel_id=1, source_target_pairs={{0,3},{1,2},{2,1},{3,0},{4,7},{5,6},{6,5},{7,4},{8,11},{9,10},{10,... | collective-permute-start | bytes 184328 | tf_op jit(solution)/shard_map/ppermute | solution.py:425
  58.2 1.2 collective-permute-done.9.refs_3_
  59.8 2.4 %shard_map.92 = (bf16[128,768]{1,0:T(8,128)(2,1)}, bf16[128,768]{1,0:T(8,128)(2,1)S(1)}, bf16[128,768]{1,0:T(8,128)(2,1)S(1)}, f32[128,768]{1,0:T(8,128)}) custom-call(f32[128,384]{1,0:T(8,128)S(1)} %get-tuple-element.56.see_ref, bf16[128,1536]{1,0:T(8,128)(2,1)S(1)} %shard_map.89.gq_ref.refs_0_, bf16[128,768]{1,0:T(8,128)(2,1)S(1)} %bitcast.9, ...), custom_call_target="tpu_custom_call" | custom-call | flops 16777216 | bytes 2949120 | tf_op jit(solution)/shard_map/pallas_call | solution.py:35
  62.2 2.6 %shard_map.94 = (bf16[32,1920]{1,0:T(8,128)(2,1)S(1)}, bf16[32,1920]{1,0:T(8,128)(2,1)S(1)}, bf16[32,1920]{1,0:T(8,128)(2,1)S(1)}, bf16[32,1920]{1,0:T(8,128)(2,1)S(1)}) custom-call(f32[128,384]{1,0:T(8,128)S(1)} %get-tuple-element.56.see_ref, bf16[128,1536]{1,0:T(8,128)(2,1)S(1)} %shard_map.89.gq_ref.refs_0_, ...), custom_call_target="tpu_custom_call" | custom-call | flops 16777216 | bytes 2818048 | tf_op jit(solution)/shard_map/pallas_call | solution.py:35
  64.7 2.3 %collective-permute-start.34 = (bf16[32,1920]{1,0:T(8,128)(2,1)S(1)}, bf16[32,1920]{1,0:T(8,128)(2,1)S(1)}, u32[]{:S(2)}, u32[]{:S(2)}) collective-permute-start(bf16[32,1920]{1,0:T(8,128)(2,1)S(1)} %get-tuple-element.99), channel_id=1, source_target_pairs={{0,2},{1,3},{2,0},{3,1},{4,6},{5,7},{6,4},{7,5},{8,10},{9,11},{10,... | collective-permute-start | bytes 368648 | tf_op jit(solution)/shard_map/ppermute | solution.py:425
  67.0 1.7 %collective-permute-start.35 = (bf16[32,1920]{1,0:T(8,128)(2,1)S(1)}, bf16[32,1920]{1,0:T(8,128)(2,1)S(1)}, u32[]{:S(2)}, u32[]{:S(2)}) collective-permute-start(bf16[32,1920]{1,0:T(8,128)(2,1)S(1)} %get-tuple-element.100), channel_id=1, source_target_pairs={{0,4},{1,5},{2,6},{3,7},{4,0},{5,1},{6,2},{7,3},{8,12},{9,13},{10,... | collective-permute-start | bytes 368648 | tf_op jit(solution)/shard_map/ppermute | solution.py:425
  69.5 4.6 %collective-permute-start.23 = (bf16[128,768]{1,0:T(8,128)(2,1)S(1)}, bf16[128,768]{1,0:T(8,128)(2,1)S(1)}, u32[]{:S(2)}, u32[]{:S(2)}) collective-permute-start(bf16[128,768]{1,0:T(8,128)(2,1)S(1)} %slice.20), channel_id=1, source_target_pairs={{8,0},{16,8},{24,16},{9,1},{17,9},{25,17},{10,2},{18,10},{26,18},{... | collective-permute-start | bytes 589832 | tf_op jit(solution)/shard_map/ppermute | solution.py:432
  74.1 1.3 %collective-permute-start.24 = (bf16[128,768]{1,0:T(8,128)(2,1)S(1)}, bf16[128,768]{1,0:T(8,128)(2,1)S(1)}, u32[]{:S(2)}, u32[]{:S(2)}) collective-permute-start(bf16[128,768]{1,0:T(8,128)(2,1)S(1)} %slice.20), channel_id=1, source_target_pairs={{16,0},{24,8},{17,1},{25,9},{18,2},{26,10},{19,3},{27,11},{20,4},{... | collective-permute-start | bytes 589832 | tf_op jit(solution)/shard_map/ppermute | solution.py:432
  75.4 1.9 %collective-permute-start.25 = (bf16[128,768]{1,0:T(8,128)(2,1)S(1)}, bf16[128,768]{1,0:T(8,128)(2,1)S(1)}, u32[]{:S(2)}, u32[]{:S(2)}) collective-permute-start(bf16[128,768]{1,0:T(8,128)(2,1)S(1)} %get-tuple-element.87.refs_3_.grad_ref), channel_id=1, source_target_pairs={{8,0},{16,8},{24,16},{9,1},{17,9},{25,17},{10,2},{18,10},{26,18},{... | collective-permute-start | bytes 589832 | tf_op jit(solution)/shard_map/ppermute | solution.py:432
  77.3 1.9 %collective-permute-done.35.refs_2_ = bf16[32,1920]{1,0:T(8,128)(2,1)S(1)} collective-permute-done((bf16[32,1920]{1,0:T(8,128)(2,1)S(1)}, bf16[32,1920]{1,0:T(8,128)(2,1)S(1)}, u32[]{:S(2)}, u32[]{:S(2)}) %collective-permute-start.35) | collective-permute-done | bytes 122912 | tf_op jit(solution)/shard_map/ppermute | solution.py:425
  79.3 1.5 %collective-permute-start.26 = (bf16[128,768]{1,0:T(8,128)(2,1)S(1)}, bf16[128,768]{1,0:T(8,128)(2,1)S(1)}, u32[]{:S(2)}, u32[]{:S(2)}) collective-permute-start(bf16[128,768]{1,0:T(8,128)(2,1)S(1)} %get-tuple-element.87.refs_3_.grad_ref), channel_id=1, source_target_pairs={{16,0},{24,8},{17,1},{25,9},{18,2},{26,10},{19,3},{27,11},{20,4},{... | collective-permute-start | bytes 589832 | tf_op jit(solution)/shard_map/ppermute | solution.py:432
  80.9 7.0 %collective-permute-done.24.refs_2_ = bf16[128,768]{1,0:T(8,128)(2,1)S(1)} collective-permute-done((bf16[128,768]{1,0:T(8,128)(2,1)S(1)}, bf16[128,768]{1,0:T(8,128)(2,1)S(1)}, u32[]{:S(2)}, u32[]{:S(2)}) %collective-permute-start.24) | collective-permute-done | bytes 196640 | tf_op jit(solution)/shard_map/ppermute | solution.py:432
  87.9 3.3 %collective-permute-done.26.refs_5_ = bf16[128,768]{1,0:T(8,128)(2,1)S(1)} collective-permute-done((bf16[128,768]{1,0:T(8,128)(2,1)S(1)}, bf16[128,768]{1,0:T(8,128)(2,1)S(1)}, u32[]{:S(2)}, u32[]{:S(2)}) %collective-permute-start.26) | collective-permute-done | bytes 196640 | tf_op jit(solution)/shard_map/ppermute | solution.py:432
  91.3 3.1 %shard_map.93 = (bf16[16,1920]{1,0:T(8,128)(2,1)S(1)}, bf16[16,1920]{1,0:T(8,128)(2,1)S(1)}, bf16[16,1920]{1,0:T(8,128)(2,1)S(1)}, bf16[16,1920]{1,0:T(8,128)(2,...) custom-call(f32[128,384]{1,0:T(8,128)S(1)} %get-tuple-element.85.see, ...), custom_call_target="tpu_custom_call" | custom-call | flops 16777216 | bytes 2621440 | tf_op jit(solution)/shard_map/pallas_call | solution.py:35
  95.3 1.0 collective-permute-start.29
  96.3 1.3 collective-permute-start.30
  97.6 1.4 %collective-permute-start.31 = (bf16[16,1920]{1,0:T(8,128)(2,1)S(1)}, bf16[16,1920]{1,0:T(8,128)(2,1)S(1)}, u32[]{:S(2)}, u32[]{:S(2)}) collective-permute-start(bf16[16,1920]{1,0:T(8,128)(2,1)S(1)} %get-tuple-element.93), channel_id=1, source_target_pairs={{0,5},{1,4},{2,7},{3,6},{4,1},{5,0},{6,3},{7,2},{8,13},{9,12},{10,... | collective-permute-start | bytes 184328 | tf_op jit(solution)/shard_map/ppermute | solution.py:425
  99.4 2.4 %collective-permute-start.32 = (bf16[16,1920]{1,0:T(8,128)(2,1)S(1)}, bf16[16,1920]{1,0:T(8,128)(2,1)S(1)}, u32[]{:S(2)}, u32[]{:S(2)}) collective-permute-start(bf16[16,1920]{1,0:T(8,128)(2,1)S(1)} %get-tuple-element.94), channel_id=1, source_target_pairs={{0,6},{1,7},{2,4},{3,5},{4,2},{5,3},{6,0},{7,1},{8,14},{9,15},{10,... | collective-permute-start | bytes 184328 | tf_op jit(solution)/shard_map/ppermute | solution.py:425
  102.5 1.8 %shard_map.95.refs_8_ = f32[160,1536]{1,0:T(8,128)S(1)} custom-call(f32[160,1536]{1,0:T(8,128)S(1)} %get-tuple-element.96.slope_ref, bf16[1536,3072]{1,0:T(8,128)(2,1)S(1)} %get-tuple-element.58.w_ref, bf16[32,1920]{1,0:T(8,128)(2,1)S(1)} %get-tuple-element.98.refs_0_, bf16[32,1920]{1,0:T(8,128)(2,1)S(1)} %collective-permute-done.34.refs_1_, ...), custom_call_target="tpu_custom_call" | custom-call | flops 16777216 | bytes 12140544 | tf_op jit(solution)/shard_map/pallas_call | solution.py:35
  104.3 1.4 %collective-permute-done.30.refs_4_ = bf16[16,1920]{1,0:T(8,128)(2,1)S(1)} collective-permute-done((bf16[16,1920]{1,0:T(8,128)(2,1)S(1)}, bf16[16,1920]{1,0:T(8,128)(2,1)S(1)}, u32[]{:S(2)}, u32[]{:S(2)}) %collective-permute-start.30) | collective-permute-done | bytes 61472 | tf_op jit(solution)/shard_map/ppermute | solution.py:425
  106.5 1.4 %collective-permute-done.33.refs_7_ = bf16[16,1920]{1,0:T(8,128)(2,1)S(1)} collective-permute-done((bf16[16,1920]{1,0:T(8,128)(2,1)S(1)}, bf16[16,1920]{1,0:T(8,128)(2,1)S(1)}, u32[]{:S(2)}, u32[]{:S(2)}) %collective-permute-start.33) | collective-permute-done | bytes 61472 | tf_op jit(solution)/shard_map/ppermute | solution.py:425
  107.9 2.0 %shard_map.96 = (bf16[16,1920]{1,0:T(8,128)(2,1)S(1)}, bf16[16,1920]{1,0:T(8,128)(2,1)S(1)}, bf16[16,1920]{1,0:T(8,128)(2,1)S(1)}, bf16[16,1920]{1,0:T(8,128)(2,...) custom-call(f32[160,1536]{1,0:T(8,128)S(1)} %get-tuple-element.84.sl, ...), custom_call_target="tpu_custom_call" | custom-call | flops 16777216 | bytes 12386304 | tf_op jit(solution)/shard_map/pallas_call | solution.py:35
  110.2 2.9 %collective-permute-start.39 = (bf16[16,1920]{1,0:T(8,128)(2,1)S(1)}, bf16[16,1920]{1,0:T(8,128)(2,1)S(1)}, u32[]{:S(2)}, u32[]{:S(2)}) collective-permute-start(bf16[16,1920]{1,0:T(8,128)(2,1)S(1)} %get-tuple-element.104), channel_id=1, source_target_pairs={{0,2},{1,3},{2,0},{3,1},{4,6},{5,7},{6,4},{7,5},{8,10},{9,11},{10,... | collective-permute-start | bytes 184328 | tf_op jit(solution)/shard_map/ppermute | solution.py:425
  113.2 2.7 %collective-permute-start.41 = (bf16[16,1920]{1,0:T(8,128)(2,1)S(1)}, bf16[16,1920]{1,0:T(8,128)(2,1)S(1)}, u32[]{:S(2)}, u32[]{:S(2)}) collective-permute-start(bf16[16,1920]{1,0:T(8,128)(2,1)S(1)} %get-tuple-element.106), channel_id=1, source_target_pairs={{0,4},{1,5},{2,6},{3,7},{4,0},{5,1},{6,2},{7,3},{8,12},{9,13},{10,... | collective-permute-start | bytes 184328 | tf_op jit(solution)/shard_map/ppermute | solution.py:425
  115.8 2.1 %collective-permute-start.43 = (bf16[16,1920]{1,0:T(8,128)(2,1)S(1)}, bf16[16,1920]{1,0:T(8,128)(2,1)S(1)}, u32[]{:S(2)}, u32[]{:S(2)}) collective-permute-start(bf16[16,1920]{1,0:T(8,128)(2,1)S(1)} %get-tuple-element.108), channel_id=1, source_target_pairs={{0,6},{1,7},{2,4},{3,5},{4,2},{5,3},{6,0},{7,1},{8,14},{9,15},{10,... | collective-permute-start | bytes 184328 | tf_op jit(solution)/shard_map/ppermute | solution.py:425
  117.9 1.4 %collective-permute-start.44 = (bf16[16,1920]{1,0:T(8,128)(2,1)S(1)}, bf16[16,1920]{1,0:T(8,128)(2,1)S(1)}, u32[]{:S(2)}, u32[]{:S(2)}) collective-permute-start(bf16[16,1920]{1,0:T(8,128)(2,1)S(1)} %get-tuple-element.109), channel_id=1, source_target_pairs={{0,7},{1,6},{2,5},{3,4},{4,3},{5,2},{6,1},{7,0},{8,15},{9,14},{10,... | collective-permute-start | bytes 184328 | tf_op jit(solution)/shard_map/ppermute | solution.py:425
  119.4 6.3 %collective-permute-done.42.refs_5_ = bf16[16,1920]{1,0:T(8,128)(2,1)S(1)} collective-permute-done((bf16[16,1920]{1,0:T(8,128)(2,1)S(1)}, bf16[16,1920]{1,0:T(8,128)(2,1)S(1)}, u32[]{:S(2)}, u32[]{:S(2)}) %collective-permute-start.42) | collective-permute-done | bytes 61472 | tf_op jit(solution)/shard_map/ppermute | solution.py:425
  125.7 1.2 shard_map.97
  (78 shorter events, 8.8 us)
Async XLA Ops:
  3.0 4.5 %collective-permute-start = (bf16[16,1920]{1,0:T(8,128)(2,1)}, bf16[16,1920]{1,0:T(8,128)(2,1)S(1)}, u32[]{:S(2)}, u32[]{:S(2)}) collective-permute-start(bf16[16,1920]{1,0:T(8,128)(2,1)} %get-tuple-element.60), channel_id=1, source_target_pairs={{0,1},{1,0},{2,3},{3,2},{4,5},{5,4},{6,7},{7,6},{8,9},{9,8},{10,11... | collective-permute-start | bytes 184328 | tf_op jit(solution)/shard_map/ppermute | solution.py:425
  3.0 8.1 %collective-permute-start.1 = (bf16[16,1920]{1,0:T(8,128)(2,1)}, bf16[16,1920]{1,0:T(8,128)(2,1)S(1)}, u32[]{:S(2)}, u32[]{:S(2)}) collective-permute-start(bf16[16,1920]{1,0:T(8,128)(2,1)} %get-tuple-element.61), channel_id=1, source_target_pairs={{0,2},{1,3},{2,0},{3,1},{4,6},{5,7},{6,4},{7,5},{8,10},{9,11},{10,... | collective-permute-start | bytes 184328 | tf_op jit(solution)/shard_map/ppermute | solution.py:425
  4.7 13.2 %collective-permute-start.2 = (bf16[16,1920]{1,0:T(8,128)(2,1)}, bf16[16,1920]{1,0:T(8,128)(2,1)S(1)}, u32[]{:S(2)}, u32[]{:S(2)}) collective-permute-start(bf16[16,1920]{1,0:T(8,128)(2,1)} %get-tuple-element.62), channel_id=1, source_target_pairs={{0,3},{1,2},{2,1},{3,0},{4,7},{5,6},{6,5},{7,4},{8,11},{9,10},{10,... | collective-permute-start | bytes 184328 | tf_op jit(solution)/shard_map/ppermute | solution.py:425
  4.9 13.0 %collective-permute-start.3 = (bf16[16,1920]{1,0:T(8,128)(2,1)}, bf16[16,1920]{1,0:T(8,128)(2,1)S(1)}, u32[]{:S(2)}, u32[]{:S(2)}) collective-permute-start(bf16[16,1920]{1,0:T(8,128)(2,1)} %get-tuple-element.63), channel_id=1, source_target_pairs={{0,4},{1,5},{2,6},{3,7},{4,0},{5,1},{6,2},{7,3},{8,12},{9,13},{10,... | collective-permute-start | bytes 184328 | tf_op jit(solution)/shard_map/ppermute | solution.py:425
  7.5 10.5 %collective-permute-start.4 = (bf16[16,1920]{1,0:T(8,128)(2,1)}, bf16[16,1920]{1,0:T(8,128)(2,1)S(1)}, u32[]{:S(2)}, u32[]{:S(2)}) collective-permute-start(bf16[16,1920]{1,0:T(8,128)(2,1)} %get-tuple-element.64), channel_id=1, source_target_pairs={{0,5},{1,4},{2,7},{3,6},{4,1},{5,0},{6,3},{7,2},{8,13},{9,12},{10,... | collective-permute-start | bytes 184328 | tf_op jit(solution)/shard_map/ppermute | solution.py:425
  7.5 10.4 %collective-permute-start.5 = (bf16[16,1920]{1,0:T(8,128)(2,1)}, bf16[16,1920]{1,0:T(8,128)(2,1)S(1)}, u32[]{:S(2)}, u32[]{:S(2)}) collective-permute-start(bf16[16,1920]{1,0:T(8,128)(2,1)} %get-tuple-element.65), channel_id=1, source_target_pairs={{0,6},{1,7},{2,4},{3,5},{4,2},{5,3},{6,0},{7,1},{8,14},{9,15},{10,... | collective-permute-start | bytes 184328 | tf_op jit(solution)/shard_map/ppermute | solution.py:425
  11.1 6.8 %collective-permute-start.6 = (bf16[16,1920]{1,0:T(8,128)(2,1)}, bf16[16,1920]{1,0:T(8,128)(2,1)S(1)}, u32[]{:S(2)}, u32[]{:S(2)}) collective-permute-start(bf16[16,1920]{1,0:T(8,128)(2,1)} %get-tuple-element.66), channel_id=1, source_target_pairs={{0,7},{1,6},{2,5},{3,4},{4,3},{5,2},{6,1},{7,0},{8,15},{9,14},{10,... | collective-permute-start | bytes 184328 | tf_op jit(solution)/shard_map/ppermute | solution.py:425
  18.0 41.8 %copy-start.4 = (bf16[1,128,768]{2,1,0:T(8,128)(2,1)S(1)}, bf16[1,128,768]{2,1,0:T(8,128)(2,1)}, u32[]{:S(2)}) copy-start(bf16[1,128,768]{2,1,0:T(8,128)(2,1)} %param.13) | copy-start | bytes 589828
  19.4 42.7 %copy-start.2 = (bf16[5,128,128]{2,1,0:T(8,128)(2,1)S(1)}, bf16[5,128,128]{2,1,0:T(8,128)(2,1)}, u32[]{:S(2)}) copy-start(bf16[5,128,128]{2,1,0:T(8,128)(2,1)} %get-tuple-element.86.slots_ref) | copy-start | bytes 491524
  19.4 6.0 %collective-permute-start.14 = (bf16[16,1920]{1,0:T(8,128)(2,1)S(1)}, bf16[16,1920]{1,0:T(8,128)(2,1)S(1)}, u32[]{:S(2)}, u32[]{:S(2)}) collective-permute-start(bf16[16,1920]{1,0:T(8,128)(2,1)S(1)} %get-tuple-element.76), channel_id=1, source_target_pairs={{0,1},{1,0},{2,3},{3,2},{4,5},{5,4},{6,7},{7,6},{8,9},{9,8},{10,11... | collective-permute-start | bytes 184328 | tf_op jit(solution)/shard_map/ppermute | solution.py:425
  20.2 7.5 %collective-permute-start.15 = (bf16[16,1920]{1,0:T(8,128)(2,1)S(1)}, bf16[16,1920]{1,0:T(8,128)(2,1)S(1)}, u32[]{:S(2)}, u32[]{:S(2)}) collective-permute-start(bf16[16,1920]{1,0:T(8,128)(2,1)S(1)} %get-tuple-element.77), channel_id=1, source_target_pairs={{0,2},{1,3},{2,0},{3,1},{4,6},{5,7},{6,4},{7,5},{8,10},{9,11},{10,... | collective-permute-start | bytes 184328 | tf_op jit(solution)/shard_map/ppermute | solution.py:425
  22.6 6.2 %collective-permute-start.16 = (bf16[16,1920]{1,0:T(8,128)(2,1)S(1)}, bf16[16,1920]{1,0:T(8,128)(2,1)S(1)}, u32[]{:S(2)}, u32[]{:S(2)}) collective-permute-start(bf16[16,1920]{1,0:T(8,128)(2,1)S(1)} %get-tuple-element.78), channel_id=1, source_target_pairs={{0,3},{1,2},{2,1},{3,0},{4,7},{5,6},{6,5},{7,4},{8,11},{9,10},{10,... | collective-permute-start | bytes 184328 | tf_op jit(solution)/shard_map/ppermute | solution.py:425
  22.6 6.2 %collective-permute-start.17 = (bf16[16,1920]{1,0:T(8,128)(2,1)S(1)}, bf16[16,1920]{1,0:T(8,128)(2,1)S(1)}, u32[]{:S(2)}, u32[]{:S(2)}) collective-permute-start(bf16[16,1920]{1,0:T(8,128)(2,1)S(1)} %get-tuple-element.79), channel_id=1, source_target_pairs={{0,4},{1,5},{2,6},{3,7},{4,0},{5,1},{6,2},{7,3},{8,12},{9,13},{10,... | collective-permute-start | bytes 184328 | tf_op jit(solution)/shard_map/ppermute | solution.py:425
  25.4 9.9 %collective-permute-start.18 = (bf16[16,1920]{1,0:T(8,128)(2,1)S(1)}, bf16[16,1920]{1,0:T(8,128)(2,1)S(1)}, u32[]{:S(2)}, u32[]{:S(2)}) collective-permute-start(bf16[16,1920]{1,0:T(8,128)(2,1)S(1)} %get-tuple-element.80), channel_id=1, source_target_pairs={{0,5},{1,4},{2,7},{3,6},{4,1},{5,0},{6,3},{7,2},{8,13},{9,12},{10,... | collective-permute-start | bytes 184328 | tf_op jit(solution)/shard_map/ppermute | solution.py:425
  25.4 9.9 %collective-permute-start.19 = (bf16[16,1920]{1,0:T(8,128)(2,1)S(1)}, bf16[16,1920]{1,0:T(8,128)(2,1)S(1)}, u32[]{:S(2)}, u32[]{:S(2)}) collective-permute-start(bf16[16,1920]{1,0:T(8,128)(2,1)S(1)} %get-tuple-element.81), channel_id=1, source_target_pairs={{0,6},{1,7},{2,4},{3,5},{4,2},{5,3},{6,0},{7,1},{8,14},{9,15},{10,... | collective-permute-start | bytes 184328 | tf_op jit(solution)/shard_map/ppermute | solution.py:425
  27.7 7.5 %collective-permute-start.20 = (bf16[16,1920]{1,0:T(8,128)(2,1)S(1)}, bf16[16,1920]{1,0:T(8,128)(2,1)S(1)}, u32[]{:S(2)}, u32[]{:S(2)}) collective-permute-start(bf16[16,1920]{1,0:T(8,128)(2,1)S(1)} %get-tuple-element.82), channel_id=1, source_target_pairs={{0,7},{1,6},{2,5},{3,4},{4,3},{5,2},{6,1},{7,0},{8,15},{9,14},{10,... | collective-permute-start | bytes 184328 | tf_op jit(solution)/shard_map/ppermute | solution.py:425
  35.6 24.2 %collective-permute-start.21 = (bf16[128,1536]{1,0:T(8,128)(2,1)S(1)}, bf16[128,1536]{1,0:T(8,128)(2,1)S(1)}, u32[]{:S(2)}, u32[]{:S(2)}) collective-permute-start(bf16[128,1536]{1,0:T(8,128)(2,1)S(1)} %shard_map.91.refs_0_.pair_ref), channel_id=1, source_target_pairs={{0,8},{8,16},{16,24},{1,9},{9,17},{17,25},{2,10},{10,18},{18,26},{... | collective-permute-start | bytes 1179656 | tf_op jit(solution)/shard_map/ppermute | solution.py:432
  39.0 20.8 %collective-permute-start.22 = (bf16[128,1536]{1,0:T(8,128)(2,1)S(1)}, bf16[128,1536]{1,0:T(8,128)(2,1)S(1)}, u32[]{:S(2)}, u32[]{:S(2)}) collective-permute-start(bf16[128,1536]{1,0:T(8,128)(2,1)S(1)} %shard_map.91.refs_0_.pair_ref), channel_id=1, source_target_pairs={{0,16},{8,24},{1,17},{9,25},{2,18},{10,26},{3,19},{11,27},{4,20},{... | collective-permute-start | bytes 1179656 | tf_op jit(solution)/shard_map/ppermute | solution.py:432
  41.8 5.6 %collective-permute-start.10 = (bf16[16,1920]{1,0:T(8,128)(2,1)S(1)}, bf16[16,1920]{1,0:T(8,128)(2,1)S(1)}, u32[]{:S(2)}, u32[]{:S(2)}) collective-permute-start(bf16[16,1920]{1,0:T(8,128)(2,1)S(1)} %get-tuple-element.71), channel_id=1, source_target_pairs={{0,4},{1,5},{2,6},{3,7},{4,0},{5,1},{6,2},{7,3},{8,12},{9,13},{10,... | collective-permute-start | bytes 184328 | tf_op jit(solution)/shard_map/ppermute | solution.py:425
  45.2 8.6 %collective-permute-start.11 = (bf16[16,1920]{1,0:T(8,128)(2,1)S(1)}, bf16[16,1920]{1,0:T(8,128)(2,1)S(1)}, u32[]{:S(2)}, u32[]{:S(2)}) collective-permute-start(bf16[16,1920]{1,0:T(8,128)(2,1)S(1)} %get-tuple-element.72), channel_id=1, source_target_pairs={{0,5},{1,4},{2,7},{3,6},{4,1},{5,0},{6,3},{7,2},{8,13},{9,12},{10,... | collective-permute-start | bytes 184328 | tf_op jit(solution)/shard_map/ppermute | solution.py:425
  45.2 8.7 %collective-permute-start.12 = (bf16[16,1920]{1,0:T(8,128)(2,1)S(1)}, bf16[16,1920]{1,0:T(8,128)(2,1)S(1)}, u32[]{:S(2)}, u32[]{:S(2)}) collective-permute-start(bf16[16,1920]{1,0:T(8,128)(2,1)S(1)} %get-tuple-element.73), channel_id=1, source_target_pairs={{0,6},{1,7},{2,4},{3,5},{4,2},{5,3},{6,0},{7,1},{8,14},{9,15},{10,... | collective-permute-start | bytes 184328 | tf_op jit(solution)/shard_map/ppermute | solution.py:425
  47.4 8.2 %collective-permute-start.13 = (bf16[16,1920]{1,0:T(8,128)(2,1)S(1)}, bf16[16,1920]{1,0:T(8,128)(2,1)S(1)}, u32[]{:S(2)}, u32[]{:S(2)}) collective-permute-start(bf16[16,1920]{1,0:T(8,128)(2,1)S(1)} %get-tuple-element.74), channel_id=1, source_target_pairs={{0,7},{1,6},{2,5},{3,4},{4,3},{5,2},{6,1},{7,0},{8,15},{9,14},{10,... | collective-permute-start | bytes 184328 | tf_op jit(solution)/shard_map/ppermute | solution.py:425
  53.8 3.5 %collective-permute-start.7 = (bf16[16,1920]{1,0:T(8,128)(2,1)S(1)}, bf16[16,1920]{1,0:T(8,128)(2,1)S(1)}, u32[]{:S(2)}, u32[]{:S(2)}) collective-permute-start(bf16[16,1920]{1,0:T(8,128)(2,1)S(1)} %get-tuple-element.68), channel_id=1, source_target_pairs={{0,1},{1,0},{2,3},{3,2},{4,5},{5,4},{6,7},{7,6},{8,9},{9,8},{10,11... | collective-permute-start | bytes 184328 | tf_op jit(solution)/shard_map/ppermute | solution.py:425
  53.8 4.3 %collective-permute-start.8 = (bf16[16,1920]{1,0:T(8,128)(2,1)S(1)}, bf16[16,1920]{1,0:T(8,128)(2,1)S(1)}, u32[]{:S(2)}, u32[]{:S(2)}) collective-permute-start(bf16[16,1920]{1,0:T(8,128)(2,1)S(1)} %get-tuple-element.69), channel_id=1, source_target_pairs={{0,2},{1,3},{2,0},{3,1},{4,6},{5,7},{6,4},{7,5},{8,10},{9,11},{10,... | collective-permute-start | bytes 184328 | tf_op jit(solution)/shard_map/ppermute | solution.py:425
  55.6 3.8 %collective-permute-start.9 = (bf16[16,1920]{1,0:T(8,128)(2,1)S(1)}, bf16[16,1920]{1,0:T(8,128)(2,1)S(1)}, u32[]{:S(2)}, u32[]{:S(2)}) collective-permute-start(bf16[16,1920]{1,0:T(8,128)(2,1)S(1)} %get-tuple-element.70), channel_id=1, source_target_pairs={{0,3},{1,2},{2,1},{3,0},{4,7},{5,6},{6,5},{7,4},{8,11},{9,10},{10,... | collective-permute-start | bytes 184328 | tf_op jit(solution)/shard_map/ppermute | solution.py:425
  64.7 10.6 %collective-permute-start.34 = (bf16[32,1920]{1,0:T(8,128)(2,1)S(1)}, bf16[32,1920]{1,0:T(8,128)(2,1)S(1)}, u32[]{:S(2)}, u32[]{:S(2)}) collective-permute-start(bf16[32,1920]{1,0:T(8,128)(2,1)S(1)} %get-tuple-element.99), channel_id=1, source_target_pairs={{0,2},{1,3},{2,0},{3,1},{4,6},{5,7},{6,4},{7,5},{8,10},{9,11},{10,... | collective-permute-start | bytes 368648 | tf_op jit(solution)/shard_map/ppermute | solution.py:425
  67.0 12.2 %collective-permute-start.35 = (bf16[32,1920]{1,0:T(8,128)(2,1)S(1)}, bf16[32,1920]{1,0:T(8,128)(2,1)S(1)}, u32[]{:S(2)}, u32[]{:S(2)}) collective-permute-start(bf16[32,1920]{1,0:T(8,128)(2,1)S(1)} %get-tuple-element.100), channel_id=1, source_target_pairs={{0,4},{1,5},{2,6},{3,7},{4,0},{5,1},{6,2},{7,3},{8,12},{9,13},{10,... | collective-permute-start | bytes 368648 | tf_op jit(solution)/shard_map/ppermute | solution.py:425
  68.8 12.0 %collective-permute-start.36 = (bf16[32,1920]{1,0:T(8,128)(2,1)S(1)}, bf16[32,1920]{1,0:T(8,128)(2,1)S(1)}, u32[]{:S(2)}, u32[]{:S(2)}) collective-permute-start(bf16[32,1920]{1,0:T(8,128)(2,1)S(1)} %get-tuple-element.101), channel_id=1, source_target_pairs={{0,6},{1,7},{2,4},{3,5},{4,2},{5,3},{6,0},{7,1},{8,14},{9,15},{10,... | collective-permute-start | bytes 368648 | tf_op jit(solution)/shard_map/ppermute | solution.py:425
  69.5 11.4 %collective-permute-start.23 = (bf16[128,768]{1,0:T(8,128)(2,1)S(1)}, bf16[128,768]{1,0:T(8,128)(2,1)S(1)}, u32[]{:S(2)}, u32[]{:S(2)}) collective-permute-start(bf16[128,768]{1,0:T(8,128)(2,1)S(1)} %slice.20), channel_id=1, source_target_pairs={{8,0},{16,8},{24,16},{9,1},{17,9},{25,17},{10,2},{18,10},{26,18},{... | collective-permute-start | bytes 589832 | tf_op jit(solution)/shard_map/ppermute | solution.py:432
  74.1 13.9 %collective-permute-start.24 = (bf16[128,768]{1,0:T(8,128)(2,1)S(1)}, bf16[128,768]{1,0:T(8,128)(2,1)S(1)}, u32[]{:S(2)}, u32[]{:S(2)}) collective-permute-start(bf16[128,768]{1,0:T(8,128)(2,1)S(1)} %slice.20), channel_id=1, source_target_pairs={{16,0},{24,8},{17,1},{25,9},{18,2},{26,10},{19,3},{27,11},{20,4},{... | collective-permute-start | bytes 589832 | tf_op jit(solution)/shard_map/ppermute | solution.py:432
  75.4 12.6 %collective-permute-start.25 = (bf16[128,768]{1,0:T(8,128)(2,1)S(1)}, bf16[128,768]{1,0:T(8,128)(2,1)S(1)}, u32[]{:S(2)}, u32[]{:S(2)}) collective-permute-start(bf16[128,768]{1,0:T(8,128)(2,1)S(1)} %get-tuple-element.87.refs_3_.grad_ref), channel_id=1, source_target_pairs={{8,0},{16,8},{24,16},{9,1},{17,9},{25,17},{10,2},{18,10},{26,18},{... | collective-permute-start | bytes 589832 | tf_op jit(solution)/shard_map/ppermute | solution.py:432
  79.3 12.0 %collective-permute-start.26 = (bf16[128,768]{1,0:T(8,128)(2,1)S(1)}, bf16[128,768]{1,0:T(8,128)(2,1)S(1)}, u32[]{:S(2)}, u32[]{:S(2)}) collective-permute-start(bf16[128,768]{1,0:T(8,128)(2,1)S(1)} %get-tuple-element.87.refs_3_.grad_ref), channel_id=1, source_target_pairs={{16,0},{24,8},{17,1},{25,9},{18,2},{26,10},{19,3},{27,11},{20,4},{... | collective-permute-start | bytes 589832 | tf_op jit(solution)/shard_map/ppermute | solution.py:432
  80.8 21.1 %collective-permute-start.37 = (bf16[64,1920]{1,0:T(8,128)(2,1)S(1)}, bf16[64,1920]{1,0:T(8,128)(2,1)S(1)}, u32[]{:S(2)}, u32[]{:S(2)}) collective-permute-start(bf16[64,1920]{1,0:T(8,128)(2,1)S(1)} %pad_maximum_fusion), channel_id=1, source_target_pairs={{0,1},{1,0},{2,3},{3,2},{4,5},{5,4},{6,7},{7,6},{8,9},{9,8},{10,11... | collective-permute-start | bytes 737288 | tf_op jit(solution)/shard_map/ppermute | solution.py:412
  94.4 3.2 %collective-permute-start.27 = (bf16[16,1920]{1,0:T(8,128)(2,1)S(1)}, bf16[16,1920]{1,0:T(8,128)(2,1)S(1)}, u32[]{:S(2)}, u32[]{:S(2)}) collective-permute-start(bf16[16,1920]{1,0:T(8,128)(2,1)S(1)} %get-tuple-element.89), channel_id=1, source_target_pairs={{0,1},{1,0},{2,3},{3,2},{4,5},{5,4},{6,7},{7,6},{8,9},{9,8},{10,11... | collective-permute-start | bytes 184328 | tf_op jit(solution)/shard_map/ppermute | solution.py:425
  94.5 4.9 %collective-permute-start.28 = (bf16[16,1920]{1,0:T(8,128)(2,1)S(1)}, bf16[16,1920]{1,0:T(8,128)(2,1)S(1)}, u32[]{:S(2)}, u32[]{:S(2)}) collective-permute-start(bf16[16,1920]{1,0:T(8,128)(2,1)S(1)} %get-tuple-element.90), channel_id=1, source_target_pairs={{0,2},{1,3},{2,0},{3,1},{4,6},{5,7},{6,4},{7,5},{8,10},{9,11},{10,... | collective-permute-start | bytes 184328 | tf_op jit(solution)/shard_map/ppermute | solution.py:425
  95.3 9.0 %collective-permute-start.29 = (bf16[16,1920]{1,0:T(8,128)(2,1)S(1)}, bf16[16,1920]{1,0:T(8,128)(2,1)S(1)}, u32[]{:S(2)}, u32[]{:S(2)}) collective-permute-start(bf16[16,1920]{1,0:T(8,128)(2,1)S(1)} %get-tuple-element.91), channel_id=1, source_target_pairs={{0,3},{1,2},{2,1},{3,0},{4,7},{5,6},{6,5},{7,4},{8,11},{9,10},{10,... | collective-permute-start | bytes 184328 | tf_op jit(solution)/shard_map/ppermute | solution.py:425
  96.3 9.4 %collective-permute-start.30 = (bf16[16,1920]{1,0:T(8,128)(2,1)S(1)}, bf16[16,1920]{1,0:T(8,128)(2,1)S(1)}, u32[]{:S(2)}, u32[]{:S(2)}) collective-permute-start(bf16[16,1920]{1,0:T(8,128)(2,1)S(1)} %get-tuple-element.92), channel_id=1, source_target_pairs={{0,4},{1,5},{2,6},{3,7},{4,0},{5,1},{6,2},{7,3},{8,12},{9,13},{10,... | collective-permute-start | bytes 184328 | tf_op jit(solution)/shard_map/ppermute | solution.py:425
  97.6 8.9 %collective-permute-start.31 = (bf16[16,1920]{1,0:T(8,128)(2,1)S(1)}, bf16[16,1920]{1,0:T(8,128)(2,1)S(1)}, u32[]{:S(2)}, u32[]{:S(2)}) collective-permute-start(bf16[16,1920]{1,0:T(8,128)(2,1)S(1)} %get-tuple-element.93), channel_id=1, source_target_pairs={{0,5},{1,4},{2,7},{3,6},{4,1},{5,0},{6,3},{7,2},{8,13},{9,12},{10,... | collective-permute-start | bytes 184328 | tf_op jit(solution)/shard_map/ppermute | solution.py:425
  99.4 7.1 %collective-permute-start.32 = (bf16[16,1920]{1,0:T(8,128)(2,1)S(1)}, bf16[16,1920]{1,0:T(8,128)(2,1)S(1)}, u32[]{:S(2)}, u32[]{:S(2)}) collective-permute-start(bf16[16,1920]{1,0:T(8,128)(2,1)S(1)} %get-tuple-element.94), channel_id=1, source_target_pairs={{0,6},{1,7},{2,4},{3,5},{4,2},{5,3},{6,0},{7,1},{8,14},{9,15},{10,... | collective-permute-start | bytes 184328 | tf_op jit(solution)/shard_map/ppermute | solution.py:425
  101.9 6.1 %collective-permute-start.33 = (bf16[16,1920]{1,0:T(8,128)(2,1)S(1)}, bf16[16,1920]{1,0:T(8,128)(2,1)S(1)}, u32[]{:S(2)}, u32[]{:S(2)}) collective-permute-start(bf16[16,1920]{1,0:T(8,128)(2,1)S(1)} %get-tuple-element.95), channel_id=1, source_target_pairs={{0,7},{1,6},{2,5},{3,4},{4,3},{5,2},{6,1},{7,0},{8,15},{9,14},{10,... | collective-permute-start | bytes 184328 | tf_op jit(solution)/shard_map/ppermute | solution.py:425
  102.5 23.2 %copy-start.5 = (f32[1536]{0:T(1024)S(1)}, f32[1536]{0:T(1024)}, u32[]{:S(2)}) copy-start(f32[1536]{0:T(1024)} %param.11) | copy-start | bytes 18436
  109.9 5.9 %collective-permute-start.38 = (bf16[16,1920]{1,0:T(8,128)(2,1)S(1)}, bf16[16,1920]{1,0:T(8,128)(2,1)S(1)}, u32[]{:S(2)}, u32[]{:S(2)}) collective-permute-start(bf16[16,1920]{1,0:T(8,128)(2,1)S(1)} %get-tuple-element.103), channel_id=1, source_target_pairs={{0,1},{1,0},{2,3},{3,2},{4,5},{5,4},{6,7},{7,6},{8,9},{9,8},{10,11... | collective-permute-start | bytes 184328 | tf_op jit(solution)/shard_map/ppermute | solution.py:425
  110.2 7.7 %collective-permute-start.39 = (bf16[16,1920]{1,0:T(8,128)(2,1)S(1)}, bf16[16,1920]{1,0:T(8,128)(2,1)S(1)}, u32[]{:S(2)}, u32[]{:S(2)}) collective-permute-start(bf16[16,1920]{1,0:T(8,128)(2,1)S(1)} %get-tuple-element.104), channel_id=1, source_target_pairs={{0,2},{1,3},{2,0},{3,1},{4,6},{5,7},{6,4},{7,5},{8,10},{9,11},{10,... | collective-permute-start | bytes 184328 | tf_op jit(solution)/shard_map/ppermute | solution.py:425
  113.1 6.2 %collective-permute-start.40 = (bf16[16,1920]{1,0:T(8,128)(2,1)S(1)}, bf16[16,1920]{1,0:T(8,128)(2,1)S(1)}, u32[]{:S(2)}, u32[]{:S(2)}) collective-permute-start(bf16[16,1920]{1,0:T(8,128)(2,1)S(1)} %get-tuple-element.105), channel_id=1, source_target_pairs={{0,3},{1,2},{2,1},{3,0},{4,7},{5,6},{6,5},{7,4},{8,11},{9,10},{10,... | collective-permute-start | bytes 184328 | tf_op jit(solution)/shard_map/ppermute | solution.py:425
  113.2 6.2 %collective-permute-start.41 = (bf16[16,1920]{1,0:T(8,128)(2,1)S(1)}, bf16[16,1920]{1,0:T(8,128)(2,1)S(1)}, u32[]{:S(2)}, u32[]{:S(2)}) collective-permute-start(bf16[16,1920]{1,0:T(8,128)(2,1)S(1)} %get-tuple-element.106), channel_id=1, source_target_pairs={{0,4},{1,5},{2,6},{3,7},{4,0},{5,1},{6,2},{7,3},{8,12},{9,13},{10,... | collective-permute-start | bytes 184328 | tf_op jit(solution)/shard_map/ppermute | solution.py:425
  115.8 9.9 %collective-permute-start.42 = (bf16[16,1920]{1,0:T(8,128)(2,1)S(1)}, bf16[16,1920]{1,0:T(8,128)(2,1)S(1)}, u32[]{:S(2)}, u32[]{:S(2)}) collective-permute-start(bf16[16,1920]{1,0:T(8,128)(2,1)S(1)} %get-tuple-element.107), channel_id=1, source_target_pairs={{0,5},{1,4},{2,7},{3,6},{4,1},{5,0},{6,3},{7,2},{8,13},{9,12},{10,... | collective-permute-start | bytes 184328 | tf_op jit(solution)/shard_map/ppermute | solution.py:425
  115.8 9.9 %collective-permute-start.43 = (bf16[16,1920]{1,0:T(8,128)(2,1)S(1)}, bf16[16,1920]{1,0:T(8,128)(2,1)S(1)}, u32[]{:S(2)}, u32[]{:S(2)}) collective-permute-start(bf16[16,1920]{1,0:T(8,128)(2,1)S(1)} %get-tuple-element.108), channel_id=1, source_target_pairs={{0,6},{1,7},{2,4},{3,5},{4,2},{5,3},{6,0},{7,1},{8,14},{9,15},{10,... | collective-permute-start | bytes 184328 | tf_op jit(solution)/shard_map/ppermute | solution.py:425
  117.9 7.7 %collective-permute-start.44 = (bf16[16,1920]{1,0:T(8,128)(2,1)S(1)}, bf16[16,1920]{1,0:T(8,128)(2,1)S(1)}, u32[]{:S(2)}, u32[]{:S(2)}) collective-permute-start(bf16[16,1920]{1,0:T(8,128)(2,1)S(1)} %get-tuple-element.109), channel_id=1, source_target_pairs={{0,7},{1,6},{2,5},{3,4},{4,3},{5,2},{6,1},{7,0},{8,15},{9,14},{10,... | collective-permute-start | bytes 184328 | tf_op jit(solution)/shard_map/ppermute | solution.py:425
  (6 other events, 29.9 us)

commit v4 on v3

--- a/solution.py
+++ b/solution.py
@@ -421,14 +421,14 @@
         return [done.reshape(blocks[0].shape)]
     done = list(blocks)
     merged = count // len(blocks)
-    for k in range(len(blocks) - 1, 0, -1):
+    for k in range(1, len(blocks)):
         done[k] = lax.ppermute(blocks[k], "user", [(i, i ^ (merged * k)) for i in range(count)])
     return done
 
 
 def shifted(block, distance):
-    devices = range(lax.axis_size("seq"))
-    route = [(i - distance, i) for i in devices if i - distance in devices]
+    count = lax.axis_size("seq")
+    route = [((i - distance) % count, i) for i in range(count)]
     return lax.ppermute(block, "seq", route)
 
 

time: 129 us -> 124 us (0.961)
  starting transfers between devices: 63.7 us -> 57.2 us
  waiting for transfers between devices: 36.6 us -> 37.9 us
    ppermute x6, starting transfers between devices: 14 us -> 7.19 us  [shifted(): return lax.ppermute(block, 'seq', route)]
    ppermute x38, waiting for transfers between devices: 26.2 us -> 29.5 us  [exchanged(): lax.ppermute(blocks[k], 'user', [(i, i ^ merged * k) for i in range(count)])]
    ppermute x6, waiting for transfers between devices: 10.4 us -> 8.47 us  [shifted(): return lax.ppermute(block, 'seq', route)]
where the time goes in v4:
time: 124 us; the launch traced here: 122 us
  starting transfers between devices  57.2 us (46%)
  waiting for transfers between devices  37.9 us (31%)
  Pallas kernels  19.9 us (16%)
  local copies, waits for them, and re-layouts  5.7 us (5%)
    ppermute x38, starting transfers between devices, exchanged(): lax.ppermute(blocks[k], 'user', [(i, i ^ merged * k) for i in range(count)])  49.9 us
    ppermute x38, waiting for transfers between devices, exchanged(): lax.ppermute(blocks[k], 'user', [(i, i ^ merged * k) for i in range(count)])  29.5 us
    pallas_call x12, Pallas kernels, call(): pl.pallas_call(kernel, out_shape=tuple(outs), in_specs=[pl.BlockSpec(memo...  19.9 us
    ppermute x6, waiting for transfers between devices, shifted(): return lax.ppermute(block, 'seq', route)  8.47 us
    ppermute x6, starting transfers between devices, shifted(): return lax.ppermute(block, 'seq', route)  7.19 us
    unnamed x18, local copies, waits for them, and re-layouts  5.67 us
  transfers between devices with their start and end apart: 45, of which 12 were waited for; matrix products, arithmetic and copies ran while one was open for 0% of the time, Pallas kernels for 6%

profile of v4, /device:TPU:2, one launch (start us, length us, event | category | flops | bytes accessed | tf_op | source)
XLA Modules:
  0.0 121.7 jit_solution(3583893329834724174)
XLA Ops:
  0.6 2.3 %shard_map.87 = (bf16[5,128,128]{2,1,0:T(8,128)(2,1)}, bf16[16,1920]{1,0:T(8,128)(2,1)}, bf16[16,1920]{1,0:T(8,128)(2,1)}, bf16[16,1920]{1,0:T(8,128)(2,1)}, bf1...) custom-call(bf16[128,1536]{1,0:T(8,128)(2,1)} %bitcast.7, ...), custom_call_target="tpu_custom_call" | custom-call | flops 16777216 | bytes 1055232 | tf_op jit(solution)/shard_map/pallas_call | solution.py:35
  3.0 1.6 %collective-permute-start.1 = (bf16[16,1920]{1,0:T(8,128)(2,1)}, bf16[16,1920]{1,0:T(8,128)(2,1)S(1)}, u32[]{:S(2)}, u32[]{:S(2)}) collective-permute-start(bf16[16,1920]{1,0:T(8,128)(2,1)} %get-tuple-element.61), channel_id=1, source_target_pairs={{0,2},{1,3},{2,0},{3,1},{4,6},{5,7},{6,4},{7,5},{8,10},{9,11},{10,... | collective-permute-start | bytes 184328 | tf_op jit(solution)/shard_map/ppermute | solution.py:425
  4.9 2.6 %collective-permute-start.3 = (bf16[16,1920]{1,0:T(8,128)(2,1)}, bf16[16,1920]{1,0:T(8,128)(2,1)S(1)}, u32[]{:S(2)}, u32[]{:S(2)}) collective-permute-start(bf16[16,1920]{1,0:T(8,128)(2,1)} %get-tuple-element.63), channel_id=1, source_target_pairs={{0,4},{1,5},{2,6},{3,7},{4,0},{5,1},{6,2},{7,3},{8,12},{9,13},{10,... | collective-permute-start | bytes 184328 | tf_op jit(solution)/shard_map/ppermute | solution.py:425
  7.5 3.6 %collective-permute-start.5 = (bf16[16,1920]{1,0:T(8,128)(2,1)}, bf16[16,1920]{1,0:T(8,128)(2,1)S(1)}, u32[]{:S(2)}, u32[]{:S(2)}) collective-permute-start(bf16[16,1920]{1,0:T(8,128)(2,1)} %get-tuple-element.65), channel_id=1, source_target_pairs={{0,6},{1,7},{2,4},{3,5},{4,2},{5,3},{6,0},{7,1},{8,14},{9,15},{10,... | collective-permute-start | bytes 184328 | tf_op jit(solution)/shard_map/ppermute | solution.py:425
  11.2 3.7 %copy-done = bf16[1,1536,3072]{2,1,0:T(8,128)(2,1)S(1)} copy-done((bf16[1,1536,3072]{2,1,0:T(8,128)(2,1)S(1)}, bf16[1,1536,3072]{2,1,0:T(8,128)(2,1)}, u32[]{:S(2)}) %copy-start) | copy-done | bytes 9437208
  16.9 1.0 shard_map.86
  18.0 1.4 %shard_map.90 = (bf16[16,1920]{1,0:T(8,128)(2,1)S(1)}, bf16[16,1920]{1,0:T(8,128)(2,1)S(1)}, bf16[16,1920]{1,0:T(8,128)(2,1)S(1)}, bf16[16,1920]{1,0:T(8,128)(2,...) custom-call(bf16[1536,3072]{1,0:T(8,128)(2,1)S(1)} %get-tuple-elemen, ...), custom_call_target="tpu_custom_call" | custom-call | flops 16777216 | bytes 11403264 | tf_op jit(solution)/shard_map/pallas_call | solution.py:35
  20.2 2.4 %collective-permute-start.15 = (bf16[16,1920]{1,0:T(8,128)(2,1)S(1)}, bf16[16,1920]{1,0:T(8,128)(2,1)S(1)}, u32[]{:S(2)}, u32[]{:S(2)}) collective-permute-start(bf16[16,1920]{1,0:T(8,128)(2,1)S(1)} %get-tuple-element.77), channel_id=1, source_target_pairs={{0,2},{1,3},{2,0},{3,1},{4,6},{5,7},{6,4},{7,5},{8,10},{9,11},{10,... | collective-permute-start | bytes 184328 | tf_op jit(solution)/shard_map/ppermute | solution.py:425
  22.6 2.8 %collective-permute-start.17 = (bf16[16,1920]{1,0:T(8,128)(2,1)S(1)}, bf16[16,1920]{1,0:T(8,128)(2,1)S(1)}, u32[]{:S(2)}, u32[]{:S(2)}) collective-permute-start(bf16[16,1920]{1,0:T(8,128)(2,1)S(1)} %get-tuple-element.79), channel_id=1, source_target_pairs={{0,4},{1,5},{2,6},{3,7},{4,0},{5,1},{6,2},{7,3},{8,12},{9,13},{10,... | collective-permute-start | bytes 184328 | tf_op jit(solution)/shard_map/ppermute | solution.py:425
  25.4 2.3 %collective-permute-start.19 = (bf16[16,1920]{1,0:T(8,128)(2,1)S(1)}, bf16[16,1920]{1,0:T(8,128)(2,1)S(1)}, u32[]{:S(2)}, u32[]{:S(2)}) collective-permute-start(bf16[16,1920]{1,0:T(8,128)(2,1)S(1)} %get-tuple-element.81), channel_id=1, source_target_pairs={{0,6},{1,7},{2,4},{3,5},{4,2},{5,3},{6,0},{7,1},{8,14},{9,15},{10,... | collective-permute-start | bytes 184328 | tf_op jit(solution)/shard_map/ppermute | solution.py:425
  27.7 1.1 collective-permute-start.20
  28.8 6.4 %collective-permute-done.18.refs_5_ = bf16[16,1920]{1,0:T(8,128)(2,1)S(1)} collective-permute-done((bf16[16,1920]{1,0:T(8,128)(2,1)S(1)}, bf16[16,1920]{1,0:T(8,128)(2,1)S(1)}, u32[]{:S(2)}, u32[]{:S(2)}) %collective-permute-start.18) | collective-permute-done | bytes 61472 | tf_op jit(solution)/shard_map/ppermute | solution.py:425
  35.6 1.5 %collective-permute-start.21 = (bf16[128,1536]{1,0:T(8,128)(2,1)S(1)}, bf16[128,1536]{1,0:T(8,128)(2,1)S(1)}, u32[]{:S(2)}, u32[]{:S(2)}) collective-permute-start(bf16[128,1536]{1,0:T(8,128)(2,1)S(1)} %shard_map.91.refs_0_.pair_ref), channel_id=1, source_target_pairs={{24,0},{0,8},{8,16},{16,24},{25,1},{1,9},{9,17},{17,25},{26,2},{2,... | collective-permute-start | bytes 1179656 | tf_op jit(solution)/shard_map/ppermute | solution.py:432
  37.6 1.4 %shard_map.88 = (bf16[16,1920]{1,0:T(8,128)(2,1)S(1)}, bf16[16,1920]{1,0:T(8,128)(2,1)S(1)}, bf16[16,1920]{1,0:T(8,128)(2,1)S(1)}, bf16[16,1920]{1,0:T(8,128)(2,...) custom-call(bf16[1536,3072]{1,0:T(8,128)(2,1)S(1)} %get-tuple-elemen, ...), custom_call_target="tpu_custom_call" | custom-call | flops 16777216 | bytes 11403264 | tf_op jit(solution)/shard_map/pallas_call | solution.py:35
  39.1 3.4 %collective-permute-start.10 = (bf16[16,1920]{1,0:T(8,128)(2,1)S(1)}, bf16[16,1920]{1,0:T(8,128)(2,1)S(1)}, u32[]{:S(2)}, u32[]{:S(2)}) collective-permute-start(bf16[16,1920]{1,0:T(8,128)(2,1)S(1)} %get-tuple-element.71), channel_id=1, source_target_pairs={{0,4},{1,5},{2,6},{3,7},{4,0},{5,1},{6,2},{7,3},{8,12},{9,13},{10,... | collective-permute-start | bytes 184328 | tf_op jit(solution)/shard_map/ppermute | solution.py:425
  42.5 2.2 %collective-permute-start.12 = (bf16[16,1920]{1,0:T(8,128)(2,1)S(1)}, bf16[16,1920]{1,0:T(8,128)(2,1)S(1)}, u32[]{:S(2)}, u32[]{:S(2)}) collective-permute-start(bf16[16,1920]{1,0:T(8,128)(2,1)S(1)} %get-tuple-element.73), channel_id=1, source_target_pairs={{0,6},{1,7},{2,4},{3,5},{4,2},{5,3},{6,0},{7,1},{8,14},{9,15},{10,... | collective-permute-start | bytes 184328 | tf_op jit(solution)/shard_map/ppermute | solution.py:425
  44.7 1.1 collective-permute-start.13
  45.8 5.2 %collective-permute-done.11.refs_5_ = bf16[16,1920]{1,0:T(8,128)(2,1)S(1)} collective-permute-done((bf16[16,1920]{1,0:T(8,128)(2,1)S(1)}, bf16[16,1920]{1,0:T(8,128)(2,1)S(1)}, u32[]{:S(2)}, u32[]{:S(2)}) %collective-permute-start.11) | collective-permute-done | bytes 61472 | tf_op jit(solution)/shard_map/ppermute | solution.py:425
  51.2 1.7 %collective-permute-start.8 = (bf16[16,1920]{1,0:T(8,128)(2,1)S(1)}, bf16[16,1920]{1,0:T(8,128)(2,1)S(1)}, u32[]{:S(2)}, u32[]{:S(2)}) collective-permute-start(bf16[16,1920]{1,0:T(8,128)(2,1)S(1)} %get-tuple-element.69), channel_id=1, source_target_pairs={{0,2},{1,3},{2,0},{3,1},{4,6},{5,7},{6,4},{7,5},{8,10},{9,11},{10,... | collective-permute-start | bytes 184328 | tf_op jit(solution)/shard_map/ppermute | solution.py:425
  52.8 1.7 %collective-permute-start.9 = (bf16[16,1920]{1,0:T(8,128)(2,1)S(1)}, bf16[16,1920]{1,0:T(8,128)(2,1)S(1)}, u32[]{:S(2)}, u32[]{:S(2)}) collective-permute-start(bf16[16,1920]{1,0:T(8,128)(2,1)S(1)} %get-tuple-element.70), channel_id=1, source_target_pairs={{0,3},{1,2},{2,1},{3,0},{4,7},{5,6},{6,5},{7,4},{8,11},{9,10},{10,... | collective-permute-start | bytes 184328 | tf_op jit(solution)/shard_map/ppermute | solution.py:425
  54.5 0.9 collective-permute-done.8.refs_2_
  55.5 1.2 collective-permute-done.9.refs_3_
  57.0 2.4 %shard_map.92 = (bf16[128,768]{1,0:T(8,128)(2,1)}, bf16[128,768]{1,0:T(8,128)(2,1)S(1)}, bf16[128,768]{1,0:T(8,128)(2,1)S(1)}, f32[128,768]{1,0:T(8,128)}) custom-call(f32[128,384]{1,0:T(8,128)S(1)} %get-tuple-element.56.see_ref, bf16[128,1536]{1,0:T(8,128)(2,1)S(1)} %shard_map.89.gq_ref.refs_0_, bf16[128,768]{1,0:T(8,128)(2,1)S(1)} %bitcast.9, ...), custom_call_target="tpu_custom_call" | custom-call | flops 16777216 | bytes 2949120 | tf_op jit(solution)/shard_map/pallas_call | solution.py:35
  59.4 2.6 %shard_map.94 = (bf16[32,1920]{1,0:T(8,128)(2,1)S(1)}, bf16[32,1920]{1,0:T(8,128)(2,1)S(1)}, bf16[32,1920]{1,0:T(8,128)(2,1)S(1)}, bf16[32,1920]{1,0:T(8,128)(2,1)S(1)}) custom-call(f32[128,384]{1,0:T(8,128)S(1)} %get-tuple-element.56.see_ref, bf16[128,1536]{1,0:T(8,128)(2,1)S(1)} %shard_map.89.gq_ref.refs_0_, ...), custom_call_target="tpu_custom_call" | custom-call | flops 16777216 | bytes 2818048 | tf_op jit(solution)/shard_map/pallas_call | solution.py:35
  62.0 2.3 %collective-permute-start.34 = (bf16[32,1920]{1,0:T(8,128)(2,1)S(1)}, bf16[32,1920]{1,0:T(8,128)(2,1)S(1)}, u32[]{:S(2)}, u32[]{:S(2)}) collective-permute-start(bf16[32,1920]{1,0:T(8,128)(2,1)S(1)} %get-tuple-element.99), channel_id=1, source_target_pairs={{0,2},{1,3},{2,0},{3,1},{4,6},{5,7},{6,4},{7,5},{8,10},{9,11},{10,... | collective-permute-start | bytes 368648 | tf_op jit(solution)/shard_map/ppermute | solution.py:425
  64.3 1.9 %collective-permute-start.35 = (bf16[32,1920]{1,0:T(8,128)(2,1)S(1)}, bf16[32,1920]{1,0:T(8,128)(2,1)S(1)}, u32[]{:S(2)}, u32[]{:S(2)}) collective-permute-start(bf16[32,1920]{1,0:T(8,128)(2,1)S(1)} %get-tuple-element.100), channel_id=1, source_target_pairs={{0,4},{1,5},{2,6},{3,7},{4,0},{5,1},{6,2},{7,3},{8,12},{9,13},{10,... | collective-permute-start | bytes 368648 | tf_op jit(solution)/shard_map/ppermute | solution.py:425
  66.8 1.6 %collective-permute-start.23 = (bf16[128,768]{1,0:T(8,128)(2,1)S(1)}, bf16[128,768]{1,0:T(8,128)(2,1)S(1)}, u32[]{:S(2)}, u32[]{:S(2)}) collective-permute-start(bf16[128,768]{1,0:T(8,128)(2,1)S(1)} %slice.20), channel_id=1, source_target_pairs={{8,0},{16,8},{24,16},{0,24},{9,1},{17,9},{25,17},{1,25},{10,2},{18... | collective-permute-start | bytes 589832 | tf_op jit(solution)/shard_map/ppermute | solution.py:432
  69.1 1.5 %collective-permute-start.25 = (bf16[128,768]{1,0:T(8,128)(2,1)S(1)}, bf16[128,768]{1,0:T(8,128)(2,1)S(1)}, u32[]{:S(2)}, u32[]{:S(2)}) collective-permute-start(bf16[128,768]{1,0:T(8,128)(2,1)S(1)} %get-tuple-element.87.refs_3_.grad_ref), channel_id=1, source_target_pairs={{8,0},{16,8},{24,16},{0,24},{9,1},{17,9},{25,17},{1,25},{10,2},{18... | collective-permute-start | bytes 589832 | tf_op jit(solution)/shard_map/ppermute | solution.py:432
  70.7 6.0 %collective-permute-done.35.refs_2_ = bf16[32,1920]{1,0:T(8,128)(2,1)S(1)} collective-permute-done((bf16[32,1920]{1,0:T(8,128)(2,1)S(1)}, bf16[32,1920]{1,0:T(8,128)(2,1)S(1)}, u32[]{:S(2)}, u32[]{:S(2)}) %collective-permute-start.35) | collective-permute-done | bytes 122912 | tf_op jit(solution)/shard_map/ppermute | solution.py:425
  76.7 1.5 %collective-permute-start.26 = (bf16[128,768]{1,0:T(8,128)(2,1)S(1)}, bf16[128,768]{1,0:T(8,128)(2,1)S(1)}, u32[]{:S(2)}, u32[]{:S(2)}) collective-permute-start(bf16[128,768]{1,0:T(8,128)(2,1)S(1)} %get-tuple-element.87.refs_3_.grad_ref), channel_id=1, source_target_pairs={{16,0},{24,8},{0,16},{8,24},{17,1},{25,9},{1,17},{9,25},{18,2},{26... | collective-permute-start | bytes 589832 | tf_op jit(solution)/shard_map/ppermute | solution.py:432
  78.3 4.3 %collective-permute-done.24.refs_2_ = bf16[128,768]{1,0:T(8,128)(2,1)S(1)} collective-permute-done((bf16[128,768]{1,0:T(8,128)(2,1)S(1)}, bf16[128,768]{1,0:T(8,128)(2,1)S(1)}, u32[]{:S(2)}, u32[]{:S(2)}) %collective-permute-start.24) | collective-permute-done | bytes 196640 | tf_op jit(solution)/shard_map/ppermute | solution.py:432
  82.6 4.1 %collective-permute-done.26.refs_5_ = bf16[128,768]{1,0:T(8,128)(2,1)S(1)} collective-permute-done((bf16[128,768]{1,0:T(8,128)(2,1)S(1)}, bf16[128,768]{1,0:T(8,128)(2,1)S(1)}, u32[]{:S(2)}, u32[]{:S(2)}) %collective-permute-start.26) | collective-permute-done | bytes 196640 | tf_op jit(solution)/shard_map/ppermute | solution.py:432
  86.7 3.1 %shard_map.93 = (bf16[16,1920]{1,0:T(8,128)(2,1)S(1)}, bf16[16,1920]{1,0:T(8,128)(2,1)S(1)}, bf16[16,1920]{1,0:T(8,128)(2,1)S(1)}, bf16[16,1920]{1,0:T(8,128)(2,...) custom-call(f32[128,384]{1,0:T(8,128)S(1)} %get-tuple-element.85.see, ...), custom_call_target="tpu_custom_call" | custom-call | flops 16777216 | bytes 2621440 | tf_op jit(solution)/shard_map/pallas_call | solution.py:35
  90.0 0.8 collective-permute-start.28
  90.8 1.0 collective-permute-start.29
  91.8 0.9 collective-permute-start.30
  92.7 1.7 %collective-permute-start.31 = (bf16[16,1920]{1,0:T(8,128)(2,1)S(1)}, bf16[16,1920]{1,0:T(8,128)(2,1)S(1)}, u32[]{:S(2)}, u32[]{:S(2)}) collective-permute-start(bf16[16,1920]{1,0:T(8,128)(2,1)S(1)} %get-tuple-element.93), channel_id=1, source_target_pairs={{0,5},{1,4},{2,7},{3,6},{4,1},{5,0},{6,3},{7,2},{8,13},{9,12},{10,... | collective-permute-start | bytes 184328 | tf_op jit(solution)/shard_map/ppermute | solution.py:425
  94.9 1.6 %collective-permute-start.32 = (bf16[16,1920]{1,0:T(8,128)(2,1)S(1)}, bf16[16,1920]{1,0:T(8,128)(2,1)S(1)}, u32[]{:S(2)}, u32[]{:S(2)}) collective-permute-start(bf16[16,1920]{1,0:T(8,128)(2,1)S(1)} %get-tuple-element.94), channel_id=1, source_target_pairs={{0,6},{1,7},{2,4},{3,5},{4,2},{5,3},{6,0},{7,1},{8,14},{9,15},{10,... | collective-permute-start | bytes 184328 | tf_op jit(solution)/shard_map/ppermute | solution.py:425
  96.5 1.5 %collective-permute-start.33 = (bf16[16,1920]{1,0:T(8,128)(2,1)S(1)}, bf16[16,1920]{1,0:T(8,128)(2,1)S(1)}, u32[]{:S(2)}, u32[]{:S(2)}) collective-permute-start(bf16[16,1920]{1,0:T(8,128)(2,1)S(1)} %get-tuple-element.95), channel_id=1, source_target_pairs={{0,7},{1,6},{2,5},{3,4},{4,3},{5,2},{6,1},{7,0},{8,15},{9,14},{10,... | collective-permute-start | bytes 184328 | tf_op jit(solution)/shard_map/ppermute | solution.py:425
  98.0 1.8 %shard_map.95.refs_8_ = f32[160,1536]{1,0:T(8,128)S(1)} custom-call(f32[160,1536]{1,0:T(8,128)S(1)} %get-tuple-element.96.slope_ref, bf16[1536,3072]{1,0:T(8,128)(2,1)S(1)} %get-tuple-element.58.w_ref, bf16[32,1920]{1,0:T(8,128)(2,1)S(1)} %get-tuple-element.98.refs_0_, bf16[32,1920]{1,0:T(8,128)(2,1)S(1)} %collective-permute-done.34.refs_1_, ...), custom_call_target="tpu_custom_call" | custom-call | flops 16777216 | bytes 12140544 | tf_op jit(solution)/shard_map/pallas_call | solution.py:35
  99.8 2.9 %collective-permute-done.30.refs_4_ = bf16[16,1920]{1,0:T(8,128)(2,1)S(1)} collective-permute-done((bf16[16,1920]{1,0:T(8,128)(2,1)S(1)}, bf16[16,1920]{1,0:T(8,128)(2,1)S(1)}, u32[]{:S(2)}, u32[]{:S(2)}) %collective-permute-start.30) | collective-permute-done | bytes 61472 | tf_op jit(solution)/shard_map/ppermute | solution.py:425
  103.1 2.0 %shard_map.96 = (bf16[16,1920]{1,0:T(8,128)(2,1)S(1)}, bf16[16,1920]{1,0:T(8,128)(2,1)S(1)}, bf16[16,1920]{1,0:T(8,128)(2,1)S(1)}, bf16[16,1920]{1,0:T(8,128)(2,...) custom-call(f32[160,1536]{1,0:T(8,128)S(1)} %get-tuple-element.84.sl, ...), custom_call_target="tpu_custom_call" | custom-call | flops 16777216 | bytes 12386304 | tf_op jit(solution)/shard_map/pallas_call | solution.py:35
  105.8 2.8 %collective-permute-start.39 = (bf16[16,1920]{1,0:T(8,128)(2,1)S(1)}, bf16[16,1920]{1,0:T(8,128)(2,1)S(1)}, u32[]{:S(2)}, u32[]{:S(2)}) collective-permute-start(bf16[16,1920]{1,0:T(8,128)(2,1)S(1)} %get-tuple-element.104), channel_id=1, source_target_pairs={{0,2},{1,3},{2,0},{3,1},{4,6},{5,7},{6,4},{7,5},{8,10},{9,11},{10,... | collective-permute-start | bytes 184328 | tf_op jit(solution)/shard_map/ppermute | solution.py:425
  108.6 1.9 %collective-permute-start.41 = (bf16[16,1920]{1,0:T(8,128)(2,1)S(1)}, bf16[16,1920]{1,0:T(8,128)(2,1)S(1)}, u32[]{:S(2)}, u32[]{:S(2)}) collective-permute-start(bf16[16,1920]{1,0:T(8,128)(2,1)S(1)} %get-tuple-element.106), channel_id=1, source_target_pairs={{0,4},{1,5},{2,6},{3,7},{4,0},{5,1},{6,2},{7,3},{8,12},{9,13},{10,... | collective-permute-start | bytes 184328 | tf_op jit(solution)/shard_map/ppermute | solution.py:425
  111.0 1.7 %collective-permute-start.43 = (bf16[16,1920]{1,0:T(8,128)(2,1)S(1)}, bf16[16,1920]{1,0:T(8,128)(2,1)S(1)}, u32[]{:S(2)}, u32[]{:S(2)}) collective-permute-start(bf16[16,1920]{1,0:T(8,128)(2,1)S(1)} %get-tuple-element.108), channel_id=1, source_target_pairs={{0,6},{1,7},{2,4},{3,5},{4,2},{5,3},{6,0},{7,1},{8,14},{9,15},{10,... | collective-permute-start | bytes 184328 | tf_op jit(solution)/shard_map/ppermute | solution.py:425
  112.7 2.1 %collective-permute-start.44 = (bf16[16,1920]{1,0:T(8,128)(2,1)S(1)}, bf16[16,1920]{1,0:T(8,128)(2,1)S(1)}, u32[]{:S(2)}, u32[]{:S(2)}) collective-permute-start(bf16[16,1920]{1,0:T(8,128)(2,1)S(1)} %get-tuple-element.109), channel_id=1, source_target_pairs={{0,7},{1,6},{2,5},{3,4},{4,3},{5,2},{6,1},{7,0},{8,15},{9,14},{10,... | collective-permute-start | bytes 184328 | tf_op jit(solution)/shard_map/ppermute | solution.py:425
  114.8 5.6 %collective-permute-done.42.refs_5_ = bf16[16,1920]{1,0:T(8,128)(2,1)S(1)} collective-permute-done((bf16[16,1920]{1,0:T(8,128)(2,1)S(1)}, bf16[16,1920]{1,0:T(8,128)(2,1)S(1)}, u32[]{:S(2)}, u32[]{:S(2)}) %collective-permute-start.42) | collective-permute-done | bytes 61472 | tf_op jit(solution)/shard_map/ppermute | solution.py:425
  120.4 1.2 %shard_map.97 = bf16[128,1536]{1,0:T(8,128)(2,1)} custom-call(bf16[5,128,128]{2,1,0:T(8,128)(2,1)S(1)} %get-tuple-element.57.rows_ref, bf16[128,1536]{1,0:T(8,128)(2,1)S(1)} %bitcast.8, f32[12,128]{1,0:T(8,128)S(1)} %bitcast.11, bf16[16,1920]{1,0:T(8,128)(2,1)S(1)} %get-tuple-element.102.refs_0_, bf16[16,1920]{1,0:T(8,128)(2,1)S(1)} %collective-permute-done.38.refs_1_, ...), custom_call_target="tpu_custom_call" | custom-call | flops 16777216 | bytes 1447936 | tf_op jit(solution)/shard_map/pallas_call | solution.py:35
  (78 shorter events, 8.1 us)
Async XLA Ops:
  3.0 4.5 %collective-permute-start = (bf16[16,1920]{1,0:T(8,128)(2,1)}, bf16[16,1920]{1,0:T(8,128)(2,1)S(1)}, u32[]{:S(2)}, u32[]{:S(2)}) collective-permute-start(bf16[16,1920]{1,0:T(8,128)(2,1)} %get-tuple-element.60), channel_id=1, source_target_pairs={{0,1},{1,0},{2,3},{3,2},{4,5},{5,4},{6,7},{7,6},{8,9},{9,8},{10,11... | collective-permute-start | bytes 184328 | tf_op jit(solution)/shard_map/ppermute | solution.py:425
  3.0 8.1 %collective-permute-start.1 = (bf16[16,1920]{1,0:T(8,128)(2,1)}, bf16[16,1920]{1,0:T(8,128)(2,1)S(1)}, u32[]{:S(2)}, u32[]{:S(2)}) collective-permute-start(bf16[16,1920]{1,0:T(8,128)(2,1)} %get-tuple-element.61), channel_id=1, source_target_pairs={{0,2},{1,3},{2,0},{3,1},{4,6},{5,7},{6,4},{7,5},{8,10},{9,11},{10,... | collective-permute-start | bytes 184328 | tf_op jit(solution)/shard_map/ppermute | solution.py:425
  4.7 13.2 %collective-permute-start.2 = (bf16[16,1920]{1,0:T(8,128)(2,1)}, bf16[16,1920]{1,0:T(8,128)(2,1)S(1)}, u32[]{:S(2)}, u32[]{:S(2)}) collective-permute-start(bf16[16,1920]{1,0:T(8,128)(2,1)} %get-tuple-element.62), channel_id=1, source_target_pairs={{0,3},{1,2},{2,1},{3,0},{4,7},{5,6},{6,5},{7,4},{8,11},{9,10},{10,... | collective-permute-start | bytes 184328 | tf_op jit(solution)/shard_map/ppermute | solution.py:425
  4.9 13.0 %collective-permute-start.3 = (bf16[16,1920]{1,0:T(8,128)(2,1)}, bf16[16,1920]{1,0:T(8,128)(2,1)S(1)}, u32[]{:S(2)}, u32[]{:S(2)}) collective-permute-start(bf16[16,1920]{1,0:T(8,128)(2,1)} %get-tuple-element.63), channel_id=1, source_target_pairs={{0,4},{1,5},{2,6},{3,7},{4,0},{5,1},{6,2},{7,3},{8,12},{9,13},{10,... | collective-permute-start | bytes 184328 | tf_op jit(solution)/shard_map/ppermute | solution.py:425
  7.5 10.5 %collective-permute-start.4 = (bf16[16,1920]{1,0:T(8,128)(2,1)}, bf16[16,1920]{1,0:T(8,128)(2,1)S(1)}, u32[]{:S(2)}, u32[]{:S(2)}) collective-permute-start(bf16[16,1920]{1,0:T(8,128)(2,1)} %get-tuple-element.64), channel_id=1, source_target_pairs={{0,5},{1,4},{2,7},{3,6},{4,1},{5,0},{6,3},{7,2},{8,13},{9,12},{10,... | collective-permute-start | bytes 184328 | tf_op jit(solution)/shard_map/ppermute | solution.py:425
  7.5 10.4 %collective-permute-start.5 = (bf16[16,1920]{1,0:T(8,128)(2,1)}, bf16[16,1920]{1,0:T(8,128)(2,1)S(1)}, u32[]{:S(2)}, u32[]{:S(2)}) collective-permute-start(bf16[16,1920]{1,0:T(8,128)(2,1)} %get-tuple-element.65), channel_id=1, source_target_pairs={{0,6},{1,7},{2,4},{3,5},{4,2},{5,3},{6,0},{7,1},{8,14},{9,15},{10,... | collective-permute-start | bytes 184328 | tf_op jit(solution)/shard_map/ppermute | solution.py:425
  11.1 6.8 %collective-permute-start.6 = (bf16[16,1920]{1,0:T(8,128)(2,1)}, bf16[16,1920]{1,0:T(8,128)(2,1)S(1)}, u32[]{:S(2)}, u32[]{:S(2)}) collective-permute-start(bf16[16,1920]{1,0:T(8,128)(2,1)} %get-tuple-element.66), channel_id=1, source_target_pairs={{0,7},{1,6},{2,5},{3,4},{4,3},{5,2},{6,1},{7,0},{8,15},{9,14},{10,... | collective-permute-start | bytes 184328 | tf_op jit(solution)/shard_map/ppermute | solution.py:425
  18.0 39.0 %copy-start.4 = (bf16[1,128,768]{2,1,0:T(8,128)(2,1)S(1)}, bf16[1,128,768]{2,1,0:T(8,128)(2,1)}, u32[]{:S(2)}) copy-start(bf16[1,128,768]{2,1,0:T(8,128)(2,1)} %param.13) | copy-start | bytes 589828
  19.4 40.0 %copy-start.2 = (bf16[5,128,128]{2,1,0:T(8,128)(2,1)S(1)}, bf16[5,128,128]{2,1,0:T(8,128)(2,1)}, u32[]{:S(2)}) copy-start(bf16[5,128,128]{2,1,0:T(8,128)(2,1)} %get-tuple-element.86.slots_ref) | copy-start | bytes 491524
  19.4 6.0 %collective-permute-start.14 = (bf16[16,1920]{1,0:T(8,128)(2,1)S(1)}, bf16[16,1920]{1,0:T(8,128)(2,1)S(1)}, u32[]{:S(2)}, u32[]{:S(2)}) collective-permute-start(bf16[16,1920]{1,0:T(8,128)(2,1)S(1)} %get-tuple-element.76), channel_id=1, source_target_pairs={{0,1},{1,0},{2,3},{3,2},{4,5},{5,4},{6,7},{7,6},{8,9},{9,8},{10,11... | collective-permute-start | bytes 184328 | tf_op jit(solution)/shard_map/ppermute | solution.py:425
  20.2 7.5 %collective-permute-start.15 = (bf16[16,1920]{1,0:T(8,128)(2,1)S(1)}, bf16[16,1920]{1,0:T(8,128)(2,1)S(1)}, u32[]{:S(2)}, u32[]{:S(2)}) collective-permute-start(bf16[16,1920]{1,0:T(8,128)(2,1)S(1)} %get-tuple-element.77), channel_id=1, source_target_pairs={{0,2},{1,3},{2,0},{3,1},{4,6},{5,7},{6,4},{7,5},{8,10},{9,11},{10,... | collective-permute-start | bytes 184328 | tf_op jit(solution)/shard_map/ppermute | solution.py:425
  22.6 6.2 %collective-permute-start.16 = (bf16[16,1920]{1,0:T(8,128)(2,1)S(1)}, bf16[16,1920]{1,0:T(8,128)(2,1)S(1)}, u32[]{:S(2)}, u32[]{:S(2)}) collective-permute-start(bf16[16,1920]{1,0:T(8,128)(2,1)S(1)} %get-tuple-element.78), channel_id=1, source_target_pairs={{0,3},{1,2},{2,1},{3,0},{4,7},{5,6},{6,5},{7,4},{8,11},{9,10},{10,... | collective-permute-start | bytes 184328 | tf_op jit(solution)/shard_map/ppermute | solution.py:425
  22.6 6.2 %collective-permute-start.17 = (bf16[16,1920]{1,0:T(8,128)(2,1)S(1)}, bf16[16,1920]{1,0:T(8,128)(2,1)S(1)}, u32[]{:S(2)}, u32[]{:S(2)}) collective-permute-start(bf16[16,1920]{1,0:T(8,128)(2,1)S(1)} %get-tuple-element.79), channel_id=1, source_target_pairs={{0,4},{1,5},{2,6},{3,7},{4,0},{5,1},{6,2},{7,3},{8,12},{9,13},{10,... | collective-permute-start | bytes 184328 | tf_op jit(solution)/shard_map/ppermute | solution.py:425
  25.4 9.9 %collective-permute-start.18 = (bf16[16,1920]{1,0:T(8,128)(2,1)S(1)}, bf16[16,1920]{1,0:T(8,128)(2,1)S(1)}, u32[]{:S(2)}, u32[]{:S(2)}) collective-permute-start(bf16[16,1920]{1,0:T(8,128)(2,1)S(1)} %get-tuple-element.80), channel_id=1, source_target_pairs={{0,5},{1,4},{2,7},{3,6},{4,1},{5,0},{6,3},{7,2},{8,13},{9,12},{10,... | collective-permute-start | bytes 184328 | tf_op jit(solution)/shard_map/ppermute | solution.py:425
  25.4 9.9 %collective-permute-start.19 = (bf16[16,1920]{1,0:T(8,128)(2,1)S(1)}, bf16[16,1920]{1,0:T(8,128)(2,1)S(1)}, u32[]{:S(2)}, u32[]{:S(2)}) collective-permute-start(bf16[16,1920]{1,0:T(8,128)(2,1)S(1)} %get-tuple-element.81), channel_id=1, source_target_pairs={{0,6},{1,7},{2,4},{3,5},{4,2},{5,3},{6,0},{7,1},{8,14},{9,15},{10,... | collective-permute-start | bytes 184328 | tf_op jit(solution)/shard_map/ppermute | solution.py:425
  27.7 7.5 %collective-permute-start.20 = (bf16[16,1920]{1,0:T(8,128)(2,1)S(1)}, bf16[16,1920]{1,0:T(8,128)(2,1)S(1)}, u32[]{:S(2)}, u32[]{:S(2)}) collective-permute-start(bf16[16,1920]{1,0:T(8,128)(2,1)S(1)} %get-tuple-element.82), channel_id=1, source_target_pairs={{0,7},{1,6},{2,5},{3,4},{4,3},{5,2},{6,1},{7,0},{8,15},{9,14},{10,... | collective-permute-start | bytes 184328 | tf_op jit(solution)/shard_map/ppermute | solution.py:425
  35.6 21.4 %collective-permute-start.21 = (bf16[128,1536]{1,0:T(8,128)(2,1)S(1)}, bf16[128,1536]{1,0:T(8,128)(2,1)S(1)}, u32[]{:S(2)}, u32[]{:S(2)}) collective-permute-start(bf16[128,1536]{1,0:T(8,128)(2,1)S(1)} %shard_map.91.refs_0_.pair_ref), channel_id=1, source_target_pairs={{24,0},{0,8},{8,16},{16,24},{25,1},{1,9},{9,17},{17,25},{26,2},{2,... | collective-permute-start | bytes 1179656 | tf_op jit(solution)/shard_map/ppermute | solution.py:432
  37.1 19.9 %collective-permute-start.22 = (bf16[128,1536]{1,0:T(8,128)(2,1)S(1)}, bf16[128,1536]{1,0:T(8,128)(2,1)S(1)}, u32[]{:S(2)}, u32[]{:S(2)}) collective-permute-start(bf16[128,1536]{1,0:T(8,128)(2,1)S(1)} %shard_map.91.refs_0_.pair_ref), channel_id=1, source_target_pairs={{16,0},{24,8},{0,16},{8,24},{17,1},{25,9},{1,17},{9,25},{18,2},{26... | collective-permute-start | bytes 1179656 | tf_op jit(solution)/shard_map/ppermute | solution.py:432
  39.1 5.6 %collective-permute-start.10 = (bf16[16,1920]{1,0:T(8,128)(2,1)S(1)}, bf16[16,1920]{1,0:T(8,128)(2,1)S(1)}, u32[]{:S(2)}, u32[]{:S(2)}) collective-permute-start(bf16[16,1920]{1,0:T(8,128)(2,1)S(1)} %get-tuple-element.71), channel_id=1, source_target_pairs={{0,4},{1,5},{2,6},{3,7},{4,0},{5,1},{6,2},{7,3},{8,12},{9,13},{10,... | collective-permute-start | bytes 184328 | tf_op jit(solution)/shard_map/ppermute | solution.py:425
  42.5 8.6 %collective-permute-start.11 = (bf16[16,1920]{1,0:T(8,128)(2,1)S(1)}, bf16[16,1920]{1,0:T(8,128)(2,1)S(1)}, u32[]{:S(2)}, u32[]{:S(2)}) collective-permute-start(bf16[16,1920]{1,0:T(8,128)(2,1)S(1)} %get-tuple-element.72), channel_id=1, source_target_pairs={{0,5},{1,4},{2,7},{3,6},{4,1},{5,0},{6,3},{7,2},{8,13},{9,12},{10,... | collective-permute-start | bytes 184328 | tf_op jit(solution)/shard_map/ppermute | solution.py:425
  42.5 8.7 %collective-permute-start.12 = (bf16[16,1920]{1,0:T(8,128)(2,1)S(1)}, bf16[16,1920]{1,0:T(8,128)(2,1)S(1)}, u32[]{:S(2)}, u32[]{:S(2)}) collective-permute-start(bf16[16,1920]{1,0:T(8,128)(2,1)S(1)} %get-tuple-element.73), channel_id=1, source_target_pairs={{0,6},{1,7},{2,4},{3,5},{4,2},{5,3},{6,0},{7,1},{8,14},{9,15},{10,... | collective-permute-start | bytes 184328 | tf_op jit(solution)/shard_map/ppermute | solution.py:425
  44.7 8.1 %collective-permute-start.13 = (bf16[16,1920]{1,0:T(8,128)(2,1)S(1)}, bf16[16,1920]{1,0:T(8,128)(2,1)S(1)}, u32[]{:S(2)}, u32[]{:S(2)}) collective-permute-start(bf16[16,1920]{1,0:T(8,128)(2,1)S(1)} %get-tuple-element.74), channel_id=1, source_target_pairs={{0,7},{1,6},{2,5},{3,4},{4,3},{5,2},{6,1},{7,0},{8,15},{9,14},{10,... | collective-permute-start | bytes 184328 | tf_op jit(solution)/shard_map/ppermute | solution.py:425
  51.1 3.5 %collective-permute-start.7 = (bf16[16,1920]{1,0:T(8,128)(2,1)S(1)}, bf16[16,1920]{1,0:T(8,128)(2,1)S(1)}, u32[]{:S(2)}, u32[]{:S(2)}) collective-permute-start(bf16[16,1920]{1,0:T(8,128)(2,1)S(1)} %get-tuple-element.68), channel_id=1, source_target_pairs={{0,1},{1,0},{2,3},{3,2},{4,5},{5,4},{6,7},{7,6},{8,9},{9,8},{10,11... | collective-permute-start | bytes 184328 | tf_op jit(solution)/shard_map/ppermute | solution.py:425
  51.2 4.3 %collective-permute-start.8 = (bf16[16,1920]{1,0:T(8,128)(2,1)S(1)}, bf16[16,1920]{1,0:T(8,128)(2,1)S(1)}, u32[]{:S(2)}, u32[]{:S(2)}) collective-permute-start(bf16[16,1920]{1,0:T(8,128)(2,1)S(1)} %get-tuple-element.69), channel_id=1, source_target_pairs={{0,2},{1,3},{2,0},{3,1},{4,6},{5,7},{6,4},{7,5},{8,10},{9,11},{10,... | collective-permute-start | bytes 184328 | tf_op jit(solution)/shard_map/ppermute | solution.py:425
  52.8 3.9 %collective-permute-start.9 = (bf16[16,1920]{1,0:T(8,128)(2,1)S(1)}, bf16[16,1920]{1,0:T(8,128)(2,1)S(1)}, u32[]{:S(2)}, u32[]{:S(2)}) collective-permute-start(bf16[16,1920]{1,0:T(8,128)(2,1)S(1)} %get-tuple-element.70), channel_id=1, source_target_pairs={{0,3},{1,2},{2,1},{3,0},{4,7},{5,6},{6,5},{7,4},{8,11},{9,10},{10,... | collective-permute-start | bytes 184328 | tf_op jit(solution)/shard_map/ppermute | solution.py:425
  62.0 7.1 %collective-permute-start.34 = (bf16[32,1920]{1,0:T(8,128)(2,1)S(1)}, bf16[32,1920]{1,0:T(8,128)(2,1)S(1)}, u32[]{:S(2)}, u32[]{:S(2)}) collective-permute-start(bf16[32,1920]{1,0:T(8,128)(2,1)S(1)} %get-tuple-element.99), channel_id=1, source_target_pairs={{0,2},{1,3},{2,0},{3,1},{4,6},{5,7},{6,4},{7,5},{8,10},{9,11},{10,... | collective-permute-start | bytes 368648 | tf_op jit(solution)/shard_map/ppermute | solution.py:425
  64.3 12.3 %collective-permute-start.35 = (bf16[32,1920]{1,0:T(8,128)(2,1)S(1)}, bf16[32,1920]{1,0:T(8,128)(2,1)S(1)}, u32[]{:S(2)}, u32[]{:S(2)}) collective-permute-start(bf16[32,1920]{1,0:T(8,128)(2,1)S(1)} %get-tuple-element.100), channel_id=1, source_target_pairs={{0,4},{1,5},{2,6},{3,7},{4,0},{5,1},{6,2},{7,3},{8,12},{9,13},{10,... | collective-permute-start | bytes 368648 | tf_op jit(solution)/shard_map/ppermute | solution.py:425
  66.2 11.9 %collective-permute-start.36 = (bf16[32,1920]{1,0:T(8,128)(2,1)S(1)}, bf16[32,1920]{1,0:T(8,128)(2,1)S(1)}, u32[]{:S(2)}, u32[]{:S(2)}) collective-permute-start(bf16[32,1920]{1,0:T(8,128)(2,1)S(1)} %get-tuple-element.101), channel_id=1, source_target_pairs={{0,6},{1,7},{2,4},{3,5},{4,2},{5,3},{6,0},{7,1},{8,14},{9,15},{10,... | collective-permute-start | bytes 368648 | tf_op jit(solution)/shard_map/ppermute | solution.py:425
  66.8 11.5 %collective-permute-start.23 = (bf16[128,768]{1,0:T(8,128)(2,1)S(1)}, bf16[128,768]{1,0:T(8,128)(2,1)S(1)}, u32[]{:S(2)}, u32[]{:S(2)}) collective-permute-start(bf16[128,768]{1,0:T(8,128)(2,1)S(1)} %slice.20), channel_id=1, source_target_pairs={{8,0},{16,8},{24,16},{0,24},{9,1},{17,9},{25,17},{1,25},{10,2},{18... | collective-permute-start | bytes 589832 | tf_op jit(solution)/shard_map/ppermute | solution.py:432
  68.4 14.2 %collective-permute-start.24 = (bf16[128,768]{1,0:T(8,128)(2,1)S(1)}, bf16[128,768]{1,0:T(8,128)(2,1)S(1)}, u32[]{:S(2)}, u32[]{:S(2)}) collective-permute-start(bf16[128,768]{1,0:T(8,128)(2,1)S(1)} %slice.20), channel_id=1, source_target_pairs={{16,0},{24,8},{0,16},{8,24},{17,1},{25,9},{1,17},{9,25},{18,2},{26... | collective-permute-start | bytes 589832 | tf_op jit(solution)/shard_map/ppermute | solution.py:432
  69.1 13.5 %collective-permute-start.25 = (bf16[128,768]{1,0:T(8,128)(2,1)S(1)}, bf16[128,768]{1,0:T(8,128)(2,1)S(1)}, u32[]{:S(2)}, u32[]{:S(2)}) collective-permute-start(bf16[128,768]{1,0:T(8,128)(2,1)S(1)} %get-tuple-element.87.refs_3_.grad_ref), channel_id=1, source_target_pairs={{8,0},{16,8},{24,16},{0,24},{9,1},{17,9},{25,17},{1,25},{10,2},{18... | collective-permute-start | bytes 589832 | tf_op jit(solution)/shard_map/ppermute | solution.py:432
  76.7 10.1 %collective-permute-start.26 = (bf16[128,768]{1,0:T(8,128)(2,1)S(1)}, bf16[128,768]{1,0:T(8,128)(2,1)S(1)}, u32[]{:S(2)}, u32[]{:S(2)}) collective-permute-start(bf16[128,768]{1,0:T(8,128)(2,1)S(1)} %get-tuple-element.87.refs_3_.grad_ref), channel_id=1, source_target_pairs={{16,0},{24,8},{0,16},{8,24},{17,1},{25,9},{1,17},{9,25},{18,2},{26... | collective-permute-start | bytes 589832 | tf_op jit(solution)/shard_map/ppermute | solution.py:432
  78.2 18.3 %collective-permute-start.37 = (bf16[64,1920]{1,0:T(8,128)(2,1)S(1)}, bf16[64,1920]{1,0:T(8,128)(2,1)S(1)}, u32[]{:S(2)}, u32[]{:S(2)}) collective-permute-start(bf16[64,1920]{1,0:T(8,128)(2,1)S(1)} %pad_maximum_fusion), channel_id=1, source_target_pairs={{0,1},{1,0},{2,3},{3,2},{4,5},{5,4},{6,7},{7,6},{8,9},{9,8},{10,11... | collective-permute-start | bytes 737288 | tf_op jit(solution)/shard_map/ppermute | solution.py:412
  89.9 2.8 %collective-permute-start.27 = (bf16[16,1920]{1,0:T(8,128)(2,1)S(1)}, bf16[16,1920]{1,0:T(8,128)(2,1)S(1)}, u32[]{:S(2)}, u32[]{:S(2)}) collective-permute-start(bf16[16,1920]{1,0:T(8,128)(2,1)S(1)} %get-tuple-element.89), channel_id=1, source_target_pairs={{0,1},{1,0},{2,3},{3,2},{4,5},{5,4},{6,7},{7,6},{8,9},{9,8},{10,11... | collective-permute-start | bytes 184328 | tf_op jit(solution)/shard_map/ppermute | solution.py:425
  90.0 4.9 %collective-permute-start.28 = (bf16[16,1920]{1,0:T(8,128)(2,1)S(1)}, bf16[16,1920]{1,0:T(8,128)(2,1)S(1)}, u32[]{:S(2)}, u32[]{:S(2)}) collective-permute-start(bf16[16,1920]{1,0:T(8,128)(2,1)S(1)} %get-tuple-element.90), channel_id=1, source_target_pairs={{0,2},{1,3},{2,0},{3,1},{4,6},{5,7},{6,4},{7,5},{8,10},{9,11},{10,... | collective-permute-start | bytes 184328 | tf_op jit(solution)/shard_map/ppermute | solution.py:425
  90.8 9.0 %collective-permute-start.29 = (bf16[16,1920]{1,0:T(8,128)(2,1)S(1)}, bf16[16,1920]{1,0:T(8,128)(2,1)S(1)}, u32[]{:S(2)}, u32[]{:S(2)}) collective-permute-start(bf16[16,1920]{1,0:T(8,128)(2,1)S(1)} %get-tuple-element.91), channel_id=1, source_target_pairs={{0,3},{1,2},{2,1},{3,0},{4,7},{5,6},{6,5},{7,4},{8,11},{9,10},{10,... | collective-permute-start | bytes 184328 | tf_op jit(solution)/shard_map/ppermute | solution.py:425
  91.8 10.9 %collective-permute-start.30 = (bf16[16,1920]{1,0:T(8,128)(2,1)S(1)}, bf16[16,1920]{1,0:T(8,128)(2,1)S(1)}, u32[]{:S(2)}, u32[]{:S(2)}) collective-permute-start(bf16[16,1920]{1,0:T(8,128)(2,1)S(1)} %get-tuple-element.92), channel_id=1, source_target_pairs={{0,4},{1,5},{2,6},{3,7},{4,0},{5,1},{6,2},{7,3},{8,12},{9,13},{10,... | collective-permute-start | bytes 184328 | tf_op jit(solution)/shard_map/ppermute | solution.py:425
  92.7 10.4 %collective-permute-start.31 = (bf16[16,1920]{1,0:T(8,128)(2,1)S(1)}, bf16[16,1920]{1,0:T(8,128)(2,1)S(1)}, u32[]{:S(2)}, u32[]{:S(2)}) collective-permute-start(bf16[16,1920]{1,0:T(8,128)(2,1)S(1)} %get-tuple-element.93), channel_id=1, source_target_pairs={{0,5},{1,4},{2,7},{3,6},{4,1},{5,0},{6,3},{7,2},{8,13},{9,12},{10,... | collective-permute-start | bytes 184328 | tf_op jit(solution)/shard_map/ppermute | solution.py:425
  94.9 8.2 %collective-permute-start.32 = (bf16[16,1920]{1,0:T(8,128)(2,1)S(1)}, bf16[16,1920]{1,0:T(8,128)(2,1)S(1)}, u32[]{:S(2)}, u32[]{:S(2)}) collective-permute-start(bf16[16,1920]{1,0:T(8,128)(2,1)S(1)} %get-tuple-element.94), channel_id=1, source_target_pairs={{0,6},{1,7},{2,4},{3,5},{4,2},{5,3},{6,0},{7,1},{8,14},{9,15},{10,... | collective-permute-start | bytes 184328 | tf_op jit(solution)/shard_map/ppermute | solution.py:425
  96.5 6.6 %collective-permute-start.33 = (bf16[16,1920]{1,0:T(8,128)(2,1)S(1)}, bf16[16,1920]{1,0:T(8,128)(2,1)S(1)}, u32[]{:S(2)}, u32[]{:S(2)}) collective-permute-start(bf16[16,1920]{1,0:T(8,128)(2,1)S(1)} %get-tuple-element.95), channel_id=1, source_target_pairs={{0,7},{1,6},{2,5},{3,4},{4,3},{5,2},{6,1},{7,0},{8,15},{9,14},{10,... | collective-permute-start | bytes 184328 | tf_op jit(solution)/shard_map/ppermute | solution.py:425
  98.0 22.4 %copy-start.5 = (f32[1536]{0:T(1024)S(1)}, f32[1536]{0:T(1024)}, u32[]{:S(2)}) copy-start(f32[1536]{0:T(1024)} %param.11) | copy-start | bytes 18436
  105.1 5.9 %collective-permute-start.38 = (bf16[16,1920]{1,0:T(8,128)(2,1)S(1)}, bf16[16,1920]{1,0:T(8,128)(2,1)S(1)}, u32[]{:S(2)}, u32[]{:S(2)}) collective-permute-start(bf16[16,1920]{1,0:T(8,128)(2,1)S(1)} %get-tuple-element.103), channel_id=1, source_target_pairs={{0,1},{1,0},{2,3},{3,2},{4,5},{5,4},{6,7},{7,6},{8,9},{9,8},{10,11... | collective-permute-start | bytes 184328 | tf_op jit(solution)/shard_map/ppermute | solution.py:425
  105.8 6.9 %collective-permute-start.39 = (bf16[16,1920]{1,0:T(8,128)(2,1)S(1)}, bf16[16,1920]{1,0:T(8,128)(2,1)S(1)}, u32[]{:S(2)}, u32[]{:S(2)}) collective-permute-start(bf16[16,1920]{1,0:T(8,128)(2,1)S(1)} %get-tuple-element.104), channel_id=1, source_target_pairs={{0,2},{1,3},{2,0},{3,1},{4,6},{5,7},{6,4},{7,5},{8,10},{9,11},{10,... | collective-permute-start | bytes 184328 | tf_op jit(solution)/shard_map/ppermute | solution.py:425
  108.6 6.2 %collective-permute-start.40 = (bf16[16,1920]{1,0:T(8,128)(2,1)S(1)}, bf16[16,1920]{1,0:T(8,128)(2,1)S(1)}, u32[]{:S(2)}, u32[]{:S(2)}) collective-permute-start(bf16[16,1920]{1,0:T(8,128)(2,1)S(1)} %get-tuple-element.105), channel_id=1, source_target_pairs={{0,3},{1,2},{2,1},{3,0},{4,7},{5,6},{6,5},{7,4},{8,11},{9,10},{10,... | collective-permute-start | bytes 184328 | tf_op jit(solution)/shard_map/ppermute | solution.py:425
  108.6 6.2 %collective-permute-start.41 = (bf16[16,1920]{1,0:T(8,128)(2,1)S(1)}, bf16[16,1920]{1,0:T(8,128)(2,1)S(1)}, u32[]{:S(2)}, u32[]{:S(2)}) collective-permute-start(bf16[16,1920]{1,0:T(8,128)(2,1)S(1)} %get-tuple-element.106), channel_id=1, source_target_pairs={{0,4},{1,5},{2,6},{3,7},{4,0},{5,1},{6,2},{7,3},{8,12},{9,13},{10,... | collective-permute-start | bytes 184328 | tf_op jit(solution)/shard_map/ppermute | solution.py:425
  110.5 9.9 %collective-permute-start.42 = (bf16[16,1920]{1,0:T(8,128)(2,1)S(1)}, bf16[16,1920]{1,0:T(8,128)(2,1)S(1)}, u32[]{:S(2)}, u32[]{:S(2)}) collective-permute-start(bf16[16,1920]{1,0:T(8,128)(2,1)S(1)} %get-tuple-element.107), channel_id=1, source_target_pairs={{0,5},{1,4},{2,7},{3,6},{4,1},{5,0},{6,3},{7,2},{8,13},{9,12},{10,... | collective-permute-start | bytes 184328 | tf_op jit(solution)/shard_map/ppermute | solution.py:425
  111.0 9.4 %collective-permute-start.43 = (bf16[16,1920]{1,0:T(8,128)(2,1)S(1)}, bf16[16,1920]{1,0:T(8,128)(2,1)S(1)}, u32[]{:S(2)}, u32[]{:S(2)}) collective-permute-start(bf16[16,1920]{1,0:T(8,128)(2,1)S(1)} %get-tuple-element.108), channel_id=1, source_target_pairs={{0,6},{1,7},{2,4},{3,5},{4,2},{5,3},{6,0},{7,1},{8,14},{9,15},{10,... | collective-permute-start | bytes 184328 | tf_op jit(solution)/shard_map/ppermute | solution.py:425
  112.7 7.7 %collective-permute-start.44 = (bf16[16,1920]{1,0:T(8,128)(2,1)S(1)}, bf16[16,1920]{1,0:T(8,128)(2,1)S(1)}, u32[]{:S(2)}, u32[]{:S(2)}) collective-permute-start(bf16[16,1920]{1,0:T(8,128)(2,1)S(1)} %get-tuple-element.109), channel_id=1, source_target_pairs={{0,7},{1,6},{2,5},{3,4},{4,3},{5,2},{6,1},{7,0},{8,15},{9,14},{10,... | collective-permute-start | bytes 184328 | tf_op jit(solution)/shard_map/ppermute | solution.py:425
  (6 other events, 29.2 us)

commit v5 on v4

--- a/solution.py
+++ b/solution.py
@@ -20,7 +20,6 @@
 FOLD = MAIN // EXTRA
 
 VMEM_LIMIT = 24 << 20
-VMEM_ALL = 67043328
 LANES = 128
 
 eps = 1e-05
@@ -32,6 +31,10 @@
 def call(kernel, outs, operands, spaces=(), scratch=(), flops=1 << 24, limit=VMEM_LIMIT):
     spaces = list(spaces) + [pltpu.VMEM] * (len(operands) - len(spaces))
     moved = sum(o.size * o.dtype.itemsize for o in list(outs) + list(operands))
+    operands = [
+        pltpu.with_memory_space_constraint(operand, space) if space == pltpu.HBM else operand
+        for operand, space in zip(operands, spaces)
+    ]
     return pl.pallas_call(
         kernel,
         out_shape=tuple(outs),
@@ -199,16 +202,17 @@
             [(events_hbm, events_ref), (gain_hbm, gain_ref), (scen_hbm, scen_ref)]
         )
     ]
-    for load_ in loads:
+    for load_ in reversed(loads):
         load_.start()
-    for load_ in loads:
-        load_.wait()
+    loads[2].wait()
+    matrices = slot_matrices(own_scenarios(scen_ref, direct), True)
+    for i, matrix in enumerate(matrices):
+        slots_ref[i] = matrix
+    loads[1].wait()
+    loads[0].wait()
     events = events_ref[...].astype(f32)
     row_inv = lax.rsqrt(jnp.mean(events * events, axis=1, keepdims=True) + eps)
     normed = (events * row_inv * gain_of(gain_ref)).astype(bf16)
-    matrices = slot_matrices(own_scenarios(scen_ref, direct), True)
-    for i, matrix in enumerate(matrices):
-        slots_ref[i] = matrix
     to_slots(matrices, normed, refs)
 
 
@@ -220,10 +224,10 @@
     return sum(jnp.where(history == i, limit, 0) for i, limit in enumerate(limits))
 
 
-def mask_kernel(direct, blocks, w_hbm, *refs):
-    small, (w_ref, rows_ref, see_ref, seen_ref), rest = refs[:3], refs[3:7], refs[7:]
-    lengths_ref, offsets_ref, scen_ref, sems = rest
-    count = sems.shape[0] - len(small)
+def mask_kernel(
+    direct, blocks, histories, w_hbm, small_ref, w_ref, rows_ref, see_ref, seen_ref, sems
+):
+    count = sems.shape[0]
     depth = w_ref.shape[0] // count
     loads = [
         pltpu.make_async_copy(
@@ -231,22 +235,18 @@
         )
         for i in range(count)
     ]
-    first_loads = [
-        pltpu.make_async_copy(source, target, sems.at[count + i])
-        for i, (source, target) in enumerate(zip(small, rest))
-    ]
-    for load_ in first_loads + loads:
+    for load_ in loads:
         load_.start()
-    for load_ in first_loads:
-        load_.wait()
-    for i, matrix in enumerate(slot_matrices(own_scenarios(scen_ref, direct), False)):
+    for i, matrix in enumerate(
+        slot_matrices(own_scenarios(small_ref.at[:, 2 * histories :], direct), False)
+    ):
         rows_ref[i] = matrix
     rows = see_ref.shape[0]
     ends, total = [], 0
-    for i in range(lengths_ref.shape[1]):
-        total = total + lengths_ref[0, i]
+    for i in range(histories):
+        total = total + small_ref[:, i : i + 1]
         ends.append(total)
-    limits = [offsets_ref[0, i] for i in range(offsets_ref.shape[1])]
+    limits = [small_ref[:, i : i + 1] for i in range(histories, 2 * histories)]
     first = lax.axis_index("seq") * rows
     shift = MB.bit_length() - 1
 
@@ -288,23 +288,24 @@
     return slice(start, start + HD)
 
 
+def stack(refs, cols):
+    return jnp.concatenate([ref[:, cols] for ref in refs], axis=0)
+
+
 def forward_kernel(blocks, see_ref, gq_ref, cotan_ref, *refs):
-    pairs, (out_ref, grad_ref, gate_ref, mixed_ref) = refs[:blocks], refs[blocks:]
-    rows = gq_ref.shape[0]
+    pairs, (out_ref, grad_ref, gate_ref) = refs[:blocks], refs[blocks:]
     scale = HD ** (-0.5)
-    total = jnp.zeros((rows, 1), f32)
+    see = see_ref[...]
+    done = []
     for head in range(HEADS):
-        query = gq_ref[:, head_cols(head, 1)]
-        mixed = jnp.zeros((rows, HD), f32)
-        for block in range(blocks):
-            score = dot_nt(query, pairs[block][:, head_cols(head, 1)]) * scale
-            weight = score * sigmoid(score) * see_ref[:, block * rows : (block + 1) * rows]
-            mixed = mixed + dot(weight.astype(bf16), pairs[block][:, head_cols(head)])
-        mixed_ref[:, head_cols(head)] = mixed
-        total = total + jnp.sum(mixed * mixed, axis=1, keepdims=True)
+        keys = stack(pairs, head_cols(head, 1))
+        score = dot_nt(gq_ref[:, head_cols(head, 1)], keys) * scale
+        weight = (score * sigmoid(score) * see).astype(bf16)
+        done.append(dot(weight, stack(pairs, head_cols(head))))
     width = HEADS * HD
-    row_scale = lax.rsqrt(total / width + eps)
-    normed = mixed_ref[...] * row_scale
+    mixed = jnp.concatenate(done, axis=1)
+    row_scale = lax.rsqrt(jnp.mean(mixed * mixed, axis=1, keepdims=True) + eps)
+    normed = mixed * row_scale
     gate = gq_ref[:, :width].astype(f32)
     cotan = cotan_ref[...].astype(f32)
     grad_norm = cotan * gate
@@ -325,48 +326,53 @@
 
 def query_kernel(count, blocks, see_ref, gq_ref, grad_ref, gate_ref, slots_ref, *refs):
     pairs, wires = refs[:blocks], wires_out(count, refs[blocks:])
-    rows = gq_ref.shape[0]
     scale = HD ** (-0.5)
+    see = see_ref[...]
     done = []
     for head in range(HEADS):
-        query = gq_ref[:, head_cols(head, 1)]
-        grad = grad_ref[:, head_cols(head)]
-        grad_query = jnp.zeros((rows, HD), f32)
-        for block in range(blocks):
-            key = pairs[block][:, head_cols(head, 1)]
-            score = dot_nt(query, key) * scale
-            _, slope = slope_of(score)
-            att = dot_nt(grad, pairs[block][:, head_cols(head)])
-            grad_score = att * slope * see_ref[:, block * rows : (block + 1) * rows]
-            grad_query = grad_query + dot(grad_score.astype(bf16), key)
-        done.append((grad_query * scale).astype(bf16))
+        keys = stack(pairs, head_cols(head, 1))
+        _, slope = slope_of(dot_nt(gq_ref[:, head_cols(head, 1)], keys) * scale)
+        att = dot_nt(grad_ref[:, head_cols(head)], stack(pairs, head_cols(head)))
+        done.append((dot((att * slope * see).astype(bf16), keys) * scale).astype(bf16))
     parts_to_slots(slots_ref, [gate_ref[...], jnp.concatenate(done, axis=1)], wires)
 
 
-def key_kernel(count, blocks, seen_ref, pair_ref, slots_ref, *refs):
-    queries, grads = refs[:blocks], refs[blocks : 2 * blocks]
-    wires = wires_out(count, refs[2 * blocks :])
+def score_kernel(blocks, seen_ref, pair_ref, gq_ref, grad_ref, *refs):
+    queries, (weight_ref, slope_ref, value_sum_ref, key_sum_ref) = refs[: blocks - 1], refs[blocks - 1 :]
     rows = pair_ref.shape[0]
     scale = HD ** (-0.5)
-    grad_keys, grad_values = [], []
+    seen = seen_ref[...]
     for head in range(HEADS):
-        key = pair_ref[:, head_cols(head, 1)]
-        value = pair_ref[:, head_cols(head)]
-        grad_key = jnp.zeros((rows, HD), f32)
-        grad_value = jnp.zeros((rows, HD), f32)
-        for block in range(blocks):
-            mask = seen_ref[:, block * rows : (block + 1) * rows]
-            query = queries[block][:, head_cols(head, 1 if block == 0 else 0)]
-            grad = grads[block][:, head_cols(head)]
-            score = dot_nt(key, query) * scale
-            sig, slope = slope_of(score)
-            weight = score * sig * mask
-            grad_score = dot_nt(value, grad) * slope * mask
-            grad_key = grad_key + dot(grad_score.astype(bf16), query)
-            grad_value = grad_value + dot(weight.astype(bf16), grad)
-        grad_keys.append((grad_key * scale).astype(bf16))
-        grad_values.append(grad_value.astype(bf16))
-    parts = [jnp.concatenate(one, axis=1) for one in (grad_values, grad_keys)]
+        own = gq_ref[:, head_cols(head, 1)]
+        query = jnp.concatenate([own, stack(queries, head_cols(head))], axis=0)
+        score = dot_nt(pair_ref[:, head_cols(head, 1)], query) * scale
+        sig, slope = slope_of(score)
+        weight = (score * sig * seen).astype(bf16)
+        slope = slope * seen
+        grad = grad_ref[:, head_cols(head)]
+        att = dot_nt(pair_ref[:, head_cols(head)], grad)
+        value_sum_ref[:, head_cols(head)] = dot(weight[:, :rows], grad)
+        key_sum_ref[:, head_cols(head)] = dot((att * slope[:, :rows]).astype(bf16), own)
+        weight_ref[head] = weight[:, rows:]
+        slope_ref[head] = slope[:, rows:]
+
+
+def key_kernel(count, blocks, pair_ref, slots_ref, weight_ref, slope_ref, *refs):
+    later = blocks - 1
+    value_sum_ref, key_sum_ref = refs[:2]
+    queries, grads = refs[2 : 2 + later], refs[2 + later : 2 + 2 * later]
+    wires = wires_out(count, refs[2 + 2 * later :])
+    scale = HD ** (-0.5)
+    values, keys = [], []
+    for head in range(HEADS):
+        cols = head_cols(head)
+        grad = stack(grads, cols)
+        grad_score = (dot_nt(pair_ref[:, cols], grad) * slope_ref[head]).astype(bf16)
+        value = dot(weight_ref[head], grad) + value_sum_ref[:, cols]
+        key = dot(grad_score, stack(queries, cols)) + key_sum_ref[:, cols]
+        values.append(value.astype(bf16))
+        keys.append((key * scale).astype(bf16))
+    parts = [jnp.concatenate(one, axis=1) for one in (values, keys)]
     parts_to_slots(slots_ref, parts, wires)
 
 
@@ -461,7 +467,7 @@
 
     slots = wire(SCEN * MAIN, feats)
     matrices = shape((1 + FOLD, rows, SCEN * MAIN), bf16)
-    events, w_hbm, cotan = events[0], w_proj[0], cotangent[0]
+    events, w_local, cotan = events[0], w_proj[0], cotangent[0]
     gain = gain.reshape(-1, LANES)
 
     to_slot, *outbox = call(
@@ -475,20 +481,15 @@
             pltpu.VMEM(scenario.shape, jnp.int32),
             pltpu.SemaphoreType.DMA((3,)),
         ],
-        limit=VMEM_ALL - (1 << 20),
     )
     inbound = exchange(outbox if direct else wires_of(outbox * split))
+    small = jnp.concatenate([lengths, offsets, scenario], axis=1)
     w_local, to_row, see, seen = call(
-        functools.partial(mask_kernel, direct, blocks),
-        [shape(w_hbm.shape, bf16), matrices] + [shape((rows, blocks * rows), f32)] * 2,
-        [w_hbm, lengths, offsets, scenario],
-        [pltpu.HBM] * 4,
-        [
-            pltpu.SMEM(lengths.shape, jnp.int32),
-            pltpu.SMEM(offsets.shape, jnp.int32),
-            pltpu.VMEM(scenario.shape, jnp.int32),
-            pltpu.SemaphoreType.DMA((7,)),
-        ],
+        functools.partial(mask_kernel, direct, blocks, lengths.shape[1]),
+        [shape(w_local.shape, bf16), matrices] + [shape((rows, blocks * rows), f32)] * 2,
+        [w_local, small],
+        [pltpu.HBM],
+        [pltpu.SemaphoreType.DMA((4,))],
     )
 
     def project(parts, merged=1):
@@ -517,14 +518,12 @@
         gq = jnp.concatenate([gate, query], axis=1)
     pairs = [pair_own] + [shifted(pair_own, d) for d in range(1, blocks)]
     query_own = gq[:, width:]
-    queries = [gq] + [shifted(query_own, -d) for d in range(1, blocks)]
+    queries = [shifted(query_own, -d) for d in range(1, blocks)]
     half = shape((rows, width), bf16)
-    output, grad_own, grad_gate, _ = call(
-        functools.partial(forward_kernel, blocks),
-        [half, half, half, shape((rows, width), f32)],
-        [see, gq, cotan] + pairs,
-    )
-    grads = [grad_own] + [shifted(grad_own, -d) for d in range(1, blocks)]
+    output, grad_own, grad_gate = call(
+        functools.partial(forward_kernel, blocks), [half] * 3, [see, gq, cotan] + pairs
+    )
+    grads = [shifted(grad_own, -d) for d in range(1, blocks)]
 
     def boxes(merged=1):
         cols = 2 * width if direct else width
@@ -535,10 +534,16 @@
         boxes(2),
         [see, gq, grad_own, grad_gate, to_slot] + pairs,
     )
+    each = (HEADS, rows, reach * rows)
+    scores = call(
+        functools.partial(score_kernel, blocks),
+        [shape(each, bf16), shape(each, f32)] + [shape((rows, width), f32)] * 2,
+        [seen, pair_own, gq, grad_own] + queries,
+    )
     pair_grad = call(
         functools.partial(key_kernel, senders, blocks),
         boxes(),
-        [seen, pair_own, to_slot] + queries + grads,
+        [pair_own, to_slot, *scores] + queries + grads,
     )
     term = shape((n_user * CAP, feats), f32)
     if direct:

time: 124 us -> 119 us (0.960)
  local copies, waits for them, and re-layouts: 5.7 us -> 0.05 us
    unnamed x18 -> x6, local copies, waits for them, and re-layouts: 5.67 us -> 0.01 us
    pallas_call x12 -> x13, Pallas kernels: 19.9 us -> 19.5 us  [call(): pl.pallas_call(kernel, out_shape=tuple(outs), in_specs=[pl.BlockSpec(memo...]
  transfers between devices with their start and end apart: 45 -> 45, of which waited for: 12 -> 13; matrix products, arithmetic and copies ran while one was open for 0% -> 1% of each run, Pallas kernels for 6% -> 8%
where the time goes in v5:
time: 119 us; the launch traced here: 117 us
  starting transfers between devices  58.3 us (49%)
  waiting for transfers between devices  37.9 us (32%)
  Pallas kernels  19.5 us (16%)
    ppermute x38, starting transfers between devices, exchanged(): lax.ppermute(blocks[k], 'user', [(i, i ^ merged * k) for i in range(count)])  50 us
    ppermute x38, waiting for transfers between devices, exchanged(): lax.ppermute(blocks[k], 'user', [(i, i ^ merged * k) for i in range(count)])  30.3 us
    pallas_call x13, Pallas kernels, call(): pl.pallas_call(kernel, out_shape=tuple(outs), in_specs=[pl.BlockSpec(memo...  19.5 us
    ppermute x6, starting transfers between devices, shifted(): return lax.ppermute(block, 'seq', route)  8.23 us
    ppermute x6, waiting for transfers between devices, shifted(): return lax.ppermute(block, 'seq', route)  7.51 us
  transfers between devices with their start and end apart: 45, of which 13 were waited for; matrix products, arithmetic and copies ran while one was open for 1% of the time, Pallas kernels for 8%

profile of v5, /device:TPU:2, one launch (start us, length us, event | category | flops | bytes accessed | tf_op | source)
XLA Modules:
  0.0 117.3 jit_solution(6547287420911537193)
XLA Ops:
  0.6 1.6 %shard_map.87 = (bf16[5,128,128]{2,1,0:T(8,128)(2,1)S(1)}, bf16[16,1920]{1,0:T(8,128)(2,1)S(1)}, bf16[16,1920]{1,0:T(8,128)(2,1)S(1)}, bf16[16,1920]{1,0:T(8,128...) custom-call(bf16[128,1536]{1,0:T(8,128)(2,1)} %bitcast.6, ...), custom_call_target="tpu_custom_call" | custom-call | flops 16777216 | bytes 1055232 | tf_op jit(solution)/shard_map/pallas_call | solution.py:38
  2.3 1.6 %collective-permute-start.1 = (bf16[16,1920]{1,0:T(8,128)(2,1)S(1)}, bf16[16,1920]{1,0:T(8,128)(2,1)S(1)}, u32[]{:S(2)}, u32[]{:S(2)}) collective-permute-start(bf16[16,1920]{1,0:T(8,128)(2,1)S(1)} %get-tuple-element.65), channel_id=1, source_target_pairs={{0,2},{1,3},{2,0},{3,1},{4,6},{5,7},{6,4},{7,5},{8,10},{9,11},{10,... | collective-permute-start | bytes 184328 | tf_op jit(solution)/shard_map/ppermute | solution.py:431
  4.1 2.6 %collective-permute-start.3 = (bf16[16,1920]{1,0:T(8,128)(2,1)S(1)}, bf16[16,1920]{1,0:T(8,128)(2,1)S(1)}, u32[]{:S(2)}, u32[]{:S(2)}) collective-permute-start(bf16[16,1920]{1,0:T(8,128)(2,1)S(1)} %get-tuple-element.67), channel_id=1, source_target_pairs={{0,4},{1,5},{2,6},{3,7},{4,0},{5,1},{6,2},{7,3},{8,12},{9,13},{10,... | collective-permute-start | bytes 184328 | tf_op jit(solution)/shard_map/ppermute | solution.py:431
  6.7 3.6 %collective-permute-start.5 = (bf16[16,1920]{1,0:T(8,128)(2,1)S(1)}, bf16[16,1920]{1,0:T(8,128)(2,1)S(1)}, u32[]{:S(2)}, u32[]{:S(2)}) collective-permute-start(bf16[16,1920]{1,0:T(8,128)(2,1)S(1)} %get-tuple-element.69), channel_id=1, source_target_pairs={{0,6},{1,7},{2,4},{3,5},{4,2},{5,3},{6,0},{7,1},{8,14},{9,15},{10,... | collective-permute-start | bytes 184328 | tf_op jit(solution)/shard_map/ppermute | solution.py:431
  11.2 3.9 %shard_map.86 = (bf16[1536,3072]{1,0:T(8,128)(2,1)S(1)}, bf16[5,128,128]{2,1,0:T(8,128)(2,1)S(1)}, f32[128,384]{1,0:T(8,128)S(1)}, f32[128,384]{1,0:T(8,128)S(1)}) custom-call(bf16[1536,3072]{1,0:T(8,128)(2,1)} %bitcast.11, s32[1,136]{1,0:T(1,128)S(1)} %pad_add_fusion.small_ref), custom_call_target="tpu_custom_call" | custom-call | flops 16777216 | bytes 19431968 | tf_op jit(solution)/shard_map/pallas_call | solution.py:38
  15.1 1.7 %collective-permute-done.4.refs_5_ = bf16[16,1920]{1,0:T(8,128)(2,1)S(1)} collective-permute-done((bf16[16,1920]{1,0:T(8,128)(2,1)S(1)}, bf16[16,1920]{1,0:T(8,128)(2,1)S(1)}, u32[]{:S(2)}, u32[]{:S(2)}) %collective-permute-start.4) | collective-permute-done | bytes 61472 | tf_op jit(solution)/shard_map/ppermute | solution.py:431
  16.8 1.4 %shard_map.90 = (bf16[16,1920]{1,0:T(8,128)(2,1)S(1)}, bf16[16,1920]{1,0:T(8,128)(2,1)S(1)}, bf16[16,1920]{1,0:T(8,128)(2,1)S(1)}, bf16[16,1920]{1,0:T(8,128)(2,...) custom-call(bf16[1536,3072]{1,0:T(8,128)(2,1)S(1)} %get-tuple-elemen, ...), custom_call_target="tpu_custom_call" | custom-call | flops 16777216 | bytes 11403264 | tf_op jit(solution)/shard_map/pallas_call | solution.py:38
  18.4 3.2 %collective-permute-start.15 = (bf16[16,1920]{1,0:T(8,128)(2,1)S(1)}, bf16[16,1920]{1,0:T(8,128)(2,1)S(1)}, u32[]{:S(2)}, u32[]{:S(2)}) collective-permute-start(bf16[16,1920]{1,0:T(8,128)(2,1)S(1)} %get-tuple-element.81), channel_id=1, source_target_pairs={{0,2},{1,3},{2,0},{3,1},{4,6},{5,7},{6,4},{7,5},{8,10},{9,11},{10,... | collective-permute-start | bytes 184328 | tf_op jit(solution)/shard_map/ppermute | solution.py:431
  21.6 2.8 %collective-permute-start.17 = (bf16[16,1920]{1,0:T(8,128)(2,1)S(1)}, bf16[16,1920]{1,0:T(8,128)(2,1)S(1)}, u32[]{:S(2)}, u32[]{:S(2)}) collective-permute-start(bf16[16,1920]{1,0:T(8,128)(2,1)S(1)} %get-tuple-element.83), channel_id=1, source_target_pairs={{0,4},{1,5},{2,6},{3,7},{4,0},{5,1},{6,2},{7,3},{8,12},{9,13},{10,... | collective-permute-start | bytes 184328 | tf_op jit(solution)/shard_map/ppermute | solution.py:431
  24.4 2.1 %collective-permute-start.19 = (bf16[16,1920]{1,0:T(8,128)(2,1)S(1)}, bf16[16,1920]{1,0:T(8,128)(2,1)S(1)}, u32[]{:S(2)}, u32[]{:S(2)}) collective-permute-start(bf16[16,1920]{1,0:T(8,128)(2,1)S(1)} %get-tuple-element.85), channel_id=1, source_target_pairs={{0,6},{1,7},{2,4},{3,5},{4,2},{5,3},{6,0},{7,1},{8,14},{9,15},{10,... | collective-permute-start | bytes 184328 | tf_op jit(solution)/shard_map/ppermute | solution.py:431
  26.5 1.3 %collective-permute-start.20 = (bf16[16,1920]{1,0:T(8,128)(2,1)S(1)}, bf16[16,1920]{1,0:T(8,128)(2,1)S(1)}, u32[]{:S(2)}, u32[]{:S(2)}) collective-permute-start(bf16[16,1920]{1,0:T(8,128)(2,1)S(1)} %get-tuple-element.86), channel_id=1, source_target_pairs={{0,7},{1,6},{2,5},{3,4},{4,3},{5,2},{6,1},{7,0},{8,15},{9,14},{10,... | collective-permute-start | bytes 184328 | tf_op jit(solution)/shard_map/ppermute | solution.py:431
  27.8 6.4 %collective-permute-done.18.refs_5_ = bf16[16,1920]{1,0:T(8,128)(2,1)S(1)} collective-permute-done((bf16[16,1920]{1,0:T(8,128)(2,1)S(1)}, bf16[16,1920]{1,0:T(8,128)(2,1)S(1)}, u32[]{:S(2)}, u32[]{:S(2)}) %collective-permute-start.18) | collective-permute-done | bytes 61472 | tf_op jit(solution)/shard_map/ppermute | solution.py:431
  34.6 1.5 %collective-permute-start.21 = (bf16[128,1536]{1,0:T(8,128)(2,1)S(1)}, bf16[128,1536]{1,0:T(8,128)(2,1)S(1)}, u32[]{:S(2)}, u32[]{:S(2)}) collective-permute-start(bf16[128,1536]{1,0:T(8,128)(2,1)S(1)} %shard_map.91.refs_0_.pair_ref), channel_id=1, source_target_pairs={{24,0},{0,8},{8,16},{16,24},{25,1},{1,9},{9,17},{17,25},{26,2},{2,... | collective-permute-start | bytes 1179656 | tf_op jit(solution)/shard_map/ppermute | solution.py:438
  36.6 1.5 %shard_map.88 = (bf16[16,1920]{1,0:T(8,128)(2,1)S(1)}, bf16[16,1920]{1,0:T(8,128)(2,1)S(1)}, bf16[16,1920]{1,0:T(8,128)(2,1)S(1)}, bf16[16,1920]{1,0:T(8,128)(2,...) custom-call(bf16[1536,3072]{1,0:T(8,128)(2,1)S(1)} %get-tuple-elemen, ...), custom_call_target="tpu_custom_call" | custom-call | flops 16777216 | bytes 11403264 | tf_op jit(solution)/shard_map/pallas_call | solution.py:38
  38.1 3.3 %collective-permute-start.10 = (bf16[16,1920]{1,0:T(8,128)(2,1)S(1)}, bf16[16,1920]{1,0:T(8,128)(2,1)S(1)}, u32[]{:S(2)}, u32[]{:S(2)}) collective-permute-start(bf16[16,1920]{1,0:T(8,128)(2,1)S(1)} %get-tuple-element.75), channel_id=1, source_target_pairs={{0,4},{1,5},{2,6},{3,7},{4,0},{5,1},{6,2},{7,3},{8,12},{9,13},{10,... | collective-permute-start | bytes 184328 | tf_op jit(solution)/shard_map/ppermute | solution.py:431
  41.4 2.3 %collective-permute-start.12 = (bf16[16,1920]{1,0:T(8,128)(2,1)S(1)}, bf16[16,1920]{1,0:T(8,128)(2,1)S(1)}, u32[]{:S(2)}, u32[]{:S(2)}) collective-permute-start(bf16[16,1920]{1,0:T(8,128)(2,1)S(1)} %get-tuple-element.77), channel_id=1, source_target_pairs={{0,6},{1,7},{2,4},{3,5},{4,2},{5,3},{6,0},{7,1},{8,14},{9,15},{10,... | collective-permute-start | bytes 184328 | tf_op jit(solution)/shard_map/ppermute | solution.py:431
  43.7 1.1 collective-permute-start.13
  44.8 5.3 %collective-permute-done.11.refs_5_ = bf16[16,1920]{1,0:T(8,128)(2,1)S(1)} collective-permute-done((bf16[16,1920]{1,0:T(8,128)(2,1)S(1)}, bf16[16,1920]{1,0:T(8,128)(2,1)S(1)}, u32[]{:S(2)}, u32[]{:S(2)}) %collective-permute-start.11) | collective-permute-done | bytes 61472 | tf_op jit(solution)/shard_map/ppermute | solution.py:431
  50.3 1.6 %collective-permute-start.8 = (bf16[16,1920]{1,0:T(8,128)(2,1)S(1)}, bf16[16,1920]{1,0:T(8,128)(2,1)S(1)}, u32[]{:S(2)}, u32[]{:S(2)}) collective-permute-start(bf16[16,1920]{1,0:T(8,128)(2,1)S(1)} %get-tuple-element.73), channel_id=1, source_target_pairs={{0,2},{1,3},{2,0},{3,1},{4,6},{5,7},{6,4},{7,5},{8,10},{9,11},{10,... | collective-permute-start | bytes 184328 | tf_op jit(solution)/shard_map/ppermute | solution.py:431
  51.8 1.7 %collective-permute-start.9 = (bf16[16,1920]{1,0:T(8,128)(2,1)S(1)}, bf16[16,1920]{1,0:T(8,128)(2,1)S(1)}, u32[]{:S(2)}, u32[]{:S(2)}) collective-permute-start(bf16[16,1920]{1,0:T(8,128)(2,1)S(1)} %get-tuple-element.74), channel_id=1, source_target_pairs={{0,3},{1,2},{2,1},{3,0},{4,7},{5,6},{6,5},{7,4},{8,11},{9,10},{10,... | collective-permute-start | bytes 184328 | tf_op jit(solution)/shard_map/ppermute | solution.py:431
  53.5 0.9 collective-permute-done.8.refs_2_
  54.5 1.2 %collective-permute-done.9.refs_3_ = bf16[16,1920]{1,0:T(8,128)(2,1)S(1)} collective-permute-done((bf16[16,1920]{1,0:T(8,128)(2,1)S(1)}, bf16[16,1920]{1,0:T(8,128)(2,1)S(1)}, u32[]{:S(2)}, u32[]{:S(2)}) %collective-permute-start.9) | collective-permute-done | bytes 61472 | tf_op jit(solution)/shard_map/ppermute | solution.py:431
  56.0 2.1 %shard_map.92 = (bf16[128,768]{1,0:T(8,128)(2,1)}, bf16[128,768]{1,0:T(8,128)(2,1)S(1)}, bf16[128,768]{1,0:T(8,128)(2,1)S(1)}) custom-call(f32[128,384]{1,0:T(8,128)S(1)} %get-tuple-element.60.see_ref, bf16[128,1536]{1,0:T(8,128)(2,1)S(1)} %shard_map.89.gq_ref, bf16[128,768]{1,0:T(8,128)(2,1)S(1)} %bitcast.8, ...), custom_call_target="tpu_custom_call" | custom-call | flops 16777216 | bytes 2555904 | tf_op jit(solution)/shard_map/pallas_call | solution.py:38
  58.1 1.7 %shard_map.95 = (bf16[32,1920]{1,0:T(8,128)(2,1)S(1)}, bf16[32,1920]{1,0:T(8,128)(2,1)S(1)}, bf16[32,1920]{1,0:T(8,128)(2,1)S(1)}, bf16[32,1920]{1,0:T(8,128)(2,1)S(1)}) custom-call(f32[128,384]{1,0:T(8,128)S(1)} %get-tuple-element.60.see_ref, bf16[128,1536]{1,0:T(8,128)(2,1)S(1)} %shard_map.89.gq_ref, bf16[128,768]{1,0:T(8,128)(2,1)S(1)} %get-tuple-element.91.grad_ref, ...), custom_call_target="tpu_custom_call" | custom-call | flops 16777216 | bytes 2818048 | tf_op jit(solution)/shard_map/pallas_call | solution.py:38
  59.8 2.3 %collective-permute-start.34 = (bf16[32,1920]{1,0:T(8,128)(2,1)S(1)}, bf16[32,1920]{1,0:T(8,128)(2,1)S(1)}, u32[]{:S(2)}, u32[]{:S(2)}) collective-permute-start(bf16[32,1920]{1,0:T(8,128)(2,1)S(1)} %get-tuple-element.107), channel_id=1, source_target_pairs={{0,2},{1,3},{2,0},{3,1},{4,6},{5,7},{6,4},{7,5},{8,10},{9,11},{10,... | collective-permute-start | bytes 368648 | tf_op jit(solution)/shard_map/ppermute | solution.py:431
  62.1 2.0 %collective-permute-start.35 = (bf16[32,1920]{1,0:T(8,128)(2,1)S(1)}, bf16[32,1920]{1,0:T(8,128)(2,1)S(1)}, u32[]{:S(2)}, u32[]{:S(2)}) collective-permute-start(bf16[32,1920]{1,0:T(8,128)(2,1)S(1)} %get-tuple-element.108), channel_id=1, source_target_pairs={{0,4},{1,5},{2,6},{3,7},{4,0},{5,1},{6,2},{7,3},{8,12},{9,13},{10,... | collective-permute-start | bytes 368648 | tf_op jit(solution)/shard_map/ppermute | solution.py:431
  64.5 1.8 %collective-permute-start.23 = (bf16[128,768]{1,0:T(8,128)(2,1)S(1)}, bf16[128,768]{1,0:T(8,128)(2,1)S(1)}, u32[]{:S(2)}, u32[]{:S(2)}) collective-permute-start(bf16[128,768]{1,0:T(8,128)(2,1)S(1)} %slice.20), channel_id=1, source_target_pairs={{8,0},{16,8},{24,16},{0,24},{9,1},{17,9},{25,17},{1,25},{10,2},{18... | collective-permute-start | bytes 589832 | tf_op jit(solution)/shard_map/ppermute | solution.py:438
  66.9 2.3 %collective-permute-start.25 = (bf16[128,768]{1,0:T(8,128)(2,1)S(1)}, bf16[128,768]{1,0:T(8,128)(2,1)S(1)}, u32[]{:S(2)}, u32[]{:S(2)}) collective-permute-start(bf16[128,768]{1,0:T(8,128)(2,1)S(1)} %get-tuple-element.91.grad_ref), channel_id=1, source_target_pairs={{8,0},{16,8},{24,16},{0,24},{9,1},{17,9},{25,17},{1,25},{10,2},{18... | collective-permute-start | bytes 589832 | tf_op jit(solution)/shard_map/ppermute | solution.py:438
  69.3 5.1 %collective-permute-done.35.refs_2_ = bf16[32,1920]{1,0:T(8,128)(2,1)S(1)} collective-permute-done((bf16[32,1920]{1,0:T(8,128)(2,1)S(1)}, bf16[32,1920]{1,0:T(8,128)(2,1)S(1)}, u32[]{:S(2)}, u32[]{:S(2)}) %collective-permute-start.35) | collective-permute-done | bytes 122912 | tf_op jit(solution)/shard_map/ppermute | solution.py:431
  74.4 1.6 %collective-permute-start.26 = (bf16[128,768]{1,0:T(8,128)(2,1)S(1)}, bf16[128,768]{1,0:T(8,128)(2,1)S(1)}, u32[]{:S(2)}, u32[]{:S(2)}) collective-permute-start(bf16[128,768]{1,0:T(8,128)(2,1)S(1)} %get-tuple-element.91.grad_ref), channel_id=1, source_target_pairs={{16,0},{24,8},{0,16},{8,24},{17,1},{25,9},{1,17},{9,25},{18,2},{26... | collective-permute-start | bytes 589832 | tf_op jit(solution)/shard_map/ppermute | solution.py:438
  76.1 4.3 %collective-permute-done.24.refs_1_.refs_3_ = bf16[128,768]{1,0:T(8,128)(2,1)S(1)} collective-permute-done((bf16[128,768]{1,0:T(8,128)(2,1)S(1)}, bf16[128,768]{1,0:T(8,128)(2,1)S(1)}, u32[]{:S(2)}, u32[]{:S(2)}) %collective-permute-start.24) | collective-permute-done | bytes 196640 | tf_op jit(solution)/shard_map/ppermute | solution.py:438
  80.4 0.9 shard_map.93
  81.2 3.2 %collective-permute-done.26.refs_5_ = bf16[128,768]{1,0:T(8,128)(2,1)S(1)} collective-permute-done((bf16[128,768]{1,0:T(8,128)(2,1)S(1)}, bf16[128,768]{1,0:T(8,128)(2,1)S(1)}, u32[]{:S(2)}, u32[]{:S(2)}) %collective-permute-start.26) | collective-permute-done | bytes 196640 | tf_op jit(solution)/shard_map/ppermute | solution.py:438
  84.5 1.1 shard_map.94
  86.5 1.0 collective-permute-start.29
  87.5 1.0 collective-permute-start.30
  88.5 1.6 %collective-permute-start.31 = (bf16[16,1920]{1,0:T(8,128)(2,1)S(1)}, bf16[16,1920]{1,0:T(8,128)(2,1)S(1)}, u32[]{:S(2)}, u32[]{:S(2)}) collective-permute-start(bf16[16,1920]{1,0:T(8,128)(2,1)S(1)} %get-tuple-element.101), channel_id=1, source_target_pairs={{0,5},{1,4},{2,7},{3,6},{4,1},{5,0},{6,3},{7,2},{8,13},{9,12},{10,... | collective-permute-start | bytes 184328 | tf_op jit(solution)/shard_map/ppermute | solution.py:431
  90.6 1.7 %collective-permute-start.32 = (bf16[16,1920]{1,0:T(8,128)(2,1)S(1)}, bf16[16,1920]{1,0:T(8,128)(2,1)S(1)}, u32[]{:S(2)}, u32[]{:S(2)}) collective-permute-start(bf16[16,1920]{1,0:T(8,128)(2,1)S(1)} %get-tuple-element.102), channel_id=1, source_target_pairs={{0,6},{1,7},{2,4},{3,5},{4,2},{5,3},{6,0},{7,1},{8,14},{9,15},{10,... | collective-permute-start | bytes 184328 | tf_op jit(solution)/shard_map/ppermute | solution.py:431
  92.2 1.4 %collective-permute-start.33 = (bf16[16,1920]{1,0:T(8,128)(2,1)S(1)}, bf16[16,1920]{1,0:T(8,128)(2,1)S(1)}, u32[]{:S(2)}, u32[]{:S(2)}) collective-permute-start(bf16[16,1920]{1,0:T(8,128)(2,1)S(1)} %get-tuple-element.103), channel_id=1, source_target_pairs={{0,7},{1,6},{2,5},{3,4},{4,3},{5,2},{6,1},{7,0},{8,15},{9,14},{10,... | collective-permute-start | bytes 184328 | tf_op jit(solution)/shard_map/ppermute | solution.py:431
  93.7 1.8 %shard_map.96.refs_8_ = f32[160,1536]{1,0:T(8,128)S(1)} custom-call(f32[160,1536]{1,0:T(8,128)S(1)} %get-tuple-element.104.slope_ref, bf16[1536,3072]{1,0:T(8,128)(2,1)S(1)} %get-tuple-element.62.w_ref, bf16[32,1920]{1,0:T(8,128)(2,1)S(1)} %get-tuple-element.106.refs_0_, bf16[32,1920]{1,0:T(8,128)(2,1)S(1)} %collective-permute-done.34.refs_1_, ...), custom_call_target="tpu_custom_call" | custom-call | flops 16777216 | bytes 12140544 | tf_op jit(solution)/shard_map/pallas_call | solution.py:38
  95.5 2.8 %collective-permute-done.30.refs_4_ = bf16[16,1920]{1,0:T(8,128)(2,1)S(1)} collective-permute-done((bf16[16,1920]{1,0:T(8,128)(2,1)S(1)}, bf16[16,1920]{1,0:T(8,128)(2,1)S(1)}, u32[]{:S(2)}, u32[]{:S(2)}) %collective-permute-start.30) | collective-permute-done | bytes 61472 | tf_op jit(solution)/shard_map/ppermute | solution.py:431
  98.8 1.9 %shard_map.97 = (bf16[16,1920]{1,0:T(8,128)(2,1)S(1)}, bf16[16,1920]{1,0:T(8,128)(2,1)S(1)}, bf16[16,1920]{1,0:T(8,128)(2,1)S(1)}, bf16[16,1920]{1,0:T(8,128)(2,...) custom-call(f32[160,1536]{1,0:T(8,128)S(1)} %get-tuple-element.88.sl, ...), custom_call_target="tpu_custom_call" | custom-call | flops 16777216 | bytes 12386304 | tf_op jit(solution)/shard_map/pallas_call | solution.py:38
  101.5 2.8 %collective-permute-start.39 = (bf16[16,1920]{1,0:T(8,128)(2,1)S(1)}, bf16[16,1920]{1,0:T(8,128)(2,1)S(1)}, u32[]{:S(2)}, u32[]{:S(2)}) collective-permute-start(bf16[16,1920]{1,0:T(8,128)(2,1)S(1)} %get-tuple-element.112), channel_id=1, source_target_pairs={{0,2},{1,3},{2,0},{3,1},{4,6},{5,7},{6,4},{7,5},{8,10},{9,11},{10,... | collective-permute-start | bytes 184328 | tf_op jit(solution)/shard_map/ppermute | solution.py:431
  104.3 1.9 %collective-permute-start.41 = (bf16[16,1920]{1,0:T(8,128)(2,1)S(1)}, bf16[16,1920]{1,0:T(8,128)(2,1)S(1)}, u32[]{:S(2)}, u32[]{:S(2)}) collective-permute-start(bf16[16,1920]{1,0:T(8,128)(2,1)S(1)} %get-tuple-element.114), channel_id=1, source_target_pairs={{0,4},{1,5},{2,6},{3,7},{4,0},{5,1},{6,2},{7,3},{8,12},{9,13},{10,... | collective-permute-start | bytes 184328 | tf_op jit(solution)/shard_map/ppermute | solution.py:431
  106.6 1.7 %collective-permute-start.43 = (bf16[16,1920]{1,0:T(8,128)(2,1)S(1)}, bf16[16,1920]{1,0:T(8,128)(2,1)S(1)}, u32[]{:S(2)}, u32[]{:S(2)}) collective-permute-start(bf16[16,1920]{1,0:T(8,128)(2,1)S(1)} %get-tuple-element.116), channel_id=1, source_target_pairs={{0,6},{1,7},{2,4},{3,5},{4,2},{5,3},{6,0},{7,1},{8,14},{9,15},{10,... | collective-permute-start | bytes 184328 | tf_op jit(solution)/shard_map/ppermute | solution.py:431
  108.4 2.1 %collective-permute-start.44 = (bf16[16,1920]{1,0:T(8,128)(2,1)S(1)}, bf16[16,1920]{1,0:T(8,128)(2,1)S(1)}, u32[]{:S(2)}, u32[]{:S(2)}) collective-permute-start(bf16[16,1920]{1,0:T(8,128)(2,1)S(1)} %get-tuple-element.117), channel_id=1, source_target_pairs={{0,7},{1,6},{2,5},{3,4},{4,3},{5,2},{6,1},{7,0},{8,15},{9,14},{10,... | collective-permute-start | bytes 184328 | tf_op jit(solution)/shard_map/ppermute | solution.py:431
  110.5 5.6 %collective-permute-done.42.refs_5_ = bf16[16,1920]{1,0:T(8,128)(2,1)S(1)} collective-permute-done((bf16[16,1920]{1,0:T(8,128)(2,1)S(1)}, bf16[16,1920]{1,0:T(8,128)(2,1)S(1)}, u32[]{:S(2)}, u32[]{:S(2)}) %collective-permute-start.42) | collective-permute-done | bytes 61472 | tf_op jit(solution)/shard_map/ppermute | solution.py:431
  116.1 1.2 %shard_map.98 = bf16[128,1536]{1,0:T(8,128)(2,1)} custom-call(bf16[5,128,128]{2,1,0:T(8,128)(2,1)S(1)} %get-tuple-element.61.rows_ref, bf16[128,1536]{1,0:T(8,128)(2,1)S(1)} %bitcast.7, f32[12,128]{1,0:T(8,128)S(1)} %bitcast.10, bf16[16,1920]{1,0:T(8,128)(2,1)S(1)} %get-tuple-element.110.refs_0_, bf16[16,1920]{1,0:T(8,128)(2,1)S(1)} %collective-permute-done.38.refs_1_, ...), custom_call_target="tpu_custom_call" | custom-call | flops 16777216 | bytes 1447936 | tf_op jit(solution)/shard_map/pallas_call | solution.py:38
  (68 shorter events, 7.0 us)
Async XLA Ops:
  2.2 4.5 %collective-permute-start = (bf16[16,1920]{1,0:T(8,128)(2,1)S(1)}, bf16[16,1920]{1,0:T(8,128)(2,1)S(1)}, u32[]{:S(2)}, u32[]{:S(2)}) collective-permute-start(bf16[16,1920]{1,0:T(8,128)(2,1)S(1)} %get-tuple-element.64), channel_id=1, source_target_pairs={{0,1},{1,0},{2,3},{3,2},{4,5},{5,4},{6,7},{7,6},{8,9},{9,8},{10,11... | collective-permute-start | bytes 184328 | tf_op jit(solution)/shard_map/ppermute | solution.py:431
  2.3 8.1 %collective-permute-start.1 = (bf16[16,1920]{1,0:T(8,128)(2,1)S(1)}, bf16[16,1920]{1,0:T(8,128)(2,1)S(1)}, u32[]{:S(2)}, u32[]{:S(2)}) collective-permute-start(bf16[16,1920]{1,0:T(8,128)(2,1)S(1)} %get-tuple-element.65), channel_id=1, source_target_pairs={{0,2},{1,3},{2,0},{3,1},{4,6},{5,7},{6,4},{7,5},{8,10},{9,11},{10,... | collective-permute-start | bytes 184328 | tf_op jit(solution)/shard_map/ppermute | solution.py:431
  3.9 11.2 %collective-permute-start.2 = (bf16[16,1920]{1,0:T(8,128)(2,1)S(1)}, bf16[16,1920]{1,0:T(8,128)(2,1)S(1)}, u32[]{:S(2)}, u32[]{:S(2)}) collective-permute-start(bf16[16,1920]{1,0:T(8,128)(2,1)S(1)} %get-tuple-element.66), channel_id=1, source_target_pairs={{0,3},{1,2},{2,1},{3,0},{4,7},{5,6},{6,5},{7,4},{8,11},{9,10},{10,... | collective-permute-start | bytes 184328 | tf_op jit(solution)/shard_map/ppermute | solution.py:431
  4.1 11.0 %collective-permute-start.3 = (bf16[16,1920]{1,0:T(8,128)(2,1)S(1)}, bf16[16,1920]{1,0:T(8,128)(2,1)S(1)}, u32[]{:S(2)}, u32[]{:S(2)}) collective-permute-start(bf16[16,1920]{1,0:T(8,128)(2,1)S(1)} %get-tuple-element.67), channel_id=1, source_target_pairs={{0,4},{1,5},{2,6},{3,7},{4,0},{5,1},{6,2},{7,3},{8,12},{9,13},{10,... | collective-permute-start | bytes 184328 | tf_op jit(solution)/shard_map/ppermute | solution.py:431
  6.7 10.1 %collective-permute-start.4 = (bf16[16,1920]{1,0:T(8,128)(2,1)S(1)}, bf16[16,1920]{1,0:T(8,128)(2,1)S(1)}, u32[]{:S(2)}, u32[]{:S(2)}) collective-permute-start(bf16[16,1920]{1,0:T(8,128)(2,1)S(1)} %get-tuple-element.68), channel_id=1, source_target_pairs={{0,5},{1,4},{2,7},{3,6},{4,1},{5,0},{6,3},{7,2},{8,13},{9,12},{10,... | collective-permute-start | bytes 184328 | tf_op jit(solution)/shard_map/ppermute | solution.py:431
  6.7 10.1 %collective-permute-start.5 = (bf16[16,1920]{1,0:T(8,128)(2,1)S(1)}, bf16[16,1920]{1,0:T(8,128)(2,1)S(1)}, u32[]{:S(2)}, u32[]{:S(2)}) collective-permute-start(bf16[16,1920]{1,0:T(8,128)(2,1)S(1)} %get-tuple-element.69), channel_id=1, source_target_pairs={{0,6},{1,7},{2,4},{3,5},{4,2},{5,3},{6,0},{7,1},{8,14},{9,15},{10,... | collective-permute-start | bytes 184328 | tf_op jit(solution)/shard_map/ppermute | solution.py:431
  10.3 6.5 %collective-permute-start.6 = (bf16[16,1920]{1,0:T(8,128)(2,1)S(1)}, bf16[16,1920]{1,0:T(8,128)(2,1)S(1)}, u32[]{:S(2)}, u32[]{:S(2)}) collective-permute-start(bf16[16,1920]{1,0:T(8,128)(2,1)S(1)} %get-tuple-element.70), channel_id=1, source_target_pairs={{0,7},{1,6},{2,5},{3,4},{4,3},{5,2},{6,1},{7,0},{8,15},{9,14},{10,... | collective-permute-start | bytes 184328 | tf_op jit(solution)/shard_map/ppermute | solution.py:431
  16.8 39.2 %copy-start.1 = (bf16[1,128,768]{2,1,0:T(8,128)(2,1)S(1)}, bf16[1,128,768]{2,1,0:T(8,128)(2,1)}, u32[]{:S(2)}) copy-start(bf16[1,128,768]{2,1,0:T(8,128)(2,1)} %param.13) | copy-start | bytes 589828
  18.3 6.2 %collective-permute-start.14 = (bf16[16,1920]{1,0:T(8,128)(2,1)S(1)}, bf16[16,1920]{1,0:T(8,128)(2,1)S(1)}, u32[]{:S(2)}, u32[]{:S(2)}) collective-permute-start(bf16[16,1920]{1,0:T(8,128)(2,1)S(1)} %get-tuple-element.80), channel_id=1, source_target_pairs={{0,1},{1,0},{2,3},{3,2},{4,5},{5,4},{6,7},{7,6},{8,9},{9,8},{10,11... | collective-permute-start | bytes 184328 | tf_op jit(solution)/shard_map/ppermute | solution.py:431
  18.4 8.1 %collective-permute-start.15 = (bf16[16,1920]{1,0:T(8,128)(2,1)S(1)}, bf16[16,1920]{1,0:T(8,128)(2,1)S(1)}, u32[]{:S(2)}, u32[]{:S(2)}) collective-permute-start(bf16[16,1920]{1,0:T(8,128)(2,1)S(1)} %get-tuple-element.81), channel_id=1, source_target_pairs={{0,2},{1,3},{2,0},{3,1},{4,6},{5,7},{6,4},{7,5},{8,10},{9,11},{10,... | collective-permute-start | bytes 184328 | tf_op jit(solution)/shard_map/ppermute | solution.py:431
  21.6 6.2 %collective-permute-start.16 = (bf16[16,1920]{1,0:T(8,128)(2,1)S(1)}, bf16[16,1920]{1,0:T(8,128)(2,1)S(1)}, u32[]{:S(2)}, u32[]{:S(2)}) collective-permute-start(bf16[16,1920]{1,0:T(8,128)(2,1)S(1)} %get-tuple-element.82), channel_id=1, source_target_pairs={{0,3},{1,2},{2,1},{3,0},{4,7},{5,6},{6,5},{7,4},{8,11},{9,10},{10,... | collective-permute-start | bytes 184328 | tf_op jit(solution)/shard_map/ppermute | solution.py:431
  21.6 6.2 %collective-permute-start.17 = (bf16[16,1920]{1,0:T(8,128)(2,1)S(1)}, bf16[16,1920]{1,0:T(8,128)(2,1)S(1)}, u32[]{:S(2)}, u32[]{:S(2)}) collective-permute-start(bf16[16,1920]{1,0:T(8,128)(2,1)S(1)} %get-tuple-element.83), channel_id=1, source_target_pairs={{0,4},{1,5},{2,6},{3,7},{4,0},{5,1},{6,2},{7,3},{8,12},{9,13},{10,... | collective-permute-start | bytes 184328 | tf_op jit(solution)/shard_map/ppermute | solution.py:431
  24.4 9.9 %collective-permute-start.18 = (bf16[16,1920]{1,0:T(8,128)(2,1)S(1)}, bf16[16,1920]{1,0:T(8,128)(2,1)S(1)}, u32[]{:S(2)}, u32[]{:S(2)}) collective-permute-start(bf16[16,1920]{1,0:T(8,128)(2,1)S(1)} %get-tuple-element.84), channel_id=1, source_target_pairs={{0,5},{1,4},{2,7},{3,6},{4,1},{5,0},{6,3},{7,2},{8,13},{9,12},{10,... | collective-permute-start | bytes 184328 | tf_op jit(solution)/shard_map/ppermute | solution.py:431
  24.4 9.9 %collective-permute-start.19 = (bf16[16,1920]{1,0:T(8,128)(2,1)S(1)}, bf16[16,1920]{1,0:T(8,128)(2,1)S(1)}, u32[]{:S(2)}, u32[]{:S(2)}) collective-permute-start(bf16[16,1920]{1,0:T(8,128)(2,1)S(1)} %get-tuple-element.85), channel_id=1, source_target_pairs={{0,6},{1,7},{2,4},{3,5},{4,2},{5,3},{6,0},{7,1},{8,14},{9,15},{10,... | collective-permute-start | bytes 184328 | tf_op jit(solution)/shard_map/ppermute | solution.py:431
  26.5 7.7 %collective-permute-start.20 = (bf16[16,1920]{1,0:T(8,128)(2,1)S(1)}, bf16[16,1920]{1,0:T(8,128)(2,1)S(1)}, u32[]{:S(2)}, u32[]{:S(2)}) collective-permute-start(bf16[16,1920]{1,0:T(8,128)(2,1)S(1)} %get-tuple-element.86), channel_id=1, source_target_pairs={{0,7},{1,6},{2,5},{3,4},{4,3},{5,2},{6,1},{7,0},{8,15},{9,14},{10,... | collective-permute-start | bytes 184328 | tf_op jit(solution)/shard_map/ppermute | solution.py:431
  34.6 21.4 %collective-permute-start.21 = (bf16[128,1536]{1,0:T(8,128)(2,1)S(1)}, bf16[128,1536]{1,0:T(8,128)(2,1)S(1)}, u32[]{:S(2)}, u32[]{:S(2)}) collective-permute-start(bf16[128,1536]{1,0:T(8,128)(2,1)S(1)} %shard_map.91.refs_0_.pair_ref), channel_id=1, source_target_pairs={{24,0},{0,8},{8,16},{16,24},{25,1},{1,9},{9,17},{17,25},{26,2},{2,... | collective-permute-start | bytes 1179656 | tf_op jit(solution)/shard_map/ppermute | solution.py:438
  36.1 19.9 %collective-permute-start.22 = (bf16[128,1536]{1,0:T(8,128)(2,1)S(1)}, bf16[128,1536]{1,0:T(8,128)(2,1)S(1)}, u32[]{:S(2)}, u32[]{:S(2)}) collective-permute-start(bf16[128,1536]{1,0:T(8,128)(2,1)S(1)} %shard_map.91.refs_0_.pair_ref), channel_id=1, source_target_pairs={{16,0},{24,8},{0,16},{8,24},{17,1},{25,9},{1,17},{9,25},{18,2},{26... | collective-permute-start | bytes 1179656 | tf_op jit(solution)/shard_map/ppermute | solution.py:438
  38.1 5.6 %collective-permute-start.10 = (bf16[16,1920]{1,0:T(8,128)(2,1)S(1)}, bf16[16,1920]{1,0:T(8,128)(2,1)S(1)}, u32[]{:S(2)}, u32[]{:S(2)}) collective-permute-start(bf16[16,1920]{1,0:T(8,128)(2,1)S(1)} %get-tuple-element.75), channel_id=1, source_target_pairs={{0,4},{1,5},{2,6},{3,7},{4,0},{5,1},{6,2},{7,3},{8,12},{9,13},{10,... | collective-permute-start | bytes 184328 | tf_op jit(solution)/shard_map/ppermute | solution.py:431
  41.4 8.6 %collective-permute-start.11 = (bf16[16,1920]{1,0:T(8,128)(2,1)S(1)}, bf16[16,1920]{1,0:T(8,128)(2,1)S(1)}, u32[]{:S(2)}, u32[]{:S(2)}) collective-permute-start(bf16[16,1920]{1,0:T(8,128)(2,1)S(1)} %get-tuple-element.76), channel_id=1, source_target_pairs={{0,5},{1,4},{2,7},{3,6},{4,1},{5,0},{6,3},{7,2},{8,13},{9,12},{10,... | collective-permute-start | bytes 184328 | tf_op jit(solution)/shard_map/ppermute | solution.py:431
  41.4 8.8 %collective-permute-start.12 = (bf16[16,1920]{1,0:T(8,128)(2,1)S(1)}, bf16[16,1920]{1,0:T(8,128)(2,1)S(1)}, u32[]{:S(2)}, u32[]{:S(2)}) collective-permute-start(bf16[16,1920]{1,0:T(8,128)(2,1)S(1)} %get-tuple-element.77), channel_id=1, source_target_pairs={{0,6},{1,7},{2,4},{3,5},{4,2},{5,3},{6,0},{7,1},{8,14},{9,15},{10,... | collective-permute-start | bytes 184328 | tf_op jit(solution)/shard_map/ppermute | solution.py:431
  43.7 8.1 %collective-permute-start.13 = (bf16[16,1920]{1,0:T(8,128)(2,1)S(1)}, bf16[16,1920]{1,0:T(8,128)(2,1)S(1)}, u32[]{:S(2)}, u32[]{:S(2)}) collective-permute-start(bf16[16,1920]{1,0:T(8,128)(2,1)S(1)} %get-tuple-element.78), channel_id=1, source_target_pairs={{0,7},{1,6},{2,5},{3,4},{4,3},{5,2},{6,1},{7,0},{8,15},{9,14},{10,... | collective-permute-start | bytes 184328 | tf_op jit(solution)/shard_map/ppermute | solution.py:431
  50.1 3.5 %collective-permute-start.7 = (bf16[16,1920]{1,0:T(8,128)(2,1)S(1)}, bf16[16,1920]{1,0:T(8,128)(2,1)S(1)}, u32[]{:S(2)}, u32[]{:S(2)}) collective-permute-start(bf16[16,1920]{1,0:T(8,128)(2,1)S(1)} %get-tuple-element.72), channel_id=1, source_target_pairs={{0,1},{1,0},{2,3},{3,2},{4,5},{5,4},{6,7},{7,6},{8,9},{9,8},{10,11... | collective-permute-start | bytes 184328 | tf_op jit(solution)/shard_map/ppermute | solution.py:431
  50.3 4.2 %collective-permute-start.8 = (bf16[16,1920]{1,0:T(8,128)(2,1)S(1)}, bf16[16,1920]{1,0:T(8,128)(2,1)S(1)}, u32[]{:S(2)}, u32[]{:S(2)}) collective-permute-start(bf16[16,1920]{1,0:T(8,128)(2,1)S(1)} %get-tuple-element.73), channel_id=1, source_target_pairs={{0,2},{1,3},{2,0},{3,1},{4,6},{5,7},{6,4},{7,5},{8,10},{9,11},{10,... | collective-permute-start | bytes 184328 | tf_op jit(solution)/shard_map/ppermute | solution.py:431
  51.8 3.8 %collective-permute-start.9 = (bf16[16,1920]{1,0:T(8,128)(2,1)S(1)}, bf16[16,1920]{1,0:T(8,128)(2,1)S(1)}, u32[]{:S(2)}, u32[]{:S(2)}) collective-permute-start(bf16[16,1920]{1,0:T(8,128)(2,1)S(1)} %get-tuple-element.74), channel_id=1, source_target_pairs={{0,3},{1,2},{2,1},{3,0},{4,7},{5,6},{6,5},{7,4},{8,11},{9,10},{10,... | collective-permute-start | bytes 184328 | tf_op jit(solution)/shard_map/ppermute | solution.py:431
  59.8 7.2 %collective-permute-start.34 = (bf16[32,1920]{1,0:T(8,128)(2,1)S(1)}, bf16[32,1920]{1,0:T(8,128)(2,1)S(1)}, u32[]{:S(2)}, u32[]{:S(2)}) collective-permute-start(bf16[32,1920]{1,0:T(8,128)(2,1)S(1)} %get-tuple-element.107), channel_id=1, source_target_pairs={{0,2},{1,3},{2,0},{3,1},{4,6},{5,7},{6,4},{7,5},{8,10},{9,11},{10,... | collective-permute-start | bytes 368648 | tf_op jit(solution)/shard_map/ppermute | solution.py:431
  62.1 12.3 %collective-permute-start.35 = (bf16[32,1920]{1,0:T(8,128)(2,1)S(1)}, bf16[32,1920]{1,0:T(8,128)(2,1)S(1)}, u32[]{:S(2)}, u32[]{:S(2)}) collective-permute-start(bf16[32,1920]{1,0:T(8,128)(2,1)S(1)} %get-tuple-element.108), channel_id=1, source_target_pairs={{0,4},{1,5},{2,6},{3,7},{4,0},{5,1},{6,2},{7,3},{8,12},{9,13},{10,... | collective-permute-start | bytes 368648 | tf_op jit(solution)/shard_map/ppermute | solution.py:431
  64.0 11.9 %collective-permute-start.36 = (bf16[32,1920]{1,0:T(8,128)(2,1)S(1)}, bf16[32,1920]{1,0:T(8,128)(2,1)S(1)}, u32[]{:S(2)}, u32[]{:S(2)}) collective-permute-start(bf16[32,1920]{1,0:T(8,128)(2,1)S(1)} %get-tuple-element.109), channel_id=1, source_target_pairs={{0,6},{1,7},{2,4},{3,5},{4,2},{5,3},{6,0},{7,1},{8,14},{9,15},{10,... | collective-permute-start | bytes 368648 | tf_op jit(solution)/shard_map/ppermute | solution.py:431
  64.5 11.6 %collective-permute-start.23 = (bf16[128,768]{1,0:T(8,128)(2,1)S(1)}, bf16[128,768]{1,0:T(8,128)(2,1)S(1)}, u32[]{:S(2)}, u32[]{:S(2)}) collective-permute-start(bf16[128,768]{1,0:T(8,128)(2,1)S(1)} %slice.20), channel_id=1, source_target_pairs={{8,0},{16,8},{24,16},{0,24},{9,1},{17,9},{25,17},{1,25},{10,2},{18... | collective-permute-start | bytes 589832 | tf_op jit(solution)/shard_map/ppermute | solution.py:438
  66.3 14.0 %collective-permute-start.24 = (bf16[128,768]{1,0:T(8,128)(2,1)S(1)}, bf16[128,768]{1,0:T(8,128)(2,1)S(1)}, u32[]{:S(2)}, u32[]{:S(2)}) collective-permute-start(bf16[128,768]{1,0:T(8,128)(2,1)S(1)} %slice.20), channel_id=1, source_target_pairs={{16,0},{24,8},{0,16},{8,24},{17,1},{25,9},{1,17},{9,25},{18,2},{26... | collective-permute-start | bytes 589832 | tf_op jit(solution)/shard_map/ppermute | solution.py:438
  66.9 14.3 %collective-permute-start.25 = (bf16[128,768]{1,0:T(8,128)(2,1)S(1)}, bf16[128,768]{1,0:T(8,128)(2,1)S(1)}, u32[]{:S(2)}, u32[]{:S(2)}) collective-permute-start(bf16[128,768]{1,0:T(8,128)(2,1)S(1)} %get-tuple-element.91.grad_ref), channel_id=1, source_target_pairs={{8,0},{16,8},{24,16},{0,24},{9,1},{17,9},{25,17},{1,25},{10,2},{18... | collective-permute-start | bytes 589832 | tf_op jit(solution)/shard_map/ppermute | solution.py:438
  74.4 10.1 %collective-permute-start.26 = (bf16[128,768]{1,0:T(8,128)(2,1)S(1)}, bf16[128,768]{1,0:T(8,128)(2,1)S(1)}, u32[]{:S(2)}, u32[]{:S(2)}) collective-permute-start(bf16[128,768]{1,0:T(8,128)(2,1)S(1)} %get-tuple-element.91.grad_ref), channel_id=1, source_target_pairs={{16,0},{24,8},{0,16},{8,24},{17,1},{25,9},{1,17},{9,25},{18,2},{26... | collective-permute-start | bytes 589832 | tf_op jit(solution)/shard_map/ppermute | solution.py:438
  76.0 16.2 %collective-permute-start.37 = (bf16[64,1920]{1,0:T(8,128)(2,1)S(1)}, bf16[64,1920]{1,0:T(8,128)(2,1)S(1)}, u32[]{:S(2)}, u32[]{:S(2)}) collective-permute-start(bf16[64,1920]{1,0:T(8,128)(2,1)S(1)} %pad_maximum_fusion), channel_id=1, source_target_pairs={{0,1},{1,0},{2,3},{3,2},{4,5},{5,4},{6,7},{7,6},{8,9},{9,8},{10,11... | collective-permute-start | bytes 737288 | tf_op jit(solution)/shard_map/ppermute | solution.py:418
  85.6 2.9 %collective-permute-start.27 = (bf16[16,1920]{1,0:T(8,128)(2,1)S(1)}, bf16[16,1920]{1,0:T(8,128)(2,1)S(1)}, u32[]{:S(2)}, u32[]{:S(2)}) collective-permute-start(bf16[16,1920]{1,0:T(8,128)(2,1)S(1)} %get-tuple-element.97), channel_id=1, source_target_pairs={{0,1},{1,0},{2,3},{3,2},{4,5},{5,4},{6,7},{7,6},{8,9},{9,8},{10,11... | collective-permute-start | bytes 184328 | tf_op jit(solution)/shard_map/ppermute | solution.py:431
  85.6 4.9 %collective-permute-start.28 = (bf16[16,1920]{1,0:T(8,128)(2,1)S(1)}, bf16[16,1920]{1,0:T(8,128)(2,1)S(1)}, u32[]{:S(2)}, u32[]{:S(2)}) collective-permute-start(bf16[16,1920]{1,0:T(8,128)(2,1)S(1)} %get-tuple-element.98), channel_id=1, source_target_pairs={{0,2},{1,3},{2,0},{3,1},{4,6},{5,7},{6,4},{7,5},{8,10},{9,11},{10,... | collective-permute-start | bytes 184328 | tf_op jit(solution)/shard_map/ppermute | solution.py:431
  86.5 9.0 %collective-permute-start.29 = (bf16[16,1920]{1,0:T(8,128)(2,1)S(1)}, bf16[16,1920]{1,0:T(8,128)(2,1)S(1)}, u32[]{:S(2)}, u32[]{:S(2)}) collective-permute-start(bf16[16,1920]{1,0:T(8,128)(2,1)S(1)} %get-tuple-element.99), channel_id=1, source_target_pairs={{0,3},{1,2},{2,1},{3,0},{4,7},{5,6},{6,5},{7,4},{8,11},{9,10},{10,... | collective-permute-start | bytes 184328 | tf_op jit(solution)/shard_map/ppermute | solution.py:431
  87.5 10.8 %collective-permute-start.30 = (bf16[16,1920]{1,0:T(8,128)(2,1)S(1)}, bf16[16,1920]{1,0:T(8,128)(2,1)S(1)}, u32[]{:S(2)}, u32[]{:S(2)}) collective-permute-start(bf16[16,1920]{1,0:T(8,128)(2,1)S(1)} %get-tuple-element.100), channel_id=1, source_target_pairs={{0,4},{1,5},{2,6},{3,7},{4,0},{5,1},{6,2},{7,3},{8,12},{9,13},{10,... | collective-permute-start | bytes 184328 | tf_op jit(solution)/shard_map/ppermute | solution.py:431
  88.5 10.4 %collective-permute-start.31 = (bf16[16,1920]{1,0:T(8,128)(2,1)S(1)}, bf16[16,1920]{1,0:T(8,128)(2,1)S(1)}, u32[]{:S(2)}, u32[]{:S(2)}) collective-permute-start(bf16[16,1920]{1,0:T(8,128)(2,1)S(1)} %get-tuple-element.101), channel_id=1, source_target_pairs={{0,5},{1,4},{2,7},{3,6},{4,1},{5,0},{6,3},{7,2},{8,13},{9,12},{10,... | collective-permute-start | bytes 184328 | tf_op jit(solution)/shard_map/ppermute | solution.py:431
  90.6 8.2 %collective-permute-start.32 = (bf16[16,1920]{1,0:T(8,128)(2,1)S(1)}, bf16[16,1920]{1,0:T(8,128)(2,1)S(1)}, u32[]{:S(2)}, u32[]{:S(2)}) collective-permute-start(bf16[16,1920]{1,0:T(8,128)(2,1)S(1)} %get-tuple-element.102), channel_id=1, source_target_pairs={{0,6},{1,7},{2,4},{3,5},{4,2},{5,3},{6,0},{7,1},{8,14},{9,15},{10,... | collective-permute-start | bytes 184328 | tf_op jit(solution)/shard_map/ppermute | solution.py:431
  92.2 6.6 %collective-permute-start.33 = (bf16[16,1920]{1,0:T(8,128)(2,1)S(1)}, bf16[16,1920]{1,0:T(8,128)(2,1)S(1)}, u32[]{:S(2)}, u32[]{:S(2)}) collective-permute-start(bf16[16,1920]{1,0:T(8,128)(2,1)S(1)} %get-tuple-element.103), channel_id=1, source_target_pairs={{0,7},{1,6},{2,5},{3,4},{4,3},{5,2},{6,1},{7,0},{8,15},{9,14},{10,... | collective-permute-start | bytes 184328 | tf_op jit(solution)/shard_map/ppermute | solution.py:431
  93.7 22.4 %copy-start = (bf16[1,128,1536]{2,1,0:T(8,128)(2,1)S(1)}, bf16[1,128,1536]{2,1,0:T(8,128)(2,1)}, u32[]{:S(2)}) copy-start(bf16[1,128,1536]{2,1,0:T(8,128)(2,1)} %param.7) | copy-start | bytes 1179652
  93.7 22.4 %copy-start.2 = (f32[1536]{0:T(1024)S(1)}, f32[1536]{0:T(1024)}, u32[]{:S(2)}) copy-start(f32[1536]{0:T(1024)} %param.11) | copy-start | bytes 18436
  100.8 5.9 %collective-permute-start.38 = (bf16[16,1920]{1,0:T(8,128)(2,1)S(1)}, bf16[16,1920]{1,0:T(8,128)(2,1)S(1)}, u32[]{:S(2)}, u32[]{:S(2)}) collective-permute-start(bf16[16,1920]{1,0:T(8,128)(2,1)S(1)} %get-tuple-element.111), channel_id=1, source_target_pairs={{0,1},{1,0},{2,3},{3,2},{4,5},{5,4},{6,7},{7,6},{8,9},{9,8},{10,11... | collective-permute-start | bytes 184328 | tf_op jit(solution)/shard_map/ppermute | solution.py:431
  101.5 6.9 %collective-permute-start.39 = (bf16[16,1920]{1,0:T(8,128)(2,1)S(1)}, bf16[16,1920]{1,0:T(8,128)(2,1)S(1)}, u32[]{:S(2)}, u32[]{:S(2)}) collective-permute-start(bf16[16,1920]{1,0:T(8,128)(2,1)S(1)} %get-tuple-element.112), channel_id=1, source_target_pairs={{0,2},{1,3},{2,0},{3,1},{4,6},{5,7},{6,4},{7,5},{8,10},{9,11},{10,... | collective-permute-start | bytes 184328 | tf_op jit(solution)/shard_map/ppermute | solution.py:431
  104.3 6.2 %collective-permute-start.40 = (bf16[16,1920]{1,0:T(8,128)(2,1)S(1)}, bf16[16,1920]{1,0:T(8,128)(2,1)S(1)}, u32[]{:S(2)}, u32[]{:S(2)}) collective-permute-start(bf16[16,1920]{1,0:T(8,128)(2,1)S(1)} %get-tuple-element.113), channel_id=1, source_target_pairs={{0,3},{1,2},{2,1},{3,0},{4,7},{5,6},{6,5},{7,4},{8,11},{9,10},{10,... | collective-permute-start | bytes 184328 | tf_op jit(solution)/shard_map/ppermute | solution.py:431
  104.3 6.2 %collective-permute-start.41 = (bf16[16,1920]{1,0:T(8,128)(2,1)S(1)}, bf16[16,1920]{1,0:T(8,128)(2,1)S(1)}, u32[]{:S(2)}, u32[]{:S(2)}) collective-permute-start(bf16[16,1920]{1,0:T(8,128)(2,1)S(1)} %get-tuple-element.114), channel_id=1, source_target_pairs={{0,4},{1,5},{2,6},{3,7},{4,0},{5,1},{6,2},{7,3},{8,12},{9,13},{10,... | collective-permute-start | bytes 184328 | tf_op jit(solution)/shard_map/ppermute | solution.py:431
  106.2 9.9 %collective-permute-start.42 = (bf16[16,1920]{1,0:T(8,128)(2,1)S(1)}, bf16[16,1920]{1,0:T(8,128)(2,1)S(1)}, u32[]{:S(2)}, u32[]{:S(2)}) collective-permute-start(bf16[16,1920]{1,0:T(8,128)(2,1)S(1)} %get-tuple-element.115), channel_id=1, source_target_pairs={{0,5},{1,4},{2,7},{3,6},{4,1},{5,0},{6,3},{7,2},{8,13},{9,12},{10,... | collective-permute-start | bytes 184328 | tf_op jit(solution)/shard_map/ppermute | solution.py:431
  106.6 9.4 %collective-permute-start.43 = (bf16[16,1920]{1,0:T(8,128)(2,1)S(1)}, bf16[16,1920]{1,0:T(8,128)(2,1)S(1)}, u32[]{:S(2)}, u32[]{:S(2)}) collective-permute-start(bf16[16,1920]{1,0:T(8,128)(2,1)S(1)} %get-tuple-element.116), channel_id=1, source_target_pairs={{0,6},{1,7},{2,4},{3,5},{4,2},{5,3},{6,0},{7,1},{8,14},{9,15},{10,... | collective-permute-start | bytes 184328 | tf_op jit(solution)/shard_map/ppermute | solution.py:431
  108.4 7.7 %collective-permute-start.44 = (bf16[16,1920]{1,0:T(8,128)(2,1)S(1)}, bf16[16,1920]{1,0:T(8,128)(2,1)S(1)}, u32[]{:S(2)}, u32[]{:S(2)}) collective-permute-start(bf16[16,1920]{1,0:T(8,128)(2,1)S(1)} %get-tuple-element.117), channel_id=1, source_target_pairs={{0,7},{1,6},{2,5},{3,4},{4,3},{5,2},{6,1},{7,0},{8,15},{9,14},{10,... | collective-permute-start | bytes 184328 | tf_op jit(solution)/shard_map/ppermute | solution.py:431

commit v6 on v5

--- a/solution.py
+++ b/solution.py
@@ -278,35 +278,67 @@
     fold(jnp.concatenate(done, axis=1), outs)
 
 
-def rows_kernel(rows_ref, *refs):
+def rows_kernel(outs, rows_ref, *refs):
     matrices = [rows_ref[i] for i in range(1 + FOLD)]
-    refs[-1][...] = from_slots(matrices, refs[:-1]).astype(bf16)
-
-
-def head_cols(head, part=0):
-    start = (part * HEADS + head) * HD
-    return slice(start, start + HD)
-
-
-def stack(refs, cols):
-    return jnp.concatenate([ref[:, cols] for ref in refs], axis=0)
-
-
-def forward_kernel(blocks, see_ref, gq_ref, cotan_ref, *refs):
-    pairs, (out_ref, grad_ref, gate_ref) = refs[:blocks], refs[blocks:]
+    rows = from_slots(matrices, refs[:-outs]).astype(bf16)
+    width = rows.shape[1] // outs
+    for i, ref in enumerate(refs[-outs:]):
+        ref[...] = rows[:, i * width : (i + 1) * width]
+
+
+def head_cols(head):
+    return slice(head * HD, (head + 1) * HD)
+
+
+ACROSS = [(0, 1), (1, 0), (2, 3), (3, 2)]
+
+
+def by_corner(blocks):
+    return lax.axis_size("seq") == 4 and blocks == 3
+
+
+def shifted_pairs(value, key, blocks):
+    if not by_corner(blocks):
+        return [[one] + [shifted(one, d) for d in range(1, blocks)] for one in (value, key)]
+    key_far = shifted(key, 2)
+    value_near = shifted(value, 1)
+    value_far = shifted(value, 2)
+    key_near = lax.ppermute(key, "seq", ACROSS)
+    handed = lax.ppermute(key_far, "seq", ACROSS)
+    return [value, value_near, value_far], [key, key_near, key_far, handed]
+
+
+def shifted_queries(query, blocks):
+    if not by_corner(blocks):
+        return [shifted(query, -d) for d in range(1, blocks)]
+    far = shifted(query, -2)
+    near = lax.ppermute(query, "seq", ACROSS)
+    return [near, far, lax.ppermute(far, "seq", ACROSS)]
+
+
+def stack(refs, cols, blocks, corner=0):
+    parts = [ref[:, cols] for ref in refs[:blocks]]
+    if len(refs) > blocks:
+        at = 0 if corner == 1 else 1
+        parts[at] = jnp.where(lax.axis_index("seq") == corner, refs[blocks][:, cols], parts[at])
+    return jnp.concatenate(parts, axis=0)
+
+
+def forward_kernel(blocks, see_ref, gate_in_ref, query_ref, cotan_ref, *refs):
+    out_ref, grad_ref, gate_ref = refs[-3:]
+    values, keys = refs[:blocks], refs[blocks:-3]
     scale = HD ** (-0.5)
     see = see_ref[...]
     done = []
     for head in range(HEADS):
-        keys = stack(pairs, head_cols(head, 1))
-        score = dot_nt(gq_ref[:, head_cols(head, 1)], keys) * scale
+        cols = head_cols(head)
+        score = dot_nt(query_ref[:, cols], stack(keys, cols, blocks, 2)) * scale
         weight = (score * sigmoid(score) * see).astype(bf16)
-        done.append(dot(weight, stack(pairs, head_cols(head))))
-    width = HEADS * HD
+        done.append(dot(weight, stack(values, cols, blocks)))
     mixed = jnp.concatenate(done, axis=1)
     row_scale = lax.rsqrt(jnp.mean(mixed * mixed, axis=1, keepdims=True) + eps)
     normed = mixed * row_scale
-    gate = gq_ref[:, :width].astype(f32)
+    gate = gate_in_ref[...].astype(f32)
     cotan = cotan_ref[...].astype(f32)
     grad_norm = cotan * gate
     mean = jnp.mean(grad_norm * normed, axis=1, keepdims=True)
@@ -324,52 +356,54 @@
     return [refs[i : i + count] for i in range(0, len(refs), count)]
 
 
-def query_kernel(count, blocks, see_ref, gq_ref, grad_ref, gate_ref, slots_ref, *refs):
-    pairs, wires = refs[:blocks], wires_out(count, refs[blocks:])
+def query_kernel(count, total, blocks, see_ref, query_ref, grad_ref, gate_ref, slots_ref, *refs):
+    wires = wires_out(count, refs[-total:])
+    values, keys = refs[:blocks], refs[blocks:-total]
     scale = HD ** (-0.5)
     see = see_ref[...]
     done = []
     for head in range(HEADS):
-        keys = stack(pairs, head_cols(head, 1))
-        _, slope = slope_of(dot_nt(gq_ref[:, head_cols(head, 1)], keys) * scale)
-        att = dot_nt(grad_ref[:, head_cols(head)], stack(pairs, head_cols(head)))
-        done.append((dot((att * slope * see).astype(bf16), keys) * scale).astype(bf16))
+        cols = head_cols(head)
+        key = stack(keys, cols, blocks, 2)
+        _, slope = slope_of(dot_nt(query_ref[:, cols], key) * scale)
+        att = dot_nt(grad_ref[:, cols], stack(values, cols, blocks))
+        done.append((dot((att * slope * see).astype(bf16), key) * scale).astype(bf16))
     parts_to_slots(slots_ref, [gate_ref[...], jnp.concatenate(done, axis=1)], wires)
 
 
-def score_kernel(blocks, seen_ref, pair_ref, gq_ref, grad_ref, *refs):
-    queries, (weight_ref, slope_ref, value_sum_ref, key_sum_ref) = refs[: blocks - 1], refs[blocks - 1 :]
-    rows = pair_ref.shape[0]
+def score_kernel(blocks, seen_ref, value_ref, key_ref, query_ref, grad_ref, *refs):
+    queries, (weight_ref, slope_ref, value_sum_ref, key_sum_ref) = refs[:-4], refs[-4:]
+    rows = key_ref.shape[0]
     scale = HD ** (-0.5)
     seen = seen_ref[...]
     for head in range(HEADS):
-        own = gq_ref[:, head_cols(head, 1)]
-        query = jnp.concatenate([own, stack(queries, head_cols(head))], axis=0)
-        score = dot_nt(pair_ref[:, head_cols(head, 1)], query) * scale
+        own = query_ref[:, head_cols(head)]
+        query = jnp.concatenate([own, stack(queries, head_cols(head), blocks - 1, 1)], axis=0)
+        score = dot_nt(key_ref[:, head_cols(head)], query) * scale
         sig, slope = slope_of(score)
         weight = (score * sig * seen).astype(bf16)
         slope = slope * seen
         grad = grad_ref[:, head_cols(head)]
-        att = dot_nt(pair_ref[:, head_cols(head)], grad)
+        att = dot_nt(value_ref[:, head_cols(head)], grad)
         value_sum_ref[:, head_cols(head)] = dot(weight[:, :rows], grad)
         key_sum_ref[:, head_cols(head)] = dot((att * slope[:, :rows]).astype(bf16), own)
         weight_ref[head] = weight[:, rows:]
         slope_ref[head] = slope[:, rows:]
 
 
-def key_kernel(count, blocks, pair_ref, slots_ref, weight_ref, slope_ref, *refs):
+def key_kernel(count, total, blocks, value_ref, slots_ref, weight_ref, slope_ref, *refs):
     later = blocks - 1
     value_sum_ref, key_sum_ref = refs[:2]
-    queries, grads = refs[2 : 2 + later], refs[2 + later : 2 + 2 * later]
-    wires = wires_out(count, refs[2 + 2 * later :])
+    grads, queries = refs[2 : 2 + later], refs[2 + later : -total]
+    wires = wires_out(count, refs[-total:])
     scale = HD ** (-0.5)
     values, keys = [], []
     for head in range(HEADS):
         cols = head_cols(head)
-        grad = stack(grads, cols)
-        grad_score = (dot_nt(pair_ref[:, cols], grad) * slope_ref[head]).astype(bf16)
+        grad = stack(grads, cols, later)
+        grad_score = (dot_nt(value_ref[:, cols], grad) * slope_ref[head]).astype(bf16)
         value = dot(weight_ref[head], grad) + value_sum_ref[:, cols]
-        key = dot(grad_score, stack(queries, cols)) + key_sum_ref[:, cols]
+        key = dot(grad_score, stack(queries, cols, later, 1)) + key_sum_ref[:, cols]
         values.append(value.astype(bf16))
         keys.append((key * scale).astype(bf16))
     parts = [jnp.concatenate(one, axis=1) for one in (values, keys)]
@@ -501,27 +535,26 @@
         )
         return exchange(box), slope
 
-    def rows_of(box):
-        cols = box[0].shape[1] * FOLD // (FOLD + 1)
-        return call(rows_kernel, [shape((rows, cols), bf16)], [to_row] + box)[0]
+    def rows_of(box, parts=2):
+        outs = [shape((rows, width), bf16)] * parts
+        return call(functools.partial(rows_kernel, parts), outs, [to_row] + box)
 
     if direct:
         pair_parts, query_parts = (1, 3), (0, 2)
         pair_back, pair_slope = project(pair_parts)
         query_back, query_slope = project(query_parts)
-        pair_own = rows_of(pair_back)
-        gq = rows_of(query_back)
+        value, key = rows_of(pair_back)
+        gate, query = rows_of(query_back)
     else:
         (box,), slope = project((0,))
-        gate, value, query, key = [rows_of([part]) for part in slices_of(split, box)]
-        pair_own = jnp.concatenate([value, key], axis=1)
-        gq = jnp.concatenate([gate, query], axis=1)
-    pairs = [pair_own] + [shifted(pair_own, d) for d in range(1, blocks)]
-    query_own = gq[:, width:]
-    queries = [shifted(query_own, -d) for d in range(1, blocks)]
+        gate, value, query, key = [rows_of([part], 1)[0] for part in slices_of(split, box)]
+    values, keys = shifted_pairs(value, key, blocks)
+    queries = shifted_queries(query, blocks)
     half = shape((rows, width), bf16)
     output, grad_own, grad_gate = call(
-        functools.partial(forward_kernel, blocks), [half] * 3, [see, gq, cotan] + pairs
+        functools.partial(forward_kernel, blocks),
+        [half] * 3,
+        [see, gate, query, cotan] + values + keys,
     )
     grads = [shifted(grad_own, -d) for d in range(1, blocks)]
 
@@ -530,20 +563,20 @@
         return wire(SCEN * MAIN, cols, merged) * (1 if direct else 2)
 
     query_grad = call(
-        functools.partial(query_kernel, len(boxes(2)) if direct else 1, blocks),
+        functools.partial(query_kernel, len(boxes(2)) if direct else 1, len(boxes(2)), blocks),
         boxes(2),
-        [see, gq, grad_own, grad_gate, to_slot] + pairs,
+        [see, query, grad_own, grad_gate, to_slot] + values + keys,
     )
     each = (HEADS, rows, reach * rows)
     scores = call(
         functools.partial(score_kernel, blocks),
         [shape(each, bf16), shape(each, f32)] + [shape((rows, width), f32)] * 2,
-        [seen, pair_own, gq, grad_own] + queries,
+        [seen, value, key, query, grad_own] + queries,
     )
     pair_grad = call(
-        functools.partial(key_kernel, senders, blocks),
+        functools.partial(key_kernel, senders, len(boxes()), blocks),
         boxes(),
-        [pair_own, to_slot, *scores] + queries + grads,
+        [value, to_slot, *scores] + grads + queries,
     )
     term = shape((n_user * CAP, feats), f32)
     if direct:

time: 119 us -> 124 us (1.042)
  waiting for transfers between devices: 37.9 us -> 43.1 us
    ppermute x0 -> x4, waiting for transfers between devices: none -> 5.13 us  [the longest x1 3.18 us: shifted_queries(): return [near, far, lax.ppermute(far, 'seq', ACROSS)]]
    ppermute x38, waiting for transfers between devices: 30.3 us -> 34.9 us  [exchanged(): lax.ppermute(blocks[k], 'user', [(i, i ^ merged * k) for i in range(count)])]
    ppermute x6, waiting for transfers between devices: 7.51 us -> 3.05 us  [shifted(): return lax.ppermute(block, 'seq', route)]
    ppermute x0 -> x4, starting transfers between devices: none -> 4.05 us  [the longest x1 1.51 us: shifted_queries(): return [near, far, lax.ppermute(far, 'seq', ACROSS)]]
    ppermute x6, starting transfers between devices: 8.23 us -> 5.61 us  [shifted(): return lax.ppermute(block, 'seq', route)]
    ppermute x38, starting transfers between devices: 50 us -> 47.9 us  [exchanged(): lax.ppermute(blocks[k], 'user', [(i, i ^ merged * k) for i in range(count)])]
  transfers between devices with their start and end apart: 45 -> 49, of which waited for: 13 -> 14; matrix products, arithmetic and copies ran while one was open for 1% -> 1% of each run, Pallas kernels for 8% -> 11%
where the time goes in v6:
time: 124 us; the launch traced here: 122 us
  starting transfers between devices  57.6 us (46%)
  waiting for transfers between devices  43.1 us (35%)
  Pallas kernels  19.5 us (16%)
    ppermute x38, starting transfers between devices, exchanged(): lax.ppermute(blocks[k], 'user', [(i, i ^ merged * k) for i in range(count)])  47.9 us
    ppermute x38, waiting for transfers between devices, exchanged(): lax.ppermute(blocks[k], 'user', [(i, i ^ merged * k) for i in range(count)])  34.9 us
    pallas_call x13, Pallas kernels, call(): pl.pallas_call(kernel, out_shape=tuple(outs), in_specs=[pl.BlockSpec(memo...  19.5 us
    ppermute x6, starting transfers between devices, shifted(): return lax.ppermute(block, 'seq', route)  5.61 us
    ppermute x1, waiting for transfers between devices, shifted_queries(): return [near, far, lax.ppermute(far, 'seq', ACROSS)]  3.18 us
    ppermute x6, waiting for transfers between devices, shifted(): return lax.ppermute(block, 'seq', route)  3.05 us
  transfers between devices with their start and end apart: 49, of which 14 were waited for; matrix products, arithmetic and copies ran while one was open for 1% of the time, Pallas kernels for 11%

profile of v6, /device:TPU:2, one launch (start us, length us, event | category | flops | bytes accessed | tf_op | source)
XLA Modules:
  0.0 121.9 jit_solution(13609789893088180297)
XLA Ops:
  0.6 1.6 %shard_map.87 = (bf16[5,128,128]{2,1,0:T(8,128)(2,1)S(1)}, bf16[16,1920]{1,0:T(8,128)(2,1)S(1)}, bf16[16,1920]{1,0:T(8,128)(2,1)S(1)}, bf16[16,1920]{1,0:T(8,128...) custom-call(bf16[128,1536]{1,0:T(8,128)(2,1)} %bitcast.6, ...), custom_call_target="tpu_custom_call" | custom-call | flops 16777216 | bytes 1055232 | tf_op jit(solution)/shard_map/pallas_call | solution.py:38
  2.3 1.6 %collective-permute-start.1 = (bf16[16,1920]{1,0:T(8,128)(2,1)S(1)}, bf16[16,1920]{1,0:T(8,128)(2,1)S(1)}, u32[]{:S(2)}, u32[]{:S(2)}) collective-permute-start(bf16[16,1920]{1,0:T(8,128)(2,1)S(1)} %get-tuple-element.69), channel_id=1, source_target_pairs={{0,2},{1,3},{2,0},{3,1},{4,6},{5,7},{6,4},{7,5},{8,10},{9,11},{10,... | collective-permute-start | bytes 184328 | tf_op jit(solution)/shard_map/ppermute | solution.py:465
  4.1 2.6 %collective-permute-start.3 = (bf16[16,1920]{1,0:T(8,128)(2,1)S(1)}, bf16[16,1920]{1,0:T(8,128)(2,1)S(1)}, u32[]{:S(2)}, u32[]{:S(2)}) collective-permute-start(bf16[16,1920]{1,0:T(8,128)(2,1)S(1)} %get-tuple-element.71), channel_id=1, source_target_pairs={{0,4},{1,5},{2,6},{3,7},{4,0},{5,1},{6,2},{7,3},{8,12},{9,13},{10,... | collective-permute-start | bytes 184328 | tf_op jit(solution)/shard_map/ppermute | solution.py:465
  6.7 3.6 %collective-permute-start.5 = (bf16[16,1920]{1,0:T(8,128)(2,1)S(1)}, bf16[16,1920]{1,0:T(8,128)(2,1)S(1)}, u32[]{:S(2)}, u32[]{:S(2)}) collective-permute-start(bf16[16,1920]{1,0:T(8,128)(2,1)S(1)} %get-tuple-element.73), channel_id=1, source_target_pairs={{0,6},{1,7},{2,4},{3,5},{4,2},{5,3},{6,0},{7,1},{8,14},{9,15},{10,... | collective-permute-start | bytes 184328 | tf_op jit(solution)/shard_map/ppermute | solution.py:465
  11.2 3.9 %shard_map.86 = (bf16[1536,3072]{1,0:T(8,128)(2,1)S(1)}, bf16[5,128,128]{2,1,0:T(8,128)(2,1)S(1)}, f32[128,384]{1,0:T(8,128)S(1)}, f32[128,384]{1,0:T(8,128)S(1)}) custom-call(bf16[1536,3072]{1,0:T(8,128)(2,1)} %bitcast.11, s32[1,136]{1,0:T(1,128)S(1)} %pad_add_fusion.small_ref), custom_call_target="tpu_custom_call" | custom-call | flops 16777216 | bytes 19431968 | tf_op jit(solution)/shard_map/pallas_call | solution.py:38
  15.1 1.7 %collective-permute-done.4.refs_5_ = bf16[16,1920]{1,0:T(8,128)(2,1)S(1)} collective-permute-done((bf16[16,1920]{1,0:T(8,128)(2,1)S(1)}, bf16[16,1920]{1,0:T(8,128)(2,1)S(1)}, u32[]{:S(2)}, u32[]{:S(2)}) %collective-permute-start.4) | collective-permute-done | bytes 61472 | tf_op jit(solution)/shard_map/ppermute | solution.py:465
  16.8 1.4 %shard_map.90 = (bf16[16,1920]{1,0:T(8,128)(2,1)S(1)}, bf16[16,1920]{1,0:T(8,128)(2,1)S(1)}, bf16[16,1920]{1,0:T(8,128)(2,1)S(1)}, bf16[16,1920]{1,0:T(8,128)(2,...) custom-call(bf16[1536,3072]{1,0:T(8,128)(2,1)S(1)} %get-tuple-elemen, ...), custom_call_target="tpu_custom_call" | custom-call | flops 16777216 | bytes 11403264 | tf_op jit(solution)/shard_map/pallas_call | solution.py:38
  18.4 3.2 %collective-permute-start.15 = (bf16[16,1920]{1,0:T(8,128)(2,1)S(1)}, bf16[16,1920]{1,0:T(8,128)(2,1)S(1)}, u32[]{:S(2)}, u32[]{:S(2)}) collective-permute-start(bf16[16,1920]{1,0:T(8,128)(2,1)S(1)} %get-tuple-element.87), channel_id=1, source_target_pairs={{0,2},{1,3},{2,0},{3,1},{4,6},{5,7},{6,4},{7,5},{8,10},{9,11},{10,... | collective-permute-start | bytes 184328 | tf_op jit(solution)/shard_map/ppermute | solution.py:465
  21.6 2.8 %collective-permute-start.17 = (bf16[16,1920]{1,0:T(8,128)(2,1)S(1)}, bf16[16,1920]{1,0:T(8,128)(2,1)S(1)}, u32[]{:S(2)}, u32[]{:S(2)}) collective-permute-start(bf16[16,1920]{1,0:T(8,128)(2,1)S(1)} %get-tuple-element.89), channel_id=1, source_target_pairs={{0,4},{1,5},{2,6},{3,7},{4,0},{5,1},{6,2},{7,3},{8,12},{9,13},{10,... | collective-permute-start | bytes 184328 | tf_op jit(solution)/shard_map/ppermute | solution.py:465
  24.4 2.1 %collective-permute-start.19 = (bf16[16,1920]{1,0:T(8,128)(2,1)S(1)}, bf16[16,1920]{1,0:T(8,128)(2,1)S(1)}, u32[]{:S(2)}, u32[]{:S(2)}) collective-permute-start(bf16[16,1920]{1,0:T(8,128)(2,1)S(1)} %get-tuple-element.91), channel_id=1, source_target_pairs={{0,6},{1,7},{2,4},{3,5},{4,2},{5,3},{6,0},{7,1},{8,14},{9,15},{10,... | collective-permute-start | bytes 184328 | tf_op jit(solution)/shard_map/ppermute | solution.py:465
  26.5 1.3 %collective-permute-start.20 = (bf16[16,1920]{1,0:T(8,128)(2,1)S(1)}, bf16[16,1920]{1,0:T(8,128)(2,1)S(1)}, u32[]{:S(2)}, u32[]{:S(2)}) collective-permute-start(bf16[16,1920]{1,0:T(8,128)(2,1)S(1)} %get-tuple-element.92), channel_id=1, source_target_pairs={{0,7},{1,6},{2,5},{3,4},{4,3},{5,2},{6,1},{7,0},{8,15},{9,14},{10,... | collective-permute-start | bytes 184328 | tf_op jit(solution)/shard_map/ppermute | solution.py:465
  27.8 6.4 %collective-permute-done.18.refs_5_ = bf16[16,1920]{1,0:T(8,128)(2,1)S(1)} collective-permute-done((bf16[16,1920]{1,0:T(8,128)(2,1)S(1)}, bf16[16,1920]{1,0:T(8,128)(2,1)S(1)}, u32[]{:S(2)}, u32[]{:S(2)}) %collective-permute-start.18) | collective-permute-done | bytes 61472 | tf_op jit(solution)/shard_map/ppermute | solution.py:465
  34.6 1.6 %collective-permute-start.24 = (bf16[128,768]{1,0:T(8,128)(2,1)S(1)}, bf16[128,768]{1,0:T(8,128)(2,1)S(1)}, u32[]{:S(2)}, u32[]{:S(2)}) collective-permute-start(bf16[128,768]{1,0:T(8,128)(2,1)S(1)} %get-tuple-element.94.refs_3_.key_ref), channel_id=1, source_target_pairs={{16,0},{24,8},{0,16},{8,24},{17,1},{25,9},{1,17},{9,25},{18,2},{26... | collective-permute-start | bytes 589832 | tf_op jit(solution)/shard_map/ppermute | solution.py:472
  36.2 1.4 %shard_map.88 = (bf16[16,1920]{1,0:T(8,128)(2,1)S(1)}, bf16[16,1920]{1,0:T(8,128)(2,1)S(1)}, bf16[16,1920]{1,0:T(8,128)(2,1)S(1)}, bf16[16,1920]{1,0:T(8,128)(2,...) custom-call(bf16[1536,3072]{1,0:T(8,128)(2,1)S(1)} %get-tuple-elemen, ...), custom_call_target="tpu_custom_call" | custom-call | flops 16777216 | bytes 11403264 | tf_op jit(solution)/shard_map/pallas_call | solution.py:38
  37.6 3.3 %collective-permute-start.10 = (bf16[16,1920]{1,0:T(8,128)(2,1)S(1)}, bf16[16,1920]{1,0:T(8,128)(2,1)S(1)}, u32[]{:S(2)}, u32[]{:S(2)}) collective-permute-start(bf16[16,1920]{1,0:T(8,128)(2,1)S(1)} %get-tuple-element.79), channel_id=1, source_target_pairs={{0,4},{1,5},{2,6},{3,7},{4,0},{5,1},{6,2},{7,3},{8,12},{9,13},{10,... | collective-permute-start | bytes 184328 | tf_op jit(solution)/shard_map/ppermute | solution.py:465
  40.9 2.3 %collective-permute-start.12 = (bf16[16,1920]{1,0:T(8,128)(2,1)S(1)}, bf16[16,1920]{1,0:T(8,128)(2,1)S(1)}, u32[]{:S(2)}, u32[]{:S(2)}) collective-permute-start(bf16[16,1920]{1,0:T(8,128)(2,1)S(1)} %get-tuple-element.81), channel_id=1, source_target_pairs={{0,6},{1,7},{2,4},{3,5},{4,2},{5,3},{6,0},{7,1},{8,14},{9,15},{10,... | collective-permute-start | bytes 184328 | tf_op jit(solution)/shard_map/ppermute | solution.py:465
  43.2 1.0 collective-permute-start.13
  44.9 5.4 %collective-permute-done.11.refs_5_ = bf16[16,1920]{1,0:T(8,128)(2,1)S(1)} collective-permute-done((bf16[16,1920]{1,0:T(8,128)(2,1)S(1)}, bf16[16,1920]{1,0:T(8,128)(2,1)S(1)}, u32[]{:S(2)}, u32[]{:S(2)}) %collective-permute-start.11) | collective-permute-done | bytes 61472 | tf_op jit(solution)/shard_map/ppermute | solution.py:465
  50.7 1.5 %collective-permute-start.22 = (bf16[128,768]{1,0:T(8,128)(2,1)S(1)}, bf16[128,768]{1,0:T(8,128)(2,1)S(1)}, u32[]{:S(2)}, u32[]{:S(2)}) collective-permute-start(bf16[128,768]{1,0:T(8,128)(2,1)S(1)} %get-tuple-element.93.refs_0_.value_ref), channel_id=1, source_target_pairs={{16,0},{24,8},{0,16},{8,24},{17,1},{25,9},{1,17},{9,25},{18,2},{26... | collective-permute-start | bytes 589832 | tf_op jit(solution)/shard_map/ppermute | solution.py:472
  52.8 1.5 %collective-permute-start.25 = (bf16[128,768]{1,0:T(8,128)(2,1)S(1)}, bf16[128,768]{1,0:T(8,128)(2,1)S(1)}, u32[]{:S(2)}, u32[]{:S(2)}) collective-permute-start(bf16[128,768]{1,0:T(8,128)(2,1)S(1)} %collective-permute-done.24.refs_5_), channel_id=1, source_target_pairs={{0,8},{8,0},{16,24},{24,16},{1,9},{9,1},{17,25},{25,17},{2,10},{10... | collective-permute-start | bytes 589832 | tf_op jit(solution)/shard_map/ppermute | solution.py:307
  54.3 1.2 collective-permute-start.8
  55.5 3.1 %collective-permute-done.8.refs_2_ = bf16[16,1920]{1,0:T(8,128)(2,1)S(1)} collective-permute-done((bf16[16,1920]{1,0:T(8,128)(2,1)S(1)}, bf16[16,1920]{1,0:T(8,128)(2,1)S(1)}, u32[]{:S(2)}, u32[]{:S(2)}) %collective-permute-start.8) | collective-permute-done | bytes 61472 | tf_op jit(solution)/shard_map/ppermute | solution.py:465
  58.5 4.0 %collective-permute-done.9.refs_3_ = bf16[16,1920]{1,0:T(8,128)(2,1)S(1)} collective-permute-done((bf16[16,1920]{1,0:T(8,128)(2,1)S(1)}, bf16[16,1920]{1,0:T(8,128)(2,1)S(1)}, u32[]{:S(2)}, u32[]{:S(2)}) %collective-permute-start.9) | collective-permute-done | bytes 61472 | tf_op jit(solution)/shard_map/ppermute | solution.py:465
  63.6 1.9 %collective-permute-done.25.refs_6_ = bf16[128,768]{1,0:T(8,128)(2,1)S(1)} collective-permute-done((bf16[128,768]{1,0:T(8,128)(2,1)S(1)}, bf16[128,768]{1,0:T(8,128)(2,1)S(1)}, u32[]{:S(2)}, u32[]{:S(2)}) %collective-permute-start.25) | collective-permute-done | bytes 196640 | tf_op jit(solution)/shard_map/ppermute | solution.py:307
  65.6 2.1 %shard_map.92 = (bf16[128,768]{1,0:T(8,128)(2,1)}, bf16[128,768]{1,0:T(8,128)(2,1)S(1)}, bf16[128,768]{1,0:T(8,128)(2,1)S(1)}) custom-call(f32[128,384]{1,0:T(8,128)S(1)} %get-tuple-element.64.see_ref, bf16[128,768]{1,0:T(8,128)(2,1)S(1)} %get-tuple-element.83.gate_in_ref, bf16[128,768]{1,0:T(8,128)(2,1)S(1)} %get-tuple-element.84.query_ref, ...), custom_call_target="tpu_custom_call" | custom-call | flops 16777216 | bytes 2752512 | tf_op jit(solution)/shard_map/pallas_call | solution.py:38
  67.6 1.7 %shard_map.95 = (bf16[32,1920]{1,0:T(8,128)(2,1)S(1)}, bf16[32,1920]{1,0:T(8,128)(2,1)S(1)}, bf16[32,1920]{1,0:T(8,128)(2,1)S(1)}, bf16[32,1920]{1,0:T(8,128)(2,1)S(1)}) custom-call(f32[128,384]{1,0:T(8,128)S(1)} %get-tuple-element.64.see_ref, bf16[128,768]{1,0:T(8,128)(2,1)S(1)} %get-tuple-element.84.query_ref, ...), custom_call_target="tpu_custom_call" | custom-call | flops 16777216 | bytes 2818048 | tf_op jit(solution)/shard_map/pallas_call | solution.py:38
  69.4 2.2 %collective-permute-start.39 = (bf16[32,1920]{1,0:T(8,128)(2,1)S(1)}, bf16[32,1920]{1,0:T(8,128)(2,1)S(1)}, u32[]{:S(2)}, u32[]{:S(2)}) collective-permute-start(bf16[32,1920]{1,0:T(8,128)(2,1)S(1)} %get-tuple-element.116), channel_id=1, source_target_pairs={{0,4},{1,5},{2,6},{3,7},{4,0},{5,1},{6,2},{7,3},{8,12},{9,13},{10,... | collective-permute-start | bytes 368648 | tf_op jit(solution)/shard_map/ppermute | solution.py:465
  71.6 2.1 %collective-permute-start.40 = (bf16[32,1920]{1,0:T(8,128)(2,1)S(1)}, bf16[32,1920]{1,0:T(8,128)(2,1)S(1)}, u32[]{:S(2)}, u32[]{:S(2)}) collective-permute-start(bf16[32,1920]{1,0:T(8,128)(2,1)S(1)} %get-tuple-element.117), channel_id=1, source_target_pairs={{0,6},{1,7},{2,4},{3,5},{4,2},{5,3},{6,0},{7,1},{8,14},{9,15},{10,... | collective-permute-start | bytes 368648 | tf_op jit(solution)/shard_map/ppermute | solution.py:465
  74.3 1.5 %collective-permute-start.28 = (bf16[128,768]{1,0:T(8,128)(2,1)S(1)}, bf16[128,768]{1,0:T(8,128)(2,1)S(1)}, u32[]{:S(2)}, u32[]{:S(2)}) collective-permute-start(bf16[128,768]{1,0:T(8,128)(2,1)S(1)} %collective-permute-done.27.refs_1_.refs_5_), channel_id=1, source_target_pairs={{0,8},{8,0},{16,24},{24,16},{1,9},{9,1},{17,25},{25,17},{2,10},{10... | collective-permute-start | bytes 589832 | tf_op jit(solution)/shard_map/ppermute | solution.py:316
  76.6 4.9 %collective-permute-done.39.refs_2_ = bf16[32,1920]{1,0:T(8,128)(2,1)S(1)} collective-permute-done((bf16[32,1920]{1,0:T(8,128)(2,1)S(1)}, bf16[32,1920]{1,0:T(8,128)(2,1)S(1)}, u32[]{:S(2)}, u32[]{:S(2)}) %collective-permute-start.39) | collective-permute-done | bytes 122912 | tf_op jit(solution)/shard_map/ppermute | solution.py:465
  82.1 3.2 %collective-permute-done.28.refs_2_.refs_6_ = bf16[128,768]{1,0:T(8,128)(2,1)S(1)} collective-permute-done((bf16[128,768]{1,0:T(8,128)(2,1)S(1)}, bf16[128,768]{1,0:T(8,128)(2,1)S(1)}, u32[]{:S(2)}, u32[]{:S(2)}) %collective-permute-start.28) | collective-permute-done | bytes 196640 | tf_op jit(solution)/shard_map/ppermute | solution.py:316
  86.2 1.3 %collective-permute-done.29.refs_2_ = bf16[128,768]{1,0:T(8,128)(2,1)S(1)} collective-permute-done((bf16[128,768]{1,0:T(8,128)(2,1)S(1)}, bf16[128,768]{1,0:T(8,128)(2,1)S(1)}, u32[]{:S(2)}, u32[]{:S(2)}) %collective-permute-start.29) | collective-permute-done | bytes 196640 | tf_op jit(solution)/shard_map/ppermute | solution.py:472
  87.4 1.8 %collective-permute-done.30.refs_3_ = bf16[128,768]{1,0:T(8,128)(2,1)S(1)} collective-permute-done((bf16[128,768]{1,0:T(8,128)(2,1)S(1)}, bf16[128,768]{1,0:T(8,128)(2,1)S(1)}, u32[]{:S(2)}, u32[]{:S(2)}) %collective-permute-start.30) | collective-permute-done | bytes 196640 | tf_op jit(solution)/shard_map/ppermute | solution.py:472
  89.2 1.1 shard_map.94
  90.4 1.8 %collective-permute-start.33 = (bf16[16,1920]{1,0:T(8,128)(2,1)S(1)}, bf16[16,1920]{1,0:T(8,128)(2,1)S(1)}, u32[]{:S(2)}, u32[]{:S(2)}) collective-permute-start(bf16[16,1920]{1,0:T(8,128)(2,1)S(1)} %get-tuple-element.107), channel_id=1, source_target_pairs={{0,3},{1,2},{2,1},{3,0},{4,7},{5,6},{6,5},{7,4},{8,11},{9,10},{10,... | collective-permute-start | bytes 184328 | tf_op jit(solution)/shard_map/ppermute | solution.py:465
  92.7 2.1 %collective-permute-start.35 = (bf16[16,1920]{1,0:T(8,128)(2,1)S(1)}, bf16[16,1920]{1,0:T(8,128)(2,1)S(1)}, u32[]{:S(2)}, u32[]{:S(2)}) collective-permute-start(bf16[16,1920]{1,0:T(8,128)(2,1)S(1)} %get-tuple-element.109), channel_id=1, source_target_pairs={{0,5},{1,4},{2,7},{3,6},{4,1},{5,0},{6,3},{7,2},{8,13},{9,12},{10,... | collective-permute-start | bytes 184328 | tf_op jit(solution)/shard_map/ppermute | solution.py:465
  95.3 1.7 %collective-permute-start.36 = (bf16[16,1920]{1,0:T(8,128)(2,1)S(1)}, bf16[16,1920]{1,0:T(8,128)(2,1)S(1)}, u32[]{:S(2)}, u32[]{:S(2)}) collective-permute-start(bf16[16,1920]{1,0:T(8,128)(2,1)S(1)} %get-tuple-element.110), channel_id=1, source_target_pairs={{0,6},{1,7},{2,4},{3,5},{4,2},{5,3},{6,0},{7,1},{8,14},{9,15},{10,... | collective-permute-start | bytes 184328 | tf_op jit(solution)/shard_map/ppermute | solution.py:465
  97.0 1.4 %collective-permute-start.37 = (bf16[16,1920]{1,0:T(8,128)(2,1)S(1)}, bf16[16,1920]{1,0:T(8,128)(2,1)S(1)}, u32[]{:S(2)}, u32[]{:S(2)}) collective-permute-start(bf16[16,1920]{1,0:T(8,128)(2,1)S(1)} %get-tuple-element.111), channel_id=1, source_target_pairs={{0,7},{1,6},{2,5},{3,4},{4,3},{5,2},{6,1},{7,0},{8,15},{9,14},{10,... | collective-permute-start | bytes 184328 | tf_op jit(solution)/shard_map/ppermute | solution.py:465
  98.4 1.8 %shard_map.96.refs_8_ = f32[160,1536]{1,0:T(8,128)S(1)} custom-call(f32[160,1536]{1,0:T(8,128)S(1)} %get-tuple-element.112.slope_ref, bf16[1536,3072]{1,0:T(8,128)(2,1)S(1)} %get-tuple-element.66.w_ref, bf16[32,1920]{1,0:T(8,128)(2,1)S(1)} %get-tuple-element.114.refs_0_, bf16[32,1920]{1,0:T(8,128)(2,1)S(1)} %collective-permute-done.38.refs_1_, ...), custom_call_target="tpu_custom_call" | custom-call | flops 16777216 | bytes 12140544 | tf_op jit(solution)/shard_map/pallas_call | solution.py:38
  100.2 1.5 %collective-permute-done.34.refs_4_ = bf16[16,1920]{1,0:T(8,128)(2,1)S(1)} collective-permute-done((bf16[16,1920]{1,0:T(8,128)(2,1)S(1)}, bf16[16,1920]{1,0:T(8,128)(2,1)S(1)}, u32[]{:S(2)}, u32[]{:S(2)}) %collective-permute-start.34) | collective-permute-done | bytes 61472 | tf_op jit(solution)/shard_map/ppermute | solution.py:465
  101.6 2.0 %collective-permute-done.35.refs_5_ = bf16[16,1920]{1,0:T(8,128)(2,1)S(1)} collective-permute-done((bf16[16,1920]{1,0:T(8,128)(2,1)S(1)}, bf16[16,1920]{1,0:T(8,128)(2,1)S(1)}, u32[]{:S(2)}, u32[]{:S(2)}) %collective-permute-start.35) | collective-permute-done | bytes 61472 | tf_op jit(solution)/shard_map/ppermute | solution.py:465
  103.6 1.9 %shard_map.97 = (bf16[16,1920]{1,0:T(8,128)(2,1)S(1)}, bf16[16,1920]{1,0:T(8,128)(2,1)S(1)}, bf16[16,1920]{1,0:T(8,128)(2,1)S(1)}, bf16[16,1920]{1,0:T(8,128)(2,...) custom-call(f32[160,1536]{1,0:T(8,128)S(1)} %get-tuple-element.96.sl, ...), custom_call_target="tpu_custom_call" | custom-call | flops 16777216 | bytes 12386304 | tf_op jit(solution)/shard_map/pallas_call | solution.py:38
  106.1 2.8 %collective-permute-start.43 = (bf16[16,1920]{1,0:T(8,128)(2,1)S(1)}, bf16[16,1920]{1,0:T(8,128)(2,1)S(1)}, u32[]{:S(2)}, u32[]{:S(2)}) collective-permute-start(bf16[16,1920]{1,0:T(8,128)(2,1)S(1)} %get-tuple-element.120), channel_id=1, source_target_pairs={{0,2},{1,3},{2,0},{3,1},{4,6},{5,7},{6,4},{7,5},{8,10},{9,11},{10,... | collective-permute-start | bytes 184328 | tf_op jit(solution)/shard_map/ppermute | solution.py:465
  109.0 1.8 %collective-permute-start.45 = (bf16[16,1920]{1,0:T(8,128)(2,1)S(1)}, bf16[16,1920]{1,0:T(8,128)(2,1)S(1)}, u32[]{:S(2)}, u32[]{:S(2)}) collective-permute-start(bf16[16,1920]{1,0:T(8,128)(2,1)S(1)} %get-tuple-element.122), channel_id=1, source_target_pairs={{0,4},{1,5},{2,6},{3,7},{4,0},{5,1},{6,2},{7,3},{8,12},{9,13},{10,... | collective-permute-start | bytes 184328 | tf_op jit(solution)/shard_map/ppermute | solution.py:465
  111.3 1.7 %collective-permute-start.47 = (bf16[16,1920]{1,0:T(8,128)(2,1)S(1)}, bf16[16,1920]{1,0:T(8,128)(2,1)S(1)}, u32[]{:S(2)}, u32[]{:S(2)}) collective-permute-start(bf16[16,1920]{1,0:T(8,128)(2,1)S(1)} %get-tuple-element.124), channel_id=1, source_target_pairs={{0,6},{1,7},{2,4},{3,5},{4,2},{5,3},{6,0},{7,1},{8,14},{9,15},{10,... | collective-permute-start | bytes 184328 | tf_op jit(solution)/shard_map/ppermute | solution.py:465
  113.1 2.1 %collective-permute-start.48 = (bf16[16,1920]{1,0:T(8,128)(2,1)S(1)}, bf16[16,1920]{1,0:T(8,128)(2,1)S(1)}, u32[]{:S(2)}, u32[]{:S(2)}) collective-permute-start(bf16[16,1920]{1,0:T(8,128)(2,1)S(1)} %get-tuple-element.125), channel_id=1, source_target_pairs={{0,7},{1,6},{2,5},{3,4},{4,3},{5,2},{6,1},{7,0},{8,15},{9,14},{10,... | collective-permute-start | bytes 184328 | tf_op jit(solution)/shard_map/ppermute | solution.py:465
  115.2 5.5 %collective-permute-done.46.refs_5_ = bf16[16,1920]{1,0:T(8,128)(2,1)S(1)} collective-permute-done((bf16[16,1920]{1,0:T(8,128)(2,1)S(1)}, bf16[16,1920]{1,0:T(8,128)(2,1)S(1)}, u32[]{:S(2)}, u32[]{:S(2)}) %collective-permute-start.46) | collective-permute-done | bytes 61472 | tf_op jit(solution)/shard_map/ppermute | solution.py:465
  120.6 1.2 %shard_map.98 = bf16[128,1536]{1,0:T(8,128)(2,1)} custom-call(bf16[5,128,128]{2,1,0:T(8,128)(2,1)S(1)} %get-tuple-element.65.rows_ref, bf16[128,1536]{1,0:T(8,128)(2,1)S(1)} %bitcast.7, f32[12,128]{1,0:T(8,128)S(1)} %bitcast.10, bf16[16,1920]{1,0:T(8,128)(2,1)S(1)} %get-tuple-element.118.refs_0_, bf16[16,1920]{1,0:T(8,128)(2,1)S(1)} %collective-permute-done.42.refs_1_, ...), custom_call_target="tpu_custom_call" | custom-call | flops 16777216 | bytes 1447936 | tf_op jit(solution)/shard_map/pallas_call | solution.py:38
  (75 shorter events, 9.6 us)
Async XLA Ops:
  2.2 4.5 %collective-permute-start = (bf16[16,1920]{1,0:T(8,128)(2,1)S(1)}, bf16[16,1920]{1,0:T(8,128)(2,1)S(1)}, u32[]{:S(2)}, u32[]{:S(2)}) collective-permute-start(bf16[16,1920]{1,0:T(8,128)(2,1)S(1)} %get-tuple-element.68), channel_id=1, source_target_pairs={{0,1},{1,0},{2,3},{3,2},{4,5},{5,4},{6,7},{7,6},{8,9},{9,8},{10,11... | collective-permute-start | bytes 184328 | tf_op jit(solution)/shard_map/ppermute | solution.py:465
  2.3 8.1 %collective-permute-start.1 = (bf16[16,1920]{1,0:T(8,128)(2,1)S(1)}, bf16[16,1920]{1,0:T(8,128)(2,1)S(1)}, u32[]{:S(2)}, u32[]{:S(2)}) collective-permute-start(bf16[16,1920]{1,0:T(8,128)(2,1)S(1)} %get-tuple-element.69), channel_id=1, source_target_pairs={{0,2},{1,3},{2,0},{3,1},{4,6},{5,7},{6,4},{7,5},{8,10},{9,11},{10,... | collective-permute-start | bytes 184328 | tf_op jit(solution)/shard_map/ppermute | solution.py:465
  3.9 11.2 %collective-permute-start.2 = (bf16[16,1920]{1,0:T(8,128)(2,1)S(1)}, bf16[16,1920]{1,0:T(8,128)(2,1)S(1)}, u32[]{:S(2)}, u32[]{:S(2)}) collective-permute-start(bf16[16,1920]{1,0:T(8,128)(2,1)S(1)} %get-tuple-element.70), channel_id=1, source_target_pairs={{0,3},{1,2},{2,1},{3,0},{4,7},{5,6},{6,5},{7,4},{8,11},{9,10},{10,... | collective-permute-start | bytes 184328 | tf_op jit(solution)/shard_map/ppermute | solution.py:465
  4.1 11.0 %collective-permute-start.3 = (bf16[16,1920]{1,0:T(8,128)(2,1)S(1)}, bf16[16,1920]{1,0:T(8,128)(2,1)S(1)}, u32[]{:S(2)}, u32[]{:S(2)}) collective-permute-start(bf16[16,1920]{1,0:T(8,128)(2,1)S(1)} %get-tuple-element.71), channel_id=1, source_target_pairs={{0,4},{1,5},{2,6},{3,7},{4,0},{5,1},{6,2},{7,3},{8,12},{9,13},{10,... | collective-permute-start | bytes 184328 | tf_op jit(solution)/shard_map/ppermute | solution.py:465
  6.7 10.1 %collective-permute-start.4 = (bf16[16,1920]{1,0:T(8,128)(2,1)S(1)}, bf16[16,1920]{1,0:T(8,128)(2,1)S(1)}, u32[]{:S(2)}, u32[]{:S(2)}) collective-permute-start(bf16[16,1920]{1,0:T(8,128)(2,1)S(1)} %get-tuple-element.72), channel_id=1, source_target_pairs={{0,5},{1,4},{2,7},{3,6},{4,1},{5,0},{6,3},{7,2},{8,13},{9,12},{10,... | collective-permute-start | bytes 184328 | tf_op jit(solution)/shard_map/ppermute | solution.py:465
  6.7 10.1 %collective-permute-start.5 = (bf16[16,1920]{1,0:T(8,128)(2,1)S(1)}, bf16[16,1920]{1,0:T(8,128)(2,1)S(1)}, u32[]{:S(2)}, u32[]{:S(2)}) collective-permute-start(bf16[16,1920]{1,0:T(8,128)(2,1)S(1)} %get-tuple-element.73), channel_id=1, source_target_pairs={{0,6},{1,7},{2,4},{3,5},{4,2},{5,3},{6,0},{7,1},{8,14},{9,15},{10,... | collective-permute-start | bytes 184328 | tf_op jit(solution)/shard_map/ppermute | solution.py:465
  10.3 6.5 %collective-permute-start.6 = (bf16[16,1920]{1,0:T(8,128)(2,1)S(1)}, bf16[16,1920]{1,0:T(8,128)(2,1)S(1)}, u32[]{:S(2)}, u32[]{:S(2)}) collective-permute-start(bf16[16,1920]{1,0:T(8,128)(2,1)S(1)} %get-tuple-element.74), channel_id=1, source_target_pairs={{0,7},{1,6},{2,5},{3,4},{4,3},{5,2},{6,1},{7,0},{8,15},{9,14},{10,... | collective-permute-start | bytes 184328 | tf_op jit(solution)/shard_map/ppermute | solution.py:465
  18.3 6.2 %collective-permute-start.14 = (bf16[16,1920]{1,0:T(8,128)(2,1)S(1)}, bf16[16,1920]{1,0:T(8,128)(2,1)S(1)}, u32[]{:S(2)}, u32[]{:S(2)}) collective-permute-start(bf16[16,1920]{1,0:T(8,128)(2,1)S(1)} %get-tuple-element.86), channel_id=1, source_target_pairs={{0,1},{1,0},{2,3},{3,2},{4,5},{5,4},{6,7},{7,6},{8,9},{9,8},{10,11... | collective-permute-start | bytes 184328 | tf_op jit(solution)/shard_map/ppermute | solution.py:465
  18.4 8.1 %collective-permute-start.15 = (bf16[16,1920]{1,0:T(8,128)(2,1)S(1)}, bf16[16,1920]{1,0:T(8,128)(2,1)S(1)}, u32[]{:S(2)}, u32[]{:S(2)}) collective-permute-start(bf16[16,1920]{1,0:T(8,128)(2,1)S(1)} %get-tuple-element.87), channel_id=1, source_target_pairs={{0,2},{1,3},{2,0},{3,1},{4,6},{5,7},{6,4},{7,5},{8,10},{9,11},{10,... | collective-permute-start | bytes 184328 | tf_op jit(solution)/shard_map/ppermute | solution.py:465
  21.6 6.2 %collective-permute-start.16 = (bf16[16,1920]{1,0:T(8,128)(2,1)S(1)}, bf16[16,1920]{1,0:T(8,128)(2,1)S(1)}, u32[]{:S(2)}, u32[]{:S(2)}) collective-permute-start(bf16[16,1920]{1,0:T(8,128)(2,1)S(1)} %get-tuple-element.88), channel_id=1, source_target_pairs={{0,3},{1,2},{2,1},{3,0},{4,7},{5,6},{6,5},{7,4},{8,11},{9,10},{10,... | collective-permute-start | bytes 184328 | tf_op jit(solution)/shard_map/ppermute | solution.py:465
  21.6 6.2 %collective-permute-start.17 = (bf16[16,1920]{1,0:T(8,128)(2,1)S(1)}, bf16[16,1920]{1,0:T(8,128)(2,1)S(1)}, u32[]{:S(2)}, u32[]{:S(2)}) collective-permute-start(bf16[16,1920]{1,0:T(8,128)(2,1)S(1)} %get-tuple-element.89), channel_id=1, source_target_pairs={{0,4},{1,5},{2,6},{3,7},{4,0},{5,1},{6,2},{7,3},{8,12},{9,13},{10,... | collective-permute-start | bytes 184328 | tf_op jit(solution)/shard_map/ppermute | solution.py:465
  24.4 9.9 %collective-permute-start.18 = (bf16[16,1920]{1,0:T(8,128)(2,1)S(1)}, bf16[16,1920]{1,0:T(8,128)(2,1)S(1)}, u32[]{:S(2)}, u32[]{:S(2)}) collective-permute-start(bf16[16,1920]{1,0:T(8,128)(2,1)S(1)} %get-tuple-element.90), channel_id=1, source_target_pairs={{0,5},{1,4},{2,7},{3,6},{4,1},{5,0},{6,3},{7,2},{8,13},{9,12},{10,... | collective-permute-start | bytes 184328 | tf_op jit(solution)/shard_map/ppermute | solution.py:465
  24.4 9.9 %collective-permute-start.19 = (bf16[16,1920]{1,0:T(8,128)(2,1)S(1)}, bf16[16,1920]{1,0:T(8,128)(2,1)S(1)}, u32[]{:S(2)}, u32[]{:S(2)}) collective-permute-start(bf16[16,1920]{1,0:T(8,128)(2,1)S(1)} %get-tuple-element.91), channel_id=1, source_target_pairs={{0,6},{1,7},{2,4},{3,5},{4,2},{5,3},{6,0},{7,1},{8,14},{9,15},{10,... | collective-permute-start | bytes 184328 | tf_op jit(solution)/shard_map/ppermute | solution.py:465
  26.5 7.7 %collective-permute-start.20 = (bf16[16,1920]{1,0:T(8,128)(2,1)S(1)}, bf16[16,1920]{1,0:T(8,128)(2,1)S(1)}, u32[]{:S(2)}, u32[]{:S(2)}) collective-permute-start(bf16[16,1920]{1,0:T(8,128)(2,1)S(1)} %get-tuple-element.92), channel_id=1, source_target_pairs={{0,7},{1,6},{2,5},{3,4},{4,3},{5,2},{6,1},{7,0},{8,15},{9,14},{10,... | collective-permute-start | bytes 184328 | tf_op jit(solution)/shard_map/ppermute | solution.py:465
  34.6 18.2 %collective-permute-start.24 = (bf16[128,768]{1,0:T(8,128)(2,1)S(1)}, bf16[128,768]{1,0:T(8,128)(2,1)S(1)}, u32[]{:S(2)}, u32[]{:S(2)}) collective-permute-start(bf16[128,768]{1,0:T(8,128)(2,1)S(1)} %get-tuple-element.94.refs_3_.key_ref), channel_id=1, source_target_pairs={{16,0},{24,8},{0,16},{8,24},{17,1},{25,9},{1,17},{9,25},{18,2},{26... | collective-permute-start | bytes 589832 | tf_op jit(solution)/shard_map/ppermute | solution.py:472
  37.6 6.7 %collective-permute-start.10 = (bf16[16,1920]{1,0:T(8,128)(2,1)S(1)}, bf16[16,1920]{1,0:T(8,128)(2,1)S(1)}, u32[]{:S(2)}, u32[]{:S(2)}) collective-permute-start(bf16[16,1920]{1,0:T(8,128)(2,1)S(1)} %get-tuple-element.79), channel_id=1, source_target_pairs={{0,4},{1,5},{2,6},{3,7},{4,0},{5,1},{6,2},{7,3},{8,12},{9,13},{10,... | collective-permute-start | bytes 184328 | tf_op jit(solution)/shard_map/ppermute | solution.py:465
  40.9 9.3 %collective-permute-start.11 = (bf16[16,1920]{1,0:T(8,128)(2,1)S(1)}, bf16[16,1920]{1,0:T(8,128)(2,1)S(1)}, u32[]{:S(2)}, u32[]{:S(2)}) collective-permute-start(bf16[16,1920]{1,0:T(8,128)(2,1)S(1)} %get-tuple-element.80), channel_id=1, source_target_pairs={{0,5},{1,4},{2,7},{3,6},{4,1},{5,0},{6,3},{7,2},{8,13},{9,12},{10,... | collective-permute-start | bytes 184328 | tf_op jit(solution)/shard_map/ppermute | solution.py:465
  40.9 9.8 %collective-permute-start.12 = (bf16[16,1920]{1,0:T(8,128)(2,1)S(1)}, bf16[16,1920]{1,0:T(8,128)(2,1)S(1)}, u32[]{:S(2)}, u32[]{:S(2)}) collective-permute-start(bf16[16,1920]{1,0:T(8,128)(2,1)S(1)} %get-tuple-element.81), channel_id=1, source_target_pairs={{0,6},{1,7},{2,4},{3,5},{4,2},{5,3},{6,0},{7,1},{8,14},{9,15},{10,... | collective-permute-start | bytes 184328 | tf_op jit(solution)/shard_map/ppermute | solution.py:465
  43.2 9.0 %collective-permute-start.13 = (bf16[16,1920]{1,0:T(8,128)(2,1)S(1)}, bf16[16,1920]{1,0:T(8,128)(2,1)S(1)}, u32[]{:S(2)}, u32[]{:S(2)}) collective-permute-start(bf16[16,1920]{1,0:T(8,128)(2,1)S(1)} %get-tuple-element.82), channel_id=1, source_target_pairs={{0,7},{1,6},{2,5},{3,4},{4,3},{5,2},{6,1},{7,0},{8,15},{9,14},{10,... | collective-permute-start | bytes 184328 | tf_op jit(solution)/shard_map/ppermute | solution.py:465
  44.3 10.0 %collective-permute-start.7 = (bf16[16,1920]{1,0:T(8,128)(2,1)S(1)}, bf16[16,1920]{1,0:T(8,128)(2,1)S(1)}, u32[]{:S(2)}, u32[]{:S(2)}) collective-permute-start(bf16[16,1920]{1,0:T(8,128)(2,1)S(1)} %get-tuple-element.76), channel_id=1, source_target_pairs={{0,1},{1,0},{2,3},{3,2},{4,5},{5,4},{6,7},{7,6},{8,9},{9,8},{10,11... | collective-permute-start | bytes 184328 | tf_op jit(solution)/shard_map/ppermute | solution.py:465
  50.2 13.4 %collective-permute-start.21 = (bf16[128,768]{1,0:T(8,128)(2,1)S(1)}, bf16[128,768]{1,0:T(8,128)(2,1)S(1)}, u32[]{:S(2)}, u32[]{:S(2)}) collective-permute-start(bf16[128,768]{1,0:T(8,128)(2,1)S(1)} %get-tuple-element.93.refs_0_.value_ref), channel_id=1, source_target_pairs={{24,0},{0,8},{8,16},{16,24},{25,1},{1,9},{9,17},{17,25},{26,2},{2,... | collective-permute-start | bytes 589832 | tf_op jit(solution)/shard_map/ppermute | solution.py:472
  50.7 12.9 %collective-permute-start.22 = (bf16[128,768]{1,0:T(8,128)(2,1)S(1)}, bf16[128,768]{1,0:T(8,128)(2,1)S(1)}, u32[]{:S(2)}, u32[]{:S(2)}) collective-permute-start(bf16[128,768]{1,0:T(8,128)(2,1)S(1)} %get-tuple-element.93.refs_0_.value_ref), channel_id=1, source_target_pairs={{16,0},{24,8},{0,16},{8,24},{17,1},{25,9},{1,17},{9,25},{18,2},{26... | collective-permute-start | bytes 589832 | tf_op jit(solution)/shard_map/ppermute | solution.py:472
  52.3 11.3 %collective-permute-start.23 = (bf16[128,768]{1,0:T(8,128)(2,1)S(1)}, bf16[128,768]{1,0:T(8,128)(2,1)S(1)}, u32[]{:S(2)}, u32[]{:S(2)}) collective-permute-start(bf16[128,768]{1,0:T(8,128)(2,1)S(1)} %get-tuple-element.94.refs_3_.key_ref), channel_id=1, source_target_pairs={{0,8},{8,0},{16,24},{24,16},{1,9},{9,1},{17,25},{25,17},{2,10},{10... | collective-permute-start | bytes 589832 | tf_op jit(solution)/shard_map/ppermute | solution.py:306
  52.8 12.8 %collective-permute-start.25 = (bf16[128,768]{1,0:T(8,128)(2,1)S(1)}, bf16[128,768]{1,0:T(8,128)(2,1)S(1)}, u32[]{:S(2)}, u32[]{:S(2)}) collective-permute-start(bf16[128,768]{1,0:T(8,128)(2,1)S(1)} %collective-permute-done.24.refs_5_), channel_id=1, source_target_pairs={{0,8},{8,0},{16,24},{24,16},{1,9},{9,1},{17,25},{25,17},{2,10},{10... | collective-permute-start | bytes 589832 | tf_op jit(solution)/shard_map/ppermute | solution.py:307
  54.3 4.2 %collective-permute-start.8 = (bf16[16,1920]{1,0:T(8,128)(2,1)S(1)}, bf16[16,1920]{1,0:T(8,128)(2,1)S(1)}, u32[]{:S(2)}, u32[]{:S(2)}) collective-permute-start(bf16[16,1920]{1,0:T(8,128)(2,1)S(1)} %get-tuple-element.77), channel_id=1, source_target_pairs={{0,2},{1,3},{2,0},{3,1},{4,6},{5,7},{6,4},{7,5},{8,10},{9,11},{10,... | collective-permute-start | bytes 184328 | tf_op jit(solution)/shard_map/ppermute | solution.py:465
  58.5 4.0 %collective-permute-start.9 = (bf16[16,1920]{1,0:T(8,128)(2,1)S(1)}, bf16[16,1920]{1,0:T(8,128)(2,1)S(1)}, u32[]{:S(2)}, u32[]{:S(2)}) collective-permute-start(bf16[16,1920]{1,0:T(8,128)(2,1)S(1)} %get-tuple-element.78), channel_id=1, source_target_pairs={{0,3},{1,2},{2,1},{3,0},{4,7},{5,6},{6,5},{7,4},{8,11},{9,10},{10,... | collective-permute-start | bytes 184328 | tf_op jit(solution)/shard_map/ppermute | solution.py:465
  62.8 11.4 %collective-permute-start.27 = (bf16[128,768]{1,0:T(8,128)(2,1)S(1)}, bf16[128,768]{1,0:T(8,128)(2,1)S(1)}, u32[]{:S(2)}, u32[]{:S(2)}) collective-permute-start(bf16[128,768]{1,0:T(8,128)(2,1)S(1)} %get-tuple-element.84.query_ref), channel_id=1, source_target_pairs={{16,0},{24,8},{0,16},{8,24},{17,1},{25,9},{1,17},{9,25},{18,2},{26... | collective-permute-start | bytes 589832 | tf_op jit(solution)/shard_map/ppermute | solution.py:472
  69.3 6.5 %collective-permute-start.38 = (bf16[32,1920]{1,0:T(8,128)(2,1)S(1)}, bf16[32,1920]{1,0:T(8,128)(2,1)S(1)}, u32[]{:S(2)}, u32[]{:S(2)}) collective-permute-start(bf16[32,1920]{1,0:T(8,128)(2,1)S(1)} %get-tuple-element.115), channel_id=1, source_target_pairs={{0,2},{1,3},{2,0},{3,1},{4,6},{5,7},{6,4},{7,5},{8,10},{9,11},{10,... | collective-permute-start | bytes 368648 | tf_op jit(solution)/shard_map/ppermute | solution.py:465
  69.4 12.0 %collective-permute-start.39 = (bf16[32,1920]{1,0:T(8,128)(2,1)S(1)}, bf16[32,1920]{1,0:T(8,128)(2,1)S(1)}, u32[]{:S(2)}, u32[]{:S(2)}) collective-permute-start(bf16[32,1920]{1,0:T(8,128)(2,1)S(1)} %get-tuple-element.116), channel_id=1, source_target_pairs={{0,4},{1,5},{2,6},{3,7},{4,0},{5,1},{6,2},{7,3},{8,12},{9,13},{10,... | collective-permute-start | bytes 368648 | tf_op jit(solution)/shard_map/ppermute | solution.py:465
  71.6 10.3 %collective-permute-start.40 = (bf16[32,1920]{1,0:T(8,128)(2,1)S(1)}, bf16[32,1920]{1,0:T(8,128)(2,1)S(1)}, u32[]{:S(2)}, u32[]{:S(2)}) collective-permute-start(bf16[32,1920]{1,0:T(8,128)(2,1)S(1)} %get-tuple-element.117), channel_id=1, source_target_pairs={{0,6},{1,7},{2,4},{3,5},{4,2},{5,3},{6,0},{7,1},{8,14},{9,15},{10,... | collective-permute-start | bytes 368648 | tf_op jit(solution)/shard_map/ppermute | solution.py:465
  73.8 8.3 %collective-permute-start.26 = (bf16[128,768]{1,0:T(8,128)(2,1)S(1)}, bf16[128,768]{1,0:T(8,128)(2,1)S(1)}, u32[]{:S(2)}, u32[]{:S(2)}) collective-permute-start(bf16[128,768]{1,0:T(8,128)(2,1)S(1)} %get-tuple-element.84.query_ref), channel_id=1, source_target_pairs={{0,8},{8,0},{16,24},{24,16},{1,9},{9,1},{17,25},{25,17},{2,10},{10... | collective-permute-start | bytes 589832 | tf_op jit(solution)/shard_map/ppermute | solution.py:315
  74.3 11.0 %collective-permute-start.28 = (bf16[128,768]{1,0:T(8,128)(2,1)S(1)}, bf16[128,768]{1,0:T(8,128)(2,1)S(1)}, u32[]{:S(2)}, u32[]{:S(2)}) collective-permute-start(bf16[128,768]{1,0:T(8,128)(2,1)S(1)} %collective-permute-done.27.refs_1_.refs_5_), channel_id=1, source_target_pairs={{0,8},{8,0},{16,24},{24,16},{1,9},{9,1},{17,25},{25,17},{2,10},{10... | collective-permute-start | bytes 589832 | tf_op jit(solution)/shard_map/ppermute | solution.py:316
  75.8 11.6 %collective-permute-start.29 = (bf16[128,768]{1,0:T(8,128)(2,1)S(1)}, bf16[128,768]{1,0:T(8,128)(2,1)S(1)}, u32[]{:S(2)}, u32[]{:S(2)}) collective-permute-start(bf16[128,768]{1,0:T(8,128)(2,1)S(1)} %get-tuple-element.99.grad_ref), channel_id=1, source_target_pairs={{8,0},{16,8},{24,16},{0,24},{9,1},{17,9},{25,17},{1,25},{10,2},{18... | collective-permute-start | bytes 589832 | tf_op jit(solution)/shard_map/ppermute | solution.py:472
  81.4 7.8 %collective-permute-start.30 = (bf16[128,768]{1,0:T(8,128)(2,1)S(1)}, bf16[128,768]{1,0:T(8,128)(2,1)S(1)}, u32[]{:S(2)}, u32[]{:S(2)}) collective-permute-start(bf16[128,768]{1,0:T(8,128)(2,1)S(1)} %get-tuple-element.99.grad_ref), channel_id=1, source_target_pairs={{16,0},{24,8},{0,16},{8,24},{17,1},{25,9},{1,17},{9,25},{18,2},{26... | collective-permute-start | bytes 589832 | tf_op jit(solution)/shard_map/ppermute | solution.py:472
  82.0 15.0 %collective-permute-start.41 = (bf16[64,1920]{1,0:T(8,128)(2,1)S(1)}, bf16[64,1920]{1,0:T(8,128)(2,1)S(1)}, u32[]{:S(2)}, u32[]{:S(2)}) collective-permute-start(bf16[64,1920]{1,0:T(8,128)(2,1)S(1)} %pad_maximum_fusion), channel_id=1, source_target_pairs={{0,1},{1,0},{2,3},{3,2},{4,5},{5,4},{6,7},{7,6},{8,9},{9,8},{10,11... | collective-permute-start | bytes 737288 | tf_op jit(solution)/shard_map/ppermute | solution.py:452
  90.3 4.9 %collective-permute-start.32 = (bf16[16,1920]{1,0:T(8,128)(2,1)S(1)}, bf16[16,1920]{1,0:T(8,128)(2,1)S(1)}, u32[]{:S(2)}, u32[]{:S(2)}) collective-permute-start(bf16[16,1920]{1,0:T(8,128)(2,1)S(1)} %get-tuple-element.106), channel_id=1, source_target_pairs={{0,2},{1,3},{2,0},{3,1},{4,6},{5,7},{6,4},{7,5},{8,10},{9,11},{10,... | collective-permute-start | bytes 184328 | tf_op jit(solution)/shard_map/ppermute | solution.py:465
  90.4 9.8 %collective-permute-start.33 = (bf16[16,1920]{1,0:T(8,128)(2,1)S(1)}, bf16[16,1920]{1,0:T(8,128)(2,1)S(1)}, u32[]{:S(2)}, u32[]{:S(2)}) collective-permute-start(bf16[16,1920]{1,0:T(8,128)(2,1)S(1)} %get-tuple-element.107), channel_id=1, source_target_pairs={{0,3},{1,2},{2,1},{3,0},{4,7},{5,6},{6,5},{7,4},{8,11},{9,10},{10,... | collective-permute-start | bytes 184328 | tf_op jit(solution)/shard_map/ppermute | solution.py:465
  92.2 9.5 %collective-permute-start.34 = (bf16[16,1920]{1,0:T(8,128)(2,1)S(1)}, bf16[16,1920]{1,0:T(8,128)(2,1)S(1)}, u32[]{:S(2)}, u32[]{:S(2)}) collective-permute-start(bf16[16,1920]{1,0:T(8,128)(2,1)S(1)} %get-tuple-element.108), channel_id=1, source_target_pairs={{0,4},{1,5},{2,6},{3,7},{4,0},{5,1},{6,2},{7,3},{8,12},{9,13},{10,... | collective-permute-start | bytes 184328 | tf_op jit(solution)/shard_map/ppermute | solution.py:465
  92.7 10.9 %collective-permute-start.35 = (bf16[16,1920]{1,0:T(8,128)(2,1)S(1)}, bf16[16,1920]{1,0:T(8,128)(2,1)S(1)}, u32[]{:S(2)}, u32[]{:S(2)}) collective-permute-start(bf16[16,1920]{1,0:T(8,128)(2,1)S(1)} %get-tuple-element.109), channel_id=1, source_target_pairs={{0,5},{1,4},{2,7},{3,6},{4,1},{5,0},{6,3},{7,2},{8,13},{9,12},{10,... | collective-permute-start | bytes 184328 | tf_op jit(solution)/shard_map/ppermute | solution.py:465
  95.3 8.3 %collective-permute-start.36 = (bf16[16,1920]{1,0:T(8,128)(2,1)S(1)}, bf16[16,1920]{1,0:T(8,128)(2,1)S(1)}, u32[]{:S(2)}, u32[]{:S(2)}) collective-permute-start(bf16[16,1920]{1,0:T(8,128)(2,1)S(1)} %get-tuple-element.110), channel_id=1, source_target_pairs={{0,6},{1,7},{2,4},{3,5},{4,2},{5,3},{6,0},{7,1},{8,14},{9,15},{10,... | collective-permute-start | bytes 184328 | tf_op jit(solution)/shard_map/ppermute | solution.py:465
  97.0 6.6 %collective-permute-start.37 = (bf16[16,1920]{1,0:T(8,128)(2,1)S(1)}, bf16[16,1920]{1,0:T(8,128)(2,1)S(1)}, u32[]{:S(2)}, u32[]{:S(2)}) collective-permute-start(bf16[16,1920]{1,0:T(8,128)(2,1)S(1)} %get-tuple-element.111), channel_id=1, source_target_pairs={{0,7},{1,6},{2,5},{3,4},{4,3},{5,2},{6,1},{7,0},{8,15},{9,14},{10,... | collective-permute-start | bytes 184328 | tf_op jit(solution)/shard_map/ppermute | solution.py:465
  105.5 5.8 %collective-permute-start.42 = (bf16[16,1920]{1,0:T(8,128)(2,1)S(1)}, bf16[16,1920]{1,0:T(8,128)(2,1)S(1)}, u32[]{:S(2)}, u32[]{:S(2)}) collective-permute-start(bf16[16,1920]{1,0:T(8,128)(2,1)S(1)} %get-tuple-element.119), channel_id=1, source_target_pairs={{0,1},{1,0},{2,3},{3,2},{4,5},{5,4},{6,7},{7,6},{8,9},{9,8},{10,11... | collective-permute-start | bytes 184328 | tf_op jit(solution)/shard_map/ppermute | solution.py:465
  106.1 7.0 %collective-permute-start.43 = (bf16[16,1920]{1,0:T(8,128)(2,1)S(1)}, bf16[16,1920]{1,0:T(8,128)(2,1)S(1)}, u32[]{:S(2)}, u32[]{:S(2)}) collective-permute-start(bf16[16,1920]{1,0:T(8,128)(2,1)S(1)} %get-tuple-element.120), channel_id=1, source_target_pairs={{0,2},{1,3},{2,0},{3,1},{4,6},{5,7},{6,4},{7,5},{8,10},{9,11},{10,... | collective-permute-start | bytes 184328 | tf_op jit(solution)/shard_map/ppermute | solution.py:465
  109.0 6.2 %collective-permute-start.44 = (bf16[16,1920]{1,0:T(8,128)(2,1)S(1)}, bf16[16,1920]{1,0:T(8,128)(2,1)S(1)}, u32[]{:S(2)}, u32[]{:S(2)}) collective-permute-start(bf16[16,1920]{1,0:T(8,128)(2,1)S(1)} %get-tuple-element.121), channel_id=1, source_target_pairs={{0,3},{1,2},{2,1},{3,0},{4,7},{5,6},{6,5},{7,4},{8,11},{9,10},{10,... | collective-permute-start | bytes 184328 | tf_op jit(solution)/shard_map/ppermute | solution.py:465
  109.0 6.2 %collective-permute-start.45 = (bf16[16,1920]{1,0:T(8,128)(2,1)S(1)}, bf16[16,1920]{1,0:T(8,128)(2,1)S(1)}, u32[]{:S(2)}, u32[]{:S(2)}) collective-permute-start(bf16[16,1920]{1,0:T(8,128)(2,1)S(1)} %get-tuple-element.122), channel_id=1, source_target_pairs={{0,4},{1,5},{2,6},{3,7},{4,0},{5,1},{6,2},{7,3},{8,12},{9,13},{10,... | collective-permute-start | bytes 184328 | tf_op jit(solution)/shard_map/ppermute | solution.py:465
  110.7 9.9 %collective-permute-start.46 = (bf16[16,1920]{1,0:T(8,128)(2,1)S(1)}, bf16[16,1920]{1,0:T(8,128)(2,1)S(1)}, u32[]{:S(2)}, u32[]{:S(2)}) collective-permute-start(bf16[16,1920]{1,0:T(8,128)(2,1)S(1)} %get-tuple-element.123), channel_id=1, source_target_pairs={{0,5},{1,4},{2,7},{3,6},{4,1},{5,0},{6,3},{7,2},{8,13},{9,12},{10,... | collective-permute-start | bytes 184328 | tf_op jit(solution)/shard_map/ppermute | solution.py:465
  111.3 9.3 %collective-permute-start.47 = (bf16[16,1920]{1,0:T(8,128)(2,1)S(1)}, bf16[16,1920]{1,0:T(8,128)(2,1)S(1)}, u32[]{:S(2)}, u32[]{:S(2)}) collective-permute-start(bf16[16,1920]{1,0:T(8,128)(2,1)S(1)} %get-tuple-element.124), channel_id=1, source_target_pairs={{0,6},{1,7},{2,4},{3,5},{4,2},{5,3},{6,0},{7,1},{8,14},{9,15},{10,... | collective-permute-start | bytes 184328 | tf_op jit(solution)/shard_map/ppermute | solution.py:465
  113.1 7.5 %collective-permute-start.48 = (bf16[16,1920]{1,0:T(8,128)(2,1)S(1)}, bf16[16,1920]{1,0:T(8,128)(2,1)S(1)}, u32[]{:S(2)}, u32[]{:S(2)}) collective-permute-start(bf16[16,1920]{1,0:T(8,128)(2,1)S(1)} %get-tuple-element.125), channel_id=1, source_target_pairs={{0,7},{1,6},{2,5},{3,4},{4,3},{5,2},{6,1},{7,0},{8,15},{9,14},{10,... | collective-permute-start | bytes 184328 | tf_op jit(solution)/shard_map/ppermute | solution.py:465
  (4 other events, 95.7 us)

commit v7 on v6

--- a/solution.py
+++ b/solution.py
@@ -265,15 +265,20 @@
         load_.wait()
 
 
-def project_kernel(count, parts, w_ref, *refs):
-    ins, outs, slope_ref = refs[:count], refs[count:-1], refs[-1]
+def project_kernel(count, parts, early, late, w_ref, *refs):
+    ins, rest, kept_ref = refs[:count], refs[count:-1], refs[-1]
+    if late:
+        _, rest[-1][...] = slope_of(rest[0][...])
+        rest = rest[1:-1]
+    outs = rest
     rows = unfold(ins)
     width = HEADS * HD
     done = []
     for i, part in enumerate(parts):
         pre = dot(rows, w_ref[:, part * width : (part + 1) * width])
         sig = sigmoid(pre)
-        slope_ref[:, i * width : (i + 1) * width] = sig * (1.0 + pre * (1.0 - sig))
+        cols = slice(i * width, (i + 1) * width)
+        kept_ref[:, cols] = pre if early else sig * (1.0 + pre * (1.0 - sig))
         done.append((pre * sig).astype(bf16))
     fold(jnp.concatenate(done, axis=1), outs)
 
@@ -325,8 +330,8 @@
 
 
 def forward_kernel(blocks, see_ref, gate_in_ref, query_ref, cotan_ref, *refs):
-    out_ref, grad_ref, gate_ref = refs[-3:]
-    values, keys = refs[:blocks], refs[blocks:-3]
+    grad_ref, normed_ref = refs[-2:]
+    values, keys = refs[:blocks], refs[blocks:-2]
     scale = HD ** (-0.5)
     see = see_ref[...]
     done = []
@@ -338,13 +343,14 @@
     mixed = jnp.concatenate(done, axis=1)
     row_scale = lax.rsqrt(jnp.mean(mixed * mixed, axis=1, keepdims=True) + eps)
     normed = mixed * row_scale
-    gate = gate_in_ref[...].astype(f32)
-    cotan = cotan_ref[...].astype(f32)
-    grad_norm = cotan * gate
-    mean = jnp.mean(grad_norm * normed, axis=1, keepdims=True)
+    grad_norm = cotan_ref[...].astype(f32) * gate_in_ref[...].astype(f32)
+    mean = row_scale * jnp.mean(grad_norm * mixed, axis=1, keepdims=True)
     grad_ref[...] = (row_scale * (grad_norm - normed * mean)).astype(bf16)
-    out_ref[...] = (gate * normed).astype(bf16)
-    gate_ref[...] = (cotan * normed).astype(bf16)
+    normed_ref[...] = normed
+
+
+def output_kernel(gate_ref, normed_ref, out_ref):
+    out_ref[...] = (gate_ref[...].astype(f32) * normed_ref[...]).astype(bf16)
 
 
 def slope_of(score):
@@ -356,7 +362,9 @@
     return [refs[i : i + count] for i in range(0, len(refs), count)]
 
 
-def query_kernel(count, total, blocks, see_ref, query_ref, grad_ref, gate_ref, slots_ref, *refs):
+def query_kernel(
+    count, total, blocks, see_ref, query_ref, grad_ref, cotan_ref, normed_ref, slots_ref, *refs
+):
     wires = wires_out(count, refs[-total:])
     values, keys = refs[:blocks], refs[blocks:-total]
     scale = HD ** (-0.5)
@@ -368,42 +376,56 @@
         _, slope = slope_of(dot_nt(query_ref[:, cols], key) * scale)
         att = dot_nt(grad_ref[:, cols], stack(values, cols, blocks))
         done.append((dot((att * slope * see).astype(bf16), key) * scale).astype(bf16))
-    parts_to_slots(slots_ref, [gate_ref[...], jnp.concatenate(done, axis=1)], wires)
+    grad_gate = (cotan_ref[...].astype(f32) * normed_ref[...]).astype(bf16)
+    parts_to_slots(slots_ref, [grad_gate, jnp.concatenate(done, axis=1)], wires)
+
+
+def joined(parts, axis):
+    return parts[0] if len(parts) == 1 else jnp.concatenate(parts, axis=axis)
 
 
 def score_kernel(blocks, seen_ref, value_ref, key_ref, query_ref, grad_ref, *refs):
-    queries, (weight_ref, slope_ref, value_sum_ref, key_sum_ref) = refs[:-4], refs[-4:]
+    far = blocks - 2
+    queries, (value_sum_ref, key_sum_ref), kept = refs[:far], refs[far : far + 2], refs[far + 2 :]
     rows = key_ref.shape[0]
     scale = HD ** (-0.5)
-    seen = seen_ref[...]
+    seen = joined([seen_ref[:, :rows]] + [seen_ref[:, 2 * rows :]] * (far > 0), 1)
     for head in range(HEADS):
-        own = query_ref[:, head_cols(head)]
-        query = jnp.concatenate([own, stack(queries, head_cols(head), blocks - 1, 1)], axis=0)
-        score = dot_nt(key_ref[:, head_cols(head)], query) * scale
+        cols = head_cols(head)
+        own, grad = query_ref[:, cols], grad_ref[:, cols]
+        query = joined([own] + [ref[:, cols] for ref in queries], 0)
+        score = dot_nt(key_ref[:, cols], query) * scale
         sig, slope = slope_of(score)
         weight = (score * sig * seen).astype(bf16)
         slope = slope * seen
-        grad = grad_ref[:, head_cols(head)]
-        att = dot_nt(value_ref[:, head_cols(head)], grad)
-        value_sum_ref[:, head_cols(head)] = dot(weight[:, :rows], grad)
-        key_sum_ref[:, head_cols(head)] = dot((att * slope[:, :rows]).astype(bf16), own)
-        weight_ref[head] = weight[:, rows:]
-        slope_ref[head] = slope[:, rows:]
-
-
-def key_kernel(count, total, blocks, value_ref, slots_ref, weight_ref, slope_ref, *refs):
-    later = blocks - 1
+        att = dot_nt(value_ref[:, cols], grad)
+        value_sum_ref[:, cols] = dot(weight[:, :rows], grad)
+        key_sum_ref[:, cols] = dot((att * slope[:, :rows]).astype(bf16), own)
+        for ref, one in zip(kept, (weight, slope)):
+            ref[head] = one[:, rows:]
+
+
+def key_kernel(count, total, blocks, seen_ref, value_ref, key_ref, slots_ref, *refs):
+    later, far = blocks - 1, blocks - 2
     value_sum_ref, key_sum_ref = refs[:2]
-    grads, queries = refs[2 : 2 + later], refs[2 + later : -total]
+    kept, refs = refs[2 : 2 + 2 * (far > 0)], refs[2 + 2 * (far > 0) :]
+    grads, queries = refs[:later], refs[later:-total]
     wires = wires_out(count, refs[-total:])
+    rows = key_ref.shape[0]
     scale = HD ** (-0.5)
+    seen = seen_ref[:, rows : 2 * rows]
     values, keys = [], []
     for head in range(HEADS):
         cols = head_cols(head)
+        query = stack(queries, cols, later, 1)
+        score = dot_nt(key_ref[:, cols], query[:rows]) * scale
+        sig, slope = slope_of(score)
+        near = ((score * sig * seen).astype(bf16), slope * seen)
+        weight, slope = [joined([one] + [ref[head] for ref in kept[i : i + 1]], 1) for i, one in enumerate(near)]
         grad = stack(grads, cols, later)
-        grad_score = (dot_nt(value_ref[:, cols], grad) * slope_ref[head]).astype(bf16)
-        value = dot(weight_ref[head], grad) + value_sum_ref[:, cols]
-        key = dot(grad_score, stack(queries, cols, later, 1)) + key_sum_ref[:, cols]
+        grad_score = (dot_nt(value_ref[:, cols], grad) * slope).astype(bf16)
+        value = dot(weight, grad) + value_sum_ref[:, cols]
+        key = dot(grad_score, query) + key_sum_ref[:, cols]
         values.append(value.astype(bf16))
         keys.append((key * scale).astype(bf16))
     parts = [jnp.concatenate(one, axis=1) for one in (values, keys)]
@@ -526,14 +548,15 @@
         [pltpu.SemaphoreType.DMA((4,))],
     )
 
-    def project(parts, merged=1):
+    def project(parts, early=False, sums=()):
         cols = len(parts) * width
-        *box, slope = call(
-            functools.partial(project_kernel, senders, parts),
-            wire(n_user * MAIN, cols, merged) + [shape((n_user * CAP, cols), f32)],
-            [w_local] + inbound,
+        box = wire(n_user * MAIN, cols)
+        *done, slope = call(
+            functools.partial(project_kernel, senders, parts, early, len(sums) > 0),
+            box + [shape((n_user * CAP, cols), f32)] * (1 + len(sums)),
+            [w_local] + inbound + list(sums),
         )
-        return exchange(box), slope
+        return exchange(done[: len(box)]), slope, *done[len(box) :]
 
     def rows_of(box, parts=2):
         outs = [shape((rows, width), bf16)] * parts
@@ -541,19 +564,19 @@
 
     if direct:
         pair_parts, query_parts = (1, 3), (0, 2)
-        pair_back, pair_slope = project(pair_parts)
-        query_back, query_slope = project(query_parts)
+        pair_back, pair_sums = project(pair_parts, early=True)
+        query_back, query_slope, pair_slope = project(query_parts, sums=[pair_sums])
         value, key = rows_of(pair_back)
         gate, query = rows_of(query_back)
     else:
-        (box,), slope = project((0,))
+        (box,), slope = project((0,))[:2]
         gate, value, query, key = [rows_of([part], 1)[0] for part in slices_of(split, box)]
     values, keys = shifted_pairs(value, key, blocks)
     queries = shifted_queries(query, blocks)
     half = shape((rows, width), bf16)
-    output, grad_own, grad_gate = call(
+    grad_own, normed = call(
         functools.partial(forward_kernel, blocks),
-        [half] * 3,
+        [half, shape((rows, width), f32)],
         [see, gate, query, cotan] + values + keys,
     )
     grads = [shifted(grad_own, -d) for d in range(1, blocks)]
@@ -565,18 +588,19 @@
     query_grad = call(
         functools.partial(query_kernel, len(boxes(2)) if direct else 1, len(boxes(2)), blocks),
         boxes(2),
-        [see, query, grad_own, grad_gate, to_slot] + values + keys,
-    )
-    each = (HEADS, rows, reach * rows)
+        [see, query, grad_own, cotan, normed, to_slot] + values + keys,
+    )
+    far = reach - 1
+    each = (HEADS, rows, far * rows)
     scores = call(
         functools.partial(score_kernel, blocks),
-        [shape(each, bf16), shape(each, f32)] + [shape((rows, width), f32)] * 2,
-        [seen, value, key, query, grad_own] + queries,
+        [shape((rows, width), f32)] * 2 + [shape(each, bf16), shape(each, f32)] * (far > 0),
+        [seen, value, key, query, grad_own] + queries[1:reach],
     )
     pair_grad = call(
         functools.partial(key_kernel, senders, len(boxes()), blocks),
         boxes(),
-        [value, to_slot, *scores] + grads + queries,
+        [seen, value, key, to_slot, *scores] + grads + queries,
     )
     term = shape((n_user * CAP, feats), f32)
     if direct:
@@ -592,6 +616,7 @@
     term_box = call(
         functools.partial(last_term_kernel, senders, last_parts), wire(n_user * MAIN, feats), last
     )
+    (output,) = call(output_kernel, [half], [gate, normed])
     term_back = exchange(term_box)
     (grad_events,) = call(
         functools.partial(leave_kernel, senders),

time: 124 us -> 120 us (0.968)
  waiting for transfers between devices: 43.1 us -> 38 us
    ppermute x1, waiting for transfers between devices: 1.95 us -> 0.01 us  [shifted_pairs(): handed = lax.ppermute(key_far, 'seq', ACROSS)]
    ppermute x38, waiting for transfers between devices: 34.9 us -> 33 us  [exchanged(): lax.ppermute(blocks[k], 'user', [(i, i ^ merged * k) for i in range(count)])]
    ppermute x1, waiting for transfers between devices: 3.18 us -> 1.88 us  [shifted_queries(): return [near, far, lax.ppermute(far, 'seq', ACROSS)]]
    pallas_call x13 -> x14, Pallas kernels: 19.5 us -> 20.5 us  [call(): pl.pallas_call(kernel, out_shape=tuple(outs), in_specs=[pl.BlockSpec(memo...]
  transfers between devices with their start and end apart: 49 -> 49, of which waited for: 14 -> 15; matrix products, arithmetic and copies ran while one was open for 1% -> 1% of each run, Pallas kernels for 11% -> 12%
where the time goes in v7:
time: 120 us; the launch traced here: 118 us
  starting transfers between devices  57.6 us (48%)
  waiting for transfers between devices  38 us (32%)
  Pallas kernels  20.5 us (17%)
    ppermute x38, starting transfers between devices, exchanged(): lax.ppermute(blocks[k], 'user', [(i, i ^ merged * k) for i in range(count)])  48.3 us
    ppermute x38, waiting for transfers between devices, exchanged(): lax.ppermute(blocks[k], 'user', [(i, i ^ merged * k) for i in range(count)])  33 us
    pallas_call x14, Pallas kernels, call(): pl.pallas_call(kernel, out_shape=tuple(outs), in_specs=[pl.BlockSpec(memo...  20.5 us
    ppermute x6, starting transfers between devices, shifted(): return lax.ppermute(block, 'seq', route)  5.17 us
    ppermute x6, waiting for transfers between devices, shifted(): return lax.ppermute(block, 'seq', route)  3.06 us
  transfers between devices with their start and end apart: 49, of which 15 were waited for; matrix products, arithmetic and copies ran while one was open for 1% of the time, Pallas kernels for 12%

profile of v7, /device:TPU:2, one launch (start us, length us, event | category | flops | bytes accessed | tf_op | source)
XLA Modules:
  0.0 117.8 jit_solution(12112728952124278439)
XLA Ops:
  0.6 1.6 %shard_map.87 = (bf16[5,128,128]{2,1,0:T(8,128)(2,1)S(1)}, bf16[16,1920]{1,0:T(8,128)(2,1)S(1)}, bf16[16,1920]{1,0:T(8,128)(2,1)S(1)}, bf16[16,1920]{1,0:T(8,128...) custom-call(bf16[128,1536]{1,0:T(8,128)(2,1)} %bitcast.6, ...), custom_call_target="tpu_custom_call" | custom-call | flops 16777216 | bytes 1055232 | tf_op jit(solution)/shard_map/pallas_call | solution.py:38
  2.3 1.6 %collective-permute-start.1 = (bf16[16,1920]{1,0:T(8,128)(2,1)S(1)}, bf16[16,1920]{1,0:T(8,128)(2,1)S(1)}, u32[]{:S(2)}, u32[]{:S(2)}) collective-permute-start(bf16[16,1920]{1,0:T(8,128)(2,1)S(1)} %get-tuple-element.68), channel_id=1, source_target_pairs={{0,2},{1,3},{2,0},{3,1},{4,6},{5,7},{6,4},{7,5},{8,10},{9,11},{10,... | collective-permute-start | bytes 184328 | tf_op jit(solution)/shard_map/ppermute | solution.py:487
  4.1 2.6 %collective-permute-start.3 = (bf16[16,1920]{1,0:T(8,128)(2,1)S(1)}, bf16[16,1920]{1,0:T(8,128)(2,1)S(1)}, u32[]{:S(2)}, u32[]{:S(2)}) collective-permute-start(bf16[16,1920]{1,0:T(8,128)(2,1)S(1)} %get-tuple-element.70), channel_id=1, source_target_pairs={{0,4},{1,5},{2,6},{3,7},{4,0},{5,1},{6,2},{7,3},{8,12},{9,13},{10,... | collective-permute-start | bytes 184328 | tf_op jit(solution)/shard_map/ppermute | solution.py:487
  6.7 3.6 %collective-permute-start.5 = (bf16[16,1920]{1,0:T(8,128)(2,1)S(1)}, bf16[16,1920]{1,0:T(8,128)(2,1)S(1)}, u32[]{:S(2)}, u32[]{:S(2)}) collective-permute-start(bf16[16,1920]{1,0:T(8,128)(2,1)S(1)} %get-tuple-element.72), channel_id=1, source_target_pairs={{0,6},{1,7},{2,4},{3,5},{4,2},{5,3},{6,0},{7,1},{8,14},{9,15},{10,... | collective-permute-start | bytes 184328 | tf_op jit(solution)/shard_map/ppermute | solution.py:487
  11.2 3.9 %shard_map.86 = (bf16[1536,3072]{1,0:T(8,128)(2,1)S(1)}, bf16[5,128,128]{2,1,0:T(8,128)(2,1)S(1)}, f32[128,384]{1,0:T(8,128)S(1)}, f32[128,384]{1,0:T(8,128)S(1)}) custom-call(bf16[1536,3072]{1,0:T(8,128)(2,1)} %bitcast.12, s32[1,136]{1,0:T(1,128)S(1)} %pad_add_fusion.small_ref), custom_call_target="tpu_custom_call" | custom-call | flops 16777216 | bytes 19431968 | tf_op jit(solution)/shard_map/pallas_call | solution.py:38
  15.1 1.7 %collective-permute-done.4.refs_5_ = bf16[16,1920]{1,0:T(8,128)(2,1)S(1)} collective-permute-done((bf16[16,1920]{1,0:T(8,128)(2,1)S(1)}, bf16[16,1920]{1,0:T(8,128)(2,1)S(1)}, u32[]{:S(2)}, u32[]{:S(2)}) %collective-permute-start.4) | collective-permute-done | bytes 61472 | tf_op jit(solution)/shard_map/ppermute | solution.py:487
  16.8 1.3 %shard_map.88 = (bf16[16,1920]{1,0:T(8,128)(2,1)S(1)}, bf16[16,1920]{1,0:T(8,128)(2,1)S(1)}, bf16[16,1920]{1,0:T(8,128)(2,1)S(1)}, bf16[16,1920]{1,0:T(8,128)(2,...) custom-call(bf16[1536,3072]{1,0:T(8,128)(2,1)S(1)} %get-tuple-elemen, ...), custom_call_target="tpu_custom_call" | custom-call | flops 16777216 | bytes 11403264 | tf_op jit(solution)/shard_map/pallas_call | solution.py:38
  18.3 3.2 %collective-permute-start.15 = (bf16[16,1920]{1,0:T(8,128)(2,1)S(1)}, bf16[16,1920]{1,0:T(8,128)(2,1)S(1)}, u32[]{:S(2)}, u32[]{:S(2)}) collective-permute-start(bf16[16,1920]{1,0:T(8,128)(2,1)S(1)} %get-tuple-element.88), channel_id=1, source_target_pairs={{0,2},{1,3},{2,0},{3,1},{4,6},{5,7},{6,4},{7,5},{8,10},{9,11},{10,... | collective-permute-start | bytes 184328 | tf_op jit(solution)/shard_map/ppermute | solution.py:487
  21.5 2.8 %collective-permute-start.17 = (bf16[16,1920]{1,0:T(8,128)(2,1)S(1)}, bf16[16,1920]{1,0:T(8,128)(2,1)S(1)}, u32[]{:S(2)}, u32[]{:S(2)}) collective-permute-start(bf16[16,1920]{1,0:T(8,128)(2,1)S(1)} %get-tuple-element.90), channel_id=1, source_target_pairs={{0,4},{1,5},{2,6},{3,7},{4,0},{5,1},{6,2},{7,3},{8,12},{9,13},{10,... | collective-permute-start | bytes 184328 | tf_op jit(solution)/shard_map/ppermute | solution.py:487
  24.2 2.1 %collective-permute-start.19 = (bf16[16,1920]{1,0:T(8,128)(2,1)S(1)}, bf16[16,1920]{1,0:T(8,128)(2,1)S(1)}, u32[]{:S(2)}, u32[]{:S(2)}) collective-permute-start(bf16[16,1920]{1,0:T(8,128)(2,1)S(1)} %get-tuple-element.92), channel_id=1, source_target_pairs={{0,6},{1,7},{2,4},{3,5},{4,2},{5,3},{6,0},{7,1},{8,14},{9,15},{10,... | collective-permute-start | bytes 184328 | tf_op jit(solution)/shard_map/ppermute | solution.py:487
  26.4 1.3 %collective-permute-start.20 = (bf16[16,1920]{1,0:T(8,128)(2,1)S(1)}, bf16[16,1920]{1,0:T(8,128)(2,1)S(1)}, u32[]{:S(2)}, u32[]{:S(2)}) collective-permute-start(bf16[16,1920]{1,0:T(8,128)(2,1)S(1)} %get-tuple-element.93), channel_id=1, source_target_pairs={{0,7},{1,6},{2,5},{3,4},{4,3},{5,2},{6,1},{7,0},{8,15},{9,14},{10,... | collective-permute-start | bytes 184328 | tf_op jit(solution)/shard_map/ppermute | solution.py:487
  27.7 6.4 %collective-permute-done.18.refs_5_ = bf16[16,1920]{1,0:T(8,128)(2,1)S(1)} collective-permute-done((bf16[16,1920]{1,0:T(8,128)(2,1)S(1)}, bf16[16,1920]{1,0:T(8,128)(2,1)S(1)}, u32[]{:S(2)}, u32[]{:S(2)}) %collective-permute-start.18) | collective-permute-done | bytes 61472 | tf_op jit(solution)/shard_map/ppermute | solution.py:487
  34.4 1.6 %collective-permute-start.24 = (bf16[128,768]{1,0:T(8,128)(2,1)S(1)}, bf16[128,768]{1,0:T(8,128)(2,1)S(1)}, u32[]{:S(2)}, u32[]{:S(2)}) collective-permute-start(bf16[128,768]{1,0:T(8,128)(2,1)S(1)} %get-tuple-element.95.refs_3_.key_ref), channel_id=1, source_target_pairs={{16,0},{24,8},{0,16},{8,24},{17,1},{25,9},{1,17},{9,25},{18,2},{26... | collective-permute-start | bytes 589832 | tf_op jit(solution)/shard_map/ppermute | solution.py:494
  36.0 1.8 %shard_map.89 = (bf16[16,1920]{1,0:T(8,128)(2,1)S(1)}, bf16[16,1920]{1,0:T(8,128)(2,1)S(1)}, bf16[16,1920]{1,0:T(8,128)(2,1)S(1)}, bf16[16,1920]{1,0:T(8,128)(2,...) custom-call(bf16[1536,3072]{1,0:T(8,128)(2,1)S(1)} %get-tuple-elemen, ...), custom_call_target="tpu_custom_call" | custom-call | flops 16777216 | bytes 13369344 | tf_op jit(solution)/shard_map/pallas_call | solution.py:38
  37.9 3.3 %collective-permute-start.8 = (bf16[16,1920]{1,0:T(8,128)(2,1)S(1)}, bf16[16,1920]{1,0:T(8,128)(2,1)S(1)}, u32[]{:S(2)}, u32[]{:S(2)}) collective-permute-start(bf16[16,1920]{1,0:T(8,128)(2,1)S(1)} %get-tuple-element.77), channel_id=1, source_target_pairs={{0,2},{1,3},{2,0},{3,1},{4,6},{5,7},{6,4},{7,5},{8,10},{9,11},{10,... | collective-permute-start | bytes 184328 | tf_op jit(solution)/shard_map/ppermute | solution.py:487
  41.2 1.8 %collective-permute-start.10 = (bf16[16,1920]{1,0:T(8,128)(2,1)S(1)}, bf16[16,1920]{1,0:T(8,128)(2,1)S(1)}, u32[]{:S(2)}, u32[]{:S(2)}) collective-permute-start(bf16[16,1920]{1,0:T(8,128)(2,1)S(1)} %get-tuple-element.79), channel_id=1, source_target_pairs={{0,4},{1,5},{2,6},{3,7},{4,0},{5,1},{6,2},{7,3},{8,12},{9,13},{10,... | collective-permute-start | bytes 184328 | tf_op jit(solution)/shard_map/ppermute | solution.py:487
  44.3 2.2 %collective-permute-done.9.refs_3_ = bf16[16,1920]{1,0:T(8,128)(2,1)S(1)} collective-permute-done((bf16[16,1920]{1,0:T(8,128)(2,1)S(1)}, bf16[16,1920]{1,0:T(8,128)(2,1)S(1)}, u32[]{:S(2)}, u32[]{:S(2)}) %collective-permute-start.9) | collective-permute-done | bytes 61472 | tf_op jit(solution)/shard_map/ppermute | solution.py:487
  47.0 1.5 %collective-permute-start.23 = (bf16[128,768]{1,0:T(8,128)(2,1)S(1)}, bf16[128,768]{1,0:T(8,128)(2,1)S(1)}, u32[]{:S(2)}, u32[]{:S(2)}) collective-permute-start(bf16[128,768]{1,0:T(8,128)(2,1)S(1)} %get-tuple-element.95.refs_3_.key_ref), channel_id=1, source_target_pairs={{0,8},{8,0},{16,24},{24,16},{1,9},{9,1},{17,25},{25,17},{2,10},{10... | collective-permute-start | bytes 589832 | tf_op jit(solution)/shard_map/ppermute | solution.py:311
  49.0 1.3 %collective-permute-done.11.refs_5_ = bf16[16,1920]{1,0:T(8,128)(2,1)S(1)} collective-permute-done((bf16[16,1920]{1,0:T(8,128)(2,1)S(1)}, bf16[16,1920]{1,0:T(8,128)(2,1)S(1)}, u32[]{:S(2)}, u32[]{:S(2)}) %collective-permute-start.11) | collective-permute-done | bytes 61472 | tf_op jit(solution)/shard_map/ppermute | solution.py:487
  50.3 2.3 %collective-permute-start.12 = (bf16[16,1920]{1,0:T(8,128)(2,1)S(1)}, bf16[16,1920]{1,0:T(8,128)(2,1)S(1)}, u32[]{:S(2)}, u32[]{:S(2)}) collective-permute-start(bf16[16,1920]{1,0:T(8,128)(2,1)S(1)} %get-tuple-element.81), channel_id=1, source_target_pairs={{0,6},{1,7},{2,4},{3,5},{4,2},{5,3},{6,0},{7,1},{8,14},{9,15},{10,... | collective-permute-start | bytes 184328 | tf_op jit(solution)/shard_map/ppermute | solution.py:487
  52.6 3.7 %collective-permute-done.12.refs_6_ = bf16[16,1920]{1,0:T(8,128)(2,1)S(1)} collective-permute-done((bf16[16,1920]{1,0:T(8,128)(2,1)S(1)}, bf16[16,1920]{1,0:T(8,128)(2,1)S(1)}, u32[]{:S(2)}, u32[]{:S(2)}) %collective-permute-start.12) | collective-permute-done | bytes 61472 | tf_op jit(solution)/shard_map/ppermute | solution.py:487
  56.3 0.8 collective-permute-start.13
  57.1 4.6 %collective-permute-done.13.refs_7_ = bf16[16,1920]{1,0:T(8,128)(2,1)S(1)} collective-permute-done((bf16[16,1920]{1,0:T(8,128)(2,1)S(1)}, bf16[16,1920]{1,0:T(8,128)(2,1)S(1)}, u32[]{:S(2)}, u32[]{:S(2)}) %collective-permute-start.13) | collective-permute-done | bytes 61472 | tf_op jit(solution)/shard_map/ppermute | solution.py:487
  62.7 1.4 %shard_map.92 = (bf16[128,768]{1,0:T(8,128)(2,1)S(1)}, f32[128,768]{1,0:T(8,128)S(1)}) custom-call(f32[128,384]{1,0:T(8,128)S(1)} %get-tuple-element.84.see_ref, bf16[128,768]{1,0:T(8,128)(2,1)S(1)} %get-tuple-element.83.gate_in_ref.gate_ref, bf16[128,768]{1,0:T(8,128)(2,1)S(1)} %get-tuple-element.85.query_ref, bf16[128,768]{1,0:T(8,128)(2,1)S(1)} %bitcast.8, ...), custom_call_target="tpu_custom_call" | custom-call | flops 16777216 | bytes 2752512 | tf_op jit(solution)/shard_map/pallas_call | solution.py:38
  64.0 1.7 %shard_map.96 = (bf16[32,1920]{1,0:T(8,128)(2,1)S(1)}, bf16[32,1920]{1,0:T(8,128)(2,1)S(1)}, bf16[32,1920]{1,0:T(8,128)(2,1)S(1)}, bf16[32,1920]{1,0:T(8,128)(2,1)S(1)}) custom-call(f32[128,384]{1,0:T(8,128)S(1)} %get-tuple-element.84.see_ref, bf16[128,768]{1,0:T(8,128)(2,1)S(1)} %get-tuple-element.85.query_ref, ...), custom_call_target="tpu_custom_call" | custom-call | flops 16777216 | bytes 3211264 | tf_op jit(solution)/shard_map/pallas_call | solution.py:38
  65.8 2.8 %collective-permute-start.39 = (bf16[32,1920]{1,0:T(8,128)(2,1)S(1)}, bf16[32,1920]{1,0:T(8,128)(2,1)S(1)}, u32[]{:S(2)}, u32[]{:S(2)}) collective-permute-start(bf16[32,1920]{1,0:T(8,128)(2,1)S(1)} %get-tuple-element.116), channel_id=1, source_target_pairs={{0,4},{1,5},{2,6},{3,7},{4,0},{5,1},{6,2},{7,3},{8,12},{9,13},{10,... | collective-permute-start | bytes 368648 | tf_op jit(solution)/shard_map/ppermute | solution.py:487
  68.6 1.6 %collective-permute-start.40 = (bf16[32,1920]{1,0:T(8,128)(2,1)S(1)}, bf16[32,1920]{1,0:T(8,128)(2,1)S(1)}, u32[]{:S(2)}, u32[]{:S(2)}) collective-permute-start(bf16[32,1920]{1,0:T(8,128)(2,1)S(1)} %get-tuple-element.117), channel_id=1, source_target_pairs={{0,6},{1,7},{2,4},{3,5},{4,2},{5,3},{6,0},{7,1},{8,14},{9,15},{10,... | collective-permute-start | bytes 368648 | tf_op jit(solution)/shard_map/ppermute | solution.py:487
  70.7 1.5 %collective-permute-start.30 = (bf16[128,768]{1,0:T(8,128)(2,1)S(1)}, bf16[128,768]{1,0:T(8,128)(2,1)S(1)}, u32[]{:S(2)}, u32[]{:S(2)}) collective-permute-start(bf16[128,768]{1,0:T(8,128)(2,1)S(1)} %collective-permute-done.26.refs_0_.refs_7_), channel_id=1, source_target_pairs={{0,8},{8,0},{16,24},{24,16},{1,9},{9,1},{17,25},{25,17},{2,10},{10... | collective-permute-start | bytes 589832 | tf_op jit(solution)/shard_map/ppermute | solution.py:321
  72.2 1.6 %collective-permute-start.28 = (bf16[128,768]{1,0:T(8,128)(2,1)S(1)}, bf16[128,768]{1,0:T(8,128)(2,1)S(1)}, u32[]{:S(2)}, u32[]{:S(2)}) collective-permute-start(bf16[128,768]{1,0:T(8,128)(2,1)S(1)} %get-tuple-element.100.grad_ref), channel_id=1, source_target_pairs={{16,0},{24,8},{0,16},{8,24},{17,1},{25,9},{1,17},{9,25},{18,2},{26... | collective-permute-start | bytes 589832 | tf_op jit(solution)/shard_map/ppermute | solution.py:494
  73.8 3.6 %collective-permute-done.39.refs_2_ = bf16[32,1920]{1,0:T(8,128)(2,1)S(1)} collective-permute-done((bf16[32,1920]{1,0:T(8,128)(2,1)S(1)}, bf16[32,1920]{1,0:T(8,128)(2,1)S(1)}, u32[]{:S(2)}, u32[]{:S(2)}) %collective-permute-start.39) | collective-permute-done | bytes 122912 | tf_op jit(solution)/shard_map/ppermute | solution.py:487
  78.0 1.3 %shard_map.94 = (f32[128,768]{1,0:T(8,128)S(1)}, f32[128,768]{1,0:T(8,128)S(1)}, bf16[6,128,128]{2,1,0:T(8,128)(2,1)S(1)}, f32[6,128,128]{2,1,0:T(8,128)S(1)}) custom-call(f32[128,384]{1,0:T(8,128)S(1)} %get-tuple-element.98.seen_ref, bf16[128,768]{1,0:T(8,128)(2,1)S(1)} %get-tuple-element.94.refs_0_.value_ref, ...), custom_call_target="tpu_custom_call" | custom-call | flops 16777216 | bytes 2555904 | tf_op jit(solution)/shard_map/pallas_call | solution.py:38
  79.2 1.9 %collective-permute-done.30.refs_8_ = bf16[128,768]{1,0:T(8,128)(2,1)S(1)} collective-permute-done((bf16[128,768]{1,0:T(8,128)(2,1)S(1)}, bf16[128,768]{1,0:T(8,128)(2,1)S(1)}, u32[]{:S(2)}, u32[]{:S(2)}) %collective-permute-start.30) | collective-permute-done | bytes 196640 | tf_op jit(solution)/shard_map/ppermute | solution.py:321
  81.1 3.1 %collective-permute-done.27.refs_4_ = bf16[128,768]{1,0:T(8,128)(2,1)S(1)} collective-permute-done((bf16[128,768]{1,0:T(8,128)(2,1)S(1)}, bf16[128,768]{1,0:T(8,128)(2,1)S(1)}, u32[]{:S(2)}, u32[]{:S(2)}) %collective-permute-start.27) | collective-permute-done | bytes 196640 | tf_op jit(solution)/shard_map/ppermute | solution.py:494
  84.2 1.4 %shard_map.95 = (bf16[16,1920]{1,0:T(8,128)(2,1)S(1)}, bf16[16,1920]{1,0:T(8,128)(2,1)S(1)}, bf16[16,1920]{1,0:T(8,128)(2,1)S(1)}, bf16[16,1920]{1,0:T(8,128)(2,...) custom-call(f32[128,384]{1,0:T(8,128)S(1)} %get-tuple-element.98.see, ...), custom_call_target="tpu_custom_call" | custom-call | flops 16777216 | bytes 3604480 | tf_op jit(solution)/shard_map/pallas_call | solution.py:38
  85.8 1.8 %collective-permute-start.33 = (bf16[16,1920]{1,0:T(8,128)(2,1)S(1)}, bf16[16,1920]{1,0:T(8,128)(2,1)S(1)}, u32[]{:S(2)}, u32[]{:S(2)}) collective-permute-start(bf16[16,1920]{1,0:T(8,128)(2,1)S(1)} %get-tuple-element.108), channel_id=1, source_target_pairs={{0,3},{1,2},{2,1},{3,0},{4,7},{5,6},{6,5},{7,4},{8,11},{9,10},{10,... | collective-permute-start | bytes 184328 | tf_op jit(solution)/shard_map/ppermute | solution.py:487
  87.5 1.1 collective-permute-start.34
  88.6 1.5 %collective-permute-start.35 = (bf16[16,1920]{1,0:T(8,128)(2,1)S(1)}, bf16[16,1920]{1,0:T(8,128)(2,1)S(1)}, u32[]{:S(2)}, u32[]{:S(2)}) collective-permute-start(bf16[16,1920]{1,0:T(8,128)(2,1)S(1)} %get-tuple-element.110), channel_id=1, source_target_pairs={{0,5},{1,4},{2,7},{3,6},{4,1},{5,0},{6,3},{7,2},{8,13},{9,12},{10,... | collective-permute-start | bytes 184328 | tf_op jit(solution)/shard_map/ppermute | solution.py:487
  90.6 2.3 %collective-permute-start.36 = (bf16[16,1920]{1,0:T(8,128)(2,1)S(1)}, bf16[16,1920]{1,0:T(8,128)(2,1)S(1)}, u32[]{:S(2)}, u32[]{:S(2)}) collective-permute-start(bf16[16,1920]{1,0:T(8,128)(2,1)S(1)} %get-tuple-element.111), channel_id=1, source_target_pairs={{0,6},{1,7},{2,4},{3,5},{4,2},{5,3},{6,0},{7,1},{8,14},{9,15},{10,... | collective-permute-start | bytes 184328 | tf_op jit(solution)/shard_map/ppermute | solution.py:487
  93.7 1.8 %shard_map.97.refs_8_ = f32[160,1536]{1,0:T(8,128)S(1)} custom-call(f32[160,1536]{1,0:T(8,128)S(1)} %get-tuple-element.113.slope_ref, bf16[1536,3072]{1,0:T(8,128)(2,1)S(1)} %get-tuple-element.65.w_ref, bf16[32,1920]{1,0:T(8,128)(2,1)S(1)} %get-tuple-element.114.refs_0_, bf16[32,1920]{1,0:T(8,128)(2,1)S(1)} %collective-permute-done.38.refs_1_, ...), custom_call_target="tpu_custom_call" | custom-call | flops 16777216 | bytes 12140544 | tf_op jit(solution)/shard_map/pallas_call | solution.py:38
  95.5 1.6 %collective-permute-done.34.refs_4_ = bf16[16,1920]{1,0:T(8,128)(2,1)S(1)} collective-permute-done((bf16[16,1920]{1,0:T(8,128)(2,1)S(1)}, bf16[16,1920]{1,0:T(8,128)(2,1)S(1)}, u32[]{:S(2)}, u32[]{:S(2)}) %collective-permute-start.34) | collective-permute-done | bytes 61472 | tf_op jit(solution)/shard_map/ppermute | solution.py:487
  97.5 1.4 %collective-permute-done.37.refs_7_ = bf16[16,1920]{1,0:T(8,128)(2,1)S(1)} collective-permute-done((bf16[16,1920]{1,0:T(8,128)(2,1)S(1)}, bf16[16,1920]{1,0:T(8,128)(2,1)S(1)}, u32[]{:S(2)}, u32[]{:S(2)}) %collective-permute-start.37) | collective-permute-done | bytes 61472 | tf_op jit(solution)/shard_map/ppermute | solution.py:487
  99.0 1.9 %shard_map.98 = (bf16[16,1920]{1,0:T(8,128)(2,1)S(1)}, bf16[16,1920]{1,0:T(8,128)(2,1)S(1)}, bf16[16,1920]{1,0:T(8,128)(2,1)S(1)}, bf16[16,1920]{1,0:T(8,128)(2,...) custom-call(f32[160,1536]{1,0:T(8,128)S(1)} %get-tuple-element.97.sl, ...), custom_call_target="tpu_custom_call" | custom-call | flops 16777216 | bytes 12386304 | tf_op jit(solution)/shard_map/pallas_call | solution.py:38
  101.6 2.8 %collective-permute-start.43 = (bf16[16,1920]{1,0:T(8,128)(2,1)S(1)}, bf16[16,1920]{1,0:T(8,128)(2,1)S(1)}, u32[]{:S(2)}, u32[]{:S(2)}) collective-permute-start(bf16[16,1920]{1,0:T(8,128)(2,1)S(1)} %get-tuple-element.120), channel_id=1, source_target_pairs={{0,2},{1,3},{2,0},{3,1},{4,6},{5,7},{6,4},{7,5},{8,10},{9,11},{10,... | collective-permute-start | bytes 184328 | tf_op jit(solution)/shard_map/ppermute | solution.py:487
  104.3 2.5 %collective-permute-start.45 = (bf16[16,1920]{1,0:T(8,128)(2,1)S(1)}, bf16[16,1920]{1,0:T(8,128)(2,1)S(1)}, u32[]{:S(2)}, u32[]{:S(2)}) collective-permute-start(bf16[16,1920]{1,0:T(8,128)(2,1)S(1)} %get-tuple-element.122), channel_id=1, source_target_pairs={{0,4},{1,5},{2,6},{3,7},{4,0},{5,1},{6,2},{7,3},{8,12},{9,13},{10,... | collective-permute-start | bytes 184328 | tf_op jit(solution)/shard_map/ppermute | solution.py:487
  106.8 2.1 %collective-permute-start.47 = (bf16[16,1920]{1,0:T(8,128)(2,1)S(1)}, bf16[16,1920]{1,0:T(8,128)(2,1)S(1)}, u32[]{:S(2)}, u32[]{:S(2)}) collective-permute-start(bf16[16,1920]{1,0:T(8,128)(2,1)S(1)} %get-tuple-element.124), channel_id=1, source_target_pairs={{0,6},{1,7},{2,4},{3,5},{4,2},{5,3},{6,0},{7,1},{8,14},{9,15},{10,... | collective-permute-start | bytes 184328 | tf_op jit(solution)/shard_map/ppermute | solution.py:487
  108.9 1.6 %collective-permute-start.48 = (bf16[16,1920]{1,0:T(8,128)(2,1)S(1)}, bf16[16,1920]{1,0:T(8,128)(2,1)S(1)}, u32[]{:S(2)}, u32[]{:S(2)}) collective-permute-start(bf16[16,1920]{1,0:T(8,128)(2,1)S(1)} %get-tuple-element.125), channel_id=1, source_target_pairs={{0,7},{1,6},{2,5},{3,4},{4,3},{5,2},{6,1},{7,0},{8,15},{9,14},{10,... | collective-permute-start | bytes 184328 | tf_op jit(solution)/shard_map/ppermute | solution.py:487
  111.2 5.3 %collective-permute-done.46.refs_5_ = bf16[16,1920]{1,0:T(8,128)(2,1)S(1)} collective-permute-done((bf16[16,1920]{1,0:T(8,128)(2,1)S(1)}, bf16[16,1920]{1,0:T(8,128)(2,1)S(1)}, u32[]{:S(2)}, u32[]{:S(2)}) %collective-permute-start.46) | collective-permute-done | bytes 61472 | tf_op jit(solution)/shard_map/ppermute | solution.py:487
  116.6 1.2 %shard_map.99 = bf16[128,1536]{1,0:T(8,128)(2,1)} custom-call(bf16[5,128,128]{2,1,0:T(8,128)(2,1)S(1)} %get-tuple-element.64.rows_ref, bf16[128,1536]{1,0:T(8,128)(2,1)S(1)} %bitcast.7, f32[12,128]{1,0:T(8,128)S(1)} %bitcast.11, bf16[16,1920]{1,0:T(8,128)(2,1)S(1)} %get-tuple-element.118.refs_0_, bf16[16,1920]{1,0:T(8,128)(2,1)S(1)} %collective-permute-done.42.refs_1_, ...), custom_call_target="tpu_custom_call" | custom-call | flops 16777216 | bytes 1447936 | tf_op jit(solution)/shard_map/pallas_call | solution.py:38
  (76 shorter events, 9.4 us)
Async XLA Ops:
  2.2 4.5 %collective-permute-start = (bf16[16,1920]{1,0:T(8,128)(2,1)S(1)}, bf16[16,1920]{1,0:T(8,128)(2,1)S(1)}, u32[]{:S(2)}, u32[]{:S(2)}) collective-permute-start(bf16[16,1920]{1,0:T(8,128)(2,1)S(1)} %get-tuple-element.67), channel_id=1, source_target_pairs={{0,1},{1,0},{2,3},{3,2},{4,5},{5,4},{6,7},{7,6},{8,9},{9,8},{10,11... | collective-permute-start | bytes 184328 | tf_op jit(solution)/shard_map/ppermute | solution.py:487
  2.3 8.1 %collective-permute-start.1 = (bf16[16,1920]{1,0:T(8,128)(2,1)S(1)}, bf16[16,1920]{1,0:T(8,128)(2,1)S(1)}, u32[]{:S(2)}, u32[]{:S(2)}) collective-permute-start(bf16[16,1920]{1,0:T(8,128)(2,1)S(1)} %get-tuple-element.68), channel_id=1, source_target_pairs={{0,2},{1,3},{2,0},{3,1},{4,6},{5,7},{6,4},{7,5},{8,10},{9,11},{10,... | collective-permute-start | bytes 184328 | tf_op jit(solution)/shard_map/ppermute | solution.py:487
  3.9 11.2 %collective-permute-start.2 = (bf16[16,1920]{1,0:T(8,128)(2,1)S(1)}, bf16[16,1920]{1,0:T(8,128)(2,1)S(1)}, u32[]{:S(2)}, u32[]{:S(2)}) collective-permute-start(bf16[16,1920]{1,0:T(8,128)(2,1)S(1)} %get-tuple-element.69), channel_id=1, source_target_pairs={{0,3},{1,2},{2,1},{3,0},{4,7},{5,6},{6,5},{7,4},{8,11},{9,10},{10,... | collective-permute-start | bytes 184328 | tf_op jit(solution)/shard_map/ppermute | solution.py:487
  4.1 11.0 %collective-permute-start.3 = (bf16[16,1920]{1,0:T(8,128)(2,1)S(1)}, bf16[16,1920]{1,0:T(8,128)(2,1)S(1)}, u32[]{:S(2)}, u32[]{:S(2)}) collective-permute-start(bf16[16,1920]{1,0:T(8,128)(2,1)S(1)} %get-tuple-element.70), channel_id=1, source_target_pairs={{0,4},{1,5},{2,6},{3,7},{4,0},{5,1},{6,2},{7,3},{8,12},{9,13},{10,... | collective-permute-start | bytes 184328 | tf_op jit(solution)/shard_map/ppermute | solution.py:487
  6.7 10.1 %collective-permute-start.4 = (bf16[16,1920]{1,0:T(8,128)(2,1)S(1)}, bf16[16,1920]{1,0:T(8,128)(2,1)S(1)}, u32[]{:S(2)}, u32[]{:S(2)}) collective-permute-start(bf16[16,1920]{1,0:T(8,128)(2,1)S(1)} %get-tuple-element.71), channel_id=1, source_target_pairs={{0,5},{1,4},{2,7},{3,6},{4,1},{5,0},{6,3},{7,2},{8,13},{9,12},{10,... | collective-permute-start | bytes 184328 | tf_op jit(solution)/shard_map/ppermute | solution.py:487
  6.7 10.1 %collective-permute-start.5 = (bf16[16,1920]{1,0:T(8,128)(2,1)S(1)}, bf16[16,1920]{1,0:T(8,128)(2,1)S(1)}, u32[]{:S(2)}, u32[]{:S(2)}) collective-permute-start(bf16[16,1920]{1,0:T(8,128)(2,1)S(1)} %get-tuple-element.72), channel_id=1, source_target_pairs={{0,6},{1,7},{2,4},{3,5},{4,2},{5,3},{6,0},{7,1},{8,14},{9,15},{10,... | collective-permute-start | bytes 184328 | tf_op jit(solution)/shard_map/ppermute | solution.py:487
  10.3 6.5 %collective-permute-start.6 = (bf16[16,1920]{1,0:T(8,128)(2,1)S(1)}, bf16[16,1920]{1,0:T(8,128)(2,1)S(1)}, u32[]{:S(2)}, u32[]{:S(2)}) collective-permute-start(bf16[16,1920]{1,0:T(8,128)(2,1)S(1)} %get-tuple-element.73), channel_id=1, source_target_pairs={{0,7},{1,6},{2,5},{3,4},{4,3},{5,2},{6,1},{7,0},{8,15},{9,14},{10,... | collective-permute-start | bytes 184328 | tf_op jit(solution)/shard_map/ppermute | solution.py:487
  18.1 6.1 %collective-permute-start.14 = (bf16[16,1920]{1,0:T(8,128)(2,1)S(1)}, bf16[16,1920]{1,0:T(8,128)(2,1)S(1)}, u32[]{:S(2)}, u32[]{:S(2)}) collective-permute-start(bf16[16,1920]{1,0:T(8,128)(2,1)S(1)} %get-tuple-element.87), channel_id=1, source_target_pairs={{0,1},{1,0},{2,3},{3,2},{4,5},{5,4},{6,7},{7,6},{8,9},{9,8},{10,11... | collective-permute-start | bytes 184328 | tf_op jit(solution)/shard_map/ppermute | solution.py:487
  18.3 8.1 %collective-permute-start.15 = (bf16[16,1920]{1,0:T(8,128)(2,1)S(1)}, bf16[16,1920]{1,0:T(8,128)(2,1)S(1)}, u32[]{:S(2)}, u32[]{:S(2)}) collective-permute-start(bf16[16,1920]{1,0:T(8,128)(2,1)S(1)} %get-tuple-element.88), channel_id=1, source_target_pairs={{0,2},{1,3},{2,0},{3,1},{4,6},{5,7},{6,4},{7,5},{8,10},{9,11},{10,... | collective-permute-start | bytes 184328 | tf_op jit(solution)/shard_map/ppermute | solution.py:487
  21.5 6.2 %collective-permute-start.16 = (bf16[16,1920]{1,0:T(8,128)(2,1)S(1)}, bf16[16,1920]{1,0:T(8,128)(2,1)S(1)}, u32[]{:S(2)}, u32[]{:S(2)}) collective-permute-start(bf16[16,1920]{1,0:T(8,128)(2,1)S(1)} %get-tuple-element.89), channel_id=1, source_target_pairs={{0,3},{1,2},{2,1},{3,0},{4,7},{5,6},{6,5},{7,4},{8,11},{9,10},{10,... | collective-permute-start | bytes 184328 | tf_op jit(solution)/shard_map/ppermute | solution.py:487
  21.5 6.2 %collective-permute-start.17 = (bf16[16,1920]{1,0:T(8,128)(2,1)S(1)}, bf16[16,1920]{1,0:T(8,128)(2,1)S(1)}, u32[]{:S(2)}, u32[]{:S(2)}) collective-permute-start(bf16[16,1920]{1,0:T(8,128)(2,1)S(1)} %get-tuple-element.90), channel_id=1, source_target_pairs={{0,4},{1,5},{2,6},{3,7},{4,0},{5,1},{6,2},{7,3},{8,12},{9,13},{10,... | collective-permute-start | bytes 184328 | tf_op jit(solution)/shard_map/ppermute | solution.py:487
  24.2 9.9 %collective-permute-start.18 = (bf16[16,1920]{1,0:T(8,128)(2,1)S(1)}, bf16[16,1920]{1,0:T(8,128)(2,1)S(1)}, u32[]{:S(2)}, u32[]{:S(2)}) collective-permute-start(bf16[16,1920]{1,0:T(8,128)(2,1)S(1)} %get-tuple-element.91), channel_id=1, source_target_pairs={{0,5},{1,4},{2,7},{3,6},{4,1},{5,0},{6,3},{7,2},{8,13},{9,12},{10,... | collective-permute-start | bytes 184328 | tf_op jit(solution)/shard_map/ppermute | solution.py:487
  24.2 9.9 %collective-permute-start.19 = (bf16[16,1920]{1,0:T(8,128)(2,1)S(1)}, bf16[16,1920]{1,0:T(8,128)(2,1)S(1)}, u32[]{:S(2)}, u32[]{:S(2)}) collective-permute-start(bf16[16,1920]{1,0:T(8,128)(2,1)S(1)} %get-tuple-element.92), channel_id=1, source_target_pairs={{0,6},{1,7},{2,4},{3,5},{4,2},{5,3},{6,0},{7,1},{8,14},{9,15},{10,... | collective-permute-start | bytes 184328 | tf_op jit(solution)/shard_map/ppermute | solution.py:487
  26.4 7.7 %collective-permute-start.20 = (bf16[16,1920]{1,0:T(8,128)(2,1)S(1)}, bf16[16,1920]{1,0:T(8,128)(2,1)S(1)}, u32[]{:S(2)}, u32[]{:S(2)}) collective-permute-start(bf16[16,1920]{1,0:T(8,128)(2,1)S(1)} %get-tuple-element.93), channel_id=1, source_target_pairs={{0,7},{1,6},{2,5},{3,4},{4,3},{5,2},{6,1},{7,0},{8,15},{9,14},{10,... | collective-permute-start | bytes 184328 | tf_op jit(solution)/shard_map/ppermute | solution.py:487
  34.4 14.1 %collective-permute-start.24 = (bf16[128,768]{1,0:T(8,128)(2,1)S(1)}, bf16[128,768]{1,0:T(8,128)(2,1)S(1)}, u32[]{:S(2)}, u32[]{:S(2)}) collective-permute-start(bf16[128,768]{1,0:T(8,128)(2,1)S(1)} %get-tuple-element.95.refs_3_.key_ref), channel_id=1, source_target_pairs={{16,0},{24,8},{0,16},{8,24},{17,1},{25,9},{1,17},{9,25},{18,2},{26... | collective-permute-start | bytes 589832 | tf_op jit(solution)/shard_map/ppermute | solution.py:494
  37.8 5.2 %collective-permute-start.7 = (bf16[16,1920]{1,0:T(8,128)(2,1)S(1)}, bf16[16,1920]{1,0:T(8,128)(2,1)S(1)}, u32[]{:S(2)}, u32[]{:S(2)}) collective-permute-start(bf16[16,1920]{1,0:T(8,128)(2,1)S(1)} %get-tuple-element.76), channel_id=1, source_target_pairs={{0,1},{1,0},{2,3},{3,2},{4,5},{5,4},{6,7},{7,6},{8,9},{9,8},{10,11... | collective-permute-start | bytes 184328 | tf_op jit(solution)/shard_map/ppermute | solution.py:487
  37.9 5.8 %collective-permute-start.8 = (bf16[16,1920]{1,0:T(8,128)(2,1)S(1)}, bf16[16,1920]{1,0:T(8,128)(2,1)S(1)}, u32[]{:S(2)}, u32[]{:S(2)}) collective-permute-start(bf16[16,1920]{1,0:T(8,128)(2,1)S(1)} %get-tuple-element.77), channel_id=1, source_target_pairs={{0,2},{1,3},{2,0},{3,1},{4,6},{5,7},{6,4},{7,5},{8,10},{9,11},{10,... | collective-permute-start | bytes 184328 | tf_op jit(solution)/shard_map/ppermute | solution.py:487
  41.2 5.3 %collective-permute-start.9 = (bf16[16,1920]{1,0:T(8,128)(2,1)S(1)}, bf16[16,1920]{1,0:T(8,128)(2,1)S(1)}, u32[]{:S(2)}, u32[]{:S(2)}) collective-permute-start(bf16[16,1920]{1,0:T(8,128)(2,1)S(1)} %get-tuple-element.78), channel_id=1, source_target_pairs={{0,3},{1,2},{2,1},{3,0},{4,7},{5,6},{6,5},{7,4},{8,11},{9,10},{10,... | collective-permute-start | bytes 184328 | tf_op jit(solution)/shard_map/ppermute | solution.py:487
  41.2 5.8 %collective-permute-start.10 = (bf16[16,1920]{1,0:T(8,128)(2,1)S(1)}, bf16[16,1920]{1,0:T(8,128)(2,1)S(1)}, u32[]{:S(2)}, u32[]{:S(2)}) collective-permute-start(bf16[16,1920]{1,0:T(8,128)(2,1)S(1)} %get-tuple-element.79), channel_id=1, source_target_pairs={{0,4},{1,5},{2,6},{3,7},{4,0},{5,1},{6,2},{7,3},{8,12},{9,13},{10,... | collective-permute-start | bytes 184328 | tf_op jit(solution)/shard_map/ppermute | solution.py:487
  43.0 7.2 %collective-permute-start.11 = (bf16[16,1920]{1,0:T(8,128)(2,1)S(1)}, bf16[16,1920]{1,0:T(8,128)(2,1)S(1)}, u32[]{:S(2)}, u32[]{:S(2)}) collective-permute-start(bf16[16,1920]{1,0:T(8,128)(2,1)S(1)} %get-tuple-element.80), channel_id=1, source_target_pairs={{0,5},{1,4},{2,7},{3,6},{4,1},{5,0},{6,3},{7,2},{8,13},{9,12},{10,... | collective-permute-start | bytes 184328 | tf_op jit(solution)/shard_map/ppermute | solution.py:487
  43.8 18.9 %collective-permute-start.22 = (bf16[128,768]{1,0:T(8,128)(2,1)S(1)}, bf16[128,768]{1,0:T(8,128)(2,1)S(1)}, u32[]{:S(2)}, u32[]{:S(2)}) collective-permute-start(bf16[128,768]{1,0:T(8,128)(2,1)S(1)} %get-tuple-element.94.refs_0_.value_ref), channel_id=1, source_target_pairs={{16,0},{24,8},{0,16},{8,24},{17,1},{25,9},{1,17},{9,25},{18,2},{26... | collective-permute-start | bytes 589832 | tf_op jit(solution)/shard_map/ppermute | solution.py:494
  46.5 16.2 %collective-permute-start.21 = (bf16[128,768]{1,0:T(8,128)(2,1)S(1)}, bf16[128,768]{1,0:T(8,128)(2,1)S(1)}, u32[]{:S(2)}, u32[]{:S(2)}) collective-permute-start(bf16[128,768]{1,0:T(8,128)(2,1)S(1)} %get-tuple-element.94.refs_0_.value_ref), channel_id=1, source_target_pairs={{24,0},{0,8},{8,16},{16,24},{25,1},{1,9},{9,17},{17,25},{26,2},{2,... | collective-permute-start | bytes 589832 | tf_op jit(solution)/shard_map/ppermute | solution.py:494
  47.0 15.7 %collective-permute-start.23 = (bf16[128,768]{1,0:T(8,128)(2,1)S(1)}, bf16[128,768]{1,0:T(8,128)(2,1)S(1)}, u32[]{:S(2)}, u32[]{:S(2)}) collective-permute-start(bf16[128,768]{1,0:T(8,128)(2,1)S(1)} %get-tuple-element.95.refs_3_.key_ref), channel_id=1, source_target_pairs={{0,8},{8,0},{16,24},{24,16},{1,9},{9,1},{17,25},{25,17},{2,10},{10... | collective-permute-start | bytes 589832 | tf_op jit(solution)/shard_map/ppermute | solution.py:311
  48.5 14.2 %collective-permute-start.25 = (bf16[128,768]{1,0:T(8,128)(2,1)S(1)}, bf16[128,768]{1,0:T(8,128)(2,1)S(1)}, u32[]{:S(2)}, u32[]{:S(2)}) collective-permute-start(bf16[128,768]{1,0:T(8,128)(2,1)S(1)} %collective-permute-done.24.refs_5_), channel_id=1, source_target_pairs={{0,8},{8,0},{16,24},{24,16},{1,9},{9,1},{17,25},{25,17},{2,10},{10... | collective-permute-start | bytes 589832 | tf_op jit(solution)/shard_map/ppermute | solution.py:312
  50.3 6.0 %collective-permute-start.12 = (bf16[16,1920]{1,0:T(8,128)(2,1)S(1)}, bf16[16,1920]{1,0:T(8,128)(2,1)S(1)}, u32[]{:S(2)}, u32[]{:S(2)}) collective-permute-start(bf16[16,1920]{1,0:T(8,128)(2,1)S(1)} %get-tuple-element.81), channel_id=1, source_target_pairs={{0,6},{1,7},{2,4},{3,5},{4,2},{5,3},{6,0},{7,1},{8,14},{9,15},{10,... | collective-permute-start | bytes 184328 | tf_op jit(solution)/shard_map/ppermute | solution.py:487
  56.3 5.4 %collective-permute-start.13 = (bf16[16,1920]{1,0:T(8,128)(2,1)S(1)}, bf16[16,1920]{1,0:T(8,128)(2,1)S(1)}, u32[]{:S(2)}, u32[]{:S(2)}) collective-permute-start(bf16[16,1920]{1,0:T(8,128)(2,1)S(1)} %get-tuple-element.82), channel_id=1, source_target_pairs={{0,7},{1,6},{2,5},{3,4},{4,3},{5,2},{6,1},{7,0},{8,15},{9,14},{10,... | collective-permute-start | bytes 184328 | tf_op jit(solution)/shard_map/ppermute | solution.py:487
  62.0 8.6 %collective-permute-start.26 = (bf16[128,768]{1,0:T(8,128)(2,1)S(1)}, bf16[128,768]{1,0:T(8,128)(2,1)S(1)}, u32[]{:S(2)}, u32[]{:S(2)}) collective-permute-start(bf16[128,768]{1,0:T(8,128)(2,1)S(1)} %get-tuple-element.85.query_ref), channel_id=1, source_target_pairs={{16,0},{24,8},{0,16},{8,24},{17,1},{25,9},{1,17},{9,25},{18,2},{26... | collective-permute-start | bytes 589832 | tf_op jit(solution)/shard_map/ppermute | solution.py:494
  65.7 6.5 %collective-permute-start.38 = (bf16[32,1920]{1,0:T(8,128)(2,1)S(1)}, bf16[32,1920]{1,0:T(8,128)(2,1)S(1)}, u32[]{:S(2)}, u32[]{:S(2)}) collective-permute-start(bf16[32,1920]{1,0:T(8,128)(2,1)S(1)} %get-tuple-element.115), channel_id=1, source_target_pairs={{0,2},{1,3},{2,0},{3,1},{4,6},{5,7},{6,4},{7,5},{8,10},{9,11},{10,... | collective-permute-start | bytes 368648 | tf_op jit(solution)/shard_map/ppermute | solution.py:487
  65.8 11.6 %collective-permute-start.39 = (bf16[32,1920]{1,0:T(8,128)(2,1)S(1)}, bf16[32,1920]{1,0:T(8,128)(2,1)S(1)}, u32[]{:S(2)}, u32[]{:S(2)}) collective-permute-start(bf16[32,1920]{1,0:T(8,128)(2,1)S(1)} %get-tuple-element.116), channel_id=1, source_target_pairs={{0,4},{1,5},{2,6},{3,7},{4,0},{5,1},{6,2},{7,3},{8,12},{9,13},{10,... | collective-permute-start | bytes 368648 | tf_op jit(solution)/shard_map/ppermute | solution.py:487
  68.6 9.2 %collective-permute-start.40 = (bf16[32,1920]{1,0:T(8,128)(2,1)S(1)}, bf16[32,1920]{1,0:T(8,128)(2,1)S(1)}, u32[]{:S(2)}, u32[]{:S(2)}) collective-permute-start(bf16[32,1920]{1,0:T(8,128)(2,1)S(1)} %get-tuple-element.117), channel_id=1, source_target_pairs={{0,6},{1,7},{2,4},{3,5},{4,2},{5,3},{6,0},{7,1},{8,14},{9,15},{10,... | collective-permute-start | bytes 368648 | tf_op jit(solution)/shard_map/ppermute | solution.py:487
  70.2 9.1 %collective-permute-start.29 = (bf16[128,768]{1,0:T(8,128)(2,1)S(1)}, bf16[128,768]{1,0:T(8,128)(2,1)S(1)}, u32[]{:S(2)}, u32[]{:S(2)}) collective-permute-start(bf16[128,768]{1,0:T(8,128)(2,1)S(1)} %get-tuple-element.85.query_ref), channel_id=1, source_target_pairs={{0,8},{8,0},{16,24},{24,16},{1,9},{9,1},{17,25},{25,17},{2,10},{10... | collective-permute-start | bytes 589832 | tf_op jit(solution)/shard_map/ppermute | solution.py:320
  70.7 10.4 %collective-permute-start.30 = (bf16[128,768]{1,0:T(8,128)(2,1)S(1)}, bf16[128,768]{1,0:T(8,128)(2,1)S(1)}, u32[]{:S(2)}, u32[]{:S(2)}) collective-permute-start(bf16[128,768]{1,0:T(8,128)(2,1)S(1)} %collective-permute-done.26.refs_0_.refs_7_), channel_id=1, source_target_pairs={{0,8},{8,0},{16,24},{24,16},{1,9},{9,1},{17,25},{25,17},{2,10},{10... | collective-permute-start | bytes 589832 | tf_op jit(solution)/shard_map/ppermute | solution.py:321
  72.2 8.9 %collective-permute-start.28 = (bf16[128,768]{1,0:T(8,128)(2,1)S(1)}, bf16[128,768]{1,0:T(8,128)(2,1)S(1)}, u32[]{:S(2)}, u32[]{:S(2)}) collective-permute-start(bf16[128,768]{1,0:T(8,128)(2,1)S(1)} %get-tuple-element.100.grad_ref), channel_id=1, source_target_pairs={{16,0},{24,8},{0,16},{8,24},{17,1},{25,9},{1,17},{9,25},{18,2},{26... | collective-permute-start | bytes 589832 | tf_op jit(solution)/shard_map/ppermute | solution.py:494
  77.4 6.8 %collective-permute-start.27 = (bf16[128,768]{1,0:T(8,128)(2,1)S(1)}, bf16[128,768]{1,0:T(8,128)(2,1)S(1)}, u32[]{:S(2)}, u32[]{:S(2)}) collective-permute-start(bf16[128,768]{1,0:T(8,128)(2,1)S(1)} %get-tuple-element.100.grad_ref), channel_id=1, source_target_pairs={{8,0},{16,8},{24,16},{0,24},{9,1},{17,9},{25,17},{1,25},{10,2},{18... | collective-permute-start | bytes 589832 | tf_op jit(solution)/shard_map/ppermute | solution.py:494
  77.9 15.0 %collective-permute-start.41 = (bf16[64,1920]{1,0:T(8,128)(2,1)S(1)}, bf16[64,1920]{1,0:T(8,128)(2,1)S(1)}, u32[]{:S(2)}, u32[]{:S(2)}) collective-permute-start(bf16[64,1920]{1,0:T(8,128)(2,1)S(1)} %pad_maximum_fusion), channel_id=1, source_target_pairs={{0,1},{1,0},{2,3},{3,2},{4,5},{5,4},{6,7},{7,6},{8,9},{9,8},{10,11... | collective-permute-start | bytes 737288 | tf_op jit(solution)/shard_map/ppermute | solution.py:474
  85.7 4.9 %collective-permute-start.32 = (bf16[16,1920]{1,0:T(8,128)(2,1)S(1)}, bf16[16,1920]{1,0:T(8,128)(2,1)S(1)}, u32[]{:S(2)}, u32[]{:S(2)}) collective-permute-start(bf16[16,1920]{1,0:T(8,128)(2,1)S(1)} %get-tuple-element.107), channel_id=1, source_target_pairs={{0,2},{1,3},{2,0},{3,1},{4,6},{5,7},{6,4},{7,5},{8,10},{9,11},{10,... | collective-permute-start | bytes 184328 | tf_op jit(solution)/shard_map/ppermute | solution.py:487
  85.8 9.7 %collective-permute-start.33 = (bf16[16,1920]{1,0:T(8,128)(2,1)S(1)}, bf16[16,1920]{1,0:T(8,128)(2,1)S(1)}, u32[]{:S(2)}, u32[]{:S(2)}) collective-permute-start(bf16[16,1920]{1,0:T(8,128)(2,1)S(1)} %get-tuple-element.108), channel_id=1, source_target_pairs={{0,3},{1,2},{2,1},{3,0},{4,7},{5,6},{6,5},{7,4},{8,11},{9,10},{10,... | collective-permute-start | bytes 184328 | tf_op jit(solution)/shard_map/ppermute | solution.py:487
  87.5 9.6 %collective-permute-start.34 = (bf16[16,1920]{1,0:T(8,128)(2,1)S(1)}, bf16[16,1920]{1,0:T(8,128)(2,1)S(1)}, u32[]{:S(2)}, u32[]{:S(2)}) collective-permute-start(bf16[16,1920]{1,0:T(8,128)(2,1)S(1)} %get-tuple-element.109), channel_id=1, source_target_pairs={{0,4},{1,5},{2,6},{3,7},{4,0},{5,1},{6,2},{7,3},{8,12},{9,13},{10,... | collective-permute-start | bytes 184328 | tf_op jit(solution)/shard_map/ppermute | solution.py:487
  88.6 8.9 %collective-permute-start.35 = (bf16[16,1920]{1,0:T(8,128)(2,1)S(1)}, bf16[16,1920]{1,0:T(8,128)(2,1)S(1)}, u32[]{:S(2)}, u32[]{:S(2)}) collective-permute-start(bf16[16,1920]{1,0:T(8,128)(2,1)S(1)} %get-tuple-element.110), channel_id=1, source_target_pairs={{0,5},{1,4},{2,7},{3,6},{4,1},{5,0},{6,3},{7,2},{8,13},{9,12},{10,... | collective-permute-start | bytes 184328 | tf_op jit(solution)/shard_map/ppermute | solution.py:487
  90.6 6.9 %collective-permute-start.36 = (bf16[16,1920]{1,0:T(8,128)(2,1)S(1)}, bf16[16,1920]{1,0:T(8,128)(2,1)S(1)}, u32[]{:S(2)}, u32[]{:S(2)}) collective-permute-start(bf16[16,1920]{1,0:T(8,128)(2,1)S(1)} %get-tuple-element.111), channel_id=1, source_target_pairs={{0,6},{1,7},{2,4},{3,5},{4,2},{5,3},{6,0},{7,1},{8,14},{9,15},{10,... | collective-permute-start | bytes 184328 | tf_op jit(solution)/shard_map/ppermute | solution.py:487
  92.9 6.1 %collective-permute-start.37 = (bf16[16,1920]{1,0:T(8,128)(2,1)S(1)}, bf16[16,1920]{1,0:T(8,128)(2,1)S(1)}, u32[]{:S(2)}, u32[]{:S(2)}) collective-permute-start(bf16[16,1920]{1,0:T(8,128)(2,1)S(1)} %get-tuple-element.112), channel_id=1, source_target_pairs={{0,7},{1,6},{2,5},{3,4},{4,3},{5,2},{6,1},{7,0},{8,15},{9,14},{10,... | collective-permute-start | bytes 184328 | tf_op jit(solution)/shard_map/ppermute | solution.py:487
  100.9 5.9 %collective-permute-start.42 = (bf16[16,1920]{1,0:T(8,128)(2,1)S(1)}, bf16[16,1920]{1,0:T(8,128)(2,1)S(1)}, u32[]{:S(2)}, u32[]{:S(2)}) collective-permute-start(bf16[16,1920]{1,0:T(8,128)(2,1)S(1)} %get-tuple-element.119), channel_id=1, source_target_pairs={{0,1},{1,0},{2,3},{3,2},{4,5},{5,4},{6,7},{7,6},{8,9},{9,8},{10,11... | collective-permute-start | bytes 184328 | tf_op jit(solution)/shard_map/ppermute | solution.py:487
  101.6 7.4 %collective-permute-start.43 = (bf16[16,1920]{1,0:T(8,128)(2,1)S(1)}, bf16[16,1920]{1,0:T(8,128)(2,1)S(1)}, u32[]{:S(2)}, u32[]{:S(2)}) collective-permute-start(bf16[16,1920]{1,0:T(8,128)(2,1)S(1)} %get-tuple-element.120), channel_id=1, source_target_pairs={{0,2},{1,3},{2,0},{3,1},{4,6},{5,7},{6,4},{7,5},{8,10},{9,11},{10,... | collective-permute-start | bytes 184328 | tf_op jit(solution)/shard_map/ppermute | solution.py:487
  104.3 6.9 %collective-permute-start.44 = (bf16[16,1920]{1,0:T(8,128)(2,1)S(1)}, bf16[16,1920]{1,0:T(8,128)(2,1)S(1)}, u32[]{:S(2)}, u32[]{:S(2)}) collective-permute-start(bf16[16,1920]{1,0:T(8,128)(2,1)S(1)} %get-tuple-element.121), channel_id=1, source_target_pairs={{0,3},{1,2},{2,1},{3,0},{4,7},{5,6},{6,5},{7,4},{8,11},{9,10},{10,... | collective-permute-start | bytes 184328 | tf_op jit(solution)/shard_map/ppermute | solution.py:487
  104.3 6.9 %collective-permute-start.45 = (bf16[16,1920]{1,0:T(8,128)(2,1)S(1)}, bf16[16,1920]{1,0:T(8,128)(2,1)S(1)}, u32[]{:S(2)}, u32[]{:S(2)}) collective-permute-start(bf16[16,1920]{1,0:T(8,128)(2,1)S(1)} %get-tuple-element.122), channel_id=1, source_target_pairs={{0,4},{1,5},{2,6},{3,7},{4,0},{5,1},{6,2},{7,3},{8,12},{9,13},{10,... | collective-permute-start | bytes 184328 | tf_op jit(solution)/shard_map/ppermute | solution.py:487
  106.8 9.8 %collective-permute-start.46 = (bf16[16,1920]{1,0:T(8,128)(2,1)S(1)}, bf16[16,1920]{1,0:T(8,128)(2,1)S(1)}, u32[]{:S(2)}, u32[]{:S(2)}) collective-permute-start(bf16[16,1920]{1,0:T(8,128)(2,1)S(1)} %get-tuple-element.123), channel_id=1, source_target_pairs={{0,5},{1,4},{2,7},{3,6},{4,1},{5,0},{6,3},{7,2},{8,13},{9,12},{10,... | collective-permute-start | bytes 184328 | tf_op jit(solution)/shard_map/ppermute | solution.py:487
  106.8 9.7 %collective-permute-start.47 = (bf16[16,1920]{1,0:T(8,128)(2,1)S(1)}, bf16[16,1920]{1,0:T(8,128)(2,1)S(1)}, u32[]{:S(2)}, u32[]{:S(2)}) collective-permute-start(bf16[16,1920]{1,0:T(8,128)(2,1)S(1)} %get-tuple-element.124), channel_id=1, source_target_pairs={{0,6},{1,7},{2,4},{3,5},{4,2},{5,3},{6,0},{7,1},{8,14},{9,15},{10,... | collective-permute-start | bytes 184328 | tf_op jit(solution)/shard_map/ppermute | solution.py:487
  108.9 7.6 %collective-permute-start.48 = (bf16[16,1920]{1,0:T(8,128)(2,1)S(1)}, bf16[16,1920]{1,0:T(8,128)(2,1)S(1)}, u32[]{:S(2)}, u32[]{:S(2)}) collective-permute-start(bf16[16,1920]{1,0:T(8,128)(2,1)S(1)} %get-tuple-element.125), channel_id=1, source_target_pairs={{0,7},{1,6},{2,5},{3,4},{4,3},{5,2},{6,1},{7,0},{8,15},{9,14},{10,... | collective-permute-start | bytes 184328 | tf_op jit(solution)/shard_map/ppermute | solution.py:487
  (4 other events, 94.5 us)

commit v8 on v7

--- a/solution.py
+++ b/solution.py
@@ -444,13 +444,24 @@
     return term
 
 
+def turn_kernel(parts, w_ref, out_ref):
+    width, piece = HEADS * HD, 2 * LANES
+    for i, part in enumerate(parts):
+        for at in range(0, width, piece):
+            cols = w_ref[:, part * width + at : part * width + at + piece]
+            out_ref[i * width + at : i * width + at + piece] = cols.T
+
+
 def term_kernel(parts, slope_ref, w_ref, *refs):
     refs[-1][...] = owner_term(parts, refs[:-1], slope_ref, w_ref)
 
 
-def last_term_kernel(count, parts, slope_ref, w_ref, *refs):
+def last_term_kernel(count, parts, turned, slope_ref, w_ref, *refs):
     ins, others, outs = refs[:count], refs[count:-count], refs[-count:]
-    term = owner_term(parts, ins, slope_ref, w_ref)
+    if turned:
+        term = dot((unfold(ins).astype(f32) * slope_ref[...]).astype(bf16), w_ref[...])
+    else:
+        term = owner_term(parts, ins, slope_ref, w_ref)
     for other_ref in others:
         term = term + other_ref[...]
     fold(term.astype(bf16), outs)
@@ -609,12 +620,16 @@
             [term],
             [query_slope, w_local] + exchange(query_grad),
         )
-        last_parts, last = pair_parts, [pair_slope, w_local] + exchange(pair_grad) + [query_term]
+        turned = shape((len(pair_parts) * width, feats), bf16)
+        (w_rows,) = call(functools.partial(turn_kernel, pair_parts), [turned], [w_local])
+        last_parts, last = pair_parts, [pair_slope, w_rows] + exchange(pair_grad) + [query_term]
     else:
         order = [query_grad[0], pair_grad[0], query_grad[1], pair_grad[1]]
         last_parts, last = (0,), [slope, w_local] + exchange(wires_of(order))
     term_box = call(
-        functools.partial(last_term_kernel, senders, last_parts), wire(n_user * MAIN, feats), last
+        functools.partial(last_term_kernel, senders, last_parts, direct),
+        wire(n_user * MAIN, feats),
+        last,
     )
     (output,) = call(output_kernel, [half], [gate, normed])
     term_back = exchange(term_box)

time: 120 us -> 123 us (1.025)
  waiting for transfers between devices: 38 us -> 40.7 us
    ppermute x1, waiting for transfers between devices: 0.01 us -> 1.95 us  [shifted_pairs(): handed = lax.ppermute(key_far, 'seq', ACROSS)]
    pallas_call x14 -> x15, Pallas kernels: 20.5 us -> 21 us  [call(): pl.pallas_call(kernel, out_shape=tuple(outs), in_specs=[pl.BlockSpec(memo...]
  transfers between devices with their start and end apart: 49 -> 49, of which waited for: 15 -> 14; matrix products, arithmetic and copies ran while one was open for 1% -> 1% of each run, Pallas kernels for 12% -> 13%
where the time goes in v8:
time: 123 us; the launch traced here: 121 us
  starting transfers between devices  57.7 us (47%)
  waiting for transfers between devices  40.7 us (33%)
  Pallas kernels  21 us (17%)
    ppermute x38, starting transfers between devices, exchanged(): lax.ppermute(blocks[k], 'user', [(i, i ^ merged * k) for i in range(count)])  47.9 us
    ppermute x38, waiting for transfers between devices, exchanged(): lax.ppermute(blocks[k], 'user', [(i, i ^ merged * k) for i in range(count)])  32.9 us
    pallas_call x15, Pallas kernels, call(): pl.pallas_call(kernel, out_shape=tuple(outs), in_specs=[pl.BlockSpec(memo...  21 us
    ppermute x6, starting transfers between devices, shifted(): return lax.ppermute(block, 'seq', route)  5.62 us
    ppermute x6, waiting for transfers between devices, shifted(): return lax.ppermute(block, 'seq', route)  3.95 us
  transfers between devices with their start and end apart: 49, of which 14 were waited for; matrix products, arithmetic and copies ran while one was open for 1% of the time, Pallas kernels for 13%

profile of v8, /device:TPU:2, one launch (start us, length us, event | category | flops | bytes accessed | tf_op | source)
XLA Modules:
  0.0 121.1 jit_solution(12774473706981791162)
XLA Ops:
  0.6 1.6 %shard_map.87 = (bf16[5,128,128]{2,1,0:T(8,128)(2,1)S(1)}, bf16[16,1920]{1,0:T(8,128)(2,1)S(1)}, bf16[16,1920]{1,0:T(8,128)(2,1)S(1)}, bf16[16,1920]{1,0:T(8,128...) custom-call(bf16[128,1536]{1,0:T(8,128)(2,1)} %bitcast.6, ...), custom_call_target="tpu_custom_call" | custom-call | flops 16777216 | bytes 1055232 | tf_op jit(solution)/shard_map/pallas_call | solution.py:38
  2.3 1.6 %collective-permute-start.1 = (bf16[16,1920]{1,0:T(8,128)(2,1)S(1)}, bf16[16,1920]{1,0:T(8,128)(2,1)S(1)}, u32[]{:S(2)}, u32[]{:S(2)}) collective-permute-start(bf16[16,1920]{1,0:T(8,128)(2,1)S(1)} %get-tuple-element.68), channel_id=1, source_target_pairs={{0,2},{1,3},{2,0},{3,1},{4,6},{5,7},{6,4},{7,5},{8,10},{9,11},{10,... | collective-permute-start | bytes 184328 | tf_op jit(solution)/shard_map/ppermute | solution.py:498
  4.1 2.6 %collective-permute-start.3 = (bf16[16,1920]{1,0:T(8,128)(2,1)S(1)}, bf16[16,1920]{1,0:T(8,128)(2,1)S(1)}, u32[]{:S(2)}, u32[]{:S(2)}) collective-permute-start(bf16[16,1920]{1,0:T(8,128)(2,1)S(1)} %get-tuple-element.70), channel_id=1, source_target_pairs={{0,4},{1,5},{2,6},{3,7},{4,0},{5,1},{6,2},{7,3},{8,12},{9,13},{10,... | collective-permute-start | bytes 184328 | tf_op jit(solution)/shard_map/ppermute | solution.py:498
  6.7 3.6 %collective-permute-start.5 = (bf16[16,1920]{1,0:T(8,128)(2,1)S(1)}, bf16[16,1920]{1,0:T(8,128)(2,1)S(1)}, u32[]{:S(2)}, u32[]{:S(2)}) collective-permute-start(bf16[16,1920]{1,0:T(8,128)(2,1)S(1)} %get-tuple-element.72), channel_id=1, source_target_pairs={{0,6},{1,7},{2,4},{3,5},{4,2},{5,3},{6,0},{7,1},{8,14},{9,15},{10,... | collective-permute-start | bytes 184328 | tf_op jit(solution)/shard_map/ppermute | solution.py:498
  11.2 3.9 %shard_map.86 = (bf16[1536,3072]{1,0:T(8,128)(2,1)S(1)}, bf16[5,128,128]{2,1,0:T(8,128)(2,1)S(1)}, f32[128,384]{1,0:T(8,128)S(1)}, f32[128,384]{1,0:T(8,128)S(1)}) custom-call(bf16[1536,3072]{1,0:T(8,128)(2,1)} %bitcast.12, s32[1,136]{1,0:T(1,128)S(1)} %pad_add_fusion.small_ref), custom_call_target="tpu_custom_call" | custom-call | flops 16777216 | bytes 19431968 | tf_op jit(solution)/shard_map/pallas_call | solution.py:38
  15.1 1.7 %collective-permute-done.4.refs_5_ = bf16[16,1920]{1,0:T(8,128)(2,1)S(1)} collective-permute-done((bf16[16,1920]{1,0:T(8,128)(2,1)S(1)}, bf16[16,1920]{1,0:T(8,128)(2,1)S(1)}, u32[]{:S(2)}, u32[]{:S(2)}) %collective-permute-start.4) | collective-permute-done | bytes 61472 | tf_op jit(solution)/shard_map/ppermute | solution.py:498
  16.8 1.3 %shard_map.88 = (bf16[16,1920]{1,0:T(8,128)(2,1)S(1)}, bf16[16,1920]{1,0:T(8,128)(2,1)S(1)}, bf16[16,1920]{1,0:T(8,128)(2,1)S(1)}, bf16[16,1920]{1,0:T(8,128)(2,...) custom-call(bf16[1536,3072]{1,0:T(8,128)(2,1)S(1)} %get-tuple-elemen, ...), custom_call_target="tpu_custom_call" | custom-call | flops 16777216 | bytes 11403264 | tf_op jit(solution)/shard_map/pallas_call | solution.py:38
  18.3 3.2 %collective-permute-start.15 = (bf16[16,1920]{1,0:T(8,128)(2,1)S(1)}, bf16[16,1920]{1,0:T(8,128)(2,1)S(1)}, u32[]{:S(2)}, u32[]{:S(2)}) collective-permute-start(bf16[16,1920]{1,0:T(8,128)(2,1)S(1)} %get-tuple-element.88), channel_id=1, source_target_pairs={{0,2},{1,3},{2,0},{3,1},{4,6},{5,7},{6,4},{7,5},{8,10},{9,11},{10,... | collective-permute-start | bytes 184328 | tf_op jit(solution)/shard_map/ppermute | solution.py:498
  21.5 2.8 %collective-permute-start.17 = (bf16[16,1920]{1,0:T(8,128)(2,1)S(1)}, bf16[16,1920]{1,0:T(8,128)(2,1)S(1)}, u32[]{:S(2)}, u32[]{:S(2)}) collective-permute-start(bf16[16,1920]{1,0:T(8,128)(2,1)S(1)} %get-tuple-element.90), channel_id=1, source_target_pairs={{0,4},{1,5},{2,6},{3,7},{4,0},{5,1},{6,2},{7,3},{8,12},{9,13},{10,... | collective-permute-start | bytes 184328 | tf_op jit(solution)/shard_map/ppermute | solution.py:498
  24.2 2.1 %collective-permute-start.19 = (bf16[16,1920]{1,0:T(8,128)(2,1)S(1)}, bf16[16,1920]{1,0:T(8,128)(2,1)S(1)}, u32[]{:S(2)}, u32[]{:S(2)}) collective-permute-start(bf16[16,1920]{1,0:T(8,128)(2,1)S(1)} %get-tuple-element.92), channel_id=1, source_target_pairs={{0,6},{1,7},{2,4},{3,5},{4,2},{5,3},{6,0},{7,1},{8,14},{9,15},{10,... | collective-permute-start | bytes 184328 | tf_op jit(solution)/shard_map/ppermute | solution.py:498
  26.4 1.3 %collective-permute-start.20 = (bf16[16,1920]{1,0:T(8,128)(2,1)S(1)}, bf16[16,1920]{1,0:T(8,128)(2,1)S(1)}, u32[]{:S(2)}, u32[]{:S(2)}) collective-permute-start(bf16[16,1920]{1,0:T(8,128)(2,1)S(1)} %get-tuple-element.93), channel_id=1, source_target_pairs={{0,7},{1,6},{2,5},{3,4},{4,3},{5,2},{6,1},{7,0},{8,15},{9,14},{10,... | collective-permute-start | bytes 184328 | tf_op jit(solution)/shard_map/ppermute | solution.py:498
  27.7 6.4 %collective-permute-done.18.refs_5_ = bf16[16,1920]{1,0:T(8,128)(2,1)S(1)} collective-permute-done((bf16[16,1920]{1,0:T(8,128)(2,1)S(1)}, bf16[16,1920]{1,0:T(8,128)(2,1)S(1)}, u32[]{:S(2)}, u32[]{:S(2)}) %collective-permute-start.18) | collective-permute-done | bytes 61472 | tf_op jit(solution)/shard_map/ppermute | solution.py:498
  34.4 1.6 %collective-permute-start.24 = (bf16[128,768]{1,0:T(8,128)(2,1)S(1)}, bf16[128,768]{1,0:T(8,128)(2,1)S(1)}, u32[]{:S(2)}, u32[]{:S(2)}) collective-permute-start(bf16[128,768]{1,0:T(8,128)(2,1)S(1)} %get-tuple-element.95.refs_3_.key_ref), channel_id=1, source_target_pairs={{16,0},{24,8},{0,16},{8,24},{17,1},{25,9},{1,17},{9,25},{18,2},{26... | collective-permute-start | bytes 589832 | tf_op jit(solution)/shard_map/ppermute | solution.py:505
  36.0 1.8 %shard_map.89 = (bf16[16,1920]{1,0:T(8,128)(2,1)S(1)}, bf16[16,1920]{1,0:T(8,128)(2,1)S(1)}, bf16[16,1920]{1,0:T(8,128)(2,1)S(1)}, bf16[16,1920]{1,0:T(8,128)(2,...) custom-call(bf16[1536,3072]{1,0:T(8,128)(2,1)S(1)} %get-tuple-elemen, ...), custom_call_target="tpu_custom_call" | custom-call | flops 16777216 | bytes 13369344 | tf_op jit(solution)/shard_map/pallas_call | solution.py:38
  37.8 3.3 %collective-permute-start.10 = (bf16[16,1920]{1,0:T(8,128)(2,1)S(1)}, bf16[16,1920]{1,0:T(8,128)(2,1)S(1)}, u32[]{:S(2)}, u32[]{:S(2)}) collective-permute-start(bf16[16,1920]{1,0:T(8,128)(2,1)S(1)} %get-tuple-element.79), channel_id=1, source_target_pairs={{0,4},{1,5},{2,6},{3,7},{4,0},{5,1},{6,2},{7,3},{8,12},{9,13},{10,... | collective-permute-start | bytes 184328 | tf_op jit(solution)/shard_map/ppermute | solution.py:498
  41.2 2.3 %collective-permute-start.12 = (bf16[16,1920]{1,0:T(8,128)(2,1)S(1)}, bf16[16,1920]{1,0:T(8,128)(2,1)S(1)}, u32[]{:S(2)}, u32[]{:S(2)}) collective-permute-start(bf16[16,1920]{1,0:T(8,128)(2,1)S(1)} %get-tuple-element.81), channel_id=1, source_target_pairs={{0,6},{1,7},{2,4},{3,5},{4,2},{5,3},{6,0},{7,1},{8,14},{9,15},{10,... | collective-permute-start | bytes 184328 | tf_op jit(solution)/shard_map/ppermute | solution.py:498
  45.1 5.4 %collective-permute-done.11.refs_5_ = bf16[16,1920]{1,0:T(8,128)(2,1)S(1)} collective-permute-done((bf16[16,1920]{1,0:T(8,128)(2,1)S(1)}, bf16[16,1920]{1,0:T(8,128)(2,1)S(1)}, u32[]{:S(2)}, u32[]{:S(2)}) %collective-permute-start.11) | collective-permute-done | bytes 61472 | tf_op jit(solution)/shard_map/ppermute | solution.py:498
  50.9 1.5 %collective-permute-start.22 = (bf16[128,768]{1,0:T(8,128)(2,1)S(1)}, bf16[128,768]{1,0:T(8,128)(2,1)S(1)}, u32[]{:S(2)}, u32[]{:S(2)}) collective-permute-start(bf16[128,768]{1,0:T(8,128)(2,1)S(1)} %get-tuple-element.94.refs_0_.value_ref), channel_id=1, source_target_pairs={{16,0},{24,8},{0,16},{8,24},{17,1},{25,9},{1,17},{9,25},{18,2},{26... | collective-permute-start | bytes 589832 | tf_op jit(solution)/shard_map/ppermute | solution.py:505
  53.0 1.5 %collective-permute-start.25 = (bf16[128,768]{1,0:T(8,128)(2,1)S(1)}, bf16[128,768]{1,0:T(8,128)(2,1)S(1)}, u32[]{:S(2)}, u32[]{:S(2)}) collective-permute-start(bf16[128,768]{1,0:T(8,128)(2,1)S(1)} %collective-permute-done.24.refs_5_), channel_id=1, source_target_pairs={{0,8},{8,0},{16,24},{24,16},{1,9},{9,1},{17,25},{25,17},{2,10},{10... | collective-permute-start | bytes 589832 | tf_op jit(solution)/shard_map/ppermute | solution.py:312
  54.5 1.2 collective-permute-start.8
  55.7 3.1 %collective-permute-done.8.refs_2_ = bf16[16,1920]{1,0:T(8,128)(2,1)S(1)} collective-permute-done((bf16[16,1920]{1,0:T(8,128)(2,1)S(1)}, bf16[16,1920]{1,0:T(8,128)(2,1)S(1)}, u32[]{:S(2)}, u32[]{:S(2)}) %collective-permute-start.8) | collective-permute-done | bytes 61472 | tf_op jit(solution)/shard_map/ppermute | solution.py:498
  58.7 4.0 %collective-permute-done.9.refs_3_ = bf16[16,1920]{1,0:T(8,128)(2,1)S(1)} collective-permute-done((bf16[16,1920]{1,0:T(8,128)(2,1)S(1)}, bf16[16,1920]{1,0:T(8,128)(2,1)S(1)}, u32[]{:S(2)}, u32[]{:S(2)}) %collective-permute-start.9) | collective-permute-done | bytes 61472 | tf_op jit(solution)/shard_map/ppermute | solution.py:498
  63.8 1.9 %collective-permute-done.25.refs_6_ = bf16[128,768]{1,0:T(8,128)(2,1)S(1)} collective-permute-done((bf16[128,768]{1,0:T(8,128)(2,1)S(1)}, bf16[128,768]{1,0:T(8,128)(2,1)S(1)}, u32[]{:S(2)}, u32[]{:S(2)}) %collective-permute-start.25) | collective-permute-done | bytes 196640 | tf_op jit(solution)/shard_map/ppermute | solution.py:312
  65.8 1.4 %shard_map.92 = (bf16[128,768]{1,0:T(8,128)(2,1)S(1)}, f32[128,768]{1,0:T(8,128)S(1)}) custom-call(f32[128,384]{1,0:T(8,128)S(1)} %get-tuple-element.84.see_ref, bf16[128,768]{1,0:T(8,128)(2,1)S(1)} %get-tuple-element.83.gate_in_ref.gate_ref, bf16[128,768]{1,0:T(8,128)(2,1)S(1)} %get-tuple-element.85.query_ref, bf16[128,768]{1,0:T(8,128)(2,1)S(1)} %bitcast.8, ...), custom_call_target="tpu_custom_call" | custom-call | flops 16777216 | bytes 2752512 | tf_op jit(solution)/shard_map/pallas_call | solution.py:38
  67.1 1.7 %shard_map.97 = (bf16[32,1920]{1,0:T(8,128)(2,1)S(1)}, bf16[32,1920]{1,0:T(8,128)(2,1)S(1)}, bf16[32,1920]{1,0:T(8,128)(2,1)S(1)}, bf16[32,1920]{1,0:T(8,128)(2,1)S(1)}) custom-call(f32[128,384]{1,0:T(8,128)S(1)} %get-tuple-element.84.see_ref, bf16[128,768]{1,0:T(8,128)(2,1)S(1)} %get-tuple-element.85.query_ref, ...), custom_call_target="tpu_custom_call" | custom-call | flops 16777216 | bytes 3211264 | tf_op jit(solution)/shard_map/pallas_call | solution.py:38
  68.9 2.3 %collective-permute-start.39 = (bf16[32,1920]{1,0:T(8,128)(2,1)S(1)}, bf16[32,1920]{1,0:T(8,128)(2,1)S(1)}, u32[]{:S(2)}, u32[]{:S(2)}) collective-permute-start(bf16[32,1920]{1,0:T(8,128)(2,1)S(1)} %get-tuple-element.116), channel_id=1, source_target_pairs={{0,4},{1,5},{2,6},{3,7},{4,0},{5,1},{6,2},{7,3},{8,12},{9,13},{10,... | collective-permute-start | bytes 368648 | tf_op jit(solution)/shard_map/ppermute | solution.py:498
  71.2 2.1 %collective-permute-start.40 = (bf16[32,1920]{1,0:T(8,128)(2,1)S(1)}, bf16[32,1920]{1,0:T(8,128)(2,1)S(1)}, u32[]{:S(2)}, u32[]{:S(2)}) collective-permute-start(bf16[32,1920]{1,0:T(8,128)(2,1)S(1)} %get-tuple-element.117), channel_id=1, source_target_pairs={{0,6},{1,7},{2,4},{3,5},{4,2},{5,3},{6,0},{7,1},{8,14},{9,15},{10,... | collective-permute-start | bytes 368648 | tf_op jit(solution)/shard_map/ppermute | solution.py:498
  73.8 1.5 %collective-permute-start.30 = (bf16[128,768]{1,0:T(8,128)(2,1)S(1)}, bf16[128,768]{1,0:T(8,128)(2,1)S(1)}, u32[]{:S(2)}, u32[]{:S(2)}) collective-permute-start(bf16[128,768]{1,0:T(8,128)(2,1)S(1)} %collective-permute-done.26.refs_0_.refs_7_), channel_id=1, source_target_pairs={{0,8},{8,0},{16,24},{24,16},{1,9},{9,1},{17,25},{25,17},{2,10},{10... | collective-permute-start | bytes 589832 | tf_op jit(solution)/shard_map/ppermute | solution.py:321
  76.1 4.9 %collective-permute-done.39.refs_2_ = bf16[32,1920]{1,0:T(8,128)(2,1)S(1)} collective-permute-done((bf16[32,1920]{1,0:T(8,128)(2,1)S(1)}, bf16[32,1920]{1,0:T(8,128)(2,1)S(1)}, u32[]{:S(2)}, u32[]{:S(2)}) %collective-permute-start.39) | collective-permute-done | bytes 122912 | tf_op jit(solution)/shard_map/ppermute | solution.py:498
  81.6 1.3 %shard_map.95 = (f32[128,768]{1,0:T(8,128)S(1)}, f32[128,768]{1,0:T(8,128)S(1)}, bf16[6,128,128]{2,1,0:T(8,128)(2,1)S(1)}, f32[6,128,128]{2,1,0:T(8,128)S(1)}) custom-call(f32[128,384]{1,0:T(8,128)S(1)} %get-tuple-element.98.seen_ref, bf16[128,768]{1,0:T(8,128)(2,1)S(1)} %get-tuple-element.94.refs_0_.value_ref, ...), custom_call_target="tpu_custom_call" | custom-call | flops 16777216 | bytes 2555904 | tf_op jit(solution)/shard_map/pallas_call | solution.py:38
  82.9 1.9 %collective-permute-done.30.refs_8_ = bf16[128,768]{1,0:T(8,128)(2,1)S(1)} collective-permute-done((bf16[128,768]{1,0:T(8,128)(2,1)S(1)}, bf16[128,768]{1,0:T(8,128)(2,1)S(1)}, u32[]{:S(2)}, u32[]{:S(2)}) %collective-permute-start.30) | collective-permute-done | bytes 196640 | tf_op jit(solution)/shard_map/ppermute | solution.py:321
  84.8 2.2 %collective-permute-done.27.refs_4_ = bf16[128,768]{1,0:T(8,128)(2,1)S(1)} collective-permute-done((bf16[128,768]{1,0:T(8,128)(2,1)S(1)}, bf16[128,768]{1,0:T(8,128)(2,1)S(1)}, u32[]{:S(2)}, u32[]{:S(2)}) %collective-permute-start.27) | collective-permute-done | bytes 196640 | tf_op jit(solution)/shard_map/ppermute | solution.py:505
  86.9 1.8 %collective-permute-done.28.refs_5_ = bf16[128,768]{1,0:T(8,128)(2,1)S(1)} collective-permute-done((bf16[128,768]{1,0:T(8,128)(2,1)S(1)}, bf16[128,768]{1,0:T(8,128)(2,1)S(1)}, u32[]{:S(2)}, u32[]{:S(2)}) %collective-permute-start.28) | collective-permute-done | bytes 196640 | tf_op jit(solution)/shard_map/ppermute | solution.py:505
  88.7 1.4 %shard_map.96 = (bf16[16,1920]{1,0:T(8,128)(2,1)S(1)}, bf16[16,1920]{1,0:T(8,128)(2,1)S(1)}, bf16[16,1920]{1,0:T(8,128)(2,1)S(1)}, bf16[16,1920]{1,0:T(8,128)(2,...) custom-call(f32[128,384]{1,0:T(8,128)S(1)} %get-tuple-element.98.see, ...), custom_call_target="tpu_custom_call" | custom-call | flops 16777216 | bytes 3604480 | tf_op jit(solution)/shard_map/pallas_call | solution.py:38
  90.3 1.8 %collective-permute-start.33 = (bf16[16,1920]{1,0:T(8,128)(2,1)S(1)}, bf16[16,1920]{1,0:T(8,128)(2,1)S(1)}, u32[]{:S(2)}, u32[]{:S(2)}) collective-permute-start(bf16[16,1920]{1,0:T(8,128)(2,1)S(1)} %get-tuple-element.108), channel_id=1, source_target_pairs={{0,3},{1,2},{2,1},{3,0},{4,7},{5,6},{6,5},{7,4},{8,11},{9,10},{10,... | collective-permute-start | bytes 184328 | tf_op jit(solution)/shard_map/ppermute | solution.py:498
  92.7 2.0 %collective-permute-start.35 = (bf16[16,1920]{1,0:T(8,128)(2,1)S(1)}, bf16[16,1920]{1,0:T(8,128)(2,1)S(1)}, u32[]{:S(2)}, u32[]{:S(2)}) collective-permute-start(bf16[16,1920]{1,0:T(8,128)(2,1)S(1)} %get-tuple-element.110), channel_id=1, source_target_pairs={{0,5},{1,4},{2,7},{3,6},{4,1},{5,0},{6,3},{7,2},{8,13},{9,12},{10,... | collective-permute-start | bytes 184328 | tf_op jit(solution)/shard_map/ppermute | solution.py:498
  95.1 1.8 %collective-permute-start.36 = (bf16[16,1920]{1,0:T(8,128)(2,1)S(1)}, bf16[16,1920]{1,0:T(8,128)(2,1)S(1)}, u32[]{:S(2)}, u32[]{:S(2)}) collective-permute-start(bf16[16,1920]{1,0:T(8,128)(2,1)S(1)} %get-tuple-element.111), channel_id=1, source_target_pairs={{0,6},{1,7},{2,4},{3,5},{4,2},{5,3},{6,0},{7,1},{8,14},{9,15},{10,... | collective-permute-start | bytes 184328 | tf_op jit(solution)/shard_map/ppermute | solution.py:498
  96.9 1.3 %collective-permute-start.37 = (bf16[16,1920]{1,0:T(8,128)(2,1)S(1)}, bf16[16,1920]{1,0:T(8,128)(2,1)S(1)}, u32[]{:S(2)}, u32[]{:S(2)}) collective-permute-start(bf16[16,1920]{1,0:T(8,128)(2,1)S(1)} %get-tuple-element.112), channel_id=1, source_target_pairs={{0,7},{1,6},{2,5},{3,4},{4,3},{5,2},{6,1},{7,0},{8,15},{9,14},{10,... | collective-permute-start | bytes 184328 | tf_op jit(solution)/shard_map/ppermute | solution.py:498
  98.3 1.3 %shard_map.94.w_ref = bf16[1536,1536]{1,0:T(8,128)(2,1)S(1)} custom-call(bf16[1536,3072]{1,0:T(8,128)(2,1)S(1)} %get-tuple-element.65.w_ref), custom_call_target="tpu_custom_call" | custom-call | flops 16777216 | bytes 14155776 | tf_op jit(solution)/shard_map/pallas_call | solution.py:38
  99.5 1.8 %shard_map.98.refs_8_ = f32[160,1536]{1,0:T(8,128)S(1)} custom-call(f32[160,1536]{1,0:T(8,128)S(1)} %get-tuple-element.113.slope_ref, bf16[1536,3072]{1,0:T(8,128)(2,1)S(1)} %get-tuple-element.65.w_ref, bf16[32,1920]{1,0:T(8,128)(2,1)S(1)} %get-tuple-element.114.refs_0_, bf16[32,1920]{1,0:T(8,128)(2,1)S(1)} %collective-permute-done.38.refs_1_, ...), custom_call_target="tpu_custom_call" | custom-call | flops 16777216 | bytes 12140544 | tf_op jit(solution)/shard_map/pallas_call | solution.py:38
  101.5 1.9 %collective-permute-done.35.refs_5_ = bf16[16,1920]{1,0:T(8,128)(2,1)S(1)} collective-permute-done((bf16[16,1920]{1,0:T(8,128)(2,1)S(1)}, bf16[16,1920]{1,0:T(8,128)(2,1)S(1)}, u32[]{:S(2)}, u32[]{:S(2)}) %collective-permute-start.35) | collective-permute-done | bytes 61472 | tf_op jit(solution)/shard_map/ppermute | solution.py:498
  103.4 1.2 %shard_map.99 = (bf16[16,1920]{1,0:T(8,128)(2,1)S(1)}, bf16[16,1920]{1,0:T(8,128)(2,1)S(1)}, bf16[16,1920]{1,0:T(8,128)(2,1)S(1)}, bf16[16,1920]{1,0:T(8,128)(2,...) custom-call(f32[160,1536]{1,0:T(8,128)S(1)} %get-tuple-element.97.sl, ...), custom_call_target="tpu_custom_call" | custom-call | flops 16777216 | bytes 7667712 | tf_op jit(solution)/shard_map/pallas_call | solution.py:38
  105.3 2.8 %collective-permute-start.43 = (bf16[16,1920]{1,0:T(8,128)(2,1)S(1)}, bf16[16,1920]{1,0:T(8,128)(2,1)S(1)}, u32[]{:S(2)}, u32[]{:S(2)}) collective-permute-start(bf16[16,1920]{1,0:T(8,128)(2,1)S(1)} %get-tuple-element.120), channel_id=1, source_target_pairs={{0,2},{1,3},{2,0},{3,1},{4,6},{5,7},{6,4},{7,5},{8,10},{9,11},{10,... | collective-permute-start | bytes 184328 | tf_op jit(solution)/shard_map/ppermute | solution.py:498
  108.1 1.9 %collective-permute-start.45 = (bf16[16,1920]{1,0:T(8,128)(2,1)S(1)}, bf16[16,1920]{1,0:T(8,128)(2,1)S(1)}, u32[]{:S(2)}, u32[]{:S(2)}) collective-permute-start(bf16[16,1920]{1,0:T(8,128)(2,1)S(1)} %get-tuple-element.122), channel_id=1, source_target_pairs={{0,4},{1,5},{2,6},{3,7},{4,0},{5,1},{6,2},{7,3},{8,12},{9,13},{10,... | collective-permute-start | bytes 184328 | tf_op jit(solution)/shard_map/ppermute | solution.py:498
  110.5 1.8 %collective-permute-start.47 = (bf16[16,1920]{1,0:T(8,128)(2,1)S(1)}, bf16[16,1920]{1,0:T(8,128)(2,1)S(1)}, u32[]{:S(2)}, u32[]{:S(2)}) collective-permute-start(bf16[16,1920]{1,0:T(8,128)(2,1)S(1)} %get-tuple-element.124), channel_id=1, source_target_pairs={{0,6},{1,7},{2,4},{3,5},{4,2},{5,3},{6,0},{7,1},{8,14},{9,15},{10,... | collective-permute-start | bytes 184328 | tf_op jit(solution)/shard_map/ppermute | solution.py:498
  112.3 2.0 %collective-permute-start.48 = (bf16[16,1920]{1,0:T(8,128)(2,1)S(1)}, bf16[16,1920]{1,0:T(8,128)(2,1)S(1)}, u32[]{:S(2)}, u32[]{:S(2)}) collective-permute-start(bf16[16,1920]{1,0:T(8,128)(2,1)S(1)} %get-tuple-element.125), channel_id=1, source_target_pairs={{0,7},{1,6},{2,5},{3,4},{4,3},{5,2},{6,1},{7,0},{8,15},{9,14},{10,... | collective-permute-start | bytes 184328 | tf_op jit(solution)/shard_map/ppermute | solution.py:498
  115.0 4.8 %collective-permute-done.46.refs_5_ = bf16[16,1920]{1,0:T(8,128)(2,1)S(1)} collective-permute-done((bf16[16,1920]{1,0:T(8,128)(2,1)S(1)}, bf16[16,1920]{1,0:T(8,128)(2,1)S(1)}, u32[]{:S(2)}, u32[]{:S(2)}) %collective-permute-start.46) | collective-permute-done | bytes 61472 | tf_op jit(solution)/shard_map/ppermute | solution.py:498
  119.9 1.2 %shard_map.100 = bf16[128,1536]{1,0:T(8,128)(2,1)} custom-call(bf16[5,128,128]{2,1,0:T(8,128)(2,1)S(1)} %get-tuple-element.64.rows_ref, bf16[128,1536]{1,0:T(8,128)(2,1)S(1)} %bitcast.7, f32[12,128]{1,0:T(8,128)S(1)} %bitcast.11, bf16[16,1920]{1,0:T(8,128)(2,1)S(1)} %get-tuple-element.118.refs_0_, bf16[16,1920]{1,0:T(8,128)(2,1)S(1)} %collective-permute-done.42.refs_1_, ...), custom_call_target="tpu_custom_call" | custom-call | flops 16777216 | bytes 1447936 | tf_op jit(solution)/shard_map/pallas_call | solution.py:38
  (77 shorter events, 10.7 us)
Async XLA Ops:
  2.2 4.5 %collective-permute-start = (bf16[16,1920]{1,0:T(8,128)(2,1)S(1)}, bf16[16,1920]{1,0:T(8,128)(2,1)S(1)}, u32[]{:S(2)}, u32[]{:S(2)}) collective-permute-start(bf16[16,1920]{1,0:T(8,128)(2,1)S(1)} %get-tuple-element.67), channel_id=1, source_target_pairs={{0,1},{1,0},{2,3},{3,2},{4,5},{5,4},{6,7},{7,6},{8,9},{9,8},{10,11... | collective-permute-start | bytes 184328 | tf_op jit(solution)/shard_map/ppermute | solution.py:498
  2.3 8.1 %collective-permute-start.1 = (bf16[16,1920]{1,0:T(8,128)(2,1)S(1)}, bf16[16,1920]{1,0:T(8,128)(2,1)S(1)}, u32[]{:S(2)}, u32[]{:S(2)}) collective-permute-start(bf16[16,1920]{1,0:T(8,128)(2,1)S(1)} %get-tuple-element.68), channel_id=1, source_target_pairs={{0,2},{1,3},{2,0},{3,1},{4,6},{5,7},{6,4},{7,5},{8,10},{9,11},{10,... | collective-permute-start | bytes 184328 | tf_op jit(solution)/shard_map/ppermute | solution.py:498
  3.9 11.2 %collective-permute-start.2 = (bf16[16,1920]{1,0:T(8,128)(2,1)S(1)}, bf16[16,1920]{1,0:T(8,128)(2,1)S(1)}, u32[]{:S(2)}, u32[]{:S(2)}) collective-permute-start(bf16[16,1920]{1,0:T(8,128)(2,1)S(1)} %get-tuple-element.69), channel_id=1, source_target_pairs={{0,3},{1,2},{2,1},{3,0},{4,7},{5,6},{6,5},{7,4},{8,11},{9,10},{10,... | collective-permute-start | bytes 184328 | tf_op jit(solution)/shard_map/ppermute | solution.py:498
  4.1 11.0 %collective-permute-start.3 = (bf16[16,1920]{1,0:T(8,128)(2,1)S(1)}, bf16[16,1920]{1,0:T(8,128)(2,1)S(1)}, u32[]{:S(2)}, u32[]{:S(2)}) collective-permute-start(bf16[16,1920]{1,0:T(8,128)(2,1)S(1)} %get-tuple-element.70), channel_id=1, source_target_pairs={{0,4},{1,5},{2,6},{3,7},{4,0},{5,1},{6,2},{7,3},{8,12},{9,13},{10,... | collective-permute-start | bytes 184328 | tf_op jit(solution)/shard_map/ppermute | solution.py:498
  6.7 10.1 %collective-permute-start.4 = (bf16[16,1920]{1,0:T(8,128)(2,1)S(1)}, bf16[16,1920]{1,0:T(8,128)(2,1)S(1)}, u32[]{:S(2)}, u32[]{:S(2)}) collective-permute-start(bf16[16,1920]{1,0:T(8,128)(2,1)S(1)} %get-tuple-element.71), channel_id=1, source_target_pairs={{0,5},{1,4},{2,7},{3,6},{4,1},{5,0},{6,3},{7,2},{8,13},{9,12},{10,... | collective-permute-start | bytes 184328 | tf_op jit(solution)/shard_map/ppermute | solution.py:498
  6.7 10.1 %collective-permute-start.5 = (bf16[16,1920]{1,0:T(8,128)(2,1)S(1)}, bf16[16,1920]{1,0:T(8,128)(2,1)S(1)}, u32[]{:S(2)}, u32[]{:S(2)}) collective-permute-start(bf16[16,1920]{1,0:T(8,128)(2,1)S(1)} %get-tuple-element.72), channel_id=1, source_target_pairs={{0,6},{1,7},{2,4},{3,5},{4,2},{5,3},{6,0},{7,1},{8,14},{9,15},{10,... | collective-permute-start | bytes 184328 | tf_op jit(solution)/shard_map/ppermute | solution.py:498
  10.3 6.5 %collective-permute-start.6 = (bf16[16,1920]{1,0:T(8,128)(2,1)S(1)}, bf16[16,1920]{1,0:T(8,128)(2,1)S(1)}, u32[]{:S(2)}, u32[]{:S(2)}) collective-permute-start(bf16[16,1920]{1,0:T(8,128)(2,1)S(1)} %get-tuple-element.73), channel_id=1, source_target_pairs={{0,7},{1,6},{2,5},{3,4},{4,3},{5,2},{6,1},{7,0},{8,15},{9,14},{10,... | collective-permute-start | bytes 184328 | tf_op jit(solution)/shard_map/ppermute | solution.py:498
  18.1 6.1 %collective-permute-start.14 = (bf16[16,1920]{1,0:T(8,128)(2,1)S(1)}, bf16[16,1920]{1,0:T(8,128)(2,1)S(1)}, u32[]{:S(2)}, u32[]{:S(2)}) collective-permute-start(bf16[16,1920]{1,0:T(8,128)(2,1)S(1)} %get-tuple-element.87), channel_id=1, source_target_pairs={{0,1},{1,0},{2,3},{3,2},{4,5},{5,4},{6,7},{7,6},{8,9},{9,8},{10,11... | collective-permute-start | bytes 184328 | tf_op jit(solution)/shard_map/ppermute | solution.py:498
  18.3 8.1 %collective-permute-start.15 = (bf16[16,1920]{1,0:T(8,128)(2,1)S(1)}, bf16[16,1920]{1,0:T(8,128)(2,1)S(1)}, u32[]{:S(2)}, u32[]{:S(2)}) collective-permute-start(bf16[16,1920]{1,0:T(8,128)(2,1)S(1)} %get-tuple-element.88), channel_id=1, source_target_pairs={{0,2},{1,3},{2,0},{3,1},{4,6},{5,7},{6,4},{7,5},{8,10},{9,11},{10,... | collective-permute-start | bytes 184328 | tf_op jit(solution)/shard_map/ppermute | solution.py:498
  21.5 6.2 %collective-permute-start.16 = (bf16[16,1920]{1,0:T(8,128)(2,1)S(1)}, bf16[16,1920]{1,0:T(8,128)(2,1)S(1)}, u32[]{:S(2)}, u32[]{:S(2)}) collective-permute-start(bf16[16,1920]{1,0:T(8,128)(2,1)S(1)} %get-tuple-element.89), channel_id=1, source_target_pairs={{0,3},{1,2},{2,1},{3,0},{4,7},{5,6},{6,5},{7,4},{8,11},{9,10},{10,... | collective-permute-start | bytes 184328 | tf_op jit(solution)/shard_map/ppermute | solution.py:498
  21.5 6.2 %collective-permute-start.17 = (bf16[16,1920]{1,0:T(8,128)(2,1)S(1)}, bf16[16,1920]{1,0:T(8,128)(2,1)S(1)}, u32[]{:S(2)}, u32[]{:S(2)}) collective-permute-start(bf16[16,1920]{1,0:T(8,128)(2,1)S(1)} %get-tuple-element.90), channel_id=1, source_target_pairs={{0,4},{1,5},{2,6},{3,7},{4,0},{5,1},{6,2},{7,3},{8,12},{9,13},{10,... | collective-permute-start | bytes 184328 | tf_op jit(solution)/shard_map/ppermute | solution.py:498
  24.2 9.9 %collective-permute-start.18 = (bf16[16,1920]{1,0:T(8,128)(2,1)S(1)}, bf16[16,1920]{1,0:T(8,128)(2,1)S(1)}, u32[]{:S(2)}, u32[]{:S(2)}) collective-permute-start(bf16[16,1920]{1,0:T(8,128)(2,1)S(1)} %get-tuple-element.91), channel_id=1, source_target_pairs={{0,5},{1,4},{2,7},{3,6},{4,1},{5,0},{6,3},{7,2},{8,13},{9,12},{10,... | collective-permute-start | bytes 184328 | tf_op jit(solution)/shard_map/ppermute | solution.py:498
  24.2 9.9 %collective-permute-start.19 = (bf16[16,1920]{1,0:T(8,128)(2,1)S(1)}, bf16[16,1920]{1,0:T(8,128)(2,1)S(1)}, u32[]{:S(2)}, u32[]{:S(2)}) collective-permute-start(bf16[16,1920]{1,0:T(8,128)(2,1)S(1)} %get-tuple-element.92), channel_id=1, source_target_pairs={{0,6},{1,7},{2,4},{3,5},{4,2},{5,3},{6,0},{7,1},{8,14},{9,15},{10,... | collective-permute-start | bytes 184328 | tf_op jit(solution)/shard_map/ppermute | solution.py:498
  26.4 7.7 %collective-permute-start.20 = (bf16[16,1920]{1,0:T(8,128)(2,1)S(1)}, bf16[16,1920]{1,0:T(8,128)(2,1)S(1)}, u32[]{:S(2)}, u32[]{:S(2)}) collective-permute-start(bf16[16,1920]{1,0:T(8,128)(2,1)S(1)} %get-tuple-element.93), channel_id=1, source_target_pairs={{0,7},{1,6},{2,5},{3,4},{4,3},{5,2},{6,1},{7,0},{8,15},{9,14},{10,... | collective-permute-start | bytes 184328 | tf_op jit(solution)/shard_map/ppermute | solution.py:498
  34.4 18.6 %collective-permute-start.24 = (bf16[128,768]{1,0:T(8,128)(2,1)S(1)}, bf16[128,768]{1,0:T(8,128)(2,1)S(1)}, u32[]{:S(2)}, u32[]{:S(2)}) collective-permute-start(bf16[128,768]{1,0:T(8,128)(2,1)S(1)} %get-tuple-element.95.refs_3_.key_ref), channel_id=1, source_target_pairs={{16,0},{24,8},{0,16},{8,24},{17,1},{25,9},{1,17},{9,25},{18,2},{26... | collective-permute-start | bytes 589832 | tf_op jit(solution)/shard_map/ppermute | solution.py:505
  37.8 6.7 %collective-permute-start.10 = (bf16[16,1920]{1,0:T(8,128)(2,1)S(1)}, bf16[16,1920]{1,0:T(8,128)(2,1)S(1)}, u32[]{:S(2)}, u32[]{:S(2)}) collective-permute-start(bf16[16,1920]{1,0:T(8,128)(2,1)S(1)} %get-tuple-element.79), channel_id=1, source_target_pairs={{0,4},{1,5},{2,6},{3,7},{4,0},{5,1},{6,2},{7,3},{8,12},{9,13},{10,... | collective-permute-start | bytes 184328 | tf_op jit(solution)/shard_map/ppermute | solution.py:498
  41.2 9.3 %collective-permute-start.11 = (bf16[16,1920]{1,0:T(8,128)(2,1)S(1)}, bf16[16,1920]{1,0:T(8,128)(2,1)S(1)}, u32[]{:S(2)}, u32[]{:S(2)}) collective-permute-start(bf16[16,1920]{1,0:T(8,128)(2,1)S(1)} %get-tuple-element.80), channel_id=1, source_target_pairs={{0,5},{1,4},{2,7},{3,6},{4,1},{5,0},{6,3},{7,2},{8,13},{9,12},{10,... | collective-permute-start | bytes 184328 | tf_op jit(solution)/shard_map/ppermute | solution.py:498
  41.2 9.8 %collective-permute-start.12 = (bf16[16,1920]{1,0:T(8,128)(2,1)S(1)}, bf16[16,1920]{1,0:T(8,128)(2,1)S(1)}, u32[]{:S(2)}, u32[]{:S(2)}) collective-permute-start(bf16[16,1920]{1,0:T(8,128)(2,1)S(1)} %get-tuple-element.81), channel_id=1, source_target_pairs={{0,6},{1,7},{2,4},{3,5},{4,2},{5,3},{6,0},{7,1},{8,14},{9,15},{10,... | collective-permute-start | bytes 184328 | tf_op jit(solution)/shard_map/ppermute | solution.py:498
  43.5 9.0 %collective-permute-start.13 = (bf16[16,1920]{1,0:T(8,128)(2,1)S(1)}, bf16[16,1920]{1,0:T(8,128)(2,1)S(1)}, u32[]{:S(2)}, u32[]{:S(2)}) collective-permute-start(bf16[16,1920]{1,0:T(8,128)(2,1)S(1)} %get-tuple-element.82), channel_id=1, source_target_pairs={{0,7},{1,6},{2,5},{3,4},{4,3},{5,2},{6,1},{7,0},{8,15},{9,14},{10,... | collective-permute-start | bytes 184328 | tf_op jit(solution)/shard_map/ppermute | solution.py:498
  44.5 10.0 %collective-permute-start.7 = (bf16[16,1920]{1,0:T(8,128)(2,1)S(1)}, bf16[16,1920]{1,0:T(8,128)(2,1)S(1)}, u32[]{:S(2)}, u32[]{:S(2)}) collective-permute-start(bf16[16,1920]{1,0:T(8,128)(2,1)S(1)} %get-tuple-element.76), channel_id=1, source_target_pairs={{0,1},{1,0},{2,3},{3,2},{4,5},{5,4},{6,7},{7,6},{8,9},{9,8},{10,11... | collective-permute-start | bytes 184328 | tf_op jit(solution)/shard_map/ppermute | solution.py:498
  50.5 13.4 %collective-permute-start.21 = (bf16[128,768]{1,0:T(8,128)(2,1)S(1)}, bf16[128,768]{1,0:T(8,128)(2,1)S(1)}, u32[]{:S(2)}, u32[]{:S(2)}) collective-permute-start(bf16[128,768]{1,0:T(8,128)(2,1)S(1)} %get-tuple-element.94.refs_0_.value_ref), channel_id=1, source_target_pairs={{24,0},{0,8},{8,16},{16,24},{25,1},{1,9},{9,17},{17,25},{26,2},{2,... | collective-permute-start | bytes 589832 | tf_op jit(solution)/shard_map/ppermute | solution.py:505
  50.9 12.9 %collective-permute-start.22 = (bf16[128,768]{1,0:T(8,128)(2,1)S(1)}, bf16[128,768]{1,0:T(8,128)(2,1)S(1)}, u32[]{:S(2)}, u32[]{:S(2)}) collective-permute-start(bf16[128,768]{1,0:T(8,128)(2,1)S(1)} %get-tuple-element.94.refs_0_.value_ref), channel_id=1, source_target_pairs={{16,0},{24,8},{0,16},{8,24},{17,1},{25,9},{1,17},{9,25},{18,2},{26... | collective-permute-start | bytes 589832 | tf_op jit(solution)/shard_map/ppermute | solution.py:505
  52.5 11.3 %collective-permute-start.23 = (bf16[128,768]{1,0:T(8,128)(2,1)S(1)}, bf16[128,768]{1,0:T(8,128)(2,1)S(1)}, u32[]{:S(2)}, u32[]{:S(2)}) collective-permute-start(bf16[128,768]{1,0:T(8,128)(2,1)S(1)} %get-tuple-element.95.refs_3_.key_ref), channel_id=1, source_target_pairs={{0,8},{8,0},{16,24},{24,16},{1,9},{9,1},{17,25},{25,17},{2,10},{10... | collective-permute-start | bytes 589832 | tf_op jit(solution)/shard_map/ppermute | solution.py:311
  53.0 12.8 %collective-permute-start.25 = (bf16[128,768]{1,0:T(8,128)(2,1)S(1)}, bf16[128,768]{1,0:T(8,128)(2,1)S(1)}, u32[]{:S(2)}, u32[]{:S(2)}) collective-permute-start(bf16[128,768]{1,0:T(8,128)(2,1)S(1)} %collective-permute-done.24.refs_5_), channel_id=1, source_target_pairs={{0,8},{8,0},{16,24},{24,16},{1,9},{9,1},{17,25},{25,17},{2,10},{10... | collective-permute-start | bytes 589832 | tf_op jit(solution)/shard_map/ppermute | solution.py:312
  54.5 4.2 %collective-permute-start.8 = (bf16[16,1920]{1,0:T(8,128)(2,1)S(1)}, bf16[16,1920]{1,0:T(8,128)(2,1)S(1)}, u32[]{:S(2)}, u32[]{:S(2)}) collective-permute-start(bf16[16,1920]{1,0:T(8,128)(2,1)S(1)} %get-tuple-element.77), channel_id=1, source_target_pairs={{0,2},{1,3},{2,0},{3,1},{4,6},{5,7},{6,4},{7,5},{8,10},{9,11},{10,... | collective-permute-start | bytes 184328 | tf_op jit(solution)/shard_map/ppermute | solution.py:498
  58.7 4.0 %collective-permute-start.9 = (bf16[16,1920]{1,0:T(8,128)(2,1)S(1)}, bf16[16,1920]{1,0:T(8,128)(2,1)S(1)}, u32[]{:S(2)}, u32[]{:S(2)}) collective-permute-start(bf16[16,1920]{1,0:T(8,128)(2,1)S(1)} %get-tuple-element.78), channel_id=1, source_target_pairs={{0,3},{1,2},{2,1},{3,0},{4,7},{5,6},{6,5},{7,4},{8,11},{9,10},{10,... | collective-permute-start | bytes 184328 | tf_op jit(solution)/shard_map/ppermute | solution.py:498
  63.1 10.7 %collective-permute-start.26 = (bf16[128,768]{1,0:T(8,128)(2,1)S(1)}, bf16[128,768]{1,0:T(8,128)(2,1)S(1)}, u32[]{:S(2)}, u32[]{:S(2)}) collective-permute-start(bf16[128,768]{1,0:T(8,128)(2,1)S(1)} %get-tuple-element.85.query_ref), channel_id=1, source_target_pairs={{16,0},{24,8},{0,16},{8,24},{17,1},{25,9},{1,17},{9,25},{18,2},{26... | collective-permute-start | bytes 589832 | tf_op jit(solution)/shard_map/ppermute | solution.py:505
  68.8 6.5 %collective-permute-start.38 = (bf16[32,1920]{1,0:T(8,128)(2,1)S(1)}, bf16[32,1920]{1,0:T(8,128)(2,1)S(1)}, u32[]{:S(2)}, u32[]{:S(2)}) collective-permute-start(bf16[32,1920]{1,0:T(8,128)(2,1)S(1)} %get-tuple-element.115), channel_id=1, source_target_pairs={{0,2},{1,3},{2,0},{3,1},{4,6},{5,7},{6,4},{7,5},{8,10},{9,11},{10,... | collective-permute-start | bytes 368648 | tf_op jit(solution)/shard_map/ppermute | solution.py:498
  68.9 12.0 %collective-permute-start.39 = (bf16[32,1920]{1,0:T(8,128)(2,1)S(1)}, bf16[32,1920]{1,0:T(8,128)(2,1)S(1)}, u32[]{:S(2)}, u32[]{:S(2)}) collective-permute-start(bf16[32,1920]{1,0:T(8,128)(2,1)S(1)} %get-tuple-element.116), channel_id=1, source_target_pairs={{0,4},{1,5},{2,6},{3,7},{4,0},{5,1},{6,2},{7,3},{8,12},{9,13},{10,... | collective-permute-start | bytes 368648 | tf_op jit(solution)/shard_map/ppermute | solution.py:498
  71.2 10.3 %collective-permute-start.40 = (bf16[32,1920]{1,0:T(8,128)(2,1)S(1)}, bf16[32,1920]{1,0:T(8,128)(2,1)S(1)}, u32[]{:S(2)}, u32[]{:S(2)}) collective-permute-start(bf16[32,1920]{1,0:T(8,128)(2,1)S(1)} %get-tuple-element.117), channel_id=1, source_target_pairs={{0,6},{1,7},{2,4},{3,5},{4,2},{5,3},{6,0},{7,1},{8,14},{9,15},{10,... | collective-permute-start | bytes 368648 | tf_op jit(solution)/shard_map/ppermute | solution.py:498
  73.3 9.6 %collective-permute-start.29 = (bf16[128,768]{1,0:T(8,128)(2,1)S(1)}, bf16[128,768]{1,0:T(8,128)(2,1)S(1)}, u32[]{:S(2)}, u32[]{:S(2)}) collective-permute-start(bf16[128,768]{1,0:T(8,128)(2,1)S(1)} %get-tuple-element.85.query_ref), channel_id=1, source_target_pairs={{0,8},{8,0},{16,24},{24,16},{1,9},{9,1},{17,25},{25,17},{2,10},{10... | collective-permute-start | bytes 589832 | tf_op jit(solution)/shard_map/ppermute | solution.py:320
  73.8 11.0 %collective-permute-start.30 = (bf16[128,768]{1,0:T(8,128)(2,1)S(1)}, bf16[128,768]{1,0:T(8,128)(2,1)S(1)}, u32[]{:S(2)}, u32[]{:S(2)}) collective-permute-start(bf16[128,768]{1,0:T(8,128)(2,1)S(1)} %collective-permute-done.26.refs_0_.refs_7_), channel_id=1, source_target_pairs={{0,8},{8,0},{16,24},{24,16},{1,9},{9,1},{17,25},{25,17},{2,10},{10... | collective-permute-start | bytes 589832 | tf_op jit(solution)/shard_map/ppermute | solution.py:321
  75.3 11.6 %collective-permute-start.27 = (bf16[128,768]{1,0:T(8,128)(2,1)S(1)}, bf16[128,768]{1,0:T(8,128)(2,1)S(1)}, u32[]{:S(2)}, u32[]{:S(2)}) collective-permute-start(bf16[128,768]{1,0:T(8,128)(2,1)S(1)} %get-tuple-element.100.grad_ref), channel_id=1, source_target_pairs={{8,0},{16,8},{24,16},{0,24},{9,1},{17,9},{25,17},{1,25},{10,2},{18... | collective-permute-start | bytes 589832 | tf_op jit(solution)/shard_map/ppermute | solution.py:505
  80.9 7.8 %collective-permute-start.28 = (bf16[128,768]{1,0:T(8,128)(2,1)S(1)}, bf16[128,768]{1,0:T(8,128)(2,1)S(1)}, u32[]{:S(2)}, u32[]{:S(2)}) collective-permute-start(bf16[128,768]{1,0:T(8,128)(2,1)S(1)} %get-tuple-element.100.grad_ref), channel_id=1, source_target_pairs={{16,0},{24,8},{0,16},{8,24},{17,1},{25,9},{1,17},{9,25},{18,2},{26... | collective-permute-start | bytes 589832 | tf_op jit(solution)/shard_map/ppermute | solution.py:505
  81.5 15.4 %collective-permute-start.41 = (bf16[64,1920]{1,0:T(8,128)(2,1)S(1)}, bf16[64,1920]{1,0:T(8,128)(2,1)S(1)}, u32[]{:S(2)}, u32[]{:S(2)}) collective-permute-start(bf16[64,1920]{1,0:T(8,128)(2,1)S(1)} %pad_maximum_fusion), channel_id=1, source_target_pairs={{0,1},{1,0},{2,3},{3,2},{4,5},{5,4},{6,7},{7,6},{8,9},{9,8},{10,11... | collective-permute-start | bytes 737288 | tf_op jit(solution)/shard_map/ppermute | solution.py:485
  90.2 4.9 %collective-permute-start.32 = (bf16[16,1920]{1,0:T(8,128)(2,1)S(1)}, bf16[16,1920]{1,0:T(8,128)(2,1)S(1)}, u32[]{:S(2)}, u32[]{:S(2)}) collective-permute-start(bf16[16,1920]{1,0:T(8,128)(2,1)S(1)} %get-tuple-element.107), channel_id=1, source_target_pairs={{0,2},{1,3},{2,0},{3,1},{4,6},{5,7},{6,4},{7,5},{8,10},{9,11},{10,... | collective-permute-start | bytes 184328 | tf_op jit(solution)/shard_map/ppermute | solution.py:498
  90.3 11.1 %collective-permute-start.33 = (bf16[16,1920]{1,0:T(8,128)(2,1)S(1)}, bf16[16,1920]{1,0:T(8,128)(2,1)S(1)}, u32[]{:S(2)}, u32[]{:S(2)}) collective-permute-start(bf16[16,1920]{1,0:T(8,128)(2,1)S(1)} %get-tuple-element.108), channel_id=1, source_target_pairs={{0,3},{1,2},{2,1},{3,0},{4,7},{5,6},{6,5},{7,4},{8,11},{9,10},{10,... | collective-permute-start | bytes 184328 | tf_op jit(solution)/shard_map/ppermute | solution.py:498
  92.0 9.5 %collective-permute-start.34 = (bf16[16,1920]{1,0:T(8,128)(2,1)S(1)}, bf16[16,1920]{1,0:T(8,128)(2,1)S(1)}, u32[]{:S(2)}, u32[]{:S(2)}) collective-permute-start(bf16[16,1920]{1,0:T(8,128)(2,1)S(1)} %get-tuple-element.109), channel_id=1, source_target_pairs={{0,4},{1,5},{2,6},{3,7},{4,0},{5,1},{6,2},{7,3},{8,12},{9,13},{10,... | collective-permute-start | bytes 184328 | tf_op jit(solution)/shard_map/ppermute | solution.py:498
  92.7 10.8 %collective-permute-start.35 = (bf16[16,1920]{1,0:T(8,128)(2,1)S(1)}, bf16[16,1920]{1,0:T(8,128)(2,1)S(1)}, u32[]{:S(2)}, u32[]{:S(2)}) collective-permute-start(bf16[16,1920]{1,0:T(8,128)(2,1)S(1)} %get-tuple-element.110), channel_id=1, source_target_pairs={{0,5},{1,4},{2,7},{3,6},{4,1},{5,0},{6,3},{7,2},{8,13},{9,12},{10,... | collective-permute-start | bytes 184328 | tf_op jit(solution)/shard_map/ppermute | solution.py:498
  95.1 8.3 %collective-permute-start.36 = (bf16[16,1920]{1,0:T(8,128)(2,1)S(1)}, bf16[16,1920]{1,0:T(8,128)(2,1)S(1)}, u32[]{:S(2)}, u32[]{:S(2)}) collective-permute-start(bf16[16,1920]{1,0:T(8,128)(2,1)S(1)} %get-tuple-element.111), channel_id=1, source_target_pairs={{0,6},{1,7},{2,4},{3,5},{4,2},{5,3},{6,0},{7,1},{8,14},{9,15},{10,... | collective-permute-start | bytes 184328 | tf_op jit(solution)/shard_map/ppermute | solution.py:498
  96.9 6.5 %collective-permute-start.37 = (bf16[16,1920]{1,0:T(8,128)(2,1)S(1)}, bf16[16,1920]{1,0:T(8,128)(2,1)S(1)}, u32[]{:S(2)}, u32[]{:S(2)}) collective-permute-start(bf16[16,1920]{1,0:T(8,128)(2,1)S(1)} %get-tuple-element.112), channel_id=1, source_target_pairs={{0,7},{1,6},{2,5},{3,4},{4,3},{5,2},{6,1},{7,0},{8,15},{9,14},{10,... | collective-permute-start | bytes 184328 | tf_op jit(solution)/shard_map/ppermute | solution.py:498
  104.7 5.8 %collective-permute-start.42 = (bf16[16,1920]{1,0:T(8,128)(2,1)S(1)}, bf16[16,1920]{1,0:T(8,128)(2,1)S(1)}, u32[]{:S(2)}, u32[]{:S(2)}) collective-permute-start(bf16[16,1920]{1,0:T(8,128)(2,1)S(1)} %get-tuple-element.119), channel_id=1, source_target_pairs={{0,1},{1,0},{2,3},{3,2},{4,5},{5,4},{6,7},{7,6},{8,9},{9,8},{10,11... | collective-permute-start | bytes 184328 | tf_op jit(solution)/shard_map/ppermute | solution.py:498
  105.3 7.0 %collective-permute-start.43 = (bf16[16,1920]{1,0:T(8,128)(2,1)S(1)}, bf16[16,1920]{1,0:T(8,128)(2,1)S(1)}, u32[]{:S(2)}, u32[]{:S(2)}) collective-permute-start(bf16[16,1920]{1,0:T(8,128)(2,1)S(1)} %get-tuple-element.120), channel_id=1, source_target_pairs={{0,2},{1,3},{2,0},{3,1},{4,6},{5,7},{6,4},{7,5},{8,10},{9,11},{10,... | collective-permute-start | bytes 184328 | tf_op jit(solution)/shard_map/ppermute | solution.py:498
  108.1 6.9 %collective-permute-start.44 = (bf16[16,1920]{1,0:T(8,128)(2,1)S(1)}, bf16[16,1920]{1,0:T(8,128)(2,1)S(1)}, u32[]{:S(2)}, u32[]{:S(2)}) collective-permute-start(bf16[16,1920]{1,0:T(8,128)(2,1)S(1)} %get-tuple-element.121), channel_id=1, source_target_pairs={{0,3},{1,2},{2,1},{3,0},{4,7},{5,6},{6,5},{7,4},{8,11},{9,10},{10,... | collective-permute-start | bytes 184328 | tf_op jit(solution)/shard_map/ppermute | solution.py:498
  108.1 6.9 %collective-permute-start.45 = (bf16[16,1920]{1,0:T(8,128)(2,1)S(1)}, bf16[16,1920]{1,0:T(8,128)(2,1)S(1)}, u32[]{:S(2)}, u32[]{:S(2)}) collective-permute-start(bf16[16,1920]{1,0:T(8,128)(2,1)S(1)} %get-tuple-element.122), channel_id=1, source_target_pairs={{0,4},{1,5},{2,6},{3,7},{4,0},{5,1},{6,2},{7,3},{8,12},{9,13},{10,... | collective-permute-start | bytes 184328 | tf_op jit(solution)/shard_map/ppermute | solution.py:498
  110.0 9.9 %collective-permute-start.46 = (bf16[16,1920]{1,0:T(8,128)(2,1)S(1)}, bf16[16,1920]{1,0:T(8,128)(2,1)S(1)}, u32[]{:S(2)}, u32[]{:S(2)}) collective-permute-start(bf16[16,1920]{1,0:T(8,128)(2,1)S(1)} %get-tuple-element.123), channel_id=1, source_target_pairs={{0,5},{1,4},{2,7},{3,6},{4,1},{5,0},{6,3},{7,2},{8,13},{9,12},{10,... | collective-permute-start | bytes 184328 | tf_op jit(solution)/shard_map/ppermute | solution.py:498
  110.5 9.4 %collective-permute-start.47 = (bf16[16,1920]{1,0:T(8,128)(2,1)S(1)}, bf16[16,1920]{1,0:T(8,128)(2,1)S(1)}, u32[]{:S(2)}, u32[]{:S(2)}) collective-permute-start(bf16[16,1920]{1,0:T(8,128)(2,1)S(1)} %get-tuple-element.124), channel_id=1, source_target_pairs={{0,6},{1,7},{2,4},{3,5},{4,2},{5,3},{6,0},{7,1},{8,14},{9,15},{10,... | collective-permute-start | bytes 184328 | tf_op jit(solution)/shard_map/ppermute | solution.py:498
  112.3 7.6 %collective-permute-start.48 = (bf16[16,1920]{1,0:T(8,128)(2,1)S(1)}, bf16[16,1920]{1,0:T(8,128)(2,1)S(1)}, u32[]{:S(2)}, u32[]{:S(2)}) collective-permute-start(bf16[16,1920]{1,0:T(8,128)(2,1)S(1)} %get-tuple-element.125), channel_id=1, source_target_pairs={{0,7},{1,6},{2,5},{3,4},{4,3},{5,2},{6,1},{7,0},{8,15},{9,14},{10,... | collective-permute-start | bytes 184328 | tf_op jit(solution)/shard_map/ppermute | solution.py:498
  (4 other events, 92.2 us)
